TPU v7x, 32 devices: a whole 2x2x4 slice. The times are simulated.
32 devices in a mesh: gx: 4 (over z), gy: 8 (over y, x, core).
Axes of the slice: x: 2, y: 2, z: 4, core: 2. Of those that a mesh axis runs over, the one named last changes fastest.
Arguments:
- start_block: float32 [4, 8, 128, 16, 128], P('gx', 'gy'), may hold values from -6 to 6
- slot_tiles: float32 [8, 128, 128], replicated, may hold values from -0.1875 to 0.1875
- edge_weights: float32 [4, 8, 128, 8], P('gx', 'gy'), may hold values from 0.3 to 3
- block_columns: int32 [4, 8, 128, 8], P('gx', 'gy'), may hold values from 0 to 159
- halo_sends: int32 [4, 8, 4, 8], P('gx', 'gy'), may hold values from 0 to 127
- split_side: int32 [4, 8, 128], P('gx', 'gy'), may hold values from 0 to 1, as said below
Outputs:
- moved_basis: float32 [4, 8, 128, 16, 128], P('gx', 'gy')
- moved_weights: float32 [4, 8, 128, 8], P('gx', 'gy')
- moved_columns: int32 [4, 8, 128, 8], P('gx', 'gy')
- rayleigh: float32 [16, 16], replicated
Inputs may be any that keep to these rules, and one draw needn't show every extreme that they name: `split_side`: over each pair of partners exactly 128 block rows have each side; some subdomain gives all 128 of its block rows to its partner.
All inputs are finite; a program needn't handle non-finite values.
Results may differ from a plain program's by a relative error of at most 0.0003.
Values sent between devices are 32-bit elements; how exact they have to be, the bound alone decides.
No kernel may reach another device: no remote copies, remote signals or barrier semaphores. Data moves between devices by JAX's collectives and lax.ppermute only.
A program may use at most 64 MiB of HBM per device.

v0:
```python
import functools

import jax
import jax.numpy as jnp
from jax import lax
from jax.experimental import pallas as pl
from jax.experimental.pallas import tpu as pltpu
from jax.sharding import PartitionSpec as P

F32 = jnp.float32
BF16 = jnp.bfloat16
AXES = ("gx", "gy")
CHUNKS = 4
VMEM = pl.BlockSpec(memory_space=pltpu.VMEM)
SMEM = pl.BlockSpec(memory_space=pltpu.SMEM)
ANY = pl.BlockSpec(memory_space=pl.ANY)
VMEM_LIMIT = 40 << 20


def split(x):
    high = x.astype(BF16)
    return high, (x - high.astype(F32)).astype(BF16)


def lane_group(rows, cols):
    return lax.broadcasted_iota(jnp.int32, (rows, 128), 1) // cols


def spread(x, cols):
    width = 64
    while width >= cols:
        x = x + pltpu.roll(x, width, 1)
        width //= 2
    return x


def unpack(packed, cols):
    half = 128 // cols
    sub = lax.broadcasted_iota(jnp.int32, (half, 128), 0)
    own = lane_group(half, cols) == sub
    parts = []
    for start in range(0, cols, half):
        row = packed[:, start * cols : start * cols + 128]
        parts.append(spread(jnp.where(own, jnp.broadcast_to(row, (half, 128)), 0.0), cols))
    return jnp.concatenate(parts, 0)


def pack(tiled, cols):
    half = 128 // cols
    sub = lax.broadcasted_iota(jnp.int32, (half, 128), 0)
    own = lane_group(half, cols) == sub
    rows = []
    for start in range(0, cols, half):
        part = jnp.where(own, tiled[start : start + half], 0.0)
        rows.append(jnp.sum(part, 0, keepdims=True))
    return jnp.concatenate(rows, 1)


def identity(cols):
    lane = lax.broadcasted_iota(jnp.int32, (cols, 128), 1) % cols
    return (lane == lax.broadcasted_iota(jnp.int32, (cols, 128), 0)).astype(F32)


def eliminate(gram, right):
    cols = gram.shape[0]
    row = lax.broadcasted_iota(jnp.int32, (cols, 128), 0)
    for j in range(cols):
        inv = lax.rsqrt(gram[j : j + 1, j : j + 1])
        factor = gram[:, j : j + 1] * inv
        gram_row = gram[j : j + 1, :] * inv
        right_row = right[j : j + 1, :] * inv
        below = row > j
        gram = jnp.where(below, gram - factor * gram_row, gram)
        right = jnp.where(
            below, right - factor * right_row, jnp.where(row == j, right_row, right)
        )
    return right


def scaler(small):
    cols = small.shape[0]
    group = lane_group(cols, cols)
    diag = jnp.concatenate(
        [jnp.where(group == g, small, 0.0) for g in range(128 // cols)], 0
    )
    high, low = split(diag)
    return jnp.concatenate(
        [jnp.concatenate([high, high], 1), jnp.concatenate([low, low], 1)], 0
    )


def apply_scaler(left, x):
    high, low = split(x)
    both = jnp.dot(left, jnp.concatenate([high, low], 0), preferred_element_type=F32)
    return both[:128] + both[128:]


def stacked(groups):
    pairs = [split(x) for x in groups]
    return jnp.concatenate(
        [
            jnp.concatenate([p[0] for p in pairs], 1),
            jnp.concatenate([p[1] for p in pairs], 1),
        ],
        0,
    )


def inner(a, b, cols):
    full = lax.dot_general(a, b, (((1,), (1,)), ((), ())), preferred_element_type=F32)
    half = full[:128] + full[128:]
    square = half[:, :128] + half[:, 128:]
    group = lane_group(cols, cols)
    total = jnp.zeros((cols, 128), F32)
    for g in range(128 // cols):
        total = total + jnp.where(group == g, square[g * cols : (g + 1) * cols], 0.0)
    return spread(total, cols)


def read_group(ref, g, per):
    x = ref[g * per : (g + 1) * per]
    return x.reshape(128, 128)


def first_sends_kernel(sends, block, *rest):
    outs, sems = rest[:4], rest[4]
    count = outs[0].shape[0]
    copies = []
    for d in range(4):
        for h in range(count):
            copies.append(
                pltpu.make_async_copy(
                    block.at[sends[d, h]], outs[d].at[h], sems.at[d, h]
                )
            )
    for copy in copies:
        copy.start()
    for copy in copies:
        copy.wait()


def tiles_kernel(tiles, high_out, low_out):
    for pair in range(tiles.shape[0] // 2):
        for j in range(2):
            high, low = split(tiles[2 * pair + j])
            for half in range(2):
                rows = slice(128 * half, 128 * half + 128)
                high_out[pair, rows, 128 * j : 128 * j + 128] = high
                low_out[pair, rows, 128 * j : 128 * j + 128] = low


def products(z, x, tiles_high, tiles_low, blocks, cols):
    step = 32
    pairs = tiles_high.shape[0]

    @pl.loop(0, blocks // step)
    def _(i):
        first = pl.multiple_of(i * step, step)
        left = x[pl.ds(pl.multiple_of(i * step * cols, step * cols), step * cols), :]
        for pair in range(pairs):
            out = jnp.dot(left, tiles_high[pair], preferred_element_type=F32)
            out = out + jnp.dot(left, tiles_low[pair], preferred_element_type=F32)
            for j in range(2):
                z[2 * pair + j, pl.ds(first, step)] = out[:, 128 * j : 128 * j + 128].reshape(
                    step, cols, 128
                )


def load_blocks(x, block, halos, flags):
    count, cols, cells = block.shape

    def put(start, values):
        high, low = split(values)
        x[start : start + values.shape[0], :cells] = high
        x[start : start + values.shape[0], cells:] = low

    put(0, block[...].reshape(count * cols, cells))
    start = count * cols
    for d, halo in enumerate(halos):
        rows = halo.shape[0] * cols
        values = jnp.where(flags[d] != 0, halo[...].reshape(rows, cells), 0.0)
        put(start, values)
        start += rows


def combine(z, weights, columns, b, slots):
    total = weights[b * slots] * z[0, columns[b * slots]]
    for k in range(1, slots):
        total = total + weights[b * slots + k] * z[k, columns[b * slots + k]]
    return total


def step_kernel(scaled, flags, columns, weights, sends, block, h0, h1, h2, h3, th, tl, *rest):
    if scaled:
        sums, rest = rest[0], rest[1:]
    image, s0, s1, s2, s3, packed, x, z = rest
    count, cols, cells = block.shape
    slots = z.shape[0]
    load_blocks(x, block, (h0, h1, h2, h3), flags)
    products(z, x, th, tl, z.shape[1], cols)

    @pl.loop(0, count, unroll=4)
    def _(b):
        image[b] = combine(z, weights, columns, b, slots)

    per = 128 // cols
    groups = [read_group(image, g, per) for g in range(count // per)]
    if scaled:
        total = jnp.sum(sums[...], 0, keepdims=True)
        left = scaler(eliminate(unpack(total, cols), identity(cols)))
        groups = [apply_scaler(left, g) for g in groups]
        for g, value in enumerate(groups):
            image[g * per : (g + 1) * per] = value.reshape(per, cols, cells)
    both = stacked(groups)
    gram = pack(inner(both, both, cols), cols)
    packed[...] = jnp.broadcast_to(gram, packed.shape)
    for d, out in enumerate((s0, s1, s2, s3)):
        for h in range(out.shape[0]):
            out[h] = image[sends[d, h]]


def last_kernel(flags, columns, weights, order, block, h0, h1, h2, h3, th, tl, *rest):
    image, chunks, x, z = rest[0], rest[1:-2], rest[-2], rest[-1]
    count, cols, cells = block.shape
    slots = z.shape[0]
    load_blocks(x, block, (h0, h1, h2, h3), flags)
    products(z, x, th, tl, z.shape[1], cols)
    size = count // len(chunks)
    for i, chunk in enumerate(chunks):

        @pl.loop(0, size, unroll=4)
        def _(r):
            b = order[i * size + r]
            value = combine(z, weights, columns, b, slots)
            image[b] = value
            chunk[r] = value


def sums_kernel(sums, previous, image, packed, inverse):
    count, cols, cells = image.shape
    per = 128 // cols
    total = jnp.sum(sums[...], 0, keepdims=True)
    inv = eliminate(unpack(total, cols), identity(cols))
    inverse[...] = inv
    left = scaler(inv)
    now = stacked([apply_scaler(left, read_group(image, g, per)) for g in range(count // per)])
    before = stacked(
        [apply_scaler(left, read_group(previous, g, per)) for g in range(count // per)]
    )
    gram = pack(inner(now, now, cols), cols)
    cross = pack(inner(before, now, cols), cols)
    packed[...] = jnp.broadcast_to(jnp.concatenate([gram, cross], 1), packed.shape)


def final_kernel(given, sums, inverse, *rest):
    half = (len(rest) - 3) // 2
    mine, theirs = rest[:half], rest[half : 2 * half]
    out, rayleigh, rows = rest[2 * half :]
    size, cols, cells = mine[0].shape
    for i in range(half):
        rows[i * size : (i + 1) * size] = mine[i][...]
        rows[(half + i) * size : (half + i + 1) * size] = theirs[i][...]
    total = jnp.sum(sums[...], 0, keepdims=True)
    wide = cols * cols
    inv = eliminate(unpack(total[:, :wide], cols), inverse[...])
    rayleigh[...] = unpack(total[:, wide:], cols)[:, :cols]
    left = scaler(inv)
    per = 128 // cols
    for g in range(out.shape[0] // per):
        value = rows[pl.ds(given[0] + g * per, per)].reshape(128, cells)
        out[g * per : (g + 1) * per] = apply_scaler(left, value).reshape(per, cols, cells)


def call(kernel, out_shape, in_specs, out_specs, scratch=(), flops=0, moved=0):
    return pl.pallas_call(
        kernel,
        out_shape=out_shape,
        in_specs=in_specs,
        out_specs=out_specs,
        scratch_shapes=list(scratch),
        compiler_params=pltpu.CompilerParams(vmem_limit_bytes=VMEM_LIMIT),
        cost_estimate=pl.CostEstimate(flops=flops, transcendentals=0, bytes_accessed=moved),
    )


def ring(x, axis, shift):
    size = lax.axis_size(axis)
    return lax.ppermute(x, axis, [(i, (i + shift) % size) for i in range(size)])


def halo(sent):
    return (
        ring(sent[1], "gx", 1),
        ring(sent[0], "gx", -1),
        ring(sent[3], "gy", 1),
        ring(sent[2], "gy", -1),
    )


def everywhere(rows):
    return lax.all_to_all(rows, AXES, 0, 0, tiled=True)


def shape(*dims, dtype=F32):
    return jax.ShapeDtypeStruct(dims, dtype)


def per_device(start_block, slot_tiles, edge_weights, block_columns, halo_sends, split_side):
    block = start_block[0, 0]
    weights, columns, sends, sides = (
        edge_weights[0, 0],
        block_columns[0, 0],
        halo_sends[0, 0],
        split_side[0, 0],
    )
    count, cols, cells = block.shape
    slots, width = slot_tiles.shape[0], sends.shape[1]
    size_x, size_y = lax.axis_size("gx"), lax.axis_size("gy")
    devices = size_x * size_y
    place_x, place_y = lax.axis_index("gx"), lax.axis_index("gy")
    flags = jnp.stack(
        [place_x > 0, place_x < size_x - 1, place_y > 0, place_y < size_y - 1]
    ).astype(jnp.int32)
    flat_weights = weights.reshape(count * slots)
    flat_columns = columns.reshape(count * slots)

    my_side = (place_y >= size_y // 2).astype(jnp.int32)
    keep = (sides == my_side).astype(jnp.int32)
    given = count - jnp.sum(keep)
    place = jnp.where(keep == 1, given + jnp.cumsum(keep) - 1, jnp.cumsum(1 - keep) - 1)
    order = jnp.zeros((count,), jnp.int32).at[place].set(
        jnp.arange(count, dtype=jnp.int32), unique_indices=True
    )

    piece = shape(width, cols, cells)
    sent = call(
        first_sends_kernel,
        [piece] * 4,
        [SMEM, ANY],
        [VMEM] * 4,
        [pltpu.SemaphoreType.DMA((4, width))],
    )(sends, block)
    wide = 2 * cells
    tiles = call(
        tiles_kernel, [shape(slots // 2, wide, wide, dtype=BF16)] * 2, [VMEM], [VMEM] * 2
    )(slot_tiles)

    blocks = count + 4 * width
    scratch = [
        pltpu.VMEM((blocks * cols, wide), BF16),
        pltpu.VMEM((slots, blocks, cols, cells), F32),
    ]

    def step(block, near, sums):
        extra = () if sums is None else (sums,)
        out = call(
            functools.partial(step_kernel, sums is not None),
            [shape(count, cols, cells)] + [piece] * 4 + [shape(devices, cols * cols)],
            [SMEM] * 4 + [VMEM] * (7 + len(extra)),
            [VMEM] * 6,
            scratch,
        )(flags, flat_columns, flat_weights, sends, block, *near, *tiles, *extra)
        return out[0], out[1:5], out[5]

    image, sent, packed = step(block, halo(sent), None)
    near = halo(sent)
    image, sent, packed = step(image, near, everywhere(packed))
    previous = image
    near = halo(sent)
    size = count // CHUNKS
    image, *mine = call(
        last_kernel,
        [shape(count, cols, cells)] + [shape(size, cols, cells)] * CHUNKS,
        [SMEM] * 4 + [VMEM] * 7,
        [VMEM] * (1 + CHUNKS),
        scratch,
    )(flags, flat_columns, flat_weights, order, image, *near, *tiles)

    swap = [(j, j ^ (size_y // 2)) for j in range(size_y)]
    theirs = [lax.ppermute(x, "gy", swap) for x in mine]
    packed, image = lax.optimization_barrier((packed, image))
    packed, inverse = call(
        sums_kernel,
        [shape(devices, 2 * cols * cols), shape(cols, cells)],
        [VMEM] * 3,
        [VMEM] * 2,
    )(everywhere(packed), previous, image)
    sums = everywhere(packed)

    meta = jnp.concatenate([weights, columns.astype(F32)], 1)[order]
    both = jnp.concatenate([meta, lax.ppermute(meta, "gy", swap)], 0)
    moved = lax.dynamic_slice(both, (given, 0), (count, 2 * slots))
    moved_weights = moved[:, :slots]
    moved_columns = moved[:, slots:].astype(jnp.int32)

    moved_basis, rayleigh = call(
        final_kernel,
        [shape(count, cols, cells), shape(cols, cols)],
        [SMEM] + [VMEM] * (2 + 2 * CHUNKS),
        [VMEM] * 2,
        [pltpu.VMEM((2 * count, cols, cells), F32)],
    )(given.reshape(1), sums, inverse, *mine, *theirs)
    return (
        moved_basis[None, None],
        moved_weights[None, None],
        moved_columns[None, None],
        rayleigh,
    )


def solution(mesh):
    return jax.shard_map(
        per_device,
        mesh=mesh,
        in_specs=(
            P("gx", "gy", None, None, None),
            P(),
            P("gx", "gy", None, None),
            P("gx", "gy", None, None),
            P("gx", "gy", None, None),
            P("gx", "gy", None),
        ),
        out_specs=(
            P("gx", "gy", None, None, None),
            P("gx", "gy", None, None),
            P("gx", "gy", None, None),
            P(),
        ),
        check_vma=False,
    )
```

profile of v0, /device:TPU:0, one launch (start us, length us, event | category | flops | bytes accessed | tf_op | source)
XLA Modules:
  0.0 108.1 jit_solution(2875872250522106755)
XLA Ops:
  1.3 1.2 %copy-done = f32[1,1,128,16,128]{4,3,2,1,0:T(8,128)S(1)} copy-done((f32[1,1,128,16,128]{4,3,2,1,0:T(8,128)S(1)}, f32[1,1,128,16,128]{4,3,2,1,0:T(8,128)}, u32[]{:S(2)}) %copy-start) | copy-done | bytes 1048600
  2.6 1.4 %shard_map.93 = (f32[8,16,128]{2,1,0:T(8,128)S(1)}, f32[8,16,128]{2,1,0:T(8,128)S(1)}, f32[8,16,128]{2,1,0:T(8,128)S(1)}, f32[8,16,128]{2,1,0:T(8,128)S(1)}) custom-call(s32[4,8]{1,0:T(4,128)S(1)} %bitcast.41, f32[128,16,128]{2,1,0:T(8,128)S(1)} %bitcast.33), custom_call_target="tpu_custom_call" | custom-call | tf_op jit(solution)/shard_map/pallas_call | solution.py:336
  3.9 3.1 %collective-permute-start = (f32[8,16,128]{2,1,0:T(8,128)S(1)}, f32[8,16,128]{2,1,0:T(8,128)S(1)}, u32[]{:S(2)}, u32[]{:S(2)}) collective-permute-start(f32[8,16,128]{2,1,0:T(8,128)S(1)} %get-tuple-element.33), channel_id=1, source_target_pairs={{0,8},{8,16},{16,24},{24,0},{1,9},{9,17},{17,25},{25,1},{2,10},{10... | collective-permute-start | bytes 196616 | tf_op jit(solution)/shard_map/ppermute | solution.py:288
  7.0 2.1 %collective-permute-start.1 = (f32[8,16,128]{2,1,0:T(8,128)S(1)}, f32[8,16,128]{2,1,0:T(8,128)S(1)}, u32[]{:S(2)}, u32[]{:S(2)}) collective-permute-start(f32[8,16,128]{2,1,0:T(8,128)S(1)} %get-tuple-element.34), channel_id=1, source_target_pairs={{0,24},{8,0},{16,8},{24,16},{1,25},{9,1},{17,9},{25,17},{2,26},{10... | collective-permute-start | bytes 196616 | tf_op jit(solution)/shard_map/ppermute | solution.py:288
  9.1 2.6 %collective-permute-start.3 = (f32[8,16,128]{2,1,0:T(8,128)S(1)}, f32[8,16,128]{2,1,0:T(8,128)S(1)}, u32[]{:S(2)}, u32[]{:S(2)}) collective-permute-start(f32[8,16,128]{2,1,0:T(8,128)S(1)} %get-tuple-element.36), channel_id=1, source_target_pairs={{0,7},{1,0},{2,1},{3,2},{4,3},{5,4},{6,5},{7,6},{8,15},{9,8},{10,9... | collective-permute-start | bytes 196616 | tf_op jit(solution)/shard_map/ppermute | solution.py:288
  15.8 7.3 %shard_map.95 = (f32[128,16,128]{2,1,0:T(8,128)S(1)}, f32[8,16,128]{2,1,0:T(8,128)}, f32[8,16,128]{2,1,0:T(8,128)}, f32[8,16,128]{2,1,0:T(8,128)S(1)}, f32[8,16,128]{2,1,0:T(8,128)}, /*index=5*/f32[32,256]{1,0:T(8,128)S(1)}) custom-call(s32[4]{0:T(128)S(1)} %add_convert_fusion.flags, s32[1024]{0:T(1024)S(1)} %reshape_squeeze.6.columns, ...), custom_call_target="tpu_custom_call" | custom-call | tf_op jit(solution)/shard_map/pallas_call | solution.py:356
  23.2 3.8 %collective-permute-start.5 = (f32[8,16,128]{2,1,0:T(8,128)}, f32[8,16,128]{2,1,0:T(8,128)S(1)}, u32[]{:S(2)}, u32[]{:S(2)}) collective-permute-start(f32[8,16,128]{2,1,0:T(8,128)} %get-tuple-element.41), channel_id=1, source_target_pairs={{0,24},{8,0},{16,8},{24,16},{1,25},{9,1},{17,9},{25,17},{2,26},{10... | collective-permute-start | bytes 196616 | tf_op jit(solution)/shard_map/ppermute | solution.py:288
  27.0 2.6 %collective-permute-start.7 = (f32[8,16,128]{2,1,0:T(8,128)S(1)}, f32[8,16,128]{2,1,0:T(8,128)S(1)}, u32[]{:S(2)}, u32[]{:S(2)}) collective-permute-start(f32[8,16,128]{2,1,0:T(8,128)S(1)} %get-tuple-element.43), channel_id=1, source_target_pairs={{0,7},{1,0},{2,1},{3,2},{4,3},{5,4},{6,5},{7,6},{8,15},{9,8},{10,9... | collective-permute-start | bytes 196616 | tf_op jit(solution)/shard_map/ppermute | solution.py:288
  30.3 2.5 %all-to-all-start = ((f32[32,1,256]{2,1,0:T(1,128)}), f32[32,1,256]{2,1,0:T(1,128)S(1)}, u32[]{:S(2)}, u32[]{:S(2)}) async-start(f32[32,1,256]{2,1,0:T(1,128)} %copy.28), calls=%async_computation | async-start | bytes 65536 | tf_op jit(solution)/shard_map/all_to_all | solution.py:301
  33.5 6.5 %all-to-all-done = f32[32,1,256]{2,1,0:T(1,128)S(1)} async-done(((f32[32,1,256]{2,1,0:T(1,128)}), f32[32,1,256]{2,1,0:T(1,128)S(1)}, u32[]{:S(2)}, u32[]{:S(2)}) %all-to-all-start) | async-done | bytes 32800 | tf_op jit(solution)/shard_map/all_to_all | solution.py:301
  40.1 9.2 %shard_map.96 = (f32[128,16,128]{2,1,0:T(8,128)S(1)}, f32[8,16,128]{2,1,0:T(8,128)}, f32[8,16,128]{2,1,0:T(8,128)}, f32[8,16,128]{2,1,0:T(8,128)}, f32[8,16,128]{2,1,0:T(8,128)}, /*index=5*/f32[32,256]{1,0:T(8,128)S(1)}) custom-call(s32[4]{0:T(128)S(1)} %add_convert_fusion.flags, s32[1024]{0:T(1024)S(1)} %reshape_squeeze.6.columns, ...), custom_call_target="tpu_custom_call" | custom-call | tf_op jit(solution)/shard_map/pallas_call | solution.py:356
  50.5 3.2 %collective-permute-start.9 = (f32[8,16,128]{2,1,0:T(8,128)}, f32[8,16,128]{2,1,0:T(8,128)S(1)}, u32[]{:S(2)}, u32[]{:S(2)}) collective-permute-start(f32[8,16,128]{2,1,0:T(8,128)} %get-tuple-element.48), channel_id=1, source_target_pairs={{0,24},{8,0},{16,8},{24,16},{1,25},{9,1},{17,9},{25,17},{2,26},{10... | collective-permute-start | bytes 196616 | tf_op jit(solution)/shard_map/ppermute | solution.py:288
  53.7 2.6 %collective-permute-start.11 = (f32[8,16,128]{2,1,0:T(8,128)}, f32[8,16,128]{2,1,0:T(8,128)S(1)}, u32[]{:S(2)}, u32[]{:S(2)}) collective-permute-start(f32[8,16,128]{2,1,0:T(8,128)} %get-tuple-element.50), channel_id=1, source_target_pairs={{0,7},{1,0},{2,1},{3,2},{4,3},{5,4},{6,5},{7,6},{8,15},{9,8},{10,9... | collective-permute-start | bytes 196616 | tf_op jit(solution)/shard_map/ppermute | solution.py:288
  56.4 1.5 %gather_fusion = f32[128,16]{1,0:T(8,128)S(1)} fusion(f32[128,16]{1,0:T(8,128)} %copy.34, s32[1024]{0:T(1024)S(1)} %pad_clamp_fusion), kind=kCustom, calls=%fused_computation | custom fusion | bytes 16896 | tf_op jit(solution)/shard_map/gather | solution.py:390
  59.8 2.4 %collective-permute-done.16 = f32[128,16]{1,0:T(8,128)S(1)} collective-permute-done((f32[128,16]{1,0:T(8,128)S(1)}, f32[128,16]{1,0:T(8,128)S(1)}, u32[]{:S(2)}, u32[]{:S(2)}) %collective-permute-start.16) | collective-permute-done | bytes 8224 | tf_op jit(solution)/shard_map/ppermute | solution.py:391
  65.8 6.2 %shard_map.97 = (f32[128,16,128]{2,1,0:T(8,128)S(1)}, f32[32,16,128]{2,1,0:T(8,128)S(1)}, f32[32,16,128]{2,1,0:T(8,128)S(1)}, f32[32,16,128]{2,1,0:T(8,128)S(1)}, f32[32,16,128]{2,1,0:T(8,128)S(1)}) custom-call(s32[4]{0:T(128)S(1)} %add_convert_fusion.flags, s32[1024]{0:T(1024)S(1)} %reshape_squeeze.6.columns, f32[1024]{0:T(1024)S(1)} %reshape_squeeze.7.weights, ...), custom_call_target="tpu_custom_call" | custom-call | tf_op jit(solution)/shard_map/pallas_call | solution.py:371
  74.7 2.7 %all-to-all-start.1 = ((f32[32,1,256]{2,1,0:T(1,128)}), f32[32,1,256]{2,1,0:T(1,128)S(1)}, u32[]{:S(2)}, u32[]{:S(2)}) async-start(f32[32,1,256]{2,1,0:T(1,128)} %copy.32), calls=%async_computation.1 | async-start | bytes 65536 | tf_op jit(solution)/shard_map/all_to_all | solution.py:301
  77.4 1.7 %collective-permute-start.12 = (f32[32,16,128]{2,1,0:T(8,128)S(1)}, f32[32,16,128]{2,1,0:T(8,128)S(1)}, u32[]{:S(2)}, u32[]{:S(2)}) collective-permute-start(f32[32,16,128]{2,1,0:T(8,128)S(1)} %get-tuple-element.56.rest_0_), channel_id=1, source_target_pairs={{0,4},{1,5},{2,6},{3,7},{4,0},{5,1},{6,2},{7,3},{8,12},{9,13},{10,... | collective-permute-start | bytes 786440 | tf_op jit(solution)/shard_map/ppermute | solution.py:380
  79.5 1.7 %collective-permute-start.14 = (f32[32,16,128]{2,1,0:T(8,128)}, f32[32,16,128]{2,1,0:T(8,128)}, u32[]{:S(2)}, u32[]{:S(2)}) collective-permute-start(f32[32,16,128]{2,1,0:T(8,128)} %copy-done.5), channel_id=1, source_target_pairs={{0,4},{1,5},{2,6},{3,7},{4,0},{5,1},{6,2},{7,3},{8,12},{9,13},{10,... | collective-permute-start | bytes 786440 | tf_op jit(solution)/shard_map/ppermute | solution.py:380
  81.6 3.1 %all-to-all-done.1 = f32[32,1,256]{2,1,0:T(1,128)S(1)} async-done(((f32[32,1,256]{2,1,0:T(1,128)}), f32[32,1,256]{2,1,0:T(1,128)S(1)}, u32[]{:S(2)}, u32[]{:S(2)}) %all-to-all-start.1) | async-done | bytes 32800 | tf_op jit(solution)/shard_map/all_to_all | solution.py:301
  84.7 3.5 %shard_map.98 = (f32[32,512]{1,0:T(8,128)S(1)}, f32[16,128]{1,0:T(8,128)S(1)}) custom-call(f32[32,256]{1,0:T(8,128)S(1)} %bitcast.37, f32[128,16,128]{2,1,0:T(8,128)S(1)} %get-tuple-element.46.block.previous, f32[128,16,128]{2,1,0:T(8,128)S(1)} %get-tuple-element.53.image), custom_call_target="tpu_custom_call" | custom-call | tf_op jit(solution)/shard_map/pallas_call | solution.py:382
  88.9 2.8 %all-to-all-start.2 = ((f32[32,1,512]{2,1,0:T(1,128)}), f32[32,1,512]{2,1,0:T(1,128)S(1)}, u32[]{:S(2)}, u32[]{:S(2)}) async-start(f32[32,1,512]{2,1,0:T(1,128)} %copy.33), calls=%async_computation.2 | async-start | bytes 131072 | tf_op jit(solution)/shard_map/all_to_all | solution.py:301
  92.3 11.5 %all-to-all-done.2 = f32[32,1,512]{2,1,0:T(1,128)S(1)} async-done(((f32[32,1,512]{2,1,0:T(1,128)}), f32[32,1,512]{2,1,0:T(1,128)S(1)}, u32[]{:S(2)}, u32[]{:S(2)}) %all-to-all-start.2) | async-done | bytes 65568 | tf_op jit(solution)/shard_map/all_to_all | solution.py:301
  103.9 4.2 %shard_map.99 = (f32[128,16,128]{2,1,0:T(8,128)}, f32[16,16]{1,0:T(8,128)}) custom-call(s32[1]{0:T(128)} %bitcast.given, f32[32,512]{1,0:T(8,128)S(1)} %bitcast.35, f32[16,128]{1,0:T(8,128)S(1)} %get-tuple-element.55.inverse, f32[32,16,128]{2,1,0:T(8,128)S(1)} %get-tuple-element.56.rest_0_, f32[32,16,128]{2,1,0:T(8,128)S(1)} %copy-done.4, ...), custom_call_target="tpu_custom_call" | custom-call | tf_op jit(solution)/shard_map/pallas_call | solution.py:396
  (97 shorter events, 16.4 us)
Async XLA Ops:
  2.5 13.3 %copy-start.1 = (f32[1,1,128,16,128]{4,3,2,1,0:T(8,128)S(1)}, f32[1,1,128,16,128]{4,3,2,1,0:T(8,128)}, u32[]{:S(2)}) copy-start(f32[1,1,128,16,128]{4,3,2,1,0:T(8,128)} %param.6) | copy-start | bytes 3145732
  3.9 11.9 %collective-permute-start = (f32[8,16,128]{2,1,0:T(8,128)S(1)}, f32[8,16,128]{2,1,0:T(8,128)S(1)}, u32[]{:S(2)}, u32[]{:S(2)}) collective-permute-start(f32[8,16,128]{2,1,0:T(8,128)S(1)} %get-tuple-element.33), channel_id=1, source_target_pairs={{0,8},{8,16},{16,24},{24,0},{1,9},{9,17},{17,25},{25,1},{2,10},{10... | collective-permute-start | bytes 196616 | tf_op jit(solution)/shard_map/ppermute | solution.py:288
  7.0 8.8 %collective-permute-start.1 = (f32[8,16,128]{2,1,0:T(8,128)S(1)}, f32[8,16,128]{2,1,0:T(8,128)S(1)}, u32[]{:S(2)}, u32[]{:S(2)}) collective-permute-start(f32[8,16,128]{2,1,0:T(8,128)S(1)} %get-tuple-element.34), channel_id=1, source_target_pairs={{0,24},{8,0},{16,8},{24,16},{1,25},{9,1},{17,9},{25,17},{2,26},{10... | collective-permute-start | bytes 196616 | tf_op jit(solution)/shard_map/ppermute | solution.py:288
  9.1 6.7 %collective-permute-start.2 = (f32[8,16,128]{2,1,0:T(8,128)S(1)}, f32[8,16,128]{2,1,0:T(8,128)S(1)}, u32[]{:S(2)}, u32[]{:S(2)}) collective-permute-start(f32[8,16,128]{2,1,0:T(8,128)S(1)} %get-tuple-element.35), channel_id=1, source_target_pairs={{0,1},{1,2},{2,3},{3,4},{4,5},{5,6},{6,7},{7,0},{8,9},{9,10},{10,1... | collective-permute-start | bytes 196616 | tf_op jit(solution)/shard_map/ppermute | solution.py:288
  9.1 6.7 %collective-permute-start.3 = (f32[8,16,128]{2,1,0:T(8,128)S(1)}, f32[8,16,128]{2,1,0:T(8,128)S(1)}, u32[]{:S(2)}, u32[]{:S(2)}) collective-permute-start(f32[8,16,128]{2,1,0:T(8,128)S(1)} %get-tuple-element.36), channel_id=1, source_target_pairs={{0,7},{1,0},{2,1},{3,2},{4,3},{5,4},{6,5},{7,6},{8,15},{9,8},{10,9... | collective-permute-start | bytes 196616 | tf_op jit(solution)/shard_map/ppermute | solution.py:288
  23.2 16.9 %collective-permute-start.4 = (f32[8,16,128]{2,1,0:T(8,128)}, f32[8,16,128]{2,1,0:T(8,128)S(1)}, u32[]{:S(2)}, u32[]{:S(2)}) collective-permute-start(f32[8,16,128]{2,1,0:T(8,128)} %get-tuple-element.40), channel_id=1, source_target_pairs={{0,8},{8,16},{16,24},{24,0},{1,9},{9,17},{17,25},{25,1},{2,10},{10... | collective-permute-start | bytes 196616 | tf_op jit(solution)/shard_map/ppermute | solution.py:288
  23.2 16.9 %collective-permute-start.5 = (f32[8,16,128]{2,1,0:T(8,128)}, f32[8,16,128]{2,1,0:T(8,128)S(1)}, u32[]{:S(2)}, u32[]{:S(2)}) collective-permute-start(f32[8,16,128]{2,1,0:T(8,128)} %get-tuple-element.41), channel_id=1, source_target_pairs={{0,24},{8,0},{16,8},{24,16},{1,25},{9,1},{17,9},{25,17},{2,26},{10... | collective-permute-start | bytes 196616 | tf_op jit(solution)/shard_map/ppermute | solution.py:288
  27.0 13.1 %collective-permute-start.6 = (f32[8,16,128]{2,1,0:T(8,128)}, f32[8,16,128]{2,1,0:T(8,128)S(1)}, u32[]{:S(2)}, u32[]{:S(2)}) collective-permute-start(f32[8,16,128]{2,1,0:T(8,128)} %get-tuple-element.42), channel_id=1, source_target_pairs={{0,1},{1,2},{2,3},{3,4},{4,5},{5,6},{6,7},{7,0},{8,9},{9,10},{10,1... | collective-permute-start | bytes 196616 | tf_op jit(solution)/shard_map/ppermute | solution.py:288
  27.0 13.1 %collective-permute-start.7 = (f32[8,16,128]{2,1,0:T(8,128)S(1)}, f32[8,16,128]{2,1,0:T(8,128)S(1)}, u32[]{:S(2)}, u32[]{:S(2)}) collective-permute-start(f32[8,16,128]{2,1,0:T(8,128)S(1)} %get-tuple-element.43), channel_id=1, source_target_pairs={{0,7},{1,0},{2,1},{3,2},{4,3},{5,4},{6,5},{7,6},{8,15},{9,8},{10,9... | collective-permute-start | bytes 196616 | tf_op jit(solution)/shard_map/ppermute | solution.py:288
  30.3 9.8 %all-to-all-start = ((f32[32,1,256]{2,1,0:T(1,128)}), f32[32,1,256]{2,1,0:T(1,128)S(1)}, u32[]{:S(2)}, u32[]{:S(2)}) async-start(f32[32,1,256]{2,1,0:T(1,128)} %copy.28), calls=%async_computation | async-start | bytes 65536 | tf_op jit(solution)/shard_map/all_to_all | solution.py:301
  49.9 13.0 %collective-permute-start.8 = (f32[8,16,128]{2,1,0:T(8,128)}, f32[8,16,128]{2,1,0:T(8,128)S(1)}, u32[]{:S(2)}, u32[]{:S(2)}) collective-permute-start(f32[8,16,128]{2,1,0:T(8,128)} %get-tuple-element.47), channel_id=1, source_target_pairs={{0,8},{8,16},{16,24},{24,0},{1,9},{9,17},{17,25},{25,1},{2,10},{10... | collective-permute-start | bytes 196616 | tf_op jit(solution)/shard_map/ppermute | solution.py:288
  50.5 12.4 %collective-permute-start.9 = (f32[8,16,128]{2,1,0:T(8,128)}, f32[8,16,128]{2,1,0:T(8,128)S(1)}, u32[]{:S(2)}, u32[]{:S(2)}) collective-permute-start(f32[8,16,128]{2,1,0:T(8,128)} %get-tuple-element.48), channel_id=1, source_target_pairs={{0,24},{8,0},{16,8},{24,16},{1,25},{9,1},{17,9},{25,17},{2,26},{10... | collective-permute-start | bytes 196616 | tf_op jit(solution)/shard_map/ppermute | solution.py:288
  53.7 9.1 %collective-permute-start.10 = (f32[8,16,128]{2,1,0:T(8,128)}, f32[8,16,128]{2,1,0:T(8,128)S(1)}, u32[]{:S(2)}, u32[]{:S(2)}) collective-permute-start(f32[8,16,128]{2,1,0:T(8,128)} %get-tuple-element.49), channel_id=1, source_target_pairs={{0,1},{1,2},{2,3},{3,4},{4,5},{5,6},{6,7},{7,0},{8,9},{9,10},{10,1... | collective-permute-start | bytes 196616 | tf_op jit(solution)/shard_map/ppermute | solution.py:288
  53.7 9.8 %collective-permute-start.11 = (f32[8,16,128]{2,1,0:T(8,128)}, f32[8,16,128]{2,1,0:T(8,128)S(1)}, u32[]{:S(2)}, u32[]{:S(2)}) collective-permute-start(f32[8,16,128]{2,1,0:T(8,128)} %get-tuple-element.50), channel_id=1, source_target_pairs={{0,7},{1,0},{2,1},{3,2},{4,3},{5,4},{6,5},{7,6},{8,15},{9,8},{10,9... | collective-permute-start | bytes 196616 | tf_op jit(solution)/shard_map/ppermute | solution.py:288
  57.9 4.3 %collective-permute-start.16 = (f32[128,16]{1,0:T(8,128)S(1)}, f32[128,16]{1,0:T(8,128)S(1)}, u32[]{:S(2)}, u32[]{:S(2)}) collective-permute-start(f32[128,16]{1,0:T(8,128)S(1)} %gather_fusion), channel_id=1, source_target_pairs={{0,4},{1,5},{2,6},{3,7},{4,0},{5,1},{6,2},{7,3},{8,12},{9,13},{10,... | collective-permute-start | bytes 24584 | tf_op jit(solution)/shard_map/ppermute | solution.py:391
  74.7 10.0 %all-to-all-start.1 = ((f32[32,1,256]{2,1,0:T(1,128)}), f32[32,1,256]{2,1,0:T(1,128)S(1)}, u32[]{:S(2)}, u32[]{:S(2)}) async-start(f32[32,1,256]{2,1,0:T(1,128)} %copy.32), calls=%async_computation.1 | async-start | bytes 65536 | tf_op jit(solution)/shard_map/all_to_all | solution.py:301
  77.4 26.3 %collective-permute-start.12 = (f32[32,16,128]{2,1,0:T(8,128)S(1)}, f32[32,16,128]{2,1,0:T(8,128)S(1)}, u32[]{:S(2)}, u32[]{:S(2)}) collective-permute-start(f32[32,16,128]{2,1,0:T(8,128)S(1)} %get-tuple-element.56.rest_0_), channel_id=1, source_target_pairs={{0,4},{1,5},{2,6},{3,7},{4,0},{5,1},{6,2},{7,3},{8,12},{9,13},{10,... | collective-permute-start | bytes 786440 | tf_op jit(solution)/shard_map/ppermute | solution.py:380
  79.2 24.6 %collective-permute-start.13 = (f32[32,16,128]{2,1,0:T(8,128)}, f32[32,16,128]{2,1,0:T(8,128)}, u32[]{:S(2)}, u32[]{:S(2)}) collective-permute-start(f32[32,16,128]{2,1,0:T(8,128)} %copy-done.3), channel_id=1, source_target_pairs={{0,4},{1,5},{2,6},{3,7},{4,0},{5,1},{6,2},{7,3},{8,12},{9,13},{10,... | collective-permute-start | bytes 786440 | tf_op jit(solution)/shard_map/ppermute | solution.py:380
  79.5 24.3 %collective-permute-start.14 = (f32[32,16,128]{2,1,0:T(8,128)}, f32[32,16,128]{2,1,0:T(8,128)}, u32[]{:S(2)}, u32[]{:S(2)}) collective-permute-start(f32[32,16,128]{2,1,0:T(8,128)} %copy-done.5), channel_id=1, source_target_pairs={{0,4},{1,5},{2,6},{3,7},{4,0},{5,1},{6,2},{7,3},{8,12},{9,13},{10,... | collective-permute-start | bytes 786440 | tf_op jit(solution)/shard_map/ppermute | solution.py:380
  81.2 22.6 %collective-permute-start.15 = (f32[32,16,128]{2,1,0:T(8,128)}, f32[32,16,128]{2,1,0:T(8,128)}, u32[]{:S(2)}, u32[]{:S(2)}) collective-permute-start(f32[32,16,128]{2,1,0:T(8,128)} %copy-done.7), channel_id=1, source_target_pairs={{0,4},{1,5},{2,6},{3,7},{4,0},{5,1},{6,2},{7,3},{8,12},{9,13},{10,... | collective-permute-start | bytes 786440 | tf_op jit(solution)/shard_map/ppermute | solution.py:380
  84.7 19.1 %copy-start.6 = (f32[32,16,128]{2,1,0:T(8,128)S(1)}, f32[32,16,128]{2,1,0:T(8,128)}, u32[]{:S(2)}) copy-start(f32[32,16,128]{2,1,0:T(8,128)} %copy-done.5) | copy-start | bytes 786436
  84.7 19.1 %copy-start.8 = (f32[32,16,128]{2,1,0:T(8,128)S(1)}, f32[32,16,128]{2,1,0:T(8,128)}, u32[]{:S(2)}) copy-start(f32[32,16,128]{2,1,0:T(8,128)} %copy-done.7) | copy-start | bytes 786436
  88.2 15.7 %copy-start.4 = (f32[32,16,128]{2,1,0:T(8,128)S(1)}, f32[32,16,128]{2,1,0:T(8,128)}, u32[]{:S(2)}) copy-start(f32[32,16,128]{2,1,0:T(8,128)} %copy-done.3) | copy-start | bytes 786436
  88.9 14.9 %all-to-all-start.2 = ((f32[32,1,512]{2,1,0:T(1,128)}), f32[32,1,512]{2,1,0:T(1,128)S(1)}, u32[]{:S(2)}, u32[]{:S(2)}) async-start(f32[32,1,512]{2,1,0:T(1,128)} %copy.33), calls=%async_computation.2 | async-start | bytes 131072 | tf_op jit(solution)/shard_map/all_to_all | solution.py:301
  (18 other events, 71.0 us)
where the time goes:
time: 109 us; the launch traced here: 108 us
  starting transfers between devices  33.5 us (31%)
  Pallas kernels  31.9 us (29%)
  waiting for transfers between devices  23.5 us (22%)
  local copies, waits for them, and re-layouts  14.5 us (13%)
  other arithmetic  2.4 us (2%)
  between operations  2.25 us (2%)
    all_to_all x3, waiting for transfers between devices, everywhere(): return lax.all_to_all(rows, AXES, 0, 0, tiled=True)  21.1 us
    ppermute x12, starting transfers between devices, ring(): return lax.ppermute(x, axis, [(i, (i + shift) % size) for i in range(size)])  20.7 us
    pallas_call x2, Pallas kernels, step(): call(functools.partial(step_kernel, sums is not None), [shape(count, cols...  16.5 us
    all_to_all x3, starting transfers between devices, everywhere(): return lax.all_to_all(rows, AXES, 0, 0, tiled=True)  8.01 us
    unnamed x49, local copies, waits for them, and re-layouts  7.77 us
    pallas_call x1, Pallas kernels, per_device(): call(last_kernel, [shape(count, cols, cells)] + [shape(size, cols, cells)...  6.18 us
    pallas_call x1, Pallas kernels, per_device(): call(final_kernel, [shape(count, cols, cells), shape(cols, cols)], [SMEM]...  4.25 us
    ppermute x4, starting transfers between devices, per_device(): theirs = [lax.ppermute(x, 'gy', swap) for x in mine]  4.12 us
  transfers between devices with their start and end apart: 20, of which 4 were waited for; matrix products, arithmetic and copies ran while one was open for 8% of the time, Pallas kernels for 3%

commit v1 on v0

v1 whole, which is shorter than its diff:
```python
import functools

import jax
import jax.numpy as jnp
from jax import lax
from jax.experimental import pallas as pl
from jax.experimental.pallas import tpu as pltpu
from jax.sharding import PartitionSpec as P

F32 = jnp.float32
BF16 = jnp.bfloat16
AXES = ("gx", "gy")
CHUNKS = 4
VMEM = pl.BlockSpec(memory_space=pltpu.VMEM)
SMEM = pl.BlockSpec(memory_space=pltpu.SMEM)
ANY = pl.BlockSpec(memory_space=pl.ANY)
HBM = pl.BlockSpec(memory_space=pltpu.HBM)


def split(x):
    high = x.astype(BF16)
    return high, (x - high.astype(F32)).astype(BF16)


def lane_group(rows, cols):
    return lax.broadcasted_iota(jnp.int32, (rows, 128), 1) // cols


def spread(x, cols):
    width = 64
    while width >= cols:
        x = x + pltpu.roll(x, width, 1)
        width //= 2
    return x


def unpack(packed, cols):
    half = 128 // cols
    sub = lax.broadcasted_iota(jnp.int32, (half, 128), 0)
    own = lane_group(half, cols) == sub
    parts = []
    for start in range(0, cols, half):
        row = packed[:, start * cols : start * cols + 128]
        parts.append(spread(jnp.where(own, jnp.broadcast_to(row, (half, 128)), 0.0), cols))
    return jnp.concatenate(parts, 0)


def pack(tiled, cols):
    half = 128 // cols
    sub = lax.broadcasted_iota(jnp.int32, (half, 128), 0)
    own = lane_group(half, cols) == sub
    rows = []
    for start in range(0, cols, half):
        part = jnp.where(own, tiled[start : start + half], 0.0)
        rows.append(jnp.sum(part, 0, keepdims=True))
    return jnp.concatenate(rows, 1)


def identity(cols):
    lane = lax.broadcasted_iota(jnp.int32, (cols, 128), 1) % cols
    return (lane == lax.broadcasted_iota(jnp.int32, (cols, 128), 0)).astype(F32)


def eliminate(gram, right):
    cols = gram.shape[0]
    row = lax.broadcasted_iota(jnp.int32, (cols, 128), 0)
    for j in range(cols):
        inv = lax.rsqrt(gram[j : j + 1, j : j + 1])
        factor = gram[:, j : j + 1] * inv
        gram_row = gram[j : j + 1, :] * inv
        right_row = right[j : j + 1, :] * inv
        below = row > j
        gram = jnp.where(below, gram - factor * gram_row, gram)
        right = jnp.where(
            below, right - factor * right_row, jnp.where(row == j, right_row, right)
        )
    return right


def scaler(small):
    cols = small.shape[0]
    group = lane_group(cols, cols)
    diag = jnp.concatenate(
        [jnp.where(group == g, small, 0.0) for g in range(128 // cols)], 0
    )
    high, low = split(diag)
    return jnp.concatenate(
        [jnp.concatenate([high, high], 1), jnp.concatenate([low, low], 1)], 0
    )


def apply_scaler(left, x):
    high, low = split(x)
    both = jnp.dot(left, jnp.concatenate([high, low], 0), preferred_element_type=F32)
    return both[:128] + both[128:]


def stacked(groups):
    pairs = [split(x) for x in groups]
    return jnp.concatenate(
        [
            jnp.concatenate([p[0] for p in pairs], 1),
            jnp.concatenate([p[1] for p in pairs], 1),
        ],
        0,
    )


def inner(a, b, cols):
    full = lax.dot_general(a, b, (((1,), (1,)), ((), ())), preferred_element_type=F32)
    half = full[:128] + full[128:]
    square = half[:, :128] + half[:, 128:]
    group = lane_group(cols, cols)
    total = jnp.zeros((cols, 128), F32)
    for g in range(128 // cols):
        total = total + jnp.where(group == g, square[g * cols : (g + 1) * cols], 0.0)
    return spread(total, cols)


def read_group(ref, g, per):
    x = ref[g * per : (g + 1) * per]
    return x.reshape(128, 128)


def first_sends_kernel(plan, sends, block, *rest):
    outs, sems = rest[:-1], rest[-1]
    copies = []
    for n, out in enumerate(outs):
        for h in range(out.shape[0]):
            copies.append(
                pltpu.make_async_copy(block.at[sends[plan[n], h]], out.at[h], sems.at[n, h])
            )
    for copy in copies:
        copy.start()
    for copy in copies:
        copy.wait()


def tiles_kernel(tiles, high_out, low_out):
    for pair in range(tiles.shape[0] // 2):
        for j in range(2):
            high, low = split(tiles[2 * pair + j])
            for half in range(2):
                rows = slice(128 * half, 128 * half + 128)
                high_out[pair, rows, 128 * j : 128 * j + 128] = high
                low_out[pair, rows, 128 * j : 128 * j + 128] = low


def lanes_product(a, b):
    return lax.dot_general(
        a.astype(BF16), b.astype(BF16), (((1,), (1,)), ((), ())), preferred_element_type=F32
    )


def order_kernel(side, sides, weights, columns, order, meta):
    count, slots = sides.shape[1], weights.shape[0]
    row = lax.broadcasted_iota(jnp.int32, (count, count), 0)
    col = lax.broadcasted_iota(jnp.int32, (count, count), 1)
    keep = jnp.broadcast_to((sides[...] == side[0]).astype(F32), (8, count))
    kept = lanes_product(keep, (col <= row).astype(F32))
    given = count - jnp.sum(keep, 1, keepdims=True)
    lane = lax.broadcasted_iota(jnp.int32, (8, count), 1).astype(F32)
    place = jnp.where(keep > 0.5, given + kept - 1.0, lane - kept)
    pick = (place[:1].astype(jnp.int32) == row).astype(F32)
    moved = lanes_product(lane, pick)
    order[...] = jnp.where(
        lax.broadcasted_iota(jnp.int32, (8, count), 0) == 0, moved, given
    ).astype(jnp.int32)
    values = weights[...]
    total = jnp.zeros((slots, count), F32)
    for _ in range(3):
        part = values.astype(BF16)
        total = total + lanes_product(part, pick)
        values = values - part.astype(F32)
    meta[:slots] = total
    meta[slots:] = lanes_product(columns[...].astype(F32), pick)


def products(z, x, tiles_high, tiles_low, cols):
    step = 32

    @pl.loop(0, z.shape[1] // step)
    def _(i):
        first = pl.multiple_of(i * step, step)
        left = x[pl.ds(pl.multiple_of(i * step * cols, step * cols), step * cols), :]
        for pair in range(tiles_high.shape[0]):
            out = jnp.dot(left, tiles_high[pair], preferred_element_type=F32)
            out = out + jnp.dot(left, tiles_low[pair], preferred_element_type=F32)
            for j in range(2):
                z[2 * pair + j, pl.ds(first, step)] = out[:, 128 * j : 128 * j + 128].reshape(
                    step, cols, 128
                )


def load_blocks(x, block, halos, plan, left):
    count, cols, cells = block.shape

    def put(rows, values):
        high, low = split(values)
        x[rows, :cells] = high
        x[rows, cells:] = low

    put(slice(0, count * cols), block[...].reshape(count * cols, cells))
    for n, halo in enumerate(halos):
        rows = halo.shape[0] * cols
        values = jnp.where(plan[len(halos) + n] != 0, halo[...].reshape(rows, cells), 0.0)
        if left is not None:
            values = apply_scaler(left, values)
        start = pl.multiple_of((count + plan[n] * halo.shape[0]) * cols, rows)
        put(pl.ds(start, rows), values)


def combine(z, weights, columns, b, count):
    total = weights[b] * z[0, columns[b]]
    for k in range(1, z.shape[0]):
        total = total + weights[k * count + b] * z[k, columns[k * count + b]]
    return total


def operator_kernel(plan, columns, weights, sends, block, h0, h1, h2, h3, th, tl, *rest):
    image, sent, x, z = rest[0], rest[1:-2], rest[-2], rest[-1]
    count, cols, _ = block.shape
    load_blocks(x, block, (h0, h1, h2, h3), plan, None)
    products(z, x, th, tl, cols)

    @pl.loop(0, count, unroll=4)
    def _(b):
        image[b] = combine(z, weights, columns, b, count)

    for n, out in enumerate(sent):
        for h in range(out.shape[0]):
            out[h] = image[sends[plan[n], h]]


def last_kernel(plan, columns, weights, order, block, h0, h1, h2, h3, th, tl, inv, meta, *rest):
    image, chunks, x, z = rest[0], rest[1:-2], rest[-2], rest[-1]
    count, cols, _ = block.shape
    load_blocks(x, block, (h0, h1, h2, h3), plan, scaler(inv[...]))
    products(z, x, th, tl, cols)
    size = count // len(chunks)
    for i, chunk in enumerate(chunks):

        @pl.loop(0, size, unroll=4)
        def _(r):
            b = order[i * size + r]
            value = combine(z, weights, columns, b, count)
            image[b] = value
            chunk[r] = value

    chunks[0][size] = meta[...]


def row_sum(sums):
    total = sums[0]
    for d in range(1, sums.shape[0]):
        total = total + sums[d]
    return total


def put_rows(packed, row):
    for d in range(packed.shape[0]):
        packed[d] = row


def groups_of(ref):
    count, cols, _ = ref.shape
    per = 128 // cols
    return [ref[g * per : (g + 1) * per].reshape(128, 128) for g in range(count // per)]


def gram_kernel(image, packed):
    cols = image.shape[1]
    both = stacked(groups_of(image))
    put_rows(packed, pack(inner(both, both, cols), cols))


def scale_kernel(sums, image, out, inverse, packed):
    _, cols, cells = image.shape
    per = 128 // cols
    inv = eliminate(unpack(row_sum(sums), cols), identity(cols))
    inverse[...] = inv
    left = scaler(inv)
    groups = [apply_scaler(left, g) for g in groups_of(image)]
    for g, value in enumerate(groups):
        out[g * per : (g + 1) * per] = value.reshape(per, cols, cells)
    both = stacked(groups)
    put_rows(packed, pack(inner(both, both, cols), cols))


def sums_kernel(sums, previous, image, packed, inverse):
    cols = image.shape[1]
    inv = eliminate(unpack(row_sum(sums), cols), identity(cols))
    inverse[...] = inv
    left = scaler(inv)
    now = stacked([apply_scaler(left, g) for g in groups_of(image)])
    before = stacked([apply_scaler(left, g) for g in groups_of(previous)])
    gram = pack(inner(now, now, cols), cols)
    cross = pack(inner(before, now, cols), cols)
    put_rows(packed, jnp.concatenate([gram, cross], 1))


def factor_kernel(order, sums, inverse, mine, theirs, total_inverse, rayleigh, weights, columns):
    cols = inverse.shape[0]
    count = weights.shape[1]
    slots = weights.shape[0]
    wide = cols * cols
    total = row_sum(sums)
    total_inverse[...] = eliminate(unpack(total[:, :wide], cols), inverse[...])
    rayleigh[...] = unpack(total[:, wide:], cols)[:, :cols]
    last = mine.shape[0] - 1
    both = jnp.concatenate([mine[last], theirs[last]], 1)
    moved = pltpu.roll(both, 2 * count - order[count], 1)[:, :count]
    weights[...] = moved[:slots]
    columns[...] = moved[slots:].astype(jnp.int32)


def final_kernel(first, order, inverse, image, *rest):
    theirs, out, rows = rest[:-2], rest[-2], rest[-1]
    if first:
        theirs = theirs[:-1]
    count, cols, cells = image.shape
    size, per = out.shape[0], 128 // cols
    part = first + pl.program_id(0)

    @pl.when(pl.program_id(0) == 0)
    def _():
        for i, chunk in enumerate(theirs):
            rows[count + i * size : count + (i + 1) * size] = chunk[:size]

        @pl.loop(0, count, unroll=4)
        def _(r):
            rows[r] = image[order[r]]

    left = scaler(inverse[...])
    start = order[count] + part * size
    for g in range(size // per):
        value = rows[pl.ds(start + g * per, per)].reshape(128, cells)
        out[g * per : (g + 1) * per] = apply_scaler(left, value).reshape(per, cols, cells)


def call(kernel, out_shape, in_specs, out_specs, scratch=(), limit=16, flops=0, moved=0, **more):
    return pl.pallas_call(
        kernel,
        out_shape=out_shape,
        in_specs=in_specs,
        out_specs=out_specs,
        scratch_shapes=list(scratch),
        compiler_params=pltpu.CompilerParams(vmem_limit_bytes=limit << 20),
        cost_estimate=pl.CostEstimate(flops=flops, transcendentals=0, bytes_accessed=moved),
        **more,
    )


def pairs(x, axis, odd):
    size = lax.axis_size(axis)
    swap = []
    for low in range(odd, size, 2):
        high = (low + 1) % size
        swap += [(low, high), (high, low)]
    return lax.ppermute(x, axis, swap)


def halo(sent):
    return (
        pairs(sent[0], "gx", 0),
        pairs(sent[1], "gx", 1),
        pairs(sent[2], "gy", 0),
        pairs(sent[3], "gy", 1),
    )


def everywhere(rows):
    return lax.all_to_all(rows, AXES, 0, 0, tiled=True)


def shape(*dims, dtype=F32):
    return jax.ShapeDtypeStruct(dims, dtype)


def exchange_plan(size_x, size_y):
    numbers, counts = [], []
    for base, axis, size in ((0, "gx", size_x), (2, "gy", size_y)):
        place = lax.axis_index(axis)
        odd = place % 2
        edge = jnp.where(odd == 1, place < size - 1, place > 0).astype(jnp.int32)
        numbers += [base + 1 - odd, base + odd]
        counts += [jnp.int32(1), edge]
    return jnp.stack(numbers + counts).astype(jnp.int32)


def per_device(start_block, slot_tiles, edge_weights, block_columns, halo_sends, split_side):
    block = start_block[0, 0]
    sends = halo_sends[0, 0]
    weights, columns = edge_weights[0, 0].T, block_columns[0, 0].T
    count, cols, cells = block.shape
    slots, width = slot_tiles.shape[0], sends.shape[1]
    size_x, size_y = lax.axis_size("gx"), lax.axis_size("gy")
    devices = size_x * size_y
    plan = exchange_plan(size_x, size_y)
    flat_weights = weights.reshape(slots * count)
    flat_columns = columns.reshape(slots * count)

    piece = shape(width, cols, cells)
    whole = shape(count, cols, cells)
    square = shape(cols, cells)
    sent = call(
        first_sends_kernel,
        [piece] * 4,
        [SMEM, SMEM, HBM],
        [VMEM] * 4,
        [pltpu.SemaphoreType.DMA((4, width))],
    )(plan, sends, block)
    near = halo(sent)

    wide = 2 * cells
    tiles = call(
        tiles_kernel, [shape(slots // 2, wide, wide, dtype=BF16)] * 2, [VMEM], [VMEM] * 2
    )(slot_tiles)
    my_side = (lax.axis_index("gy") >= size_y // 2).astype(jnp.int32)
    order, meta = call(
        order_kernel,
        [shape(8, count, dtype=jnp.int32), shape(2 * slots, count)],
        [SMEM] + [VMEM] * 3,
        [VMEM] * 2,
    )(my_side.reshape(1), split_side[0], weights, columns)
    order = order.reshape(8 * count)

    blocks = count + 4 * width
    scratch = [
        pltpu.VMEM((blocks * cols, wide), BF16),
        pltpu.VMEM((slots, blocks, cols, cells), F32),
    ]

    def operator(block, near):
        image, *sent = call(
            operator_kernel,
            [whole] + [piece] * 4,
            [SMEM] * 4 + [VMEM] * 7,
            [VMEM] * 5,
            scratch,
            limit=24,
        )(plan, flat_columns, flat_weights, sends, block, *near, *tiles)
        return image, sent

    gram_rows = shape(devices, 1, cols * cols)
    image, sent = operator(block, near)
    near = halo(sent)
    packed = call(gram_kernel, gram_rows, [VMEM], VMEM)(image)
    sums = everywhere(packed)
    image, sent = operator(image, near)
    near = halo(sent)
    previous, inverse, packed = call(
        scale_kernel, [whole, square, gram_rows], [VMEM] * 2, [VMEM] * 3
    )(sums, image)
    sums = everywhere(packed)

    size = count // CHUNKS
    image, *mine = call(
        last_kernel,
        [whole, shape(size + 1, cols, cells)] + [shape(size, cols, cells)] * (CHUNKS - 1),
        [SMEM] * 4 + [VMEM] * 9,
        [VMEM] * (1 + CHUNKS),
        scratch,
        limit=24,
    )(plan, flat_columns, flat_weights, order, previous, *near, *tiles, inverse, meta)
    swap = [(j, j ^ (size_y // 2)) for j in range(size_y)]
    theirs = [lax.ppermute(x, "gy", swap) for x in mine]

    packed, inverse = call(
        sums_kernel,
        [shape(devices, 1, 2 * cols * cols), square],
        [VMEM] * 3,
        [VMEM] * 2,
    )(sums, previous, image)
    sums = everywhere(packed)
    inverse, rayleigh, moved_weights, moved_columns = call(
        factor_kernel,
        [
            square,
            shape(cols, cols),
            shape(slots, count),
            shape(slots, count, dtype=jnp.int32),
        ],
        [SMEM] + [VMEM] * 4,
        [VMEM] * 4,
    )(order, sums, inverse, mine[0], theirs[0])

    def final(first, parts, theirs, *before):
        return call(
            functools.partial(final_kernel, first),
            whole,
            [SMEM] + [VMEM] * (2 + len(theirs)) + [ANY] * len(before),
            pl.BlockSpec((size, cols, cells), lambda i: (first + i, 0, 0)),
            [pltpu.VMEM((2 * count, cols, cells), F32)],
            grid=(parts,),
            input_output_aliases={3 + len(theirs): 0} if before else {},
        )(order, inverse, image, *theirs, *before)

    moved_basis = final(0, CHUNKS - 1, theirs[:-1])
    moved_basis = final(CHUNKS - 1, 1, theirs, moved_basis)
    return (
        moved_basis[None, None],
        moved_weights.T[None, None],
        moved_columns.T[None, None],
        rayleigh,
    )


def solution(mesh):
    return jax.shard_map(
        per_device,
        mesh=mesh,
        in_specs=(
            P("gx", "gy", None, None, None),
            P(),
            P("gx", "gy", None, None),
            P("gx", "gy", None, None),
            P("gx", "gy", None, None),
            P("gx", "gy", None),
        ),
        out_specs=(
            P("gx", "gy", None, None, None),
            P("gx", "gy", None, None),
            P("gx", "gy", None, None),
            P(),
        ),
        check_vma=False,
    )
```

time: 109 us -> 105 us (0.963)
  blocking collectives: 0 us -> 30.8 us
  waiting for transfers between devices: 23.5 us -> 9.74 us
  local copies, waits for them, and re-layouts: 14.5 us -> 3.7 us
  starting transfers between devices: 33.5 us -> 24.1 us
  Pallas kernels: 31.9 us -> 35.8 us
  other arithmetic: 2.4 us -> 0 us
  between operations: 2.25 us -> 0.83 us
    all_to_all x0 -> x2, blocking collectives: none -> 30.8 us  [everywhere(): return lax.all_to_all(rows, AXES, 0, 0, tiled=True)]
    all_to_all x3 -> x1, waiting for transfers between devices: 21.1 us -> 6.25 us  [everywhere(): return lax.all_to_all(rows, AXES, 0, 0, tiled=True)]
    all_to_all x3 -> x1, starting transfers between devices: 8.01 us -> 2.59 us  [everywhere(): return lax.all_to_all(rows, AXES, 0, 0, tiled=True)]
    unnamed x49 -> x14, local copies, waits for them, and re-layouts: 7.77 us -> 3.61 us
    ppermute x13 -> x12, starting transfers between devices: 21.4 us -> 17.4 us  [pairs(): return lax.ppermute(x, axis, swap)]
    pallas_call x6 -> x11, Pallas kernels: 31.8 us -> 35.7 us  [the longest x2 12.1 us: operator(): call(operator_kernel, [whole] + [piece] * 4, [SMEM] * 4 + [VMEM] * 7, [VM...]
    gather x2 -> x0, local copies, waits for them, and re-layouts: 2.15 us -> none  [per_device(): meta = jnp.concatenate([weights, columns.astype(F32)], 1)[order]]
    all_to_all x3 -> x0, local copies, waits for them, and re-layouts: 1.96 us -> none  [everywhere(): return lax.all_to_all(rows, AXES, 0, 0, tiled=True)]
  transfers between devices with their start and end apart: 20 -> 17, of which waited for: 4 -> 4; matrix products, arithmetic and copies ran while one was open for 8% -> 0% of each run, Pallas kernels for 3% -> 13%
where the time goes in v1:
time: 105 us
  Pallas kernels  35.8 us (34%)
  blocking collectives  30.8 us (29%)
  starting transfers between devices  24.1 us (23%)
  waiting for transfers between devices  9.74 us (9%)
  local copies, waits for them, and re-layouts  3.7 us (4%)
    all_to_all x2, blocking collectives, everywhere(): return lax.all_to_all(rows, AXES, 0, 0, tiled=True)  30.8 us
    ppermute x12, starting transfers between devices, pairs(): return lax.ppermute(x, axis, swap)  17.4 us
    pallas_call x2, Pallas kernels, operator(): call(operator_kernel, [whole] + [piece] * 4, [SMEM] * 4 + [VMEM] * 7, [VM...  12.1 us
    pallas_call x1, Pallas kernels, per_device(): call(last_kernel, [whole, shape(size + 1, cols, cells)] + [shape(size, co...  6.55 us
    all_to_all x1, waiting for transfers between devices, everywhere(): return lax.all_to_all(rows, AXES, 0, 0, tiled=True)  6.25 us
    pallas_call x2, Pallas kernels, final(): call(functools.partial(final_kernel, first), whole, [SMEM] + [VMEM] * (2...  4.83 us
    ppermute x4, starting transfers between devices, per_device(): theirs = [lax.ppermute(x, 'gy', swap) for x in mine]  4.13 us
    unnamed x14, local copies, waits for them, and re-layouts  3.61 us
  transfers between devices with their start and end apart: 17, of which 4 were waited for; matrix products, arithmetic and copies ran while one was open for 0% of the time, Pallas kernels for 13%

profile of v1, /device:TPU:0, one launch (start us, length us, event | category | flops | bytes accessed | tf_op | source)
XLA Modules:
  0.0 104.9 jit_solution(12988436213462714030)
XLA Ops:
  1.4 1.2 %copy-done = f32[1,1,128,16,128]{4,3,2,1,0:T(8,128)S(1)} copy-done((f32[1,1,128,16,128]{4,3,2,1,0:T(8,128)S(1)}, f32[1,1,128,16,128]{4,3,2,1,0:T(8,128)}, u32[]{:S(2)}) %copy-start) | copy-done | bytes 1048600
  2.7 1.4 %shard_map.94 = (f32[8,16,128]{2,1,0:T(8,128)S(1)}, f32[8,16,128]{2,1,0:T(8,128)S(1)}, f32[8,16,128]{2,1,0:T(8,128)S(1)}, f32[8,16,128]{2,1,0:T(8,128)S(1)}) custom-call(s32[8]{0:T(128)S(1)} %stack.35.plan, s32[4,8]{1,0:T(4,128)S(1)} %bitcast.42, f32[128,16,128]{2,1,0:T(8,128)S(1)} %bitcast.28), custom_call_target="tpu_custom_call" | custom-call | tf_op jit(solution)/shard_map/pallas_call | solution.py:406
  4.1 3.1 %collective-permute-start = (f32[8,16,128]{2,1,0:T(8,128)S(1)}, f32[8,16,128]{2,1,0:T(8,128)S(1)}, u32[]{:S(2)}, u32[]{:S(2)}) collective-permute-start(f32[8,16,128]{2,1,0:T(8,128)S(1)} %get-tuple-element.37), channel_id=1, source_target_pairs={{0,8},{8,0},{16,24},{24,16},{1,9},{9,1},{17,25},{25,17},{2,10},{10... | collective-permute-start | bytes 196616 | tf_op jit(solution)/shard_map/ppermute | solution.py:360
  7.1 2.5 %collective-permute-start.1 = (f32[8,16,128]{2,1,0:T(8,128)S(1)}, f32[8,16,128]{2,1,0:T(8,128)S(1)}, u32[]{:S(2)}, u32[]{:S(2)}) collective-permute-start(f32[8,16,128]{2,1,0:T(8,128)S(1)} %get-tuple-element.38), channel_id=1, source_target_pairs={{8,16},{16,8},{24,0},{0,24},{9,17},{17,9},{25,1},{1,25},{10,18},{1... | collective-permute-start | bytes 196616 | tf_op jit(solution)/shard_map/ppermute | solution.py:360
  9.6 2.6 %collective-permute-start.3 = (f32[8,16,128]{2,1,0:T(8,128)S(1)}, f32[8,16,128]{2,1,0:T(8,128)S(1)}, u32[]{:S(2)}, u32[]{:S(2)}) collective-permute-start(f32[8,16,128]{2,1,0:T(8,128)S(1)} %get-tuple-element.40), channel_id=1, source_target_pairs={{1,2},{2,1},{3,4},{4,3},{5,6},{6,5},{7,0},{0,7},{9,10},{10,9},{11,... | collective-permute-start | bytes 196616 | tf_op jit(solution)/shard_map/ppermute | solution.py:360
  14.2 6.1 %shard_map.96 = (f32[128,16,128]{2,1,0:T(8,128)S(1)}, f32[8,16,128]{2,1,0:T(8,128)S(1)}, f32[8,16,128]{2,1,0:T(8,128)S(1)}, f32[8,16,128]{2,1,0:T(8,128)S(1)}, f32[8,16,128]{2,1,0:T(8,128)S(1)}) custom-call(s32[8]{0:T(128)S(1)} %stack.35.plan, s32[1024]{0:T(1024)S(1)} %bitcast.38, f32[1024]{0:T(1024)S(1)} %bitcast.34, s32[4,8]{1,0:T(4,128)S(1)} %bitcast.43, ...), custom_call_target="tpu_custom_call" | custom-call | tf_op jit(solution)/shard_map/pallas_call | solution.py:435
  22.0 2.6 %collective-permute-start.7 = (f32[8,16,128]{2,1,0:T(8,128)S(1)}, f32[8,16,128]{2,1,0:T(8,128)S(1)}, u32[]{:S(2)}, u32[]{:S(2)}) collective-permute-start(f32[8,16,128]{2,1,0:T(8,128)S(1)} %get-tuple-element.47), channel_id=1, source_target_pairs={{1,2},{2,1},{3,4},{4,3},{5,6},{6,5},{7,0},{0,7},{9,10},{10,9},{11,... | collective-permute-start | bytes 196616 | tf_op jit(solution)/shard_map/ppermute | solution.py:360
  24.6 2.5 %collective-permute-done.5.h1 = f32[8,16,128]{2,1,0:T(8,128)S(1)} collective-permute-done((f32[8,16,128]{2,1,0:T(8,128)S(1)}, f32[8,16,128]{2,1,0:T(8,128)S(1)}, u32[]{:S(2)}, u32[]{:S(2)}) %collective-permute-start.5) | collective-permute-done | bytes 65568 | tf_op jit(solution)/shard_map/ppermute | solution.py:360
  27.2 6.1 %shard_map.98 = (f32[128,16,128]{2,1,0:T(8,128)S(1)}, f32[8,16,128]{2,1,0:T(8,128)S(1)}, f32[8,16,128]{2,1,0:T(8,128)S(1)}, f32[8,16,128]{2,1,0:T(8,128)S(1)}, f32[8,16,128]{2,1,0:T(8,128)S(1)}) custom-call(s32[8]{0:T(128)S(1)} %stack.35.plan, s32[1024]{0:T(1024)S(1)} %bitcast.39, f32[1024]{0:T(1024)S(1)} %bitcast.35, s32[4,8]{1,0:T(4,128)S(1)} %bitcast.44, ...), custom_call_target="tpu_custom_call" | custom-call | tf_op jit(solution)/shard_map/pallas_call | solution.py:435
  34.1 2.0 %collective-permute-start.9 = (f32[8,16,128]{2,1,0:T(8,128)S(1)}, f32[8,16,128]{2,1,0:T(8,128)S(1)}, u32[]{:S(2)}, u32[]{:S(2)}) collective-permute-start(f32[8,16,128]{2,1,0:T(8,128)S(1)} %get-tuple-element.52), channel_id=1, source_target_pairs={{8,16},{16,8},{24,0},{0,24},{9,17},{17,9},{25,1},{1,25},{10,18},{1... | collective-permute-start | bytes 196616 | tf_op jit(solution)/shard_map/ppermute | solution.py:360
  36.1 2.2 %collective-permute-start.11 = (f32[8,16,128]{2,1,0:T(8,128)S(1)}, f32[8,16,128]{2,1,0:T(8,128)S(1)}, u32[]{:S(2)}, u32[]{:S(2)}) collective-permute-start(f32[8,16,128]{2,1,0:T(8,128)S(1)} %get-tuple-element.54), channel_id=1, source_target_pairs={{1,2},{2,1},{3,4},{4,3},{5,6},{6,5},{7,0},{0,7},{9,10},{10,9},{11,... | collective-permute-start | bytes 196616 | tf_op jit(solution)/shard_map/ppermute | solution.py:360
  38.3 1.3 %shard_map.97 = f32[32,1,256]{2,1,0:T(1,128)} custom-call(f32[128,16,128]{2,1,0:T(8,128)S(1)} %get-tuple-element.43.image.block), custom_call_target="tpu_custom_call" | custom-call | tf_op jit(solution)/shard_map/pallas_call | solution.py:448
  39.6 2.6 %all-to-all-start = ((f32[32,1,256]{2,1,0:T(1,128)}), f32[32,1,256]{2,1,0:T(1,128)S(1)}, u32[]{:S(2)}, u32[]{:S(2)}) async-start(f32[32,1,256]{2,1,0:T(1,128)} %shard_map.97), calls=%async_computation | async-start | bytes 65536 | tf_op jit(solution)/shard_map/all_to_all | solution.py:373
  43.2 6.2 %all-to-all-done.sums = f32[32,1,256]{2,1,0:T(1,128)S(1)} async-done(((f32[32,1,256]{2,1,0:T(1,128)}), f32[32,1,256]{2,1,0:T(1,128)S(1)}, u32[]{:S(2)}, u32[]{:S(2)}) %all-to-all-start) | async-done | bytes 32800 | tf_op jit(solution)/shard_map/all_to_all | solution.py:373
  49.5 2.9 %shard_map.99 = (f32[128,16,128]{2,1,0:T(8,128)S(1)}, f32[16,128]{1,0:T(8,128)S(1)}, f32[32,1,256]{2,1,0:T(1,128)S(1)}) custom-call(f32[32,1,256]{2,1,0:T(1,128)S(1)} %all-to-all-done.sums, f32[128,16,128]{2,1,0:T(8,128)S(1)} %get-tuple-element.48.image), custom_call_target="tpu_custom_call" | custom-call | tf_op jit(solution)/shard_map/pallas_call | solution.py:452
  52.4 6.5 %shard_map.100 = (f32[128,16,128]{2,1,0:T(8,128)S(1)}, f32[33,16,128]{2,1,0:T(8,128)S(1)}, f32[32,16,128]{2,1,0:T(8,128)S(1)}, f32[32,16,128]{2,1,0:T(8,128)S(1)}, f32[32,16,128]{2,1,0:T(8,128)S(1)}) custom-call(s32[8]{0:T(128)S(1)} %stack.35.plan, s32[1024]{0:T(1024)S(1)} %bitcast.41, f32[1024]{0:T(1024)S(1)} %bitcast.37, s32[1024]{0:T(1024)S(1)} %bitcast.30, ...), custom_call_target="tpu_custom_call" | custom-call | tf_op jit(solution)/shard_map/pallas_call | solution.py:458
  59.6 1.5 %collective-permute-start.13 = (f32[32,16,128]{2,1,0:T(8,128)S(1)}, f32[32,16,128]{2,1,0:T(8,128)S(1)}, u32[]{:S(2)}, u32[]{:S(2)}) collective-permute-start(f32[32,16,128]{2,1,0:T(8,128)S(1)} %get-tuple-element.62), channel_id=1, source_target_pairs={{0,4},{1,5},{2,6},{3,7},{4,0},{5,1},{6,2},{7,3},{8,12},{9,13},{10,... | collective-permute-start | bytes 786440 | tf_op jit(solution)/shard_map/ppermute | solution.py:467
  61.6 1.5 %collective-permute-start.15 = (f32[32,16,128]{2,1,0:T(8,128)S(1)}, f32[32,16,128]{2,1,0:T(8,128)S(1)}, u32[]{:S(2)}, u32[]{:S(2)}) collective-permute-start(f32[32,16,128]{2,1,0:T(8,128)S(1)} %get-tuple-element.64), channel_id=1, source_target_pairs={{0,4},{1,5},{2,6},{3,7},{4,0},{5,1},{6,2},{7,3},{8,12},{9,13},{10,... | collective-permute-start | bytes 786440 | tf_op jit(solution)/shard_map/ppermute | solution.py:467
  63.1 21.7 %all_to_all.15.sums = f32[32,1,256]{2,1,0:T(1,128)S(1)} all-to-all(f32[32,1,256]{2,1,0:T(1,128)S(1)} %get-tuple-element.49), channel_id=1, replica_groups=mesh['gx'=4,'gy'=8] {'gx','gy'}, dimensions={0} | all-to-all | bytes 65536 | tf_op jit(solution)/shard_map/all_to_all | solution.py:373
  84.8 3.5 %shard_map.101 = (f32[32,1,512]{2,1,0:T(1,128)S(1)}, f32[16,128]{1,0:T(8,128)S(1)}) custom-call(f32[32,1,256]{2,1,0:T(1,128)S(1)} %all_to_all.15.sums, f32[128,16,128]{2,1,0:T(8,128)S(1)} %get-tuple-element.50.block.previous, f32[128,16,128]{2,1,0:T(8,128)S(1)} %get-tuple-element.57.image), custom_call_target="tpu_custom_call" | custom-call | tf_op jit(solution)/shard_map/pallas_call | solution.py:469
  88.3 9.1 %all_to_all.16.sums = f32[32,1,512]{2,1,0:T(1,128)S(1)} all-to-all(f32[32,1,512]{2,1,0:T(1,128)S(1)} %get-tuple-element.58), channel_id=1, replica_groups=mesh['gx'=4,'gy'=8] {'gx','gy'}, dimensions={0} | all-to-all | bytes 131072 | tf_op jit(solution)/shard_map/all_to_all | solution.py:373
  97.4 2.7 %shard_map.102 = (f32[16,128]{1,0:T(8,128)S(1)}, f32[16,16]{1,0:T(8,128)}, f32[8,128]{1,0:T(8,128)}, s32[8,128]{1,0:T(8,128)}) custom-call(s32[1024]{0:T(1024)S(1)} %bitcast.31, f32[32,1,512]{2,1,0:T(1,128)S(1)} %all_to_all.16.sums, f32[16,128]{1,0:T(8,128)S(1)} %get-tuple-element.59.inverse, f32[33,16,128]{2,1,0:T(8,128)S(1)} %get-tuple-element.60.mine, ...), custom_call_target="tpu_custom_call" | custom-call | tf_op jit(solution)/shard_map/pallas_call | solution.py:476
  100.1 2.9 %shard_map.103.rest_4_ = f32[128,16,128]{2,1,0:T(8,128)} custom-call(s32[1024]{0:T(1024)S(1)} %bitcast.32, f32[16,128]{1,0:T(8,128)S(1)} %get-tuple-element.61.inverse, f32[128,16,128]{2,1,0:T(8,128)S(1)} %get-tuple-element.57.image, f32[33,16,128]{2,1,0:T(8,128)S(1)} %collective-permute-done.12.theirs.rest_0_, ...), custom_call_target="tpu_custom_call" | custom-call | tf_op jit(solution)/shard_map/pallas_call | solution.py:489
  103.0 1.9 %shard_map.104 = f32[128,16,128]{2,1,0:T(8,128)} custom-call(s32[1024]{0:T(1024)S(1)} %bitcast.33, f32[16,128]{1,0:T(8,128)S(1)} %get-tuple-element.61.inverse, f32[128,16,128]{2,1,0:T(8,128)S(1)} %get-tuple-element.57.image, f32[33,16,128]{2,1,0:T(8,128)S(1)} %collective-permute-done.12.theirs.rest_0_, ...), custom_call_target="tpu_custom_call", output_to_operand_aliasing={{}: (7, {})} | custom-call | tf_op jit(solution)/shard_map/pallas_call | solution.py:489
  (39 shorter events, 7.6 us)
Async XLA Ops:
  0.8 0.7 copy-start.5
  1.4 1.2 %copy-start = (f32[1,1,128,16,128]{4,3,2,1,0:T(8,128)S(1)}, f32[1,1,128,16,128]{4,3,2,1,0:T(8,128)}, u32[]{:S(2)}) copy-start(f32[1,1,128,16,128]{4,3,2,1,0:T(8,128)} %param.6) | copy-start | bytes 3145732
  2.7 11.6 %copy-start.1 = (f32[1,1,128,16,128]{4,3,2,1,0:T(8,128)S(1)}, f32[1,1,128,16,128]{4,3,2,1,0:T(8,128)}, u32[]{:S(2)}) copy-start(f32[1,1,128,16,128]{4,3,2,1,0:T(8,128)} %param.6) | copy-start | bytes 3145732
  4.1 9.3 %collective-permute-start = (f32[8,16,128]{2,1,0:T(8,128)S(1)}, f32[8,16,128]{2,1,0:T(8,128)S(1)}, u32[]{:S(2)}, u32[]{:S(2)}) collective-permute-start(f32[8,16,128]{2,1,0:T(8,128)S(1)} %get-tuple-element.37), channel_id=1, source_target_pairs={{0,8},{8,0},{16,24},{24,16},{1,9},{9,1},{17,25},{25,17},{2,10},{10... | collective-permute-start | bytes 196616 | tf_op jit(solution)/shard_map/ppermute | solution.py:360
  7.1 6.2 %collective-permute-start.1 = (f32[8,16,128]{2,1,0:T(8,128)S(1)}, f32[8,16,128]{2,1,0:T(8,128)S(1)}, u32[]{:S(2)}, u32[]{:S(2)}) collective-permute-start(f32[8,16,128]{2,1,0:T(8,128)S(1)} %get-tuple-element.38), channel_id=1, source_target_pairs={{8,16},{16,8},{24,0},{0,24},{9,17},{17,9},{25,1},{1,25},{10,18},{1... | collective-permute-start | bytes 196616 | tf_op jit(solution)/shard_map/ppermute | solution.py:360
  9.6 3.8 %collective-permute-start.2 = (f32[8,16,128]{2,1,0:T(8,128)S(1)}, f32[8,16,128]{2,1,0:T(8,128)S(1)}, u32[]{:S(2)}, u32[]{:S(2)}) collective-permute-start(f32[8,16,128]{2,1,0:T(8,128)S(1)} %get-tuple-element.39), channel_id=1, source_target_pairs={{0,1},{1,0},{2,3},{3,2},{4,5},{5,4},{6,7},{7,6},{8,9},{9,8},{10,11... | collective-permute-start | bytes 196616 | tf_op jit(solution)/shard_map/ppermute | solution.py:360
  9.6 4.6 %collective-permute-start.3 = (f32[8,16,128]{2,1,0:T(8,128)S(1)}, f32[8,16,128]{2,1,0:T(8,128)S(1)}, u32[]{:S(2)}, u32[]{:S(2)}) collective-permute-start(f32[8,16,128]{2,1,0:T(8,128)S(1)} %get-tuple-element.40), channel_id=1, source_target_pairs={{1,2},{2,1},{3,4},{4,3},{5,6},{6,5},{7,0},{0,7},{9,10},{10,9},{11,... | collective-permute-start | bytes 196616 | tf_op jit(solution)/shard_map/ppermute | solution.py:360
  12.2 1.0 copy-start.2
  13.2 1.0 copy-start.4
  13.4 0.9 copy-start.3
  20.3 4.3 %collective-permute-start.4 = (f32[8,16,128]{2,1,0:T(8,128)S(1)}, f32[8,16,128]{2,1,0:T(8,128)S(1)}, u32[]{:S(2)}, u32[]{:S(2)}) collective-permute-start(f32[8,16,128]{2,1,0:T(8,128)S(1)} %get-tuple-element.44), channel_id=1, source_target_pairs={{0,8},{8,0},{16,24},{24,16},{1,9},{9,1},{17,25},{25,17},{2,10},{10... | collective-permute-start | bytes 196616 | tf_op jit(solution)/shard_map/ppermute | solution.py:360
  21.0 6.1 %collective-permute-start.5 = (f32[8,16,128]{2,1,0:T(8,128)S(1)}, f32[8,16,128]{2,1,0:T(8,128)S(1)}, u32[]{:S(2)}, u32[]{:S(2)}) collective-permute-start(f32[8,16,128]{2,1,0:T(8,128)S(1)} %get-tuple-element.45), channel_id=1, source_target_pairs={{8,16},{16,8},{24,0},{0,24},{9,17},{17,9},{25,1},{1,25},{10,18},{1... | collective-permute-start | bytes 196616 | tf_op jit(solution)/shard_map/ppermute | solution.py:360
  22.0 5.2 %collective-permute-start.6 = (f32[8,16,128]{2,1,0:T(8,128)S(1)}, f32[8,16,128]{2,1,0:T(8,128)S(1)}, u32[]{:S(2)}, u32[]{:S(2)}) collective-permute-start(f32[8,16,128]{2,1,0:T(8,128)S(1)} %get-tuple-element.46), channel_id=1, source_target_pairs={{0,1},{1,0},{2,3},{3,2},{4,5},{5,4},{6,7},{7,6},{8,9},{9,8},{10,11... | collective-permute-start | bytes 196616 | tf_op jit(solution)/shard_map/ppermute | solution.py:360
  22.0 5.2 %collective-permute-start.7 = (f32[8,16,128]{2,1,0:T(8,128)S(1)}, f32[8,16,128]{2,1,0:T(8,128)S(1)}, u32[]{:S(2)}, u32[]{:S(2)}) collective-permute-start(f32[8,16,128]{2,1,0:T(8,128)S(1)} %get-tuple-element.47), channel_id=1, source_target_pairs={{1,2},{2,1},{3,4},{4,3},{5,6},{6,5},{7,0},{0,7},{9,10},{10,9},{11,... | collective-permute-start | bytes 196616 | tf_op jit(solution)/shard_map/ppermute | solution.py:360
  33.3 19.1 %collective-permute-start.8 = (f32[8,16,128]{2,1,0:T(8,128)S(1)}, f32[8,16,128]{2,1,0:T(8,128)S(1)}, u32[]{:S(2)}, u32[]{:S(2)}) collective-permute-start(f32[8,16,128]{2,1,0:T(8,128)S(1)} %get-tuple-element.51), channel_id=1, source_target_pairs={{0,8},{8,0},{16,24},{24,16},{1,9},{9,1},{17,25},{25,17},{2,10},{10... | collective-permute-start | bytes 196616 | tf_op jit(solution)/shard_map/ppermute | solution.py:360
  34.1 18.3 %collective-permute-start.9 = (f32[8,16,128]{2,1,0:T(8,128)S(1)}, f32[8,16,128]{2,1,0:T(8,128)S(1)}, u32[]{:S(2)}, u32[]{:S(2)}) collective-permute-start(f32[8,16,128]{2,1,0:T(8,128)S(1)} %get-tuple-element.52), channel_id=1, source_target_pairs={{8,16},{16,8},{24,0},{0,24},{9,17},{17,9},{25,1},{1,25},{10,18},{1... | collective-permute-start | bytes 196616 | tf_op jit(solution)/shard_map/ppermute | solution.py:360
  36.1 16.3 %collective-permute-start.10 = (f32[8,16,128]{2,1,0:T(8,128)S(1)}, f32[8,16,128]{2,1,0:T(8,128)S(1)}, u32[]{:S(2)}, u32[]{:S(2)}) collective-permute-start(f32[8,16,128]{2,1,0:T(8,128)S(1)} %get-tuple-element.53), channel_id=1, source_target_pairs={{0,1},{1,0},{2,3},{3,2},{4,5},{5,4},{6,7},{7,6},{8,9},{9,8},{10,11... | collective-permute-start | bytes 196616 | tf_op jit(solution)/shard_map/ppermute | solution.py:360
  36.1 16.3 %collective-permute-start.11 = (f32[8,16,128]{2,1,0:T(8,128)S(1)}, f32[8,16,128]{2,1,0:T(8,128)S(1)}, u32[]{:S(2)}, u32[]{:S(2)}) collective-permute-start(f32[8,16,128]{2,1,0:T(8,128)S(1)} %get-tuple-element.54), channel_id=1, source_target_pairs={{1,2},{2,1},{3,4},{4,3},{5,6},{6,5},{7,0},{0,7},{9,10},{10,9},{11,... | collective-permute-start | bytes 196616 | tf_op jit(solution)/shard_map/ppermute | solution.py:360
  39.6 9.9 %all-to-all-start = ((f32[32,1,256]{2,1,0:T(1,128)}), f32[32,1,256]{2,1,0:T(1,128)S(1)}, u32[]{:S(2)}, u32[]{:S(2)}) async-start(f32[32,1,256]{2,1,0:T(1,128)} %shard_map.97), calls=%async_computation | async-start | bytes 65536 | tf_op jit(solution)/shard_map/all_to_all | solution.py:373
  42.2 0.7 copy-start.6
  59.0 38.4 %collective-permute-start.12 = (f32[33,16,128]{2,1,0:T(8,128)S(1)}, f32[33,16,128]{2,1,0:T(8,128)S(1)}, u32[]{:S(2)}, u32[]{:S(2)}) collective-permute-start(f32[33,16,128]{2,1,0:T(8,128)S(1)} %get-tuple-element.60.mine), channel_id=1, source_target_pairs={{0,4},{1,5},{2,6},{3,7},{4,0},{5,1},{6,2},{7,3},{8,12},{9,13},{10,... | collective-permute-start | bytes 811016 | tf_op jit(solution)/shard_map/ppermute | solution.py:467
  59.6 40.5 %collective-permute-start.13 = (f32[32,16,128]{2,1,0:T(8,128)S(1)}, f32[32,16,128]{2,1,0:T(8,128)S(1)}, u32[]{:S(2)}, u32[]{:S(2)}) collective-permute-start(f32[32,16,128]{2,1,0:T(8,128)S(1)} %get-tuple-element.62), channel_id=1, source_target_pairs={{0,4},{1,5},{2,6},{3,7},{4,0},{5,1},{6,2},{7,3},{8,12},{9,13},{10,... | collective-permute-start | bytes 786440 | tf_op jit(solution)/shard_map/ppermute | solution.py:467
  61.1 39.0 %collective-permute-start.14 = (f32[32,16,128]{2,1,0:T(8,128)S(1)}, f32[32,16,128]{2,1,0:T(8,128)S(1)}, u32[]{:S(2)}, u32[]{:S(2)}) collective-permute-start(f32[32,16,128]{2,1,0:T(8,128)S(1)} %get-tuple-element.63), channel_id=1, source_target_pairs={{0,4},{1,5},{2,6},{3,7},{4,0},{5,1},{6,2},{7,3},{8,12},{9,13},{10,... | collective-permute-start | bytes 786440 | tf_op jit(solution)/shard_map/ppermute | solution.py:467
  61.6 41.4 %collective-permute-start.15 = (f32[32,16,128]{2,1,0:T(8,128)S(1)}, f32[32,16,128]{2,1,0:T(8,128)S(1)}, u32[]{:S(2)}, u32[]{:S(2)}) collective-permute-start(f32[32,16,128]{2,1,0:T(8,128)S(1)} %get-tuple-element.64), channel_id=1, source_target_pairs={{0,4},{1,5},{2,6},{3,7},{4,0},{5,1},{6,2},{7,3},{8,12},{9,13},{10,... | collective-permute-start | bytes 786440 | tf_op jit(solution)/shard_map/ppermute | solution.py:467

commit v2 on v1

--- a/solution.py
+++ b/solution.py
@@ -122,8 +122,11 @@
     return x.reshape(128, 128)
 
 
-def first_sends_kernel(plan, sends, block, *rest):
-    outs, sems = rest[:-1], rest[-1]
+def first_sends_kernel(plan, sends_hbm, block, *rest):
+    outs, (sends, sems, sem) = rest[:-3], rest[-3:]
+    copy = pltpu.make_async_copy(sends_hbm, sends, sem)
+    copy.start()
+    copy.wait()
     copies = []
     for n, out in enumerate(outs):
         for h in range(out.shape[0]):
@@ -192,8 +195,13 @@
                 )
 
 
-def load_blocks(x, block, halos, plan, left):
+def load_blocks(x, block, halos, landed, sems, plan, left):
     count, cols, cells = block.shape
+    copies = [
+        pltpu.make_async_copy(halo, landed.at[n], sems.at[n]) for n, halo in enumerate(halos)
+    ]
+    for copy in copies:
+        copy.start()
 
     def put(rows, values):
         high, low = split(values)
@@ -203,7 +211,8 @@
     put(slice(0, count * cols), block[...].reshape(count * cols, cells))
     for n, halo in enumerate(halos):
         rows = halo.shape[0] * cols
-        values = jnp.where(plan[len(halos) + n] != 0, halo[...].reshape(rows, cells), 0.0)
+        copies[n].wait()
+        values = jnp.where(plan[len(halos) + n] != 0, landed[n].reshape(rows, cells), 0.0)
         if left is not None:
             values = apply_scaler(left, values)
         start = pl.multiple_of((count + plan[n] * halo.shape[0]) * cols, rows)
@@ -218,9 +227,9 @@
 
 
 def operator_kernel(plan, columns, weights, sends, block, h0, h1, h2, h3, th, tl, *rest):
-    image, sent, x, z = rest[0], rest[1:-2], rest[-2], rest[-1]
+    image, sent, (x, z, landed, sems) = rest[0], rest[1:-4], rest[-4:]
     count, cols, _ = block.shape
-    load_blocks(x, block, (h0, h1, h2, h3), plan, None)
+    load_blocks(x, block, (h0, h1, h2, h3), landed, sems, plan, None)
     products(z, x, th, tl, cols)
 
     @pl.loop(0, count, unroll=4)
@@ -233,9 +242,9 @@
 
 
 def last_kernel(plan, columns, weights, order, block, h0, h1, h2, h3, th, tl, inv, meta, *rest):
-    image, chunks, x, z = rest[0], rest[1:-2], rest[-2], rest[-1]
+    image, chunks, (x, z, landed, sems) = rest[0], rest[1:-4], rest[-4:]
     count, cols, _ = block.shape
-    load_blocks(x, block, (h0, h1, h2, h3), plan, scaler(inv[...]))
+    load_blocks(x, block, (h0, h1, h2, h3), landed, sems, plan, scaler(inv[...]))
     products(z, x, th, tl, cols)
     size = count // len(chunks)
     for i, chunk in enumerate(chunks):
@@ -338,7 +347,7 @@
         out[g * per : (g + 1) * per] = apply_scaler(left, value).reshape(per, cols, cells)
 
 
-def call(kernel, out_shape, in_specs, out_specs, scratch=(), limit=16, flops=0, moved=0, **more):
+def call(kernel, out_shape, in_specs, out_specs, scratch=(), limit=24, cost=(0, 0), **more):
     return pl.pallas_call(
         kernel,
         out_shape=out_shape,
@@ -346,7 +355,7 @@
         out_specs=out_specs,
         scratch_shapes=list(scratch),
         compiler_params=pltpu.CompilerParams(vmem_limit_bytes=limit << 20),
-        cost_estimate=pl.CostEstimate(flops=flops, transcendentals=0, bytes_accessed=moved),
+        cost_estimate=pl.CostEstimate(flops=cost[0], transcendentals=0, bytes_accessed=cost[1]),
         **more,
     )
 
@@ -360,13 +369,18 @@
     return lax.ppermute(x, axis, swap)
 
 
+def in_hbm(x):
+    return pltpu.with_memory_space_constraint(x, pltpu.HBM)
+
+
 def halo(sent):
-    return (
+    near = (
         pairs(sent[0], "gx", 0),
         pairs(sent[1], "gx", 1),
         pairs(sent[2], "gy", 0),
         pairs(sent[3], "gy", 1),
     )
+    return near
 
 
 def everywhere(rows):
@@ -406,10 +420,14 @@
     sent = call(
         first_sends_kernel,
         [piece] * 4,
-        [SMEM, SMEM, HBM],
+        [SMEM, HBM, HBM],
         [VMEM] * 4,
-        [pltpu.SemaphoreType.DMA((4, width))],
-    )(plan, sends, block)
+        [
+            pltpu.SMEM(sends.shape, jnp.int32),
+            pltpu.SemaphoreType.DMA((4, width)),
+            pltpu.SemaphoreType.DMA,
+        ],
+    )(plan, in_hbm(sends), in_hbm(block))
     near = halo(sent)
 
     wide = 2 * cells
@@ -426,31 +444,37 @@
     order = order.reshape(8 * count)
 
     blocks = count + 4 * width
+    work = 8 * blocks * cols * cells * cells * slots, 0
+    small = 8 * count * cells * cells * cols, 0
     scratch = [
         pltpu.VMEM((blocks * cols, wide), BF16),
         pltpu.VMEM((slots, blocks, cols, cells), F32),
+        pltpu.VMEM((4, width, cols, cells), F32),
+        pltpu.SemaphoreType.DMA((4,)),
     ]
 
     def operator(block, near):
         image, *sent = call(
             operator_kernel,
             [whole] + [piece] * 4,
-            [SMEM] * 4 + [VMEM] * 7,
+            [SMEM] * 4 + [VMEM] + [ANY] * 4 + [VMEM] * 2,
             [VMEM] * 5,
             scratch,
             limit=24,
+            cost=work,
         )(plan, flat_columns, flat_weights, sends, block, *near, *tiles)
         return image, sent
 
     gram_rows = shape(devices, 1, cols * cols)
     image, sent = operator(block, near)
     near = halo(sent)
-    packed = call(gram_kernel, gram_rows, [VMEM], VMEM)(image)
+    packed = call(gram_kernel, gram_rows, [VMEM], VMEM, cost=small)(image)
+    image, packed = lax.optimization_barrier((image, packed))
     sums = everywhere(packed)
     image, sent = operator(image, near)
     near = halo(sent)
     previous, inverse, packed = call(
-        scale_kernel, [whole, square, gram_rows], [VMEM] * 2, [VMEM] * 3
+        scale_kernel, [whole, square, gram_rows], [VMEM] * 2, [VMEM] * 3, cost=small
     )(sums, image)
     sums = everywhere(packed)
 
@@ -458,21 +482,25 @@
     image, *mine = call(
         last_kernel,
         [whole, shape(size + 1, cols, cells)] + [shape(size, cols, cells)] * (CHUNKS - 1),
-        [SMEM] * 4 + [VMEM] * 9,
+        [SMEM] * 4 + [VMEM] + [ANY] * 4 + [VMEM] * 4,
         [VMEM] * (1 + CHUNKS),
         scratch,
         limit=24,
+        cost=work,
     )(plan, flat_columns, flat_weights, order, previous, *near, *tiles, inverse, meta)
+    mine, sums = lax.optimization_barrier((mine, sums))
     swap = [(j, j ^ (size_y // 2)) for j in range(size_y)]
-    theirs = [lax.ppermute(x, "gy", swap) for x in mine]
-
+    theirs = [lax.ppermute(mine[0], "gy", swap)]
     packed, inverse = call(
         sums_kernel,
         [shape(devices, 1, 2 * cols * cols), square],
         [VMEM] * 3,
         [VMEM] * 2,
+        cost=small,
     )(sums, previous, image)
+    packed, *later = lax.optimization_barrier((packed, *mine[1:]))
     sums = everywhere(packed)
+    theirs += [lax.ppermute(x, "gy", swap) for x in later]
     inverse, rayleigh, moved_weights, moved_columns = call(
         factor_kernel,
         [

time: 105 us -> 101 us (0.962)
  blocking collectives: 30.8 us -> 18.4 us
  waiting for transfers between devices: 9.74 us -> 0.85 us
  local copies, waits for them, and re-layouts: 3.7 us -> 10.4 us
  starting transfers between devices: 24.1 us -> 29.4 us
  Pallas kernels: 35.8 us -> 40.5 us
    all_to_all x2 -> x1, blocking collectives: 30.8 us -> 18.4 us  [everywhere(): return lax.all_to_all(rows, AXES, 0, 0, tiled=True)]
    unnamed x14 -> x40, local copies, waits for them, and re-layouts: 3.61 us -> 10.4 us
    all_to_all x1 -> x2, waiting for transfers between devices: 6.25 us -> 0.01 us  [everywhere(): return lax.all_to_all(rows, AXES, 0, 0, tiled=True)]
    pallas_call x5, Pallas kernels: 17.8 us -> 21.7 us  [the longest x2 14.3 us: operator(): call(operator_kernel, [whole] + [piece] * 4, [SMEM] * 4 + [VMEM] + [ANY]...]
    all_to_all x1 -> x2, starting transfers between devices: 2.59 us -> 6.22 us  [everywhere(): return lax.all_to_all(rows, AXES, 0, 0, tiled=True)]
    ppermute x12, waiting for transfers between devices: 3.48 us -> 0.83 us  [pairs(): return lax.ppermute(x, axis, swap)]
    ppermute x12, starting transfers between devices: 17.4 us -> 19 us  [pairs(): return lax.ppermute(x, axis, swap)]
  transfers between devices with their start and end apart: 17 -> 18, of which waited for: 4 -> 1; matrix products, arithmetic and copies ran while one was open for 0% -> 0% of each run, Pallas kernels for 13% -> 29%
where the time goes in v2:
time: 101 us; the launch traced here: 100 us
  Pallas kernels  40.5 us (40%)
  starting transfers between devices  29.4 us (29%)
  blocking collectives  18.4 us (18%)
  local copies, waits for them, and re-layouts  10.4 us (10%)
    ppermute x12, starting transfers between devices, pairs(): return lax.ppermute(x, axis, swap)  19 us
    all_to_all x1, blocking collectives, everywhere(): return lax.all_to_all(rows, AXES, 0, 0, tiled=True)  18.4 us
    pallas_call x2, Pallas kernels, operator(): call(operator_kernel, [whole] + [piece] * 4, [SMEM] * 4 + [VMEM] + [ANY]...  14.3 us
    unnamed x40, local copies, waits for them, and re-layouts  10.4 us
    pallas_call x1, Pallas kernels, per_device(): call(last_kernel, [whole, shape(size + 1, cols, cells)] + [shape(size, co...  7.34 us
    all_to_all x2, starting transfers between devices, everywhere(): return lax.all_to_all(rows, AXES, 0, 0, tiled=True)  6.22 us
    pallas_call x2, Pallas kernels, final(): call(functools.partial(final_kernel, first), whole, [SMEM] + [VMEM] * (2...  4.83 us
    pallas_call x1, Pallas kernels, per_device(): call(scale_kernel, [whole, square, gram_rows], [VMEM] * 2, [VMEM] * 3, co...  3.55 us
  transfers between devices with their start and end apart: 18, of which 1 were waited for; matrix products, arithmetic and copies ran while one was open for 0% of the time, Pallas kernels for 29%

profile of v2, /device:TPU:0, one launch (start us, length us, event | category | flops | bytes accessed | tf_op | source)
XLA Modules:
  0.0 100.5 jit_solution(10851842305730147996)
XLA Ops:
  0.8 2.5 %shard_map.94 = (f32[8,16,128]{2,1,0:T(8,128)S(1)}, f32[8,16,128]{2,1,0:T(8,128)S(1)}, f32[8,16,128]{2,1,0:T(8,128)S(1)}, f32[8,16,128]{2,1,0:T(8,128)S(1)}) custom-call(s32[8]{0:T(128)S(1)} %stack.35.plan, s32[4,8]{1,0:T(4,128)} %bitcast.42, f32[128,16,128]{2,1,0:T(8,128)} %bitcast.28), custom_call_target="tpu_custom_call" | custom-call | tf_op jit(solution)/shard_map/pallas_call | solution.py:420
  3.2 3.1 %collective-permute-start = (f32[8,16,128]{2,1,0:T(8,128)S(1)}, f32[8,16,128]{2,1,0:T(8,128)S(1)}, u32[]{:S(2)}, u32[]{:S(2)}) collective-permute-start(f32[8,16,128]{2,1,0:T(8,128)S(1)} %get-tuple-element.48), channel_id=1, source_target_pairs={{0,8},{8,0},{16,24},{24,16},{1,9},{9,1},{17,25},{25,17},{2,10},{10... | collective-permute-start | bytes 196616 | tf_op jit(solution)/shard_map/ppermute | solution.py:369
  6.3 2.5 %collective-permute-start.1 = (f32[8,16,128]{2,1,0:T(8,128)S(1)}, f32[8,16,128]{2,1,0:T(8,128)S(1)}, u32[]{:S(2)}, u32[]{:S(2)}) collective-permute-start(f32[8,16,128]{2,1,0:T(8,128)S(1)} %get-tuple-element.49), channel_id=1, source_target_pairs={{8,16},{16,8},{24,0},{0,24},{9,17},{17,9},{25,1},{1,25},{10,18},{1... | collective-permute-start | bytes 196616 | tf_op jit(solution)/shard_map/ppermute | solution.py:369
  8.8 2.6 %collective-permute-start.3 = (f32[8,16,128]{2,1,0:T(8,128)S(1)}, f32[8,16,128]{2,1,0:T(8,128)S(1)}, u32[]{:S(2)}, u32[]{:S(2)}) collective-permute-start(f32[8,16,128]{2,1,0:T(8,128)S(1)} %get-tuple-element.51), channel_id=1, source_target_pairs={{1,2},{2,1},{3,4},{4,3},{5,6},{6,5},{7,0},{0,7},{9,10},{10,9},{11,... | collective-permute-start | bytes 196616 | tf_op jit(solution)/shard_map/ppermute | solution.py:369
  11.4 1.0 %copy-done.1 = f32[8,128,128]{2,1,0:T(8,128)S(1)} copy-done((f32[8,128,128]{2,1,0:T(8,128)S(1)}, f32[8,128,128]{2,1,0:T(8,128)}, u32[]{:S(2)}) %copy-start.1) | copy-done | bytes 524312
  14.1 7.2 %shard_map.96 = (f32[128,16,128]{2,1,0:T(8,128)S(1)}, f32[8,16,128]{2,1,0:T(8,128)}, f32[8,16,128]{2,1,0:T(8,128)}, f32[8,16,128]{2,1,0:T(8,128)}, f32[8,16,128]{2,1,0:T(8,128)S(1)}) custom-call(s32[8]{0:T(128)S(1)} %stack.35.plan, s32[1024]{0:T(1024)S(1)} %bitcast.38, f32[1024]{0:T(1024)S(1)} %bitcast.34, s32[4,8]{1,0:T(4,128)S(1)} %bitcast.43, ...), custom_call_target="tpu_custom_call" | custom-call | flops 2684354560 | tf_op jit(solution)/shard_map/pallas_call | solution.py:457
  22.0 0.9 collective-permute-start.5
  22.9 2.6 %collective-permute-start.7 = (f32[8,16,128]{2,1,0:T(8,128)S(1)}, f32[8,16,128]{2,1,0:T(8,128)S(1)}, u32[]{:S(2)}, u32[]{:S(2)}) collective-permute-start(f32[8,16,128]{2,1,0:T(8,128)S(1)} %get-tuple-element.60), channel_id=1, source_target_pairs={{1,2},{2,1},{3,4},{4,3},{5,6},{6,5},{7,0},{0,7},{9,10},{10,9},{11,... | collective-permute-start | bytes 196616 | tf_op jit(solution)/shard_map/ppermute | solution.py:369
  25.5 1.3 %shard_map.97 = f32[32,1,256]{2,1,0:T(1,128)} custom-call(f32[128,16,128]{2,1,0:T(8,128)S(1)} %get-tuple-element.56.image.block), custom_call_target="tpu_custom_call" | custom-call | flops 268435456 | tf_op jit(solution)/shard_map/pallas_call | solution.py:471
  26.8 3.7 %all-to-all-start = ((f32[32,1,256]{2,1,0:T(1,128)}), f32[32,1,256]{2,1,0:T(1,128)S(1)}, u32[]{:S(2)}, u32[]{:S(2)}) async-start(f32[32,1,256]{2,1,0:T(1,128)} %shard_map.97), calls=%async_computation | async-start | bytes 65536 | tf_op jit(solution)/shard_map/all_to_all | solution.py:387
  33.4 7.2 %shard_map.98 = (f32[128,16,128]{2,1,0:T(8,128)S(1)}, f32[8,16,128]{2,1,0:T(8,128)}, f32[8,16,128]{2,1,0:T(8,128)}, f32[8,16,128]{2,1,0:T(8,128)}, f32[8,16,128]{2,1,0:T(8,128)S(1)}) custom-call(s32[8]{0:T(128)S(1)} %stack.35.plan, s32[1024]{0:T(1024)S(1)} %bitcast.39, f32[1024]{0:T(1024)S(1)} %bitcast.35, s32[4,8]{1,0:T(4,128)S(1)} %bitcast.44, ...), custom_call_target="tpu_custom_call" | custom-call | flops 2684354560 | tf_op jit(solution)/shard_map/pallas_call | solution.py:457
  40.6 1.8 %collective-permute-start.8 = (f32[8,16,128]{2,1,0:T(8,128)}, f32[8,16,128]{2,1,0:T(8,128)S(1)}, u32[]{:S(2)}, u32[]{:S(2)}) collective-permute-start(f32[8,16,128]{2,1,0:T(8,128)} %get-tuple-element.63), channel_id=1, source_target_pairs={{0,8},{8,0},{16,24},{24,16},{1,9},{9,1},{17,25},{25,17},{2,10},{10... | collective-permute-start | bytes 196616 | tf_op jit(solution)/shard_map/ppermute | solution.py:369
  42.5 2.4 %collective-permute-start.9 = (f32[8,16,128]{2,1,0:T(8,128)}, f32[8,16,128]{2,1,0:T(8,128)S(1)}, u32[]{:S(2)}, u32[]{:S(2)}) collective-permute-start(f32[8,16,128]{2,1,0:T(8,128)} %get-tuple-element.64), channel_id=1, source_target_pairs={{8,16},{16,8},{24,0},{0,24},{9,17},{17,9},{25,1},{1,25},{10,18},{1... | collective-permute-start | bytes 196616 | tf_op jit(solution)/shard_map/ppermute | solution.py:369
  44.8 2.5 %collective-permute-start.11 = (f32[8,16,128]{2,1,0:T(8,128)S(1)}, f32[8,16,128]{2,1,0:T(8,128)}, u32[]{:S(2)}, u32[]{:S(2)}) collective-permute-start(f32[8,16,128]{2,1,0:T(8,128)S(1)} %get-tuple-element.66), channel_id=1, source_target_pairs={{1,2},{2,1},{3,4},{4,3},{5,6},{6,5},{7,0},{0,7},{9,10},{10,9},{11,... | collective-permute-start | bytes 196616 | tf_op jit(solution)/shard_map/ppermute | solution.py:369
  48.3 3.6 %shard_map.99 = (f32[128,16,128]{2,1,0:T(8,128)S(1)}, f32[16,128]{1,0:T(8,128)S(1)}, f32[32,1,256]{2,1,0:T(1,128)}) custom-call(f32[32,1,256]{2,1,0:T(1,128)S(1)} %all-to-all-done.sums, f32[128,16,128]{2,1,0:T(8,128)S(1)} %get-tuple-element.61.image), custom_call_target="tpu_custom_call" | custom-call | flops 268435456 | tf_op jit(solution)/shard_map/pallas_call | solution.py:476
  51.9 2.5 %all-to-all-start.1 = ((f32[32,1,256]{2,1,0:T(1,128)}), f32[32,1,256]{2,1,0:T(1,128)S(1)}, u32[]{:S(2)}, u32[]{:S(2)}) async-start(f32[32,1,256]{2,1,0:T(1,128)} %get-tuple-element.73), calls=%async_computation.1 | async-start | bytes 65536 | tf_op jit(solution)/shard_map/all_to_all | solution.py:387
  57.4 7.3 %shard_map.100 = (f32[128,16,128]{2,1,0:T(8,128)S(1)}, f32[33,16,128]{2,1,0:T(8,128)S(1)}, f32[32,16,128]{2,1,0:T(8,128)S(1)}, f32[32,16,128]{2,1,0:T(8,128)S(1)}, f32[32,16,128]{2,1,0:T(8,128)S(1)}) custom-call(s32[8]{0:T(128)S(1)} %stack.35.plan, s32[1024]{0:T(1024)S(1)} %bitcast.41, f32[1024]{0:T(1024)S(1)} %bitcast.37, s32[1024]{0:T(1024)S(1)} %bitcast.30, ...), custom_call_target="tpu_custom_call" | custom-call | flops 2684354560 | tf_op jit(solution)/shard_map/pallas_call | solution.py:482
  66.8 1.7 %collective-permute-start.12 = (f32[33,16,128]{2,1,0:T(8,128)S(1)}, f32[33,16,128]{2,1,0:T(8,128)S(1)}, u32[]{:S(2)}, u32[]{:S(2)}) collective-permute-start(f32[33,16,128]{2,1,0:T(8,128)S(1)} %get-tuple-element.82.mine), channel_id=1, source_target_pairs={{0,4},{1,5},{2,6},{3,7},{4,0},{5,1},{6,2},{7,3},{8,12},{9,13},{10,... | collective-permute-start | bytes 811016 | tf_op jit(solution)/shard_map/ppermute | solution.py:493
  68.5 3.5 %shard_map.101 = (f32[32,1,512]{2,1,0:T(1,128)S(1)}, f32[16,128]{1,0:T(8,128)S(1)}) custom-call(f32[32,1,256]{2,1,0:T(1,128)S(1)} %all-to-all-done.1.sums, f32[128,16,128]{2,1,0:T(8,128)S(1)} %get-tuple-element.62.block.previous, f32[128,16,128]{2,1,0:T(8,128)S(1)} %get-tuple-element.75.image), custom_call_target="tpu_custom_call" | custom-call | flops 268435456 | tf_op jit(solution)/shard_map/pallas_call | solution.py:494
  72.5 1.7 %collective-permute-start.14 = (f32[32,16,128]{2,1,0:T(8,128)S(1)}, f32[32,16,128]{2,1,0:T(8,128)S(1)}, u32[]{:S(2)}, u32[]{:S(2)}) collective-permute-start(f32[32,16,128]{2,1,0:T(8,128)S(1)} %copy-done.9), channel_id=1, source_target_pairs={{0,4},{1,5},{2,6},{3,7},{4,0},{5,1},{6,2},{7,3},{8,12},{9,13},{10,... | collective-permute-start | bytes 786440 | tf_op jit(solution)/shard_map/ppermute | solution.py:503
  74.5 18.4 %all_to_all.15.sums = f32[32,1,512]{2,1,0:T(1,128)S(1)} all-to-all(f32[32,1,512]{2,1,0:T(1,128)S(1)} %get-tuple-element.80), channel_id=1, replica_groups=mesh['gx'=4,'gy'=8] {'gx','gy'}, dimensions={0} | all-to-all | bytes 131072 | tf_op jit(solution)/shard_map/all_to_all | solution.py:387
  92.9 2.7 %shard_map.102 = (f32[16,128]{1,0:T(8,128)S(1)}, f32[16,16]{1,0:T(8,128)}, f32[8,128]{1,0:T(8,128)}, s32[8,128]{1,0:T(8,128)}) custom-call(s32[1024]{0:T(1024)S(1)} %bitcast.31, f32[32,1,512]{2,1,0:T(1,128)S(1)} %all_to_all.15.sums, f32[16,128]{1,0:T(8,128)S(1)} %get-tuple-element.81.inverse, f32[33,16,128]{2,1,0:T(8,128)S(1)} %get-tuple-element.82.mine, ...), custom_call_target="tpu_custom_call" | custom-call | tf_op jit(solution)/shard_map/pallas_call | solution.py:504
  95.6 2.9 %shard_map.103.rest_4_ = f32[128,16,128]{2,1,0:T(8,128)} custom-call(s32[1024]{0:T(1024)S(1)} %bitcast.32, f32[16,128]{1,0:T(8,128)S(1)} %get-tuple-element.83.inverse, f32[128,16,128]{2,1,0:T(8,128)S(1)} %get-tuple-element.75.image, f32[33,16,128]{2,1,0:T(8,128)S(1)} %collective-permute-done.12.theirs.rest_0_, ...), custom_call_target="tpu_custom_call" | custom-call | tf_op jit(solution)/shard_map/pallas_call | solution.py:517
  98.6 1.9 %shard_map.104 = f32[128,16,128]{2,1,0:T(8,128)} custom-call(s32[1024]{0:T(1024)S(1)} %bitcast.33, f32[16,128]{1,0:T(8,128)S(1)} %get-tuple-element.83.inverse, f32[128,16,128]{2,1,0:T(8,128)S(1)} %get-tuple-element.75.image, f32[33,16,128]{2,1,0:T(8,128)S(1)} %collective-permute-done.12.theirs.rest_0_, ...), custom_call_target="tpu_custom_call", output_to_operand_aliasing={{}: (7, {})} | custom-call | tf_op jit(solution)/shard_map/pallas_call | solution.py:517
  (66 shorter events, 12.3 us)
Async XLA Ops:
  0.6 12.8 %copy-start = (f32[1,1,128,16,128]{4,3,2,1,0:T(8,128)S(1)}, f32[1,1,128,16,128]{4,3,2,1,0:T(8,128)}, u32[]{:S(2)}) copy-start(f32[1,1,128,16,128]{4,3,2,1,0:T(8,128)} %param.6) | copy-start | bytes 3145732
  3.2 9.3 %collective-permute-start = (f32[8,16,128]{2,1,0:T(8,128)S(1)}, f32[8,16,128]{2,1,0:T(8,128)S(1)}, u32[]{:S(2)}, u32[]{:S(2)}) collective-permute-start(f32[8,16,128]{2,1,0:T(8,128)S(1)} %get-tuple-element.48), channel_id=1, source_target_pairs={{0,8},{8,0},{16,24},{24,16},{1,9},{9,1},{17,25},{25,17},{2,10},{10... | collective-permute-start | bytes 196616 | tf_op jit(solution)/shard_map/ppermute | solution.py:369
  6.3 6.2 %collective-permute-start.1 = (f32[8,16,128]{2,1,0:T(8,128)S(1)}, f32[8,16,128]{2,1,0:T(8,128)S(1)}, u32[]{:S(2)}, u32[]{:S(2)}) collective-permute-start(f32[8,16,128]{2,1,0:T(8,128)S(1)} %get-tuple-element.49), channel_id=1, source_target_pairs={{8,16},{16,8},{24,0},{0,24},{9,17},{17,9},{25,1},{1,25},{10,18},{1... | collective-permute-start | bytes 196616 | tf_op jit(solution)/shard_map/ppermute | solution.py:369
  8.8 3.8 %collective-permute-start.2 = (f32[8,16,128]{2,1,0:T(8,128)S(1)}, f32[8,16,128]{2,1,0:T(8,128)S(1)}, u32[]{:S(2)}, u32[]{:S(2)}) collective-permute-start(f32[8,16,128]{2,1,0:T(8,128)S(1)} %get-tuple-element.50), channel_id=1, source_target_pairs={{0,1},{1,0},{2,3},{3,2},{4,5},{5,4},{6,7},{7,6},{8,9},{9,8},{10,11... | collective-permute-start | bytes 196616 | tf_op jit(solution)/shard_map/ppermute | solution.py:369
  8.8 4.6 %collective-permute-start.3 = (f32[8,16,128]{2,1,0:T(8,128)S(1)}, f32[8,16,128]{2,1,0:T(8,128)S(1)}, u32[]{:S(2)}, u32[]{:S(2)}) collective-permute-start(f32[8,16,128]{2,1,0:T(8,128)S(1)} %get-tuple-element.51), channel_id=1, source_target_pairs={{1,2},{2,1},{3,4},{4,3},{5,6},{6,5},{7,0},{0,7},{9,10},{10,9},{11,... | collective-permute-start | bytes 196616 | tf_op jit(solution)/shard_map/ppermute | solution.py:369
  11.4 1.0 %copy-start.1 = (f32[8,128,128]{2,1,0:T(8,128)S(1)}, f32[8,128,128]{2,1,0:T(8,128)}, u32[]{:S(2)}) copy-start(f32[8,128,128]{2,1,0:T(8,128)} %tiles.1) | copy-start | bytes 1572868
  12.4 1.0 copy-start.3
  21.3 9.2 %collective-permute-start.4 = (f32[8,16,128]{2,1,0:T(8,128)}, f32[8,16,128]{2,1,0:T(8,128)S(1)}, u32[]{:S(2)}, u32[]{:S(2)}) collective-permute-start(f32[8,16,128]{2,1,0:T(8,128)} %get-tuple-element.57), channel_id=1, source_target_pairs={{0,8},{8,0},{16,24},{24,16},{1,9},{9,1},{17,25},{25,17},{2,10},{10... | collective-permute-start | bytes 196616 | tf_op jit(solution)/shard_map/ppermute | solution.py:369
  22.0 8.5 %collective-permute-start.5 = (f32[8,16,128]{2,1,0:T(8,128)}, f32[8,16,128]{2,1,0:T(8,128)S(1)}, u32[]{:S(2)}, u32[]{:S(2)}) collective-permute-start(f32[8,16,128]{2,1,0:T(8,128)} %get-tuple-element.58), channel_id=1, source_target_pairs={{8,16},{16,8},{24,0},{0,24},{9,17},{17,9},{25,1},{1,25},{10,18},{1... | collective-permute-start | bytes 196616 | tf_op jit(solution)/shard_map/ppermute | solution.py:369
  22.9 7.6 %collective-permute-start.6 = (f32[8,16,128]{2,1,0:T(8,128)}, f32[8,16,128]{2,1,0:T(8,128)S(1)}, u32[]{:S(2)}, u32[]{:S(2)}) collective-permute-start(f32[8,16,128]{2,1,0:T(8,128)} %get-tuple-element.59), channel_id=1, source_target_pairs={{0,1},{1,0},{2,3},{3,2},{4,5},{5,4},{6,7},{7,6},{8,9},{9,8},{10,11... | collective-permute-start | bytes 196616 | tf_op jit(solution)/shard_map/ppermute | solution.py:369
  22.9 8.2 %collective-permute-start.7 = (f32[8,16,128]{2,1,0:T(8,128)S(1)}, f32[8,16,128]{2,1,0:T(8,128)S(1)}, u32[]{:S(2)}, u32[]{:S(2)}) collective-permute-start(f32[8,16,128]{2,1,0:T(8,128)S(1)} %get-tuple-element.60), channel_id=1, source_target_pairs={{1,2},{2,1},{3,4},{4,3},{5,6},{6,5},{7,0},{0,7},{9,10},{10,9},{11,... | collective-permute-start | bytes 196616 | tf_op jit(solution)/shard_map/ppermute | solution.py:369
  26.8 21.6 %all-to-all-start = ((f32[32,1,256]{2,1,0:T(1,128)}), f32[32,1,256]{2,1,0:T(1,128)S(1)}, u32[]{:S(2)}, u32[]{:S(2)}) async-start(f32[32,1,256]{2,1,0:T(1,128)} %shard_map.97), calls=%async_computation | async-start | bytes 65536 | tf_op jit(solution)/shard_map/all_to_all | solution.py:387
  40.6 13.8 %collective-permute-start.8 = (f32[8,16,128]{2,1,0:T(8,128)}, f32[8,16,128]{2,1,0:T(8,128)S(1)}, u32[]{:S(2)}, u32[]{:S(2)}) collective-permute-start(f32[8,16,128]{2,1,0:T(8,128)} %get-tuple-element.63), channel_id=1, source_target_pairs={{0,8},{8,0},{16,24},{24,16},{1,9},{9,1},{17,25},{25,17},{2,10},{10... | collective-permute-start | bytes 196616 | tf_op jit(solution)/shard_map/ppermute | solution.py:369
  42.5 12.0 %collective-permute-start.9 = (f32[8,16,128]{2,1,0:T(8,128)}, f32[8,16,128]{2,1,0:T(8,128)S(1)}, u32[]{:S(2)}, u32[]{:S(2)}) collective-permute-start(f32[8,16,128]{2,1,0:T(8,128)} %get-tuple-element.64), channel_id=1, source_target_pairs={{8,16},{16,8},{24,0},{0,24},{9,17},{17,9},{25,1},{1,25},{10,18},{1... | collective-permute-start | bytes 196616 | tf_op jit(solution)/shard_map/ppermute | solution.py:369
  44.8 10.2 %collective-permute-start.10 = (f32[8,16,128]{2,1,0:T(8,128)}, f32[8,16,128]{2,1,0:T(8,128)S(1)}, u32[]{:S(2)}, u32[]{:S(2)}) collective-permute-start(f32[8,16,128]{2,1,0:T(8,128)} %get-tuple-element.65), channel_id=1, source_target_pairs={{0,1},{1,0},{2,3},{3,2},{4,5},{5,4},{6,7},{7,6},{8,9},{9,8},{10,11... | collective-permute-start | bytes 196616 | tf_op jit(solution)/shard_map/ppermute | solution.py:369
  44.8 10.9 %collective-permute-start.11 = (f32[8,16,128]{2,1,0:T(8,128)S(1)}, f32[8,16,128]{2,1,0:T(8,128)}, u32[]{:S(2)}, u32[]{:S(2)}) collective-permute-start(f32[8,16,128]{2,1,0:T(8,128)S(1)} %get-tuple-element.66), channel_id=1, source_target_pairs={{1,2},{2,1},{3,4},{4,3},{5,6},{6,5},{7,0},{0,7},{9,10},{10,9},{11,... | collective-permute-start | bytes 196616 | tf_op jit(solution)/shard_map/ppermute | solution.py:369
  51.9 15.0 %all-to-all-start.1 = ((f32[32,1,256]{2,1,0:T(1,128)}), f32[32,1,256]{2,1,0:T(1,128)S(1)}, u32[]{:S(2)}, u32[]{:S(2)}) async-start(f32[32,1,256]{2,1,0:T(1,128)} %get-tuple-element.73), calls=%async_computation.1 | async-start | bytes 65536 | tf_op jit(solution)/shard_map/all_to_all | solution.py:387
  66.8 26.1 %collective-permute-start.12 = (f32[33,16,128]{2,1,0:T(8,128)S(1)}, f32[33,16,128]{2,1,0:T(8,128)S(1)}, u32[]{:S(2)}, u32[]{:S(2)}) collective-permute-start(f32[33,16,128]{2,1,0:T(8,128)S(1)} %get-tuple-element.82.mine), channel_id=1, source_target_pairs={{0,4},{1,5},{2,6},{3,7},{4,0},{5,1},{6,2},{7,3},{8,12},{9,13},{10,... | collective-permute-start | bytes 811016 | tf_op jit(solution)/shard_map/ppermute | solution.py:493
  68.5 3.5 %copy-start.11 = (f32[32,16,128]{2,1,0:T(8,128)S(1)}, f32[32,16,128]{2,1,0:T(8,128)}, u32[]{:S(2)}) copy-start(f32[32,16,128]{2,1,0:T(8,128)} %copy-done.10) | copy-start | bytes 786436
  68.5 4.0 %copy-start.9 = (f32[32,16,128]{2,1,0:T(8,128)S(1)}, f32[32,16,128]{2,1,0:T(8,128)}, u32[]{:S(2)}) copy-start(f32[32,16,128]{2,1,0:T(8,128)} %copy-done.8) | copy-start | bytes 786436
  68.5 5.6 %copy-start.7 = (f32[32,16,128]{2,1,0:T(8,128)S(1)}, f32[32,16,128]{2,1,0:T(8,128)}, u32[]{:S(2)}) copy-start(f32[32,16,128]{2,1,0:T(8,128)} %copy-done.6) | copy-start | bytes 786436
  72.0 23.6 %collective-permute-start.13 = (f32[32,16,128]{2,1,0:T(8,128)S(1)}, f32[32,16,128]{2,1,0:T(8,128)S(1)}, u32[]{:S(2)}, u32[]{:S(2)}) collective-permute-start(f32[32,16,128]{2,1,0:T(8,128)S(1)} %copy-done.11), channel_id=1, source_target_pairs={{0,4},{1,5},{2,6},{3,7},{4,0},{5,1},{6,2},{7,3},{8,12},{9,13},{10,... | collective-permute-start | bytes 786440 | tf_op jit(solution)/shard_map/ppermute | solution.py:503
  72.5 23.2 %collective-permute-start.14 = (f32[32,16,128]{2,1,0:T(8,128)S(1)}, f32[32,16,128]{2,1,0:T(8,128)S(1)}, u32[]{:S(2)}, u32[]{:S(2)}) collective-permute-start(f32[32,16,128]{2,1,0:T(8,128)S(1)} %copy-done.9), channel_id=1, source_target_pairs={{0,4},{1,5},{2,6},{3,7},{4,0},{5,1},{6,2},{7,3},{8,12},{9,13},{10,... | collective-permute-start | bytes 786440 | tf_op jit(solution)/shard_map/ppermute | solution.py:503
  74.1 24.4 %collective-permute-start.15 = (f32[32,16,128]{2,1,0:T(8,128)S(1)}, f32[32,16,128]{2,1,0:T(8,128)S(1)}, u32[]{:S(2)}, u32[]{:S(2)}) collective-permute-start(f32[32,16,128]{2,1,0:T(8,128)S(1)} %copy-done.7), channel_id=1, source_target_pairs={{0,4},{1,5},{2,6},{3,7},{4,0},{5,1},{6,2},{7,3},{8,12},{9,13},{10,... | collective-permute-start | bytes 786440 | tf_op jit(solution)/shard_map/ppermute | solution.py:503
  (14 other events, 10.2 us)

commit v3 on v2

--- a/solution.py
+++ b/solution.py
@@ -143,10 +143,8 @@
     for pair in range(tiles.shape[0] // 2):
         for j in range(2):
             high, low = split(tiles[2 * pair + j])
-            for half in range(2):
-                rows = slice(128 * half, 128 * half + 128)
-                high_out[pair, rows, 128 * j : 128 * j + 128] = high
-                low_out[pair, rows, 128 * j : 128 * j + 128] = low
+            high_out[pair, :, 128 * j : 128 * j + 128] = high
+            low_out[pair, :, 128 * j : 128 * j + 128] = low
 
 
 def lanes_product(a, b):
@@ -187,8 +185,9 @@
         first = pl.multiple_of(i * step, step)
         left = x[pl.ds(pl.multiple_of(i * step * cols, step * cols), step * cols), :]
         for pair in range(tiles_high.shape[0]):
-            out = jnp.dot(left, tiles_high[pair], preferred_element_type=F32)
-            out = out + jnp.dot(left, tiles_low[pair], preferred_element_type=F32)
+            high, low = tiles_high[pair], tiles_low[pair]
+            out = jnp.dot(left, jnp.concatenate([high, high], 0), preferred_element_type=F32)
+            out = out + jnp.dot(left, jnp.concatenate([low, low], 0), preferred_element_type=F32)
             for j in range(2):
                 z[2 * pair + j, pl.ds(first, step)] = out[:, 128 * j : 128 * j + 128].reshape(
                     step, cols, 128
@@ -242,11 +241,13 @@
 
 
 def last_kernel(plan, columns, weights, order, block, h0, h1, h2, h3, th, tl, inv, meta, *rest):
-    image, chunks, (x, z, landed, sems) = rest[0], rest[1:-4], rest[-4:]
+    image, chunks, (x, z, landed, sems, ordered, out_sems) = rest[0], rest[1:-6], rest[-6:]
     count, cols, _ = block.shape
     load_blocks(x, block, (h0, h1, h2, h3), landed, sems, plan, scaler(inv[...]))
     products(z, x, th, tl, cols)
     size = count // len(chunks)
+    ordered[0, size] = meta[...]
+    copies = []
     for i, chunk in enumerate(chunks):
 
         @pl.loop(0, size, unroll=4)
@@ -254,9 +255,15 @@
             b = order[i * size + r]
             value = combine(z, weights, columns, b, count)
             image[b] = value
-            chunk[r] = value
-
-    chunks[0][size] = meta[...]
+            ordered[i, r] = value
+
+        copy = pltpu.make_async_copy(
+            ordered.at[i, pl.ds(0, chunk.shape[0])], chunk, out_sems.at[i]
+        )
+        copy.start()
+        copies.append(copy)
+    for copy in copies:
+        copy.wait()
 
 
 def row_sum(sums):
@@ -308,43 +315,33 @@
     put_rows(packed, jnp.concatenate([gram, cross], 1))
 
 
-def factor_kernel(order, sums, inverse, mine, theirs, total_inverse, rayleigh, weights, columns):
-    cols = inverse.shape[0]
-    count = weights.shape[1]
-    slots = weights.shape[0]
-    wide = cols * cols
-    total = row_sum(sums)
-    total_inverse[...] = eliminate(unpack(total[:, :wide], cols), inverse[...])
-    rayleigh[...] = unpack(total[:, wide:], cols)[:, :cols]
-    last = mine.shape[0] - 1
-    both = jnp.concatenate([mine[last], theirs[last]], 1)
-    moved = pltpu.roll(both, 2 * count - order[count], 1)[:, :count]
-    weights[...] = moved[:slots]
-    columns[...] = moved[slots:].astype(jnp.int32)
-
-
-def final_kernel(first, order, inverse, image, *rest):
-    theirs, out, rows = rest[:-2], rest[-2], rest[-1]
-    if first:
-        theirs = theirs[:-1]
+def final_kernel(order, sums, inverse, image, meta, *rest):
+    theirs, (out, rayleigh, weights, columns, rows, left) = rest[:-6], rest[-6:]
     count, cols, cells = image.shape
     size, per = out.shape[0], 128 // cols
-    part = first + pl.program_id(0)
 
     @pl.when(pl.program_id(0) == 0)
     def _():
+        wide = cols * cols
+        total = row_sum(sums)
+        left[...] = scaler(eliminate(unpack(total[:, :wide], cols), inverse[...]))
+        rayleigh[...] = unpack(total[:, wide:], cols)[:, :cols]
+        both = jnp.concatenate([meta[...], theirs[0][size]], 1)
+        moved = pltpu.roll(both, 2 * count - order[count], 1)[:, :count]
+        slots = weights.shape[0]
+        weights[...] = moved[:slots]
+        columns[...] = moved[slots:].astype(jnp.int32)
         for i, chunk in enumerate(theirs):
             rows[count + i * size : count + (i + 1) * size] = chunk[:size]
 
-        @pl.loop(0, count, unroll=4)
+        @pl.loop(0, count, unroll=8)
         def _(r):
             rows[r] = image[order[r]]
 
-    left = scaler(inverse[...])
-    start = order[count] + part * size
+    start = order[count] + pl.program_id(0) * size
     for g in range(size // per):
         value = rows[pl.ds(start + g * per, per)].reshape(128, cells)
-        out[g * per : (g + 1) * per] = apply_scaler(left, value).reshape(per, cols, cells)
+        out[g * per : (g + 1) * per] = apply_scaler(left[...], value).reshape(per, cols, cells)
 
 
 def call(kernel, out_shape, in_specs, out_specs, scratch=(), limit=24, cost=(0, 0), **more):
@@ -432,7 +429,7 @@
 
     wide = 2 * cells
     tiles = call(
-        tiles_kernel, [shape(slots // 2, wide, wide, dtype=BF16)] * 2, [VMEM], [VMEM] * 2
+        tiles_kernel, [shape(slots // 2, cells, wide, dtype=BF16)] * 2, [VMEM], [VMEM] * 2
     )(slot_tiles)
     my_side = (lax.axis_index("gy") >= size_y // 2).astype(jnp.int32)
     order, meta = call(
@@ -469,22 +466,28 @@
     image, sent = operator(block, near)
     near = halo(sent)
     packed = call(gram_kernel, gram_rows, [VMEM], VMEM, cost=small)(image)
-    image, packed = lax.optimization_barrier((image, packed))
+    image, packed, *near = lax.optimization_barrier((image, packed, *near))
     sums = everywhere(packed)
     image, sent = operator(image, near)
     near = halo(sent)
     previous, inverse, packed = call(
         scale_kernel, [whole, square, gram_rows], [VMEM] * 2, [VMEM] * 3, cost=small
     )(sums, image)
+    packed, *near = lax.optimization_barrier((packed, *near))
     sums = everywhere(packed)
 
     size = count // CHUNKS
     image, *mine = call(
         last_kernel,
-        [whole, shape(size + 1, cols, cells)] + [shape(size, cols, cells)] * (CHUNKS - 1),
+        [whole]
+        + [pltpu.HBM((size + (i == 0), cols, cells), F32) for i in range(CHUNKS)],
         [SMEM] * 4 + [VMEM] + [ANY] * 4 + [VMEM] * 4,
-        [VMEM] * (1 + CHUNKS),
-        scratch,
+        [VMEM] + [HBM] * CHUNKS,
+        scratch
+        + [
+            pltpu.VMEM((CHUNKS, size + 1, cols, cells), F32),
+            pltpu.SemaphoreType.DMA((CHUNKS,)),
+        ],
         limit=24,
         cost=work,
     )(plan, flat_columns, flat_weights, order, previous, *near, *tiles, inverse, meta)
@@ -501,31 +504,19 @@
     packed, *later = lax.optimization_barrier((packed, *mine[1:]))
     sums = everywhere(packed)
     theirs += [lax.ppermute(x, "gy", swap) for x in later]
-    inverse, rayleigh, moved_weights, moved_columns = call(
-        factor_kernel,
+    moved_basis, rayleigh, moved_weights, moved_columns = call(
+        final_kernel,
         [
-            square,
+            whole,
             shape(cols, cols),
             shape(slots, count),
             shape(slots, count, dtype=jnp.int32),
         ],
-        [SMEM] + [VMEM] * 4,
-        [VMEM] * 4,
-    )(order, sums, inverse, mine[0], theirs[0])
-
-    def final(first, parts, theirs, *before):
-        return call(
-            functools.partial(final_kernel, first),
-            whole,
-            [SMEM] + [VMEM] * (2 + len(theirs)) + [ANY] * len(before),
-            pl.BlockSpec((size, cols, cells), lambda i: (first + i, 0, 0)),
-            [pltpu.VMEM((2 * count, cols, cells), F32)],
-            grid=(parts,),
-            input_output_aliases={3 + len(theirs): 0} if before else {},
-        )(order, inverse, image, *theirs, *before)
-
-    moved_basis = final(0, CHUNKS - 1, theirs[:-1])
-    moved_basis = final(CHUNKS - 1, 1, theirs, moved_basis)
+        [SMEM] + [VMEM] * (4 + CHUNKS),
+        [pl.BlockSpec((size, cols, cells), lambda i: (i, 0, 0))] + [VMEM] * 3,
+        [pltpu.VMEM((2 * count, cols, cells), F32), pltpu.VMEM((wide, wide), BF16)],
+        grid=(CHUNKS,),
+    )(order, sums, inverse, image, meta, *theirs)
     return (
         moved_basis[None, None],
         moved_weights.T[None, None],

time: 101 us -> 91.6 us (0.907)
  local copies, waits for them, and re-layouts: 10.4 us -> 2.48 us
  Pallas kernels: 40.5 us -> 37.1 us
  waiting for transfers between devices: 0.85 us -> 2.24 us
    unnamed x40 -> x18, local copies, waits for them, and re-layouts: 10.4 us -> 2.39 us
    pallas_call x5 -> x3, Pallas kernels: 15 us -> 12.9 us  [the longest x1 8.16 us: per_device(): call(last_kernel, [whole] + [pltpu.HBM((size + (i == 0), cols, cells), F3...]
    ppermute x12, waiting for transfers between devices: 0.83 us -> 2.22 us  [pairs(): return lax.ppermute(x, axis, swap)]
    pallas_call x2, Pallas kernels: 14.3 us -> 13 us  [operator(): call(operator_kernel, [whole] + [piece] * 4, [SMEM] * 4 + [VMEM] + [ANY]...]
  transfers between devices with their start and end apart: 18 -> 18, of which waited for: 1 -> 2; matrix products, arithmetic and copies ran while one was open for 0% -> 0% of each run, Pallas kernels for 29% -> 26%
where the time goes in v3:
time: 91.6 us; the launch traced here: 91.2 us
  Pallas kernels  37.1 us (41%)
  starting transfers between devices  29.9 us (33%)
  blocking collectives  18.6 us (20%)
  local copies, waits for them, and re-layouts  2.48 us (3%)
  waiting for transfers between devices  2.24 us (2%)
    ppermute x12, starting transfers between devices, pairs(): return lax.ppermute(x, axis, swap)  19 us
    all_to_all x1, blocking collectives, everywhere(): return lax.all_to_all(rows, AXES, 0, 0, tiled=True)  18.6 us
    pallas_call x2, Pallas kernels, operator(): call(operator_kernel, [whole] + [piece] * 4, [SMEM] * 4 + [VMEM] + [ANY]...  13 us
    pallas_call x1, Pallas kernels, per_device(): call(last_kernel, [whole] + [pltpu.HBM((size + (i == 0), cols, cells), F3...  8.16 us
    all_to_all x2, starting transfers between devices, everywhere(): return lax.all_to_all(rows, AXES, 0, 0, tiled=True)  6.71 us
    pallas_call x1, Pallas kernels, per_device(): call(final_kernel, [whole, shape(cols, cols), shape(slots, count), shape(...  4.71 us
    pallas_call x1, Pallas kernels, per_device(): call(scale_kernel, [whole, square, gram_rows], [VMEM] * 2, [VMEM] * 3, co...  3.55 us
    pallas_call x1, Pallas kernels, per_device(): call(sums_kernel, [shape(devices, 1, 2 * cols * cols), square], [VMEM] *...  3.5 us
  transfers between devices with their start and end apart: 18, of which 2 were waited for; matrix products, arithmetic and copies ran while one was open for 0% of the time, Pallas kernels for 26%

profile of v3, /device:TPU:0, one launch (start us, length us, event | category | flops | bytes accessed | tf_op | source)
XLA Modules:
  0.0 91.2 jit_solution(7574596485376356918)
XLA Ops:
  0.8 2.5 %shard_map.94 = (f32[8,16,128]{2,1,0:T(8,128)S(1)}, f32[8,16,128]{2,1,0:T(8,128)S(1)}, f32[8,16,128]{2,1,0:T(8,128)S(1)}, f32[8,16,128]{2,1,0:T(8,128)S(1)}) custom-call(s32[8]{0:T(128)S(1)} %stack.35.plan, s32[4,8]{1,0:T(4,128)} %bitcast.40, f32[128,16,128]{2,1,0:T(8,128)} %bitcast.28), custom_call_target="tpu_custom_call" | custom-call | tf_op jit(solution)/shard_map/pallas_call | solution.py:417
  3.2 3.1 %collective-permute-start = (f32[8,16,128]{2,1,0:T(8,128)S(1)}, f32[8,16,128]{2,1,0:T(8,128)S(1)}, u32[]{:S(2)}, u32[]{:S(2)}) collective-permute-start(f32[8,16,128]{2,1,0:T(8,128)S(1)} %get-tuple-element.57), channel_id=1, source_target_pairs={{0,8},{8,0},{16,24},{24,16},{1,9},{9,1},{17,25},{25,17},{2,10},{10... | collective-permute-start | bytes 196616 | tf_op jit(solution)/shard_map/ppermute | solution.py:366
  6.3 2.5 %collective-permute-start.1 = (f32[8,16,128]{2,1,0:T(8,128)S(1)}, f32[8,16,128]{2,1,0:T(8,128)S(1)}, u32[]{:S(2)}, u32[]{:S(2)}) collective-permute-start(f32[8,16,128]{2,1,0:T(8,128)S(1)} %get-tuple-element.58), channel_id=1, source_target_pairs={{8,16},{16,8},{24,0},{0,24},{9,17},{17,9},{25,1},{1,25},{10,18},{1... | collective-permute-start | bytes 196616 | tf_op jit(solution)/shard_map/ppermute | solution.py:366
  8.8 2.6 %collective-permute-start.3 = (f32[8,16,128]{2,1,0:T(8,128)S(1)}, f32[8,16,128]{2,1,0:T(8,128)S(1)}, u32[]{:S(2)}, u32[]{:S(2)}) collective-permute-start(f32[8,16,128]{2,1,0:T(8,128)S(1)} %get-tuple-element.60), channel_id=1, source_target_pairs={{1,2},{2,1},{3,4},{4,3},{5,6},{6,5},{7,0},{0,7},{9,10},{10,9},{11,... | collective-permute-start | bytes 196616 | tf_op jit(solution)/shard_map/ppermute | solution.py:366
  11.4 1.0 %copy-done.1 = f32[8,128,128]{2,1,0:T(8,128)S(1)} copy-done((f32[8,128,128]{2,1,0:T(8,128)S(1)}, f32[8,128,128]{2,1,0:T(8,128)}, u32[]{:S(2)}) %copy-start.1) | copy-done | bytes 524312
  12.6 0.9 collective-permute-done.3.h3
  14.1 6.5 %shard_map.96 = (f32[128,16,128]{2,1,0:T(8,128)S(1)}, f32[8,16,128]{2,1,0:T(8,128)S(1)}, f32[8,16,128]{2,1,0:T(8,128)S(1)}, f32[8,16,128]{2,1,0:T(8,128)S(1)}, f32[8,16,128]{2,1,0:T(8,128)S(1)}) custom-call(s32[8]{0:T(128)S(1)} %stack.35.plan, s32[1024]{0:T(1024)S(1)} %bitcast.36, f32[1024]{0:T(1024)S(1)} %bitcast.32, s32[4,8]{1,0:T(4,128)S(1)} %bitcast.41, ...), custom_call_target="tpu_custom_call" | custom-call | flops 2684354560 | tf_op jit(solution)/shard_map/pallas_call | solution.py:454
  21.3 0.9 collective-permute-start.5
  22.2 2.6 %collective-permute-start.7 = (f32[8,16,128]{2,1,0:T(8,128)S(1)}, f32[8,16,128]{2,1,0:T(8,128)S(1)}, u32[]{:S(2)}, u32[]{:S(2)}) collective-permute-start(f32[8,16,128]{2,1,0:T(8,128)S(1)} %get-tuple-element.67), channel_id=1, source_target_pairs={{1,2},{2,1},{3,4},{4,3},{5,6},{6,5},{7,0},{0,7},{9,10},{10,9},{11,... | collective-permute-start | bytes 196616 | tf_op jit(solution)/shard_map/ppermute | solution.py:366
  24.8 1.3 %shard_map.97 = f32[32,1,256]{2,1,0:T(1,128)} custom-call(f32[128,16,128]{2,1,0:T(8,128)S(1)} %get-tuple-element.69.image.block), custom_call_target="tpu_custom_call" | custom-call | flops 268435456 | tf_op jit(solution)/shard_map/pallas_call | solution.py:468
  26.1 1.3 %collective-permute-done.5.h1 = f32[8,16,128]{2,1,0:T(8,128)S(1)} collective-permute-done((f32[8,16,128]{2,1,0:T(8,128)S(1)}, f32[8,16,128]{2,1,0:T(8,128)S(1)}, u32[]{:S(2)}, u32[]{:S(2)}) %collective-permute-start.5) | collective-permute-done | bytes 65568 | tf_op jit(solution)/shard_map/ppermute | solution.py:366
  27.5 4.1 %all-to-all-start = ((f32[32,1,256]{2,1,0:T(1,128)}), f32[32,1,256]{2,1,0:T(1,128)S(1)}, u32[]{:S(2)}, u32[]{:S(2)}) async-start(f32[32,1,256]{2,1,0:T(1,128)} %shard_map.97), calls=%async_computation | async-start | bytes 65536 | tf_op jit(solution)/shard_map/all_to_all | solution.py:384
  31.6 6.5 %shard_map.98 = (f32[128,16,128]{2,1,0:T(8,128)S(1)}, f32[8,16,128]{2,1,0:T(8,128)S(1)}, f32[8,16,128]{2,1,0:T(8,128)S(1)}, f32[8,16,128]{2,1,0:T(8,128)S(1)}, f32[8,16,128]{2,1,0:T(8,128)S(1)}) custom-call(s32[8]{0:T(128)S(1)} %stack.35.plan, s32[1024]{0:T(1024)S(1)} %bitcast.37, f32[1024]{0:T(1024)S(1)} %bitcast.33, s32[4,8]{1,0:T(4,128)S(1)} %bitcast.42, ...), custom_call_target="tpu_custom_call" | custom-call | flops 2684354560 | tf_op jit(solution)/shard_map/pallas_call | solution.py:454
  38.1 1.8 %collective-permute-start.8 = (f32[8,16,128]{2,1,0:T(8,128)S(1)}, f32[8,16,128]{2,1,0:T(8,128)S(1)}, u32[]{:S(2)}, u32[]{:S(2)}) collective-permute-start(f32[8,16,128]{2,1,0:T(8,128)S(1)} %get-tuple-element.77), channel_id=1, source_target_pairs={{0,8},{8,0},{16,24},{24,16},{1,9},{9,1},{17,25},{25,17},{2,10},{10... | collective-permute-start | bytes 196616 | tf_op jit(solution)/shard_map/ppermute | solution.py:366
  39.9 2.4 %collective-permute-start.9 = (f32[8,16,128]{2,1,0:T(8,128)S(1)}, f32[8,16,128]{2,1,0:T(8,128)S(1)}, u32[]{:S(2)}, u32[]{:S(2)}) collective-permute-start(f32[8,16,128]{2,1,0:T(8,128)S(1)} %get-tuple-element.78), channel_id=1, source_target_pairs={{8,16},{16,8},{24,0},{0,24},{9,17},{17,9},{25,1},{1,25},{10,18},{1... | collective-permute-start | bytes 196616 | tf_op jit(solution)/shard_map/ppermute | solution.py:366
  42.3 2.5 %collective-permute-start.11 = (f32[8,16,128]{2,1,0:T(8,128)S(1)}, f32[8,16,128]{2,1,0:T(8,128)S(1)}, u32[]{:S(2)}, u32[]{:S(2)}) collective-permute-start(f32[8,16,128]{2,1,0:T(8,128)S(1)} %get-tuple-element.80), channel_id=1, source_target_pairs={{1,2},{2,1},{3,4},{4,3},{5,6},{6,5},{7,0},{0,7},{9,10},{10,9},{11,... | collective-permute-start | bytes 196616 | tf_op jit(solution)/shard_map/ppermute | solution.py:366
  45.8 3.6 %shard_map.99 = (f32[128,16,128]{2,1,0:T(8,128)S(1)}, f32[16,128]{1,0:T(8,128)S(1)}, f32[32,1,256]{2,1,0:T(1,128)}) custom-call(f32[32,1,256]{2,1,0:T(1,128)S(1)} %all-to-all-done.sums, f32[128,16,128]{2,1,0:T(8,128)S(1)} %get-tuple-element.74.image), custom_call_target="tpu_custom_call" | custom-call | flops 268435456 | tf_op jit(solution)/shard_map/pallas_call | solution.py:473
  49.4 2.6 %all-to-all-start.1 = ((f32[32,1,256]{2,1,0:T(1,128)}), f32[32,1,256]{2,1,0:T(1,128)S(1)}, u32[]{:S(2)}, u32[]{:S(2)}) async-start(f32[32,1,256]{2,1,0:T(1,128)} %get-tuple-element.91), calls=%async_computation.1 | async-start | bytes 65536 | tf_op jit(solution)/shard_map/all_to_all | solution.py:384
  52.0 8.2 %shard_map.100 = (f32[128,16,128]{2,1,0:T(8,128)S(1)}, f32[33,16,128]{2,1,0:T(8,128)}, f32[32,16,128]{2,1,0:T(8,128)}, f32[32,16,128]{2,1,0:T(8,128)}, f32[32,16,128]{2,1,0:T(8,128)}) custom-call(s32[8]{0:T(128)S(1)} %stack.35.plan, s32[1024]{0:T(1024)S(1)} %bitcast.39, f32[1024]{0:T(1024)S(1)} %bitcast.35, s32[1024]{0:T(1024)S(1)} %bitcast.30, ...), custom_call_target="tpu_custom_call" | custom-call | flops 2684354560 | tf_op jit(solution)/shard_map/pallas_call | solution.py:480
  60.1 1.7 %collective-permute-start.12 = (f32[33,16,128]{2,1,0:T(8,128)}, f32[33,16,128]{2,1,0:T(8,128)S(1)}, u32[]{:S(2)}, u32[]{:S(2)}) collective-permute-start(f32[33,16,128]{2,1,0:T(8,128)} %get-tuple-element.100), channel_id=1, source_target_pairs={{0,4},{1,5},{2,6},{3,7},{4,0},{5,1},{6,2},{7,3},{8,12},{9,13},{10,... | collective-permute-start | bytes 811016 | tf_op jit(solution)/shard_map/ppermute | solution.py:496
  61.9 3.5 %shard_map.101 = (f32[32,1,512]{2,1,0:T(1,128)S(1)}, f32[16,128]{1,0:T(8,128)S(1)}) custom-call(f32[32,1,256]{2,1,0:T(1,128)S(1)} %all-to-all-done.1.sums, f32[128,16,128]{2,1,0:T(8,128)S(1)} %get-tuple-element.75.block.previous, f32[128,16,128]{2,1,0:T(8,128)S(1)} %get-tuple-element.93.image), custom_call_target="tpu_custom_call" | custom-call | flops 268435456 | tf_op jit(solution)/shard_map/pallas_call | solution.py:497
  65.8 1.7 %collective-permute-start.14 = (f32[32,16,128]{2,1,0:T(8,128)S(1)}, f32[32,16,128]{2,1,0:T(8,128)S(1)}, u32[]{:S(2)}, u32[]{:S(2)}) collective-permute-start(f32[32,16,128]{2,1,0:T(8,128)S(1)} %copy-done.7), channel_id=1, source_target_pairs={{0,4},{1,5},{2,6},{3,7},{4,0},{5,1},{6,2},{7,3},{8,12},{9,13},{10,... | collective-permute-start | bytes 786440 | tf_op jit(solution)/shard_map/ppermute | solution.py:506
  67.9 18.6 %all_to_all.15.sums = f32[32,1,512]{2,1,0:T(1,128)S(1)} all-to-all(f32[32,1,512]{2,1,0:T(1,128)S(1)} %get-tuple-element.98), channel_id=1, replica_groups=mesh['gx'=4,'gy'=8] {'gx','gy'}, dimensions={0} | all-to-all | bytes 131072 | tf_op jit(solution)/shard_map/all_to_all | solution.py:384
  86.5 4.7 %shard_map.102 = (f32[128,16,128]{2,1,0:T(8,128)}, f32[16,16]{1,0:T(8,128)}, f32[8,128]{1,0:T(8,128)}, s32[8,128]{1,0:T(8,128)}) custom-call(s32[1024]{0:T(1024)S(1)} %bitcast.31, f32[32,1,512]{2,1,0:T(1,128)S(1)} %all_to_all.15.sums, f32[16,128]{1,0:T(8,128)S(1)} %get-tuple-element.99.inverse, f32[128,16,128]{2,1,0:T(8,128)S(1)} %get-tuple-element.93.image, ...), custom_call_target="tpu_custom_call" | custom-call | tf_op jit(solution)/shard_map/pallas_call | solution.py:507
  (42 shorter events, 3.5 us)
Async XLA Ops:
  0.6 12.8 %copy-start = (f32[1,1,128,16,128]{4,3,2,1,0:T(8,128)S(1)}, f32[1,1,128,16,128]{4,3,2,1,0:T(8,128)}, u32[]{:S(2)}) copy-start(f32[1,1,128,16,128]{4,3,2,1,0:T(8,128)} %param.6) | copy-start | bytes 3145732
  3.2 9.3 %collective-permute-start = (f32[8,16,128]{2,1,0:T(8,128)S(1)}, f32[8,16,128]{2,1,0:T(8,128)S(1)}, u32[]{:S(2)}, u32[]{:S(2)}) collective-permute-start(f32[8,16,128]{2,1,0:T(8,128)S(1)} %get-tuple-element.57), channel_id=1, source_target_pairs={{0,8},{8,0},{16,24},{24,16},{1,9},{9,1},{17,25},{25,17},{2,10},{10... | collective-permute-start | bytes 196616 | tf_op jit(solution)/shard_map/ppermute | solution.py:366
  6.3 6.2 %collective-permute-start.1 = (f32[8,16,128]{2,1,0:T(8,128)S(1)}, f32[8,16,128]{2,1,0:T(8,128)S(1)}, u32[]{:S(2)}, u32[]{:S(2)}) collective-permute-start(f32[8,16,128]{2,1,0:T(8,128)S(1)} %get-tuple-element.58), channel_id=1, source_target_pairs={{8,16},{16,8},{24,0},{0,24},{9,17},{17,9},{25,1},{1,25},{10,18},{1... | collective-permute-start | bytes 196616 | tf_op jit(solution)/shard_map/ppermute | solution.py:366
  8.8 3.7 %collective-permute-start.2 = (f32[8,16,128]{2,1,0:T(8,128)S(1)}, f32[8,16,128]{2,1,0:T(8,128)S(1)}, u32[]{:S(2)}, u32[]{:S(2)}) collective-permute-start(f32[8,16,128]{2,1,0:T(8,128)S(1)} %get-tuple-element.59), channel_id=1, source_target_pairs={{0,1},{1,0},{2,3},{3,2},{4,5},{5,4},{6,7},{7,6},{8,9},{9,8},{10,11... | collective-permute-start | bytes 196616 | tf_op jit(solution)/shard_map/ppermute | solution.py:366
  8.8 4.6 %collective-permute-start.3 = (f32[8,16,128]{2,1,0:T(8,128)S(1)}, f32[8,16,128]{2,1,0:T(8,128)S(1)}, u32[]{:S(2)}, u32[]{:S(2)}) collective-permute-start(f32[8,16,128]{2,1,0:T(8,128)S(1)} %get-tuple-element.60), channel_id=1, source_target_pairs={{1,2},{2,1},{3,4},{4,3},{5,6},{6,5},{7,0},{0,7},{9,10},{10,9},{11,... | collective-permute-start | bytes 196616 | tf_op jit(solution)/shard_map/ppermute | solution.py:366
  11.4 1.0 %copy-start.1 = (f32[8,128,128]{2,1,0:T(8,128)S(1)}, f32[8,128,128]{2,1,0:T(8,128)}, u32[]{:S(2)}) copy-start(f32[8,128,128]{2,1,0:T(8,128)} %tiles.1) | copy-start | bytes 1572868
  12.4 1.0 %copy-start.3 = (s32[1,1,128,8]{2,3,1,0:T(8,128)S(1)}, s32[1,1,128,8]{2,3,1,0:T(8,128)}, u32[]{:S(2)}) copy-start(s32[1,1,128,8]{2,3,1,0:T(8,128)} %param.9) | copy-start | bytes 12292
  20.6 5.5 %collective-permute-start.4 = (f32[8,16,128]{2,1,0:T(8,128)S(1)}, f32[8,16,128]{2,1,0:T(8,128)S(1)}, u32[]{:S(2)}, u32[]{:S(2)}) collective-permute-start(f32[8,16,128]{2,1,0:T(8,128)S(1)} %get-tuple-element.64), channel_id=1, source_target_pairs={{0,8},{8,0},{16,24},{24,16},{1,9},{9,1},{17,25},{25,17},{2,10},{10... | collective-permute-start | bytes 196616 | tf_op jit(solution)/shard_map/ppermute | solution.py:366
  21.3 6.1 %collective-permute-start.5 = (f32[8,16,128]{2,1,0:T(8,128)S(1)}, f32[8,16,128]{2,1,0:T(8,128)S(1)}, u32[]{:S(2)}, u32[]{:S(2)}) collective-permute-start(f32[8,16,128]{2,1,0:T(8,128)S(1)} %get-tuple-element.65), channel_id=1, source_target_pairs={{8,16},{16,8},{24,0},{0,24},{9,17},{17,9},{25,1},{1,25},{10,18},{1... | collective-permute-start | bytes 196616 | tf_op jit(solution)/shard_map/ppermute | solution.py:366
  22.2 5.2 %collective-permute-start.6 = (f32[8,16,128]{2,1,0:T(8,128)S(1)}, f32[8,16,128]{2,1,0:T(8,128)S(1)}, u32[]{:S(2)}, u32[]{:S(2)}) collective-permute-start(f32[8,16,128]{2,1,0:T(8,128)S(1)} %get-tuple-element.66), channel_id=1, source_target_pairs={{0,1},{1,0},{2,3},{3,2},{4,5},{5,4},{6,7},{7,6},{8,9},{9,8},{10,11... | collective-permute-start | bytes 196616 | tf_op jit(solution)/shard_map/ppermute | solution.py:366
  22.2 5.2 %collective-permute-start.7 = (f32[8,16,128]{2,1,0:T(8,128)S(1)}, f32[8,16,128]{2,1,0:T(8,128)S(1)}, u32[]{:S(2)}, u32[]{:S(2)}) collective-permute-start(f32[8,16,128]{2,1,0:T(8,128)S(1)} %get-tuple-element.67), channel_id=1, source_target_pairs={{1,2},{2,1},{3,4},{4,3},{5,6},{6,5},{7,0},{0,7},{9,10},{10,9},{11,... | collective-permute-start | bytes 196616 | tf_op jit(solution)/shard_map/ppermute | solution.py:366
  27.5 18.3 %all-to-all-start = ((f32[32,1,256]{2,1,0:T(1,128)}), f32[32,1,256]{2,1,0:T(1,128)S(1)}, u32[]{:S(2)}, u32[]{:S(2)}) async-start(f32[32,1,256]{2,1,0:T(1,128)} %shard_map.97), calls=%async_computation | async-start | bytes 65536 | tf_op jit(solution)/shard_map/all_to_all | solution.py:384
  38.1 11.3 %collective-permute-start.8 = (f32[8,16,128]{2,1,0:T(8,128)S(1)}, f32[8,16,128]{2,1,0:T(8,128)S(1)}, u32[]{:S(2)}, u32[]{:S(2)}) collective-permute-start(f32[8,16,128]{2,1,0:T(8,128)S(1)} %get-tuple-element.77), channel_id=1, source_target_pairs={{0,8},{8,0},{16,24},{24,16},{1,9},{9,1},{17,25},{25,17},{2,10},{10... | collective-permute-start | bytes 196616 | tf_op jit(solution)/shard_map/ppermute | solution.py:366
  39.9 9.4 %collective-permute-start.9 = (f32[8,16,128]{2,1,0:T(8,128)S(1)}, f32[8,16,128]{2,1,0:T(8,128)S(1)}, u32[]{:S(2)}, u32[]{:S(2)}) collective-permute-start(f32[8,16,128]{2,1,0:T(8,128)S(1)} %get-tuple-element.78), channel_id=1, source_target_pairs={{8,16},{16,8},{24,0},{0,24},{9,17},{17,9},{25,1},{1,25},{10,18},{1... | collective-permute-start | bytes 196616 | tf_op jit(solution)/shard_map/ppermute | solution.py:366
  42.3 7.1 %collective-permute-start.10 = (f32[8,16,128]{2,1,0:T(8,128)S(1)}, f32[8,16,128]{2,1,0:T(8,128)S(1)}, u32[]{:S(2)}, u32[]{:S(2)}) collective-permute-start(f32[8,16,128]{2,1,0:T(8,128)S(1)} %get-tuple-element.79), channel_id=1, source_target_pairs={{0,1},{1,0},{2,3},{3,2},{4,5},{5,4},{6,7},{7,6},{8,9},{9,8},{10,11... | collective-permute-start | bytes 196616 | tf_op jit(solution)/shard_map/ppermute | solution.py:366
  42.3 7.1 %collective-permute-start.11 = (f32[8,16,128]{2,1,0:T(8,128)S(1)}, f32[8,16,128]{2,1,0:T(8,128)S(1)}, u32[]{:S(2)}, u32[]{:S(2)}) collective-permute-start(f32[8,16,128]{2,1,0:T(8,128)S(1)} %get-tuple-element.80), channel_id=1, source_target_pairs={{1,2},{2,1},{3,4},{4,3},{5,6},{6,5},{7,0},{0,7},{9,10},{10,9},{11,... | collective-permute-start | bytes 196616 | tf_op jit(solution)/shard_map/ppermute | solution.py:366
  49.4 10.8 %all-to-all-start.1 = ((f32[32,1,256]{2,1,0:T(1,128)}), f32[32,1,256]{2,1,0:T(1,128)S(1)}, u32[]{:S(2)}, u32[]{:S(2)}) async-start(f32[32,1,256]{2,1,0:T(1,128)} %get-tuple-element.91), calls=%async_computation.1 | async-start | bytes 65536 | tf_op jit(solution)/shard_map/all_to_all | solution.py:384
  60.1 26.3 %collective-permute-start.12 = (f32[33,16,128]{2,1,0:T(8,128)}, f32[33,16,128]{2,1,0:T(8,128)S(1)}, u32[]{:S(2)}, u32[]{:S(2)}) collective-permute-start(f32[33,16,128]{2,1,0:T(8,128)} %get-tuple-element.100), channel_id=1, source_target_pairs={{0,4},{1,5},{2,6},{3,7},{4,0},{5,1},{6,2},{7,3},{8,12},{9,13},{10,... | collective-permute-start | bytes 811016 | tf_op jit(solution)/shard_map/ppermute | solution.py:496
  61.9 3.5 %copy-start.8 = (f32[32,16,128]{2,1,0:T(8,128)S(1)}, f32[32,16,128]{2,1,0:T(8,128)}, u32[]{:S(2)}) copy-start(f32[32,16,128]{2,1,0:T(8,128)} %get-tuple-element.101) | copy-start | bytes 786436
  61.9 4.0 %copy-start.7 = (f32[32,16,128]{2,1,0:T(8,128)S(1)}, f32[32,16,128]{2,1,0:T(8,128)}, u32[]{:S(2)}) copy-start(f32[32,16,128]{2,1,0:T(8,128)} %get-tuple-element.102) | copy-start | bytes 786436
  61.9 5.6 %copy-start.6 = (f32[32,16,128]{2,1,0:T(8,128)S(1)}, f32[32,16,128]{2,1,0:T(8,128)}, u32[]{:S(2)}) copy-start(f32[32,16,128]{2,1,0:T(8,128)} %get-tuple-element.103) | copy-start | bytes 786436
  65.4 21.1 %collective-permute-start.13 = (f32[32,16,128]{2,1,0:T(8,128)S(1)}, f32[32,16,128]{2,1,0:T(8,128)S(1)}, u32[]{:S(2)}, u32[]{:S(2)}) collective-permute-start(f32[32,16,128]{2,1,0:T(8,128)S(1)} %copy-done.8), channel_id=1, source_target_pairs={{0,4},{1,5},{2,6},{3,7},{4,0},{5,1},{6,2},{7,3},{8,12},{9,13},{10,... | collective-permute-start | bytes 786440 | tf_op jit(solution)/shard_map/ppermute | solution.py:506
  65.8 20.7 %collective-permute-start.14 = (f32[32,16,128]{2,1,0:T(8,128)S(1)}, f32[32,16,128]{2,1,0:T(8,128)S(1)}, u32[]{:S(2)}, u32[]{:S(2)}) collective-permute-start(f32[32,16,128]{2,1,0:T(8,128)S(1)} %copy-done.7), channel_id=1, source_target_pairs={{0,4},{1,5},{2,6},{3,7},{4,0},{5,1},{6,2},{7,3},{8,12},{9,13},{10,... | collective-permute-start | bytes 786440 | tf_op jit(solution)/shard_map/ppermute | solution.py:506
  67.5 19.0 %collective-permute-start.15 = (f32[32,16,128]{2,1,0:T(8,128)S(1)}, f32[32,16,128]{2,1,0:T(8,128)S(1)}, u32[]{:S(2)}, u32[]{:S(2)}) collective-permute-start(f32[32,16,128]{2,1,0:T(8,128)S(1)} %copy-done.6), channel_id=1, source_target_pairs={{0,4},{1,5},{2,6},{3,7},{4,0},{5,1},{6,2},{7,3},{8,12},{9,13},{10,... | collective-permute-start | bytes 786440 | tf_op jit(solution)/shard_map/ppermute | solution.py:506
  (3 other events, 2.2 us)

commit v4 on v3

--- a/solution.py
+++ b/solution.py
@@ -139,12 +139,12 @@
         copy.wait()
 
 
-def tiles_kernel(tiles, high_out, low_out):
-    for pair in range(tiles.shape[0] // 2):
-        for j in range(2):
-            high, low = split(tiles[2 * pair + j])
-            high_out[pair, :, 128 * j : 128 * j + 128] = high
-            low_out[pair, :, 128 * j : 128 * j + 128] = low
+def tiles_kernel(tiles, both_out):
+    cells = tiles.shape[1]
+    for k in range(tiles.shape[0]):
+        high, low = split(tiles[k])
+        both_out[k * cells : (k + 1) * cells, :cells] = high
+        both_out[k * cells : (k + 1) * cells, cells:] = low
 
 
 def lanes_product(a, b):
@@ -177,93 +177,95 @@
     meta[slots:] = lanes_product(columns[...].astype(F32), pick)
 
 
-def products(z, x, tiles_high, tiles_low, cols):
-    step = 32
-
-    @pl.loop(0, z.shape[1] // step)
+def fill(full, count, halos, plan, left):
+    _, cols, cells = full.shape
+    for n, halo in enumerate(halos):
+        width = halo.shape[0]
+        values = jnp.where(plan[len(halos) + n] != 0, halo[...], 0.0)
+        if left is not None:
+            values = apply_scaler(left, values.reshape(width * cols, cells))
+            values = values.reshape(width, cols, cells)
+        full[pl.ds(count + plan[n] * width, width)] = values
+
+
+def gather(high, low, full, columns, weights, rows, count):
+    _, cols, cells = full.shape
+    for r, b in enumerate(rows):
+        for k in range(high.shape[1] // cells):
+            at = k * count + b
+            upper, lower = split(full[columns[at]] * weights[at])
+            place = slice(r * cols, (r + 1) * cols), slice(k * cells, (k + 1) * cells)
+            high[place] = upper
+            low[place] = lower
+
+
+def multiply(high, low, tiles):
+    cells = tiles.shape[1] // 2
+    both = jnp.dot(high[...], tiles[...], preferred_element_type=F32)
+    rest = jnp.dot(low[...], tiles[:, :cells], preferred_element_type=F32)
+    return both[:, :cells] + (both[:, cells:] + rest)
+
+
+def operator_kernel(plan, columns, weights, sends_hbm, block, h0, h1, h2, h3, tiles, *rest):
+    image, sent, scratch = rest[0], rest[1:5], rest[5:]
+    full, high0, low0, high1, low1, sends, sem = scratch
+    copy = pltpu.make_async_copy(sends_hbm, sends, sem)
+    copy.start()
+    count, cols, cells = block.shape
+    step = high0.shape[0] // cols
+
+    def load(high, low, first):
+        gather(high, low, full, columns, weights, [first + r for r in range(step)], count)
+
+    def put(first, high, low):
+        image[pl.ds(first, step)] = multiply(high, low, tiles).reshape(step, cols, cells)
+
+    full[:count] = block[...]
+    fill(full, count, (h0, h1, h2, h3), plan, None)
+    load(high0, low0, 0)
+
+    @pl.loop(0, count // (2 * step))
     def _(i):
-        first = pl.multiple_of(i * step, step)
-        left = x[pl.ds(pl.multiple_of(i * step * cols, step * cols), step * cols), :]
-        for pair in range(tiles_high.shape[0]):
-            high, low = tiles_high[pair], tiles_low[pair]
-            out = jnp.dot(left, jnp.concatenate([high, high], 0), preferred_element_type=F32)
-            out = out + jnp.dot(left, jnp.concatenate([low, low], 0), preferred_element_type=F32)
-            for j in range(2):
-                z[2 * pair + j, pl.ds(first, step)] = out[:, 128 * j : 128 * j + 128].reshape(
-                    step, cols, 128
-                )
-
-
-def load_blocks(x, block, halos, landed, sems, plan, left):
-    count, cols, cells = block.shape
-    copies = [
-        pltpu.make_async_copy(halo, landed.at[n], sems.at[n]) for n, halo in enumerate(halos)
-    ]
-    for copy in copies:
-        copy.start()
-
-    def put(rows, values):
-        high, low = split(values)
-        x[rows, :cells] = high
-        x[rows, cells:] = low
-
-    put(slice(0, count * cols), block[...].reshape(count * cols, cells))
-    for n, halo in enumerate(halos):
-        rows = halo.shape[0] * cols
-        copies[n].wait()
-        values = jnp.where(plan[len(halos) + n] != 0, landed[n].reshape(rows, cells), 0.0)
-        if left is not None:
-            values = apply_scaler(left, values)
-        start = pl.multiple_of((count + plan[n] * halo.shape[0]) * cols, rows)
-        put(pl.ds(start, rows), values)
-
-
-def combine(z, weights, columns, b, count):
-    total = weights[b] * z[0, columns[b]]
-    for k in range(1, z.shape[0]):
-        total = total + weights[k * count + b] * z[k, columns[k * count + b]]
-    return total
-
-
-def operator_kernel(plan, columns, weights, sends, block, h0, h1, h2, h3, th, tl, *rest):
-    image, sent, (x, z, landed, sems) = rest[0], rest[1:-4], rest[-4:]
-    count, cols, _ = block.shape
-    load_blocks(x, block, (h0, h1, h2, h3), landed, sems, plan, None)
-    products(z, x, th, tl, cols)
-
-    @pl.loop(0, count, unroll=4)
-    def _(b):
-        image[b] = combine(z, weights, columns, b, count)
-
+        first = pl.multiple_of(i * 2 * step, 2 * step)
+        load(high1, low1, first + step)
+        put(first, high0, low0)
+        load(high0, low0, jnp.minimum(first + 2 * step, count - step))
+        put(first + step, high1, low1)
+
+    copy.wait()
     for n, out in enumerate(sent):
         for h in range(out.shape[0]):
             out[h] = image[sends[plan[n], h]]
 
 
-def last_kernel(plan, columns, weights, order, block, h0, h1, h2, h3, th, tl, inv, meta, *rest):
-    image, chunks, (x, z, landed, sems, ordered, out_sems) = rest[0], rest[1:-6], rest[-6:]
-    count, cols, _ = block.shape
-    load_blocks(x, block, (h0, h1, h2, h3), landed, sems, plan, scaler(inv[...]))
-    products(z, x, th, tl, cols)
-    size = count // len(chunks)
-    ordered[0, size] = meta[...]
-    copies = []
-    for i, chunk in enumerate(chunks):
-
-        @pl.loop(0, size, unroll=4)
-        def _(r):
-            b = order[i * size + r]
-            value = combine(z, weights, columns, b, count)
-            image[b] = value
-            ordered[i, r] = value
-
-        copy = pltpu.make_async_copy(
-            ordered.at[i, pl.ds(0, chunk.shape[0])], chunk, out_sems.at[i]
-        )
-        copy.start()
-        copies.append(copy)
-    for copy in copies:
-        copy.wait()
+def last_first_kernel(plan, columns, weights, order, own, h0, h1, h2, h3, tiles, inv, meta, *rest):
+    chunk, full, high, low = rest
+    _, cols, cells = full.shape
+    count = full.shape[0] - 4 * h0.shape[0]
+    step = high.shape[0] // cols
+    fill(full, count, (h0, h1, h2, h3), plan, scaler(inv[...]))
+    gather(high, low, full, columns, weights, [order[r] for r in range(step)], count)
+    chunk[:step] = multiply(high, low, tiles).reshape(step, cols, cells)
+    chunk[step] = meta[...]
+
+
+def last_rest_kernel(columns, weights, order, full, tiles, *rest):
+    chunks, slots = rest[:-4], (rest[-4:-2], rest[-2:])
+    _, cols, cells = full.shape
+    step = slots[0][0].shape[0] // cols
+    parts = len(chunks)
+    count = (parts + 1) * step
+
+    def load(part):
+        rows = [order[part * step + r] for r in range(step)]
+        gather(*slots[part % 2], full, columns, weights, rows, count)
+
+    load(1)
+    for part in range(1, parts + 1):
+        if part < parts:
+            load(part + 1)
+        value = multiply(*slots[part % 2], tiles)
+        chunks[part - 1][...] = value.reshape(step, cols, cells)
 
 
 def row_sum(sums):
@@ -303,21 +305,33 @@
     put_rows(packed, pack(inner(both, both, cols), cols))
 
 
-def sums_kernel(sums, previous, image, packed, inverse):
-    cols = image.shape[1]
+def sums_kernel(order, sums, full, first, *rest):
+    later, (packed, inverse) = rest[:-2], rest[-2:]
+    _, cols, cells = full.shape
+    per = 128 // cols
     inv = eliminate(unpack(row_sum(sums), cols), identity(cols))
     inverse[...] = inv
     left = scaler(inv)
-    now = stacked([apply_scaler(left, g) for g in groups_of(image)])
-    before = stacked([apply_scaler(left, g) for g in groups_of(previous)])
+    count = (first.shape[0] - 1) * (len(later) + 1)
+    own = groups_of(first.at[: first.shape[0] - 1])
+    for chunk in later:
+        own = own + groups_of(chunk)
+    previous = [
+        jnp.concatenate([full[order[g * per + r]] for r in range(per)], 0)
+        for g in range(count // per)
+    ]
+    now = stacked([apply_scaler(left, g) for g in own])
+    before = stacked([apply_scaler(left, g) for g in previous])
     gram = pack(inner(now, now, cols), cols)
     cross = pack(inner(before, now, cols), cols)
     put_rows(packed, jnp.concatenate([gram, cross], 1))
 
 
-def final_kernel(order, sums, inverse, image, meta, *rest):
-    theirs, (out, rayleigh, weights, columns, rows, left) = rest[:-6], rest[-6:]
-    count, cols, cells = image.shape
+def final_kernel(order, sums, inverse, *rest):
+    chunks, (out, rayleigh, weights, columns, rows, left) = rest[:-6], rest[-6:]
+    mine, theirs = chunks[: len(chunks) // 2], chunks[len(chunks) // 2 :]
+    slots, count = weights.shape
+    cols, cells = out.shape[1:]
     size, per = out.shape[0], 128 // cols
 
     @pl.when(pl.program_id(0) == 0)
@@ -326,17 +340,13 @@
         total = row_sum(sums)
         left[...] = scaler(eliminate(unpack(total[:, :wide], cols), inverse[...]))
         rayleigh[...] = unpack(total[:, wide:], cols)[:, :cols]
-        both = jnp.concatenate([meta[...], theirs[0][size]], 1)
+        both = jnp.concatenate([mine[0][size], theirs[0][size]], 1)
         moved = pltpu.roll(both, 2 * count - order[count], 1)[:, :count]
-        slots = weights.shape[0]
         weights[...] = moved[:slots]
         columns[...] = moved[slots:].astype(jnp.int32)
-        for i, chunk in enumerate(theirs):
-            rows[count + i * size : count + (i + 1) * size] = chunk[:size]
-
-        @pl.loop(0, count, unroll=8)
-        def _(r):
-            rows[r] = image[order[r]]
+        for i in range(len(mine)):
+            rows[i * size : (i + 1) * size] = mine[i][:size]
+            rows[count + i * size : count + (i + 1) * size] = theirs[i][:size]
 
     start = order[count] + pl.program_id(0) * size
     for g in range(size // per):
@@ -428,9 +438,7 @@
     near = halo(sent)
 
     wide = 2 * cells
-    tiles = call(
-        tiles_kernel, [shape(slots // 2, cells, wide, dtype=BF16)] * 2, [VMEM], [VMEM] * 2
-    )(slot_tiles)
+    tiles = call(tiles_kernel, shape(slots * cells, wide, dtype=BF16), [VMEM], VMEM)(slot_tiles)
     my_side = (lax.axis_index("gy") >= size_y // 2).astype(jnp.int32)
     order, meta = call(
         order_kernel,
@@ -439,27 +447,32 @@
         [VMEM] * 2,
     )(my_side.reshape(1), split_side[0], weights, columns)
     order = order.reshape(8 * count)
-
-    blocks = count + 4 * width
-    work = 8 * blocks * cols * cells * cells * slots, 0
+    near, order, meta = lax.optimization_barrier((near, order, meta))
+
+    size = count // CHUNKS
+    blocks = shape(count + 4 * width, cols, cells)
+    half = pltpu.VMEM((size * cols, slots * cells), BF16)
+    work = 6 * count * cols * cells * cells * slots, 0
     small = 8 * count * cells * cells * cols, 0
-    scratch = [
-        pltpu.VMEM((blocks * cols, wide), BF16),
-        pltpu.VMEM((slots, blocks, cols, cells), F32),
-        pltpu.VMEM((4, width, cols, cells), F32),
-        pltpu.SemaphoreType.DMA((4,)),
-    ]
-
-    def operator(block, near):
+
+    def operator(block, near, **more):
         image, *sent = call(
             operator_kernel,
             [whole] + [piece] * 4,
-            [SMEM] * 4 + [VMEM] + [ANY] * 4 + [VMEM] * 2,
+            [SMEM] * 3 + [HBM] + [VMEM] * 6,
             [VMEM] * 5,
-            scratch,
-            limit=24,
+            [
+                pltpu.VMEM(blocks.shape, F32),
+                half,
+                half,
+                half,
+                half,
+                pltpu.SMEM(sends.shape, jnp.int32),
+                pltpu.SemaphoreType.DMA,
+            ],
             cost=work,
-        )(plan, flat_columns, flat_weights, sends, block, *near, *tiles)
+            **more,
+        )(plan, flat_columns, flat_weights, in_hbm(sends), block, *near, tiles)
         return image, sent
 
     gram_rows = shape(devices, 1, cols * cols)
@@ -468,42 +481,43 @@
     packed = call(gram_kernel, gram_rows, [VMEM], VMEM, cost=small)(image)
     image, packed, *near = lax.optimization_barrier((image, packed, *near))
     sums = everywhere(packed)
-    image, sent = operator(image, near)
+    image, sent = operator(image, near, input_output_aliases={4: 0})
     near = halo(sent)
-    previous, inverse, packed = call(
-        scale_kernel, [whole, square, gram_rows], [VMEM] * 2, [VMEM] * 3, cost=small
+    full, inverse, packed = call(
+        scale_kernel, [blocks, square, gram_rows], [VMEM] * 2, [VMEM] * 3, cost=small
     )(sums, image)
     packed, *near = lax.optimization_barrier((packed, *near))
     sums = everywhere(packed)
 
-    size = count // CHUNKS
-    image, *mine = call(
-        last_kernel,
-        [whole]
-        + [pltpu.HBM((size + (i == 0), cols, cells), F32) for i in range(CHUNKS)],
-        [SMEM] * 4 + [VMEM] + [ANY] * 4 + [VMEM] * 4,
-        [VMEM] + [HBM] * CHUNKS,
-        scratch
-        + [
-            pltpu.VMEM((CHUNKS, size + 1, cols, cells), F32),
-            pltpu.SemaphoreType.DMA((CHUNKS,)),
-        ],
-        limit=24,
-        cost=work,
-    )(plan, flat_columns, flat_weights, order, previous, *near, *tiles, inverse, meta)
-    mine, sums = lax.optimization_barrier((mine, sums))
+    first, full = call(
+        last_first_kernel,
+        [shape(size + 1, cols, cells), blocks],
+        [SMEM] * 4 + [VMEM] * 8,
+        [VMEM] * 2,
+        [half] * 2,
+        cost=(work[0] // CHUNKS, 0),
+        input_output_aliases={4: 1},
+    )(plan, flat_columns, flat_weights, order, full, *near, tiles, inverse, meta)
     swap = [(j, j ^ (size_y // 2)) for j in range(size_y)]
-    theirs = [lax.ppermute(mine[0], "gy", swap)]
+    their_first = lax.ppermute(first, "gy", swap)
+    later = call(
+        last_rest_kernel,
+        [shape(size, cols, cells)] * (CHUNKS - 1),
+        [SMEM] * 3 + [VMEM] * 2,
+        [VMEM] * (CHUNKS - 1),
+        [half] * 4,
+        cost=(work[0] // CHUNKS * (CHUNKS - 1), 0),
+    )(flat_columns, flat_weights, order, full, tiles)
+    later, sums = lax.optimization_barrier((later, sums))
+    their_later = [lax.ppermute(x, "gy", swap) for x in later]
+
     packed, inverse = call(
         sums_kernel,
         [shape(devices, 1, 2 * cols * cols), square],
-        [VMEM] * 3,
+        [SMEM] + [VMEM] * (2 + CHUNKS),
         [VMEM] * 2,
-        cost=small,
-    )(sums, previous, image)
-    packed, *later = lax.optimization_barrier((packed, *mine[1:]))
+    )(order, sums, full, first, *later)
     sums = everywhere(packed)
-    theirs += [lax.ppermute(x, "gy", swap) for x in later]
     moved_basis, rayleigh, moved_weights, moved_columns = call(
         final_kernel,
         [
@@ -512,11 +526,11 @@
             shape(slots, count),
             shape(slots, count, dtype=jnp.int32),
         ],
-        [SMEM] + [VMEM] * (4 + CHUNKS),
+        [SMEM] + [VMEM] * (2 + 2 * CHUNKS),
         [pl.BlockSpec((size, cols, cells), lambda i: (i, 0, 0))] + [VMEM] * 3,
         [pltpu.VMEM((2 * count, cols, cells), F32), pltpu.VMEM((wide, wide), BF16)],
         grid=(CHUNKS,),
-    )(order, sums, inverse, image, meta, *theirs)
+    )(order, sums, inverse, first, *later, their_first, *their_later)
     return (
         moved_basis[None, None],
         moved_weights.T[None, None],

time: 91.6 us -> 78.8 us (0.86)
  Pallas kernels: 37.1 us -> 29.8 us
  blocking collectives: 18.6 us -> 14.2 us
  local copies, waits for them, and re-layouts: 2.48 us -> 1.15 us
    pallas_call x6 -> x7, Pallas kernels: 28.3 us -> 21.2 us  [the longest x2 8.44 us: operator(): call(operator_kernel, [whole] + [piece] * 4, [SMEM] * 3 + [HBM] + [VMEM]...]
    all_to_all x1, blocking collectives: 18.6 us -> 14.2 us  [everywhere(): return lax.all_to_all(rows, AXES, 0, 0, tiled=True)]
    unnamed x18 -> x10, local copies, waits for them, and re-layouts: 2.39 us -> 1.06 us
  transfers between devices with their start and end apart: 18 -> 18, of which waited for: 2 -> 3; matrix products, arithmetic and copies ran while one was open for 0% -> 0% of each run, Pallas kernels for 26% -> 24%
where the time goes in v4:
time: 78.8 us; the launch traced here: 78.4 us
  starting transfers between devices  30 us (38%)
  Pallas kernels  29.8 us (38%)
  blocking collectives  14.2 us (18%)
  waiting for transfers between devices  2.37 us (3%)
  local copies, waits for them, and re-layouts  1.15 us (1%)
  between operations  0.84 us (1%)
    ppermute x12, starting transfers between devices, pairs(): return lax.ppermute(x, axis, swap)  19 us
    all_to_all x1, blocking collectives, everywhere(): return lax.all_to_all(rows, AXES, 0, 0, tiled=True)  14.2 us
    pallas_call x2, Pallas kernels, operator(): call(operator_kernel, [whole] + [piece] * 4, [SMEM] * 3 + [HBM] + [VMEM]...  8.44 us
    all_to_all x2, starting transfers between devices, everywhere(): return lax.all_to_all(rows, AXES, 0, 0, tiled=True)  6.89 us
    pallas_call x1, Pallas kernels, per_device(): call(final_kernel, [whole, shape(cols, cols), shape(slots, count), shape(...  4.54 us
    pallas_call x1, Pallas kernels, per_device(): call(sums_kernel, [shape(devices, 1, 2 * cols * cols), square], [SMEM] +...  4.1 us
    pallas_call x1, Pallas kernels, per_device(): call(scale_kernel, [blocks, square, gram_rows], [VMEM] * 2, [VMEM] * 3, c...  3.52 us
    pallas_call x1, Pallas kernels, per_device(): call(last_rest_kernel, [shape(size, cols, cells)] * (CHUNKS - 1), [SMEM]...  3.26 us
  transfers between devices with their start and end apart: 18, of which 3 were waited for; matrix products, arithmetic and copies ran while one was open for 0% of the time, Pallas kernels for 24%

profile of v4, /device:TPU:0, one launch (start us, length us, event | category | flops | bytes accessed | tf_op | source)
XLA Modules:
  0.0 78.4 jit_solution(14058024271052379441)
XLA Ops:
  0.8 2.5 %shard_map.93 = (f32[8,16,128]{2,1,0:T(8,128)S(1)}, f32[8,16,128]{2,1,0:T(8,128)S(1)}, f32[8,16,128]{2,1,0:T(8,128)S(1)}, f32[8,16,128]{2,1,0:T(8,128)S(1)}) custom-call(s32[8]{0:T(128)S(1)} %stack.35.plan, s32[4,8]{1,0:T(4,128)} %bitcast.45, f32[128,16,128]{2,1,0:T(8,128)} %bitcast.28), custom_call_target="tpu_custom_call" | custom-call | tf_op jit(solution)/shard_map/pallas_call | solution.py:427
  3.3 3.1 %collective-permute-start = (f32[8,16,128]{2,1,0:T(8,128)S(1)}, f32[8,16,128]{2,1,0:T(8,128)S(1)}, u32[]{:S(2)}, u32[]{:S(2)}) collective-permute-start(f32[8,16,128]{2,1,0:T(8,128)S(1)} %get-tuple-element.55), channel_id=1, source_target_pairs={{0,8},{8,0},{16,24},{24,16},{1,9},{9,1},{17,25},{25,17},{2,10},{10... | collective-permute-start | bytes 196616 | tf_op jit(solution)/shard_map/ppermute | solution.py:376
  6.4 2.5 %collective-permute-start.1 = (f32[8,16,128]{2,1,0:T(8,128)S(1)}, f32[8,16,128]{2,1,0:T(8,128)S(1)}, u32[]{:S(2)}, u32[]{:S(2)}) collective-permute-start(f32[8,16,128]{2,1,0:T(8,128)S(1)} %get-tuple-element.56), channel_id=1, source_target_pairs={{8,16},{16,8},{24,0},{0,24},{9,17},{17,9},{25,1},{1,25},{10,18},{1... | collective-permute-start | bytes 196616 | tf_op jit(solution)/shard_map/ppermute | solution.py:376
  8.8 2.6 %collective-permute-start.3 = (f32[8,16,128]{2,1,0:T(8,128)S(1)}, f32[8,16,128]{2,1,0:T(8,128)S(1)}, u32[]{:S(2)}, u32[]{:S(2)}) collective-permute-start(f32[8,16,128]{2,1,0:T(8,128)S(1)} %get-tuple-element.58), channel_id=1, source_target_pairs={{1,2},{2,1},{3,4},{4,3},{5,6},{6,5},{7,0},{0,7},{9,10},{10,9},{11,... | collective-permute-start | bytes 196616 | tf_op jit(solution)/shard_map/ppermute | solution.py:376
  11.4 1.0 %copy-done.1 = f32[8,128,128]{2,1,0:T(8,128)S(1)} copy-done((f32[8,128,128]{2,1,0:T(8,128)S(1)}, f32[8,128,128]{2,1,0:T(8,128)}, u32[]{:S(2)}) %copy-start.1) | copy-done | bytes 524312
  13.4 3.9 %shard_map.96 = (f32[128,16,128]{2,1,0:T(8,128)S(1)}, f32[8,16,128]{2,1,0:T(8,128)S(1)}, f32[8,16,128]{2,1,0:T(8,128)S(1)}, f32[8,16,128]{2,1,0:T(8,128)S(1)}, f32[8,16,128]{2,1,0:T(8,128)S(1)}) custom-call(s32[8]{0:T(128)S(1)} %stack.35.plan, s32[1024]{0:T(1024)S(1)} %bitcast.40, f32[1024]{0:T(1024)S(1)} %bitcast.35, s32[4,8]{1,0:T(4,128)} %bitcast.46, ...), custom_call_target="tpu_custom_call" | custom-call | flops 1610612736 | tf_op jit(solution)/shard_map/pallas_call | solution.py:459
  18.1 0.9 %collective-permute-start.5 = (f32[8,16,128]{2,1,0:T(8,128)S(1)}, f32[8,16,128]{2,1,0:T(8,128)S(1)}, u32[]{:S(2)}, u32[]{:S(2)}) collective-permute-start(f32[8,16,128]{2,1,0:T(8,128)S(1)} %get-tuple-element.68), channel_id=1, source_target_pairs={{8,16},{16,8},{24,0},{0,24},{9,17},{17,9},{25,1},{1,25},{10,18},{1... | collective-permute-start | bytes 196616 | tf_op jit(solution)/shard_map/ppermute | solution.py:376
  19.0 2.6 %collective-permute-start.7 = (f32[8,16,128]{2,1,0:T(8,128)S(1)}, f32[8,16,128]{2,1,0:T(8,128)S(1)}, u32[]{:S(2)}, u32[]{:S(2)}) collective-permute-start(f32[8,16,128]{2,1,0:T(8,128)S(1)} %get-tuple-element.70), channel_id=1, source_target_pairs={{1,2},{2,1},{3,4},{4,3},{5,6},{6,5},{7,0},{0,7},{9,10},{10,9},{11,... | collective-permute-start | bytes 196616 | tf_op jit(solution)/shard_map/ppermute | solution.py:376
  21.5 1.3 %shard_map.97 = f32[32,1,256]{2,1,0:T(1,128)} custom-call(f32[128,16,128]{2,1,0:T(8,128)S(1)} %get-tuple-element.72.image.block), custom_call_target="tpu_custom_call" | custom-call | flops 268435456 | tf_op jit(solution)/shard_map/pallas_call | solution.py:481
  22.9 1.3 %collective-permute-done.5.h1 = f32[8,16,128]{2,1,0:T(8,128)S(1)} collective-permute-done((f32[8,16,128]{2,1,0:T(8,128)S(1)}, f32[8,16,128]{2,1,0:T(8,128)S(1)}, u32[]{:S(2)}, u32[]{:S(2)}) %collective-permute-start.5) | collective-permute-done | bytes 65568 | tf_op jit(solution)/shard_map/ppermute | solution.py:376
  24.2 4.1 %all-to-all-start = ((f32[32,1,256]{2,1,0:T(1,128)}), f32[32,1,256]{2,1,0:T(1,128)S(1)}, u32[]{:S(2)}, u32[]{:S(2)}) async-start(f32[32,1,256]{2,1,0:T(1,128)} %shard_map.97), calls=%async_computation | async-start | bytes 65536 | tf_op jit(solution)/shard_map/all_to_all | solution.py:394
  28.3 4.5 %shard_map.98 = (f32[128,16,128]{2,1,0:T(8,128)S(1)}, f32[8,16,128]{2,1,0:T(8,128)}, f32[8,16,128]{2,1,0:T(8,128)S(1)}, f32[8,16,128]{2,1,0:T(8,128)S(1)}, f32[8,16,128]{2,1,0:T(8,128)S(1)}) custom-call(s32[8]{0:T(128)S(1)} %stack.35.plan, s32[1024]{0:T(1024)S(1)} %bitcast.41, f32[1024]{0:T(1024)S(1)} %bitcast.36, ...), custom_call_target="tpu_custom_call", output_to_operand_aliasing={{0}: (4, {})} | custom-call | flops 1610612736 | tf_op jit(solution)/shard_map/pallas_call | solution.py:459
  32.9 1.8 %collective-permute-start.8 = (f32[8,16,128]{2,1,0:T(8,128)}, f32[8,16,128]{2,1,0:T(8,128)S(1)}, u32[]{:S(2)}, u32[]{:S(2)}) collective-permute-start(f32[8,16,128]{2,1,0:T(8,128)} %get-tuple-element.80), channel_id=1, source_target_pairs={{0,8},{8,0},{16,24},{24,16},{1,9},{9,1},{17,25},{25,17},{2,10},{10... | collective-permute-start | bytes 196616 | tf_op jit(solution)/shard_map/ppermute | solution.py:376
  34.7 2.4 %collective-permute-start.9 = (f32[8,16,128]{2,1,0:T(8,128)S(1)}, f32[8,16,128]{2,1,0:T(8,128)S(1)}, u32[]{:S(2)}, u32[]{:S(2)}) collective-permute-start(f32[8,16,128]{2,1,0:T(8,128)S(1)} %get-tuple-element.81), channel_id=1, source_target_pairs={{8,16},{16,8},{24,0},{0,24},{9,17},{17,9},{25,1},{1,25},{10,18},{1... | collective-permute-start | bytes 196616 | tf_op jit(solution)/shard_map/ppermute | solution.py:376
  37.1 2.5 %collective-permute-start.11 = (f32[8,16,128]{2,1,0:T(8,128)S(1)}, f32[8,16,128]{2,1,0:T(8,128)S(1)}, u32[]{:S(2)}, u32[]{:S(2)}) collective-permute-start(f32[8,16,128]{2,1,0:T(8,128)S(1)} %get-tuple-element.83), channel_id=1, source_target_pairs={{1,2},{2,1},{3,4},{4,3},{5,6},{6,5},{7,0},{0,7},{9,10},{10,9},{11,... | collective-permute-start | bytes 196616 | tf_op jit(solution)/shard_map/ppermute | solution.py:376
  39.6 3.5 %shard_map.99 = (f32[160,16,128]{2,1,0:T(8,128)S(1)}, f32[16,128]{1,0:T(8,128)S(1)}, f32[32,1,256]{2,1,0:T(1,128)}) custom-call(f32[32,1,256]{2,1,0:T(1,128)S(1)} %all-to-all-done.sums, f32[128,16,128]{2,1,0:T(8,128)S(1)} %get-tuple-element.77.image), custom_call_target="tpu_custom_call" | custom-call | flops 268435456 | tf_op jit(solution)/shard_map/pallas_call | solution.py:486
  43.1 2.8 %all-to-all-start.1 = ((f32[32,1,256]{2,1,0:T(1,128)}), f32[32,1,256]{2,1,0:T(1,128)S(1)}, u32[]{:S(2)}, u32[]{:S(2)}) async-start(f32[32,1,256]{2,1,0:T(1,128)} %get-tuple-element.94), calls=%async_computation.1 | async-start | bytes 65536 | tf_op jit(solution)/shard_map/all_to_all | solution.py:394
  45.9 1.8 %shard_map.100 = (f32[33,16,128]{2,1,0:T(8,128)S(1)}, f32[160,16,128]{2,1,0:T(8,128)S(1)}) custom-call(s32[8]{0:T(128)S(1)} %stack.35.plan, s32[1024]{0:T(1024)S(1)} %bitcast.42, f32[1024]{0:T(1024)S(1)} %bitcast.37, s32[1024]{0:T(1024)S(1)} %bitcast.30, f32[160,16,128]{2,1,0:T(8,128)S(1)} %get-tuple-element.78.own, ...), custom_call_target="tpu_custom_call", output_to_operand_aliasing={{1}: (4, {})} | custom-call | flops 402653184 | tf_op jit(solution)/shard_map/pallas_call | solution.py:492
  47.7 1.5 %collective-permute-start.12 = (f32[33,16,128]{2,1,0:T(8,128)S(1)}, f32[33,16,128]{2,1,0:T(8,128)S(1)}, u32[]{:S(2)}, u32[]{:S(2)}) collective-permute-start(f32[33,16,128]{2,1,0:T(8,128)S(1)} %get-tuple-element.96.first.rest_0_), channel_id=1, source_target_pairs={{0,4},{1,5},{2,6},{3,7},{4,0},{5,1},{6,2},{7,3},{8,12},{9,13},{10,... | collective-permute-start | bytes 811016 | tf_op jit(solution)/shard_map/ppermute | solution.py:502
  49.2 3.3 %shard_map.101 = (f32[32,16,128]{2,1,0:T(8,128)S(1)}, f32[32,16,128]{2,1,0:T(8,128)S(1)}, f32[32,16,128]{2,1,0:T(8,128)S(1)}) custom-call(s32[1024]{0:T(1024)S(1)} %bitcast.43, f32[1024]{0:T(1024)S(1)} %bitcast.38, s32[1024]{0:T(1024)S(1)} %bitcast.31, f32[160,16,128]{2,1,0:T(8,128)S(1)} %get-tuple-element.90.full, bf16[1024,256]{1,0:T(8,128)(2,1)S(1)} %shard_map.95.tiles), custom_call_target="tpu_custom_call" | custom-call | flops 1207959552 | tf_op jit(solution)/shard_map/pallas_call | solution.py:503
  53.5 1.5 %collective-permute-start.14 = (f32[32,16,128]{2,1,0:T(8,128)S(1)}, f32[32,16,128]{2,1,0:T(8,128)S(1)}, u32[]{:S(2)}, u32[]{:S(2)}) collective-permute-start(f32[32,16,128]{2,1,0:T(8,128)S(1)} %get-tuple-element.98.rest_1_.rest_2_), channel_id=1, source_target_pairs={{0,4},{1,5},{2,6},{3,7},{4,0},{5,1},{6,2},{7,3},{8,12},{9,13},{10,... | collective-permute-start | bytes 786440 | tf_op jit(solution)/shard_map/ppermute | solution.py:512
  55.6 4.1 %shard_map.102 = (f32[32,1,512]{2,1,0:T(1,128)S(1)}, f32[16,128]{1,0:T(8,128)S(1)}) custom-call(s32[1024]{0:T(1024)S(1)} %bitcast.32, f32[32,1,256]{2,1,0:T(1,128)S(1)} %all-to-all-done.1.sums, f32[160,16,128]{2,1,0:T(8,128)S(1)} %get-tuple-element.90.full, f32[33,16,128]{2,1,0:T(8,128)S(1)} %get-tuple-element.96.first.rest_0_, ...), custom_call_target="tpu_custom_call" | custom-call | tf_op jit(solution)/shard_map/pallas_call | solution.py:514
  59.7 14.2 %all_to_all.15.sums = f32[32,1,512]{2,1,0:T(1,128)S(1)} all-to-all(f32[32,1,512]{2,1,0:T(1,128)S(1)} %get-tuple-element.100), channel_id=1, replica_groups=mesh['gx'=4,'gy'=8] {'gx','gy'}, dimensions={0} | all-to-all | bytes 131072 | tf_op jit(solution)/shard_map/all_to_all | solution.py:394
  73.9 4.5 %shard_map.103 = (f32[128,16,128]{2,1,0:T(8,128)}, f32[16,16]{1,0:T(8,128)}, f32[8,128]{1,0:T(8,128)}, s32[8,128]{1,0:T(8,128)}) custom-call(s32[1024]{0:T(1024)S(1)} %bitcast.33, f32[32,1,512]{2,1,0:T(1,128)S(1)} %all_to_all.15.sums, f32[16,128]{1,0:T(8,128)S(1)} %get-tuple-element.101.inverse, f32[33,16,128]{2,1,0:T(8,128)S(1)} %get-tuple-element.96.first.rest_0_, ...), custom_call_target="tpu_custom_call" | custom-call | tf_op jit(solution)/shard_map/pallas_call | solution.py:521
  (35 shorter events, 3.4 us)
Async XLA Ops:
  0.6 12.8 %copy-start = (f32[1,1,128,16,128]{4,3,2,1,0:T(8,128)S(1)}, f32[1,1,128,16,128]{4,3,2,1,0:T(8,128)}, u32[]{:S(2)}) copy-start(f32[1,1,128,16,128]{4,3,2,1,0:T(8,128)} %param.6) | copy-start | bytes 3145732
  0.6 11.9 %copy-start.2 = (f32[1,1,128,8]{2,3,1,0:T(8,128)S(1)}, f32[1,1,128,8]{2,3,1,0:T(8,128)}, u32[]{:S(2)}) copy-start(f32[1,1,128,8]{2,3,1,0:T(8,128)} %param.8) | copy-start | bytes 12292
  0.7 11.9 %copy-start.3 = (s32[1,1,128,8]{2,3,1,0:T(8,128)S(1)}, s32[1,1,128,8]{2,3,1,0:T(8,128)}, u32[]{:S(2)}) copy-start(s32[1,1,128,8]{2,3,1,0:T(8,128)} %param.9) | copy-start | bytes 12292
  0.7 11.9 %copy-start.4 = (s32[1,1,128]{2,1,0:T(1,128)S(1)}, s32[1,1,128]{2,1,0:T(1,128)}, u32[]{:S(2)}) copy-start(s32[1,1,128]{2,1,0:T(1,128)} %param.11) | copy-start | bytes 1540
  3.3 9.6 %collective-permute-start = (f32[8,16,128]{2,1,0:T(8,128)S(1)}, f32[8,16,128]{2,1,0:T(8,128)S(1)}, u32[]{:S(2)}, u32[]{:S(2)}) collective-permute-start(f32[8,16,128]{2,1,0:T(8,128)S(1)} %get-tuple-element.55), channel_id=1, source_target_pairs={{0,8},{8,0},{16,24},{24,16},{1,9},{9,1},{17,25},{25,17},{2,10},{10... | collective-permute-start | bytes 196616 | tf_op jit(solution)/shard_map/ppermute | solution.py:376
  6.4 6.5 %collective-permute-start.1 = (f32[8,16,128]{2,1,0:T(8,128)S(1)}, f32[8,16,128]{2,1,0:T(8,128)S(1)}, u32[]{:S(2)}, u32[]{:S(2)}) collective-permute-start(f32[8,16,128]{2,1,0:T(8,128)S(1)} %get-tuple-element.56), channel_id=1, source_target_pairs={{8,16},{16,8},{24,0},{0,24},{9,17},{17,9},{25,1},{1,25},{10,18},{1... | collective-permute-start | bytes 196616 | tf_op jit(solution)/shard_map/ppermute | solution.py:376
  8.8 4.1 %collective-permute-start.2 = (f32[8,16,128]{2,1,0:T(8,128)S(1)}, f32[8,16,128]{2,1,0:T(8,128)S(1)}, u32[]{:S(2)}, u32[]{:S(2)}) collective-permute-start(f32[8,16,128]{2,1,0:T(8,128)S(1)} %get-tuple-element.57), channel_id=1, source_target_pairs={{0,1},{1,0},{2,3},{3,2},{4,5},{5,4},{6,7},{7,6},{8,9},{9,8},{10,11... | collective-permute-start | bytes 196616 | tf_op jit(solution)/shard_map/ppermute | solution.py:376
  8.8 4.6 %collective-permute-start.3 = (f32[8,16,128]{2,1,0:T(8,128)S(1)}, f32[8,16,128]{2,1,0:T(8,128)S(1)}, u32[]{:S(2)}, u32[]{:S(2)}) collective-permute-start(f32[8,16,128]{2,1,0:T(8,128)S(1)} %get-tuple-element.58), channel_id=1, source_target_pairs={{1,2},{2,1},{3,4},{4,3},{5,6},{6,5},{7,0},{0,7},{9,10},{10,9},{11,... | collective-permute-start | bytes 196616 | tf_op jit(solution)/shard_map/ppermute | solution.py:376
  11.4 1.0 %copy-start.1 = (f32[8,128,128]{2,1,0:T(8,128)S(1)}, f32[8,128,128]{2,1,0:T(8,128)}, u32[]{:S(2)}) copy-start(f32[8,128,128]{2,1,0:T(8,128)} %tiles.1) | copy-start | bytes 1572868
  17.3 5.5 %collective-permute-start.4 = (f32[8,16,128]{2,1,0:T(8,128)S(1)}, f32[8,16,128]{2,1,0:T(8,128)S(1)}, u32[]{:S(2)}, u32[]{:S(2)}) collective-permute-start(f32[8,16,128]{2,1,0:T(8,128)S(1)} %get-tuple-element.67), channel_id=1, source_target_pairs={{0,8},{8,0},{16,24},{24,16},{1,9},{9,1},{17,25},{25,17},{2,10},{10... | collective-permute-start | bytes 196616 | tf_op jit(solution)/shard_map/ppermute | solution.py:376
  18.1 6.1 %collective-permute-start.5 = (f32[8,16,128]{2,1,0:T(8,128)S(1)}, f32[8,16,128]{2,1,0:T(8,128)S(1)}, u32[]{:S(2)}, u32[]{:S(2)}) collective-permute-start(f32[8,16,128]{2,1,0:T(8,128)S(1)} %get-tuple-element.68), channel_id=1, source_target_pairs={{8,16},{16,8},{24,0},{0,24},{9,17},{17,9},{25,1},{1,25},{10,18},{1... | collective-permute-start | bytes 196616 | tf_op jit(solution)/shard_map/ppermute | solution.py:376
  19.0 5.2 %collective-permute-start.6 = (f32[8,16,128]{2,1,0:T(8,128)S(1)}, f32[8,16,128]{2,1,0:T(8,128)S(1)}, u32[]{:S(2)}, u32[]{:S(2)}) collective-permute-start(f32[8,16,128]{2,1,0:T(8,128)S(1)} %get-tuple-element.69), channel_id=1, source_target_pairs={{0,1},{1,0},{2,3},{3,2},{4,5},{5,4},{6,7},{7,6},{8,9},{9,8},{10,11... | collective-permute-start | bytes 196616 | tf_op jit(solution)/shard_map/ppermute | solution.py:376
  19.0 5.2 %collective-permute-start.7 = (f32[8,16,128]{2,1,0:T(8,128)S(1)}, f32[8,16,128]{2,1,0:T(8,128)S(1)}, u32[]{:S(2)}, u32[]{:S(2)}) collective-permute-start(f32[8,16,128]{2,1,0:T(8,128)S(1)} %get-tuple-element.70), channel_id=1, source_target_pairs={{1,2},{2,1},{3,4},{4,3},{5,6},{6,5},{7,0},{0,7},{9,10},{10,9},{11,... | collective-permute-start | bytes 196616 | tf_op jit(solution)/shard_map/ppermute | solution.py:376
  24.2 15.4 %all-to-all-start = ((f32[32,1,256]{2,1,0:T(1,128)}), f32[32,1,256]{2,1,0:T(1,128)S(1)}, u32[]{:S(2)}, u32[]{:S(2)}) async-start(f32[32,1,256]{2,1,0:T(1,128)} %shard_map.97), calls=%async_computation | async-start | bytes 65536 | tf_op jit(solution)/shard_map/all_to_all | solution.py:394
  32.9 10.2 %collective-permute-start.8 = (f32[8,16,128]{2,1,0:T(8,128)}, f32[8,16,128]{2,1,0:T(8,128)S(1)}, u32[]{:S(2)}, u32[]{:S(2)}) collective-permute-start(f32[8,16,128]{2,1,0:T(8,128)} %get-tuple-element.80), channel_id=1, source_target_pairs={{0,8},{8,0},{16,24},{24,16},{1,9},{9,1},{17,25},{25,17},{2,10},{10... | collective-permute-start | bytes 196616 | tf_op jit(solution)/shard_map/ppermute | solution.py:376
  34.7 8.4 %collective-permute-start.9 = (f32[8,16,128]{2,1,0:T(8,128)S(1)}, f32[8,16,128]{2,1,0:T(8,128)S(1)}, u32[]{:S(2)}, u32[]{:S(2)}) collective-permute-start(f32[8,16,128]{2,1,0:T(8,128)S(1)} %get-tuple-element.81), channel_id=1, source_target_pairs={{8,16},{16,8},{24,0},{0,24},{9,17},{17,9},{25,1},{1,25},{10,18},{1... | collective-permute-start | bytes 196616 | tf_op jit(solution)/shard_map/ppermute | solution.py:376
  37.1 6.1 %collective-permute-start.10 = (f32[8,16,128]{2,1,0:T(8,128)S(1)}, f32[8,16,128]{2,1,0:T(8,128)S(1)}, u32[]{:S(2)}, u32[]{:S(2)}) collective-permute-start(f32[8,16,128]{2,1,0:T(8,128)S(1)} %get-tuple-element.82), channel_id=1, source_target_pairs={{0,1},{1,0},{2,3},{3,2},{4,5},{5,4},{6,7},{7,6},{8,9},{9,8},{10,11... | collective-permute-start | bytes 196616 | tf_op jit(solution)/shard_map/ppermute | solution.py:376
  37.1 6.1 %collective-permute-start.11 = (f32[8,16,128]{2,1,0:T(8,128)S(1)}, f32[8,16,128]{2,1,0:T(8,128)S(1)}, u32[]{:S(2)}, u32[]{:S(2)}) collective-permute-start(f32[8,16,128]{2,1,0:T(8,128)S(1)} %get-tuple-element.83), channel_id=1, source_target_pairs={{1,2},{2,1},{3,4},{4,3},{5,6},{6,5},{7,0},{0,7},{9,10},{10,9},{11,... | collective-permute-start | bytes 196616 | tf_op jit(solution)/shard_map/ppermute | solution.py:376
  43.1 9.8 %all-to-all-start.1 = ((f32[32,1,256]{2,1,0:T(1,128)}), f32[32,1,256]{2,1,0:T(1,128)S(1)}, u32[]{:S(2)}, u32[]{:S(2)}) async-start(f32[32,1,256]{2,1,0:T(1,128)} %get-tuple-element.94), calls=%async_computation.1 | async-start | bytes 65536 | tf_op jit(solution)/shard_map/all_to_all | solution.py:394
  47.7 26.2 %collective-permute-start.12 = (f32[33,16,128]{2,1,0:T(8,128)S(1)}, f32[33,16,128]{2,1,0:T(8,128)S(1)}, u32[]{:S(2)}, u32[]{:S(2)}) collective-permute-start(f32[33,16,128]{2,1,0:T(8,128)S(1)} %get-tuple-element.96.first.rest_0_), channel_id=1, source_target_pairs={{0,4},{1,5},{2,6},{3,7},{4,0},{5,1},{6,2},{7,3},{8,12},{9,13},{10,... | collective-permute-start | bytes 811016 | tf_op jit(solution)/shard_map/ppermute | solution.py:502
  53.0 20.9 %collective-permute-start.13 = (f32[32,16,128]{2,1,0:T(8,128)S(1)}, f32[32,16,128]{2,1,0:T(8,128)S(1)}, u32[]{:S(2)}, u32[]{:S(2)}) collective-permute-start(f32[32,16,128]{2,1,0:T(8,128)S(1)} %get-tuple-element.97.rest_0_.rest_1_), channel_id=1, source_target_pairs={{0,4},{1,5},{2,6},{3,7},{4,0},{5,1},{6,2},{7,3},{8,12},{9,13},{10,... | collective-permute-start | bytes 786440 | tf_op jit(solution)/shard_map/ppermute | solution.py:512
  53.5 20.3 %collective-permute-start.14 = (f32[32,16,128]{2,1,0:T(8,128)S(1)}, f32[32,16,128]{2,1,0:T(8,128)S(1)}, u32[]{:S(2)}, u32[]{:S(2)}) collective-permute-start(f32[32,16,128]{2,1,0:T(8,128)S(1)} %get-tuple-element.98.rest_1_.rest_2_), channel_id=1, source_target_pairs={{0,4},{1,5},{2,6},{3,7},{4,0},{5,1},{6,2},{7,3},{8,12},{9,13},{10,... | collective-permute-start | bytes 786440 | tf_op jit(solution)/shard_map/ppermute | solution.py:512
  55.0 18.8 %collective-permute-start.15 = (f32[32,16,128]{2,1,0:T(8,128)S(1)}, f32[32,16,128]{2,1,0:T(8,128)S(1)}, u32[]{:S(2)}, u32[]{:S(2)}) collective-permute-start(f32[32,16,128]{2,1,0:T(8,128)S(1)} %get-tuple-element.99.rest_2_.rest_3_), channel_id=1, source_target_pairs={{0,4},{1,5},{2,6},{3,7},{4,0},{5,1},{6,2},{7,3},{8,12},{9,13},{10,... | collective-permute-start | bytes 786440 | tf_op jit(solution)/shard_map/ppermute | solution.py:512

commit v5 on v4

--- a/solution.py
+++ b/solution.py
@@ -62,19 +62,17 @@
 
 
 def eliminate(gram, right):
-    cols = gram.shape[0]
-    row = lax.broadcasted_iota(jnp.int32, (cols, 128), 0)
-    for j in range(cols):
-        inv = lax.rsqrt(gram[j : j + 1, j : j + 1])
-        factor = gram[:, j : j + 1] * inv
-        gram_row = gram[j : j + 1, :] * inv
-        right_row = right[j : j + 1, :] * inv
-        below = row > j
-        gram = jnp.where(below, gram - factor * gram_row, gram)
-        right = jnp.where(
-            below, right - factor * right_row, jnp.where(row == j, right_row, right)
-        )
-    return right
+    size = gram.shape[0]
+    row = lax.broadcasted_iota(jnp.int32, (size, 128), 0)
+    columns = [jnp.broadcast_to(gram[:, j : j + 1], (size, 128)) for j in range(size)]
+    pivots = []
+    for j in range(size):
+        pivots.append(columns[j][j : j + 1])
+        factor = jnp.where(row > j, columns[j], 0.0) * (1.0 / pivots[j])
+        for k in range(j + 1, size):
+            columns[k] = columns[k] - factor * columns[k][j : j + 1]
+        right = right - factor * right[j : j + 1]
+    return right * lax.rsqrt(jnp.concatenate(pivots, 0))
 
 
 def scaler(small):
@@ -122,21 +120,21 @@
     return x.reshape(128, 128)
 
 
-def first_sends_kernel(plan, sends_hbm, block, *rest):
-    outs, (sends, sems, sem) = rest[:-3], rest[-3:]
-    copy = pltpu.make_async_copy(sends_hbm, sends, sem)
-    copy.start()
-    copy.wait()
-    copies = []
+def first_sends_kernel(plan, sends_hbm, block_hbm, tiles_hbm, block, tiles, *rest):
+    outs, (sends, sems) = rest[:-2], rest[-2:]
+    copies = [
+        pltpu.make_async_copy(sends_hbm, sends, sems.at[0]),
+        pltpu.make_async_copy(block_hbm, block, sems.at[1]),
+        pltpu.make_async_copy(tiles_hbm, tiles, sems.at[2]),
+    ]
+    for copy in copies:
+        copy.start()
+    copies[0].wait()
+    copies[1].wait()
     for n, out in enumerate(outs):
         for h in range(out.shape[0]):
-            copies.append(
-                pltpu.make_async_copy(block.at[sends[plan[n], h]], out.at[h], sems.at[n, h])
-            )
-    for copy in copies:
-        copy.start()
-    for copy in copies:
-        copy.wait()
+            out[h] = block[sends[plan[n], h]]
+    copies[2].wait()
 
 
 def tiles_kernel(tiles, both_out):
@@ -328,30 +326,32 @@
 
 
 def final_kernel(order, sums, inverse, *rest):
-    chunks, (out, rayleigh, weights, columns, rows, left) = rest[:-6], rest[-6:]
+    chunks, (out, rayleigh, weights, columns, rows, ready, sems) = rest[:-7], rest[-7:]
     mine, theirs = chunks[: len(chunks) // 2], chunks[len(chunks) // 2 :]
     slots, count = weights.shape
     cols, cells = out.shape[1:]
-    size, per = out.shape[0], 128 // cols
-
-    @pl.when(pl.program_id(0) == 0)
-    def _():
-        wide = cols * cols
-        total = row_sum(sums)
-        left[...] = scaler(eliminate(unpack(total[:, :wide], cols), inverse[...]))
-        rayleigh[...] = unpack(total[:, wide:], cols)[:, :cols]
-        both = jnp.concatenate([mine[0][size], theirs[0][size]], 1)
-        moved = pltpu.roll(both, 2 * count - order[count], 1)[:, :count]
-        weights[...] = moved[:slots]
-        columns[...] = moved[slots:].astype(jnp.int32)
-        for i in range(len(mine)):
-            rows[i * size : (i + 1) * size] = mine[i][:size]
-            rows[count + i * size : count + (i + 1) * size] = theirs[i][:size]
-
-    start = order[count] + pl.program_id(0) * size
-    for g in range(size // per):
-        value = rows[pl.ds(start + g * per, per)].reshape(128, cells)
-        out[g * per : (g + 1) * per] = apply_scaler(left[...], value).reshape(per, cols, cells)
+    size, per = count // len(mine), 128 // cols
+    wide = cols * cols
+    for i in range(len(mine)):
+        rows[i * size : (i + 1) * size] = mine[i][:size]
+        rows[count + i * size : count + (i + 1) * size] = theirs[i][:size]
+    total = row_sum(sums)
+    left = scaler(eliminate(unpack(total[:, :wide], cols), inverse[...]))
+    copies = []
+    for i in range(len(mine)):
+        for g in range(i * size, (i + 1) * size, per):
+            value = rows[pl.ds(order[count] + g, per)].reshape(128, cells)
+            ready[g : g + per] = apply_scaler(left, value).reshape(per, cols, cells)
+        part = pl.ds(i * size, size)
+        copies.append(pltpu.make_async_copy(ready.at[part], out.at[part], sems.at[i]))
+        copies[i].start()
+    rayleigh[...] = unpack(total[:, wide:], cols)[:, :cols]
+    both = jnp.concatenate([mine[0][size], theirs[0][size]], 1)
+    moved = pltpu.roll(both, 2 * count - order[count], 1)[:, :count]
+    weights[...] = moved[:slots]
+    columns[...] = moved[slots:].astype(jnp.int32)
+    for copy in copies:
+        copy.wait()
 
 
 def call(kernel, out_shape, in_specs, out_specs, scratch=(), limit=24, cost=(0, 0), **more):
@@ -424,17 +424,13 @@
     piece = shape(width, cols, cells)
     whole = shape(count, cols, cells)
     square = shape(cols, cells)
-    sent = call(
+    block, slot_tiles, *sent = call(
         first_sends_kernel,
-        [piece] * 4,
-        [SMEM, HBM, HBM],
-        [VMEM] * 4,
-        [
-            pltpu.SMEM(sends.shape, jnp.int32),
-            pltpu.SemaphoreType.DMA((4, width)),
-            pltpu.SemaphoreType.DMA,
-        ],
-    )(plan, in_hbm(sends), in_hbm(block))
+        [whole, shape(*slot_tiles.shape)] + [piece] * 4,
+        [SMEM] + [HBM] * 3,
+        [VMEM] * 6,
+        [pltpu.SMEM(sends.shape, jnp.int32), pltpu.SemaphoreType.DMA((3,))],
+    )(plan, in_hbm(sends), in_hbm(block), in_hbm(slot_tiles))
     near = halo(sent)
 
     wide = 2 * cells
@@ -455,7 +451,7 @@
     work = 6 * count * cols * cells * cells * slots, 0
     small = 8 * count * cells * cells * cols, 0
 
-    def operator(block, near, **more):
+    def operator(block, near):
         image, *sent = call(
             operator_kernel,
             [whole] + [piece] * 4,
@@ -471,7 +467,7 @@
                 pltpu.SemaphoreType.DMA,
             ],
             cost=work,
-            **more,
+            input_output_aliases={4: 0},
         )(plan, flat_columns, flat_weights, in_hbm(sends), block, *near, tiles)
         return image, sent
 
@@ -481,7 +477,7 @@
     packed = call(gram_kernel, gram_rows, [VMEM], VMEM, cost=small)(image)
     image, packed, *near = lax.optimization_barrier((image, packed, *near))
     sums = everywhere(packed)
-    image, sent = operator(image, near, input_output_aliases={4: 0})
+    image, sent = operator(image, near)
     near = halo(sent)
     full, inverse, packed = call(
         scale_kernel, [blocks, square, gram_rows], [VMEM] * 2, [VMEM] * 3, cost=small
@@ -527,9 +523,12 @@
             shape(slots, count, dtype=jnp.int32),
         ],
         [SMEM] + [VMEM] * (2 + 2 * CHUNKS),
-        [pl.BlockSpec((size, cols, cells), lambda i: (i, 0, 0))] + [VMEM] * 3,
-        [pltpu.VMEM((2 * count, cols, cells), F32), pltpu.VMEM((wide, wide), BF16)],
-        grid=(CHUNKS,),
+        [ANY] + [VMEM] * 3,
+        [
+            pltpu.VMEM((2 * count, cols, cells), F32),
+            pltpu.VMEM((count, cols, cells), F32),
+            pltpu.SemaphoreType.DMA((CHUNKS,)),
+        ],
     )(order, sums, inverse, first, *later, their_first, *their_later)
     return (
         moved_basis[None, None],

time: 78.8 us -> 76.8 us (0.975)
  Pallas kernels: 29.8 us -> 26.2 us
  local copies, waits for them, and re-layouts: 1.15 us -> 0.1 us
  blocking collectives: 14.2 us -> 15.2 us
  waiting for transfers between devices: 2.37 us -> 3.33 us
  starting transfers between devices: 30 us -> 30.8 us
    pallas_call x1, Pallas kernels: 4.54 us -> 3.27 us  [per_device(): call(final_kernel, [whole, shape(cols, cols), shape(slots, count), shape(...]
    ppermute x12, waiting for transfers between devices: 1.87 us -> 2.94 us  [pairs(): return lax.ppermute(x, axis, swap)]
    all_to_all x1, blocking collectives: 14.2 us -> 15.2 us  [everywhere(): return lax.all_to_all(rows, AXES, 0, 0, tiled=True)]
    unnamed x10 -> x6, local copies, waits for them, and re-layouts: 1.06 us -> 0.01 us
    pallas_call x1, Pallas kernels: 4.1 us -> 3.17 us  [per_device(): call(sums_kernel, [shape(devices, 1, 2 * cols * cols), square], [SMEM] +...]
    pallas_call x1, Pallas kernels: 3.52 us -> 2.59 us  [per_device(): call(scale_kernel, [blocks, square, gram_rows], [VMEM] * 2, [VMEM] * 3, c...]
  transfers between devices with their start and end apart: 18 -> 18, of which waited for: 3 -> 4; matrix products, arithmetic and copies ran while one was open for 0% -> 0% of each run, Pallas kernels for 24% -> 22%
where the time goes in v5:
time: 76.8 us; the launch traced here: 76.6 us
  starting transfers between devices  30.8 us (40%)
  Pallas kernels  26.2 us (34%)
  blocking collectives  15.2 us (20%)
  waiting for transfers between devices  3.33 us (4%)
  between operations  0.97 us (1%)
    ppermute x12, starting transfers between devices, pairs(): return lax.ppermute(x, axis, swap)  19 us
    all_to_all x1, blocking collectives, everywhere(): return lax.all_to_all(rows, AXES, 0, 0, tiled=True)  15.2 us
    pallas_call x2, Pallas kernels, operator(): call(operator_kernel, [whole] + [piece] * 4, [SMEM] * 3 + [HBM] + [VMEM]...  8.45 us
    all_to_all x2, starting transfers between devices, everywhere(): return lax.all_to_all(rows, AXES, 0, 0, tiled=True)  7.53 us
    pallas_call x1, Pallas kernels, per_device(): call(final_kernel, [whole, shape(cols, cols), shape(slots, count), shape(...  3.27 us
    pallas_call x1, Pallas kernels, per_device(): call(last_rest_kernel, [shape(size, cols, cells)] * (CHUNKS - 1), [SMEM]...  3.26 us
    pallas_call x1, Pallas kernels, per_device(): call(sums_kernel, [shape(devices, 1, 2 * cols * cols), square], [SMEM] +...  3.17 us
    ppermute x12, waiting for transfers between devices, pairs(): return lax.ppermute(x, axis, swap)  2.94 us
  transfers between devices with their start and end apart: 18, of which 4 were waited for; matrix products, arithmetic and copies ran while one was open for 0% of the time, Pallas kernels for 22%

profile of v5, /device:TPU:0, one launch (start us, length us, event | category | flops | bytes accessed | tf_op | source)
XLA Modules:
  0.0 76.6 jit_solution(9496825842436603692)
XLA Ops:
  0.8 1.9 %shard_map.93 = (f32[128,16,128]{2,1,0:T(8,128)S(1)}, f32[8,128,128]{2,1,0:T(8,128)S(1)}, f32[8,16,128]{2,1,0:T(8,128)S(1)}, f32[8,16,128]{2,1,0:T(8,128)S(1)}, ...) custom-call(s32[8]{0:T(128)S(1)} %stack.35.plan, s32[4,8]{1,0:T(4,128)} %bitcast.44, f32[128,16,128]{2,1,0:T(8,128)} %bitcast.43, ...), custom_call_target="tpu_custom_call" | custom-call | tf_op jit(solution)/shard_map/pallas_call | solution.py:427
  2.7 3.1 %collective-permute-start = (f32[8,16,128]{2,1,0:T(8,128)S(1)}, f32[8,16,128]{2,1,0:T(8,128)S(1)}, u32[]{:S(2)}, u32[]{:S(2)}) collective-permute-start(f32[8,16,128]{2,1,0:T(8,128)S(1)} %get-tuple-element.57), channel_id=1, source_target_pairs={{0,8},{8,0},{16,24},{24,16},{1,9},{9,1},{17,25},{25,17},{2,10},{10... | collective-permute-start | bytes 196616 | tf_op jit(solution)/shard_map/ppermute | solution.py:376
  5.8 2.5 %collective-permute-start.1 = (f32[8,16,128]{2,1,0:T(8,128)S(1)}, f32[8,16,128]{2,1,0:T(8,128)S(1)}, u32[]{:S(2)}, u32[]{:S(2)}) collective-permute-start(f32[8,16,128]{2,1,0:T(8,128)S(1)} %get-tuple-element.58), channel_id=1, source_target_pairs={{8,16},{16,8},{24,0},{0,24},{9,17},{17,9},{25,1},{1,25},{10,18},{1... | collective-permute-start | bytes 196616 | tf_op jit(solution)/shard_map/ppermute | solution.py:376
  8.3 2.6 %collective-permute-start.3 = (f32[8,16,128]{2,1,0:T(8,128)S(1)}, f32[8,16,128]{2,1,0:T(8,128)S(1)}, u32[]{:S(2)}, u32[]{:S(2)}) collective-permute-start(f32[8,16,128]{2,1,0:T(8,128)S(1)} %get-tuple-element.60), channel_id=1, source_target_pairs={{1,2},{2,1},{3,4},{4,3},{5,6},{6,5},{7,0},{0,7},{9,10},{10,9},{11,... | collective-permute-start | bytes 196616 | tf_op jit(solution)/shard_map/ppermute | solution.py:376
  11.9 1.0 %collective-permute-done.3.h3 = f32[8,16,128]{2,1,0:T(8,128)S(1)} collective-permute-done((f32[8,16,128]{2,1,0:T(8,128)S(1)}, f32[8,16,128]{2,1,0:T(8,128)S(1)}, u32[]{:S(2)}, u32[]{:S(2)}) %collective-permute-start.3) | collective-permute-done | bytes 65568 | tf_op jit(solution)/shard_map/ppermute | solution.py:376
  12.9 3.9 %shard_map.96 = (f32[128,16,128]{2,1,0:T(8,128)S(1)}, f32[8,16,128]{2,1,0:T(8,128)S(1)}, f32[8,16,128]{2,1,0:T(8,128)S(1)}, f32[8,16,128]{2,1,0:T(8,128)S(1)}, f32[8,16,128]{2,1,0:T(8,128)S(1)}) custom-call(s32[8]{0:T(128)S(1)} %stack.35.plan, s32[1024]{0:T(1024)S(1)} %bitcast.38, f32[1024]{0:T(1024)S(1)} %bitcast.33, ...), custom_call_target="tpu_custom_call", output_to_operand_aliasing={{0}: (4, {})} | custom-call | flops 1610612736 | tf_op jit(solution)/shard_map/pallas_call | solution.py:455
  17.5 0.9 %collective-permute-start.5 = (f32[8,16,128]{2,1,0:T(8,128)S(1)}, f32[8,16,128]{2,1,0:T(8,128)S(1)}, u32[]{:S(2)}, u32[]{:S(2)}) collective-permute-start(f32[8,16,128]{2,1,0:T(8,128)S(1)} %get-tuple-element.72), channel_id=1, source_target_pairs={{8,16},{16,8},{24,0},{0,24},{9,17},{17,9},{25,1},{1,25},{10,18},{1... | collective-permute-start | bytes 196616 | tf_op jit(solution)/shard_map/ppermute | solution.py:376
  18.4 2.6 %collective-permute-start.7 = (f32[8,16,128]{2,1,0:T(8,128)S(1)}, f32[8,16,128]{2,1,0:T(8,128)S(1)}, u32[]{:S(2)}, u32[]{:S(2)}) collective-permute-start(f32[8,16,128]{2,1,0:T(8,128)S(1)} %get-tuple-element.74), channel_id=1, source_target_pairs={{1,2},{2,1},{3,4},{4,3},{5,6},{6,5},{7,0},{0,7},{9,10},{10,9},{11,... | collective-permute-start | bytes 196616 | tf_op jit(solution)/shard_map/ppermute | solution.py:376
  21.0 1.3 %shard_map.97 = f32[32,1,256]{2,1,0:T(1,128)} custom-call(f32[128,16,128]{2,1,0:T(8,128)S(1)} %get-tuple-element.76.image.block), custom_call_target="tpu_custom_call" | custom-call | flops 268435456 | tf_op jit(solution)/shard_map/pallas_call | solution.py:477
  22.3 1.4 %collective-permute-done.5.h1 = f32[8,16,128]{2,1,0:T(8,128)S(1)} collective-permute-done((f32[8,16,128]{2,1,0:T(8,128)S(1)}, f32[8,16,128]{2,1,0:T(8,128)S(1)}, u32[]{:S(2)}, u32[]{:S(2)}) %collective-permute-start.5) | collective-permute-done | bytes 65568 | tf_op jit(solution)/shard_map/ppermute | solution.py:376
  23.6 4.1 %all-to-all-start = ((f32[32,1,256]{2,1,0:T(1,128)}), f32[32,1,256]{2,1,0:T(1,128)S(1)}, u32[]{:S(2)}, u32[]{:S(2)}) async-start(f32[32,1,256]{2,1,0:T(1,128)} %shard_map.97), calls=%async_computation | async-start | bytes 65536 | tf_op jit(solution)/shard_map/all_to_all | solution.py:394
  27.8 4.5 %shard_map.98 = (f32[128,16,128]{2,1,0:T(8,128)S(1)}, f32[8,16,128]{2,1,0:T(8,128)}, f32[8,16,128]{2,1,0:T(8,128)S(1)}, f32[8,16,128]{2,1,0:T(8,128)S(1)}, f32[8,16,128]{2,1,0:T(8,128)S(1)}) custom-call(s32[8]{0:T(128)S(1)} %stack.35.plan, s32[1024]{0:T(1024)S(1)} %bitcast.39, f32[1024]{0:T(1024)S(1)} %bitcast.34, ...), custom_call_target="tpu_custom_call", output_to_operand_aliasing={{0}: (4, {})} | custom-call | flops 1610612736 | tf_op jit(solution)/shard_map/pallas_call | solution.py:455
  32.3 1.8 %collective-permute-start.8 = (f32[8,16,128]{2,1,0:T(8,128)}, f32[8,16,128]{2,1,0:T(8,128)S(1)}, u32[]{:S(2)}, u32[]{:S(2)}) collective-permute-start(f32[8,16,128]{2,1,0:T(8,128)} %get-tuple-element.84), channel_id=1, source_target_pairs={{0,8},{8,0},{16,24},{24,16},{1,9},{9,1},{17,25},{25,17},{2,10},{10... | collective-permute-start | bytes 196616 | tf_op jit(solution)/shard_map/ppermute | solution.py:376
  34.1 2.4 %collective-permute-start.9 = (f32[8,16,128]{2,1,0:T(8,128)S(1)}, f32[8,16,128]{2,1,0:T(8,128)S(1)}, u32[]{:S(2)}, u32[]{:S(2)}) collective-permute-start(f32[8,16,128]{2,1,0:T(8,128)S(1)} %get-tuple-element.85), channel_id=1, source_target_pairs={{8,16},{16,8},{24,0},{0,24},{9,17},{17,9},{25,1},{1,25},{10,18},{1... | collective-permute-start | bytes 196616 | tf_op jit(solution)/shard_map/ppermute | solution.py:376
  36.5 2.5 %collective-permute-start.11 = (f32[8,16,128]{2,1,0:T(8,128)S(1)}, f32[8,16,128]{2,1,0:T(8,128)S(1)}, u32[]{:S(2)}, u32[]{:S(2)}) collective-permute-start(f32[8,16,128]{2,1,0:T(8,128)S(1)} %get-tuple-element.87), channel_id=1, source_target_pairs={{1,2},{2,1},{3,4},{4,3},{5,6},{6,5},{7,0},{0,7},{9,10},{10,9},{11,... | collective-permute-start | bytes 196616 | tf_op jit(solution)/shard_map/ppermute | solution.py:376
  39.0 2.6 %shard_map.99 = (f32[160,16,128]{2,1,0:T(8,128)S(1)}, f32[16,128]{1,0:T(8,128)S(1)}, f32[32,1,256]{2,1,0:T(1,128)}) custom-call(f32[32,1,256]{2,1,0:T(1,128)S(1)} %all-to-all-done.sums, f32[128,16,128]{2,1,0:T(8,128)S(1)} %get-tuple-element.81.image), custom_call_target="tpu_custom_call" | custom-call | flops 268435456 | tf_op jit(solution)/shard_map/pallas_call | solution.py:482
  41.6 3.4 %all-to-all-start.1 = ((f32[32,1,256]{2,1,0:T(1,128)}), f32[32,1,256]{2,1,0:T(1,128)S(1)}, u32[]{:S(2)}, u32[]{:S(2)}) async-start(f32[32,1,256]{2,1,0:T(1,128)} %get-tuple-element.98), calls=%async_computation.1 | async-start | bytes 65536 | tf_op jit(solution)/shard_map/all_to_all | solution.py:394
  45.0 1.8 %shard_map.100 = (f32[33,16,128]{2,1,0:T(8,128)S(1)}, f32[160,16,128]{2,1,0:T(8,128)S(1)}) custom-call(s32[8]{0:T(128)S(1)} %stack.35.plan, s32[1024]{0:T(1024)S(1)} %bitcast.40, f32[1024]{0:T(1024)S(1)} %bitcast.35, s32[1024]{0:T(1024)S(1)} %bitcast.28, f32[160,16,128]{2,1,0:T(8,128)S(1)} %get-tuple-element.82.own, ...), custom_call_target="tpu_custom_call", output_to_operand_aliasing={{1}: (4, {})} | custom-call | flops 402653184 | tf_op jit(solution)/shard_map/pallas_call | solution.py:488
  46.8 1.7 %collective-permute-start.12 = (f32[33,16,128]{2,1,0:T(8,128)S(1)}, f32[33,16,128]{2,1,0:T(8,128)S(1)}, u32[]{:S(2)}, u32[]{:S(2)}) collective-permute-start(f32[33,16,128]{2,1,0:T(8,128)S(1)} %get-tuple-element.100.first.rest_0_), channel_id=1, source_target_pairs={{0,4},{1,5},{2,6},{3,7},{4,0},{5,1},{6,2},{7,3},{8,12},{9,13},{10,... | collective-permute-start | bytes 811016 | tf_op jit(solution)/shard_map/ppermute | solution.py:498
  48.5 3.3 %shard_map.101 = (f32[32,16,128]{2,1,0:T(8,128)S(1)}, f32[32,16,128]{2,1,0:T(8,128)S(1)}, f32[32,16,128]{2,1,0:T(8,128)S(1)}) custom-call(s32[1024]{0:T(1024)S(1)} %bitcast.41, f32[1024]{0:T(1024)S(1)} %bitcast.36, s32[1024]{0:T(1024)S(1)} %bitcast.29, f32[160,16,128]{2,1,0:T(8,128)S(1)} %get-tuple-element.94.full, bf16[1024,256]{1,0:T(8,128)(2,1)S(1)} %shard_map.95.tiles), custom_call_target="tpu_custom_call" | custom-call | flops 1207959552 | tf_op jit(solution)/shard_map/pallas_call | solution.py:499
  52.7 1.5 %collective-permute-start.14 = (f32[32,16,128]{2,1,0:T(8,128)S(1)}, f32[32,16,128]{2,1,0:T(8,128)S(1)}, u32[]{:S(2)}, u32[]{:S(2)}) collective-permute-start(f32[32,16,128]{2,1,0:T(8,128)S(1)} %get-tuple-element.102.rest_1_.rest_2_), channel_id=1, source_target_pairs={{0,4},{1,5},{2,6},{3,7},{4,0},{5,1},{6,2},{7,3},{8,12},{9,13},{10,... | collective-permute-start | bytes 786440 | tf_op jit(solution)/shard_map/ppermute | solution.py:508
  54.7 3.2 %shard_map.102 = (f32[32,1,512]{2,1,0:T(1,128)S(1)}, f32[16,128]{1,0:T(8,128)S(1)}) custom-call(s32[1024]{0:T(1024)S(1)} %bitcast.30, f32[32,1,256]{2,1,0:T(1,128)S(1)} %all-to-all-done.1.sums, f32[160,16,128]{2,1,0:T(8,128)S(1)} %get-tuple-element.94.full, f32[33,16,128]{2,1,0:T(8,128)S(1)} %get-tuple-element.100.first.rest_0_, ...), custom_call_target="tpu_custom_call" | custom-call | tf_op jit(solution)/shard_map/pallas_call | solution.py:510
  57.9 15.2 %all_to_all.15.sums = f32[32,1,512]{2,1,0:T(1,128)S(1)} all-to-all(f32[32,1,512]{2,1,0:T(1,128)S(1)} %get-tuple-element.104), channel_id=1, replica_groups=mesh['gx'=4,'gy'=8] {'gx','gy'}, dimensions={0} | all-to-all | bytes 131072 | tf_op jit(solution)/shard_map/all_to_all | solution.py:394
  73.1 3.3 %shard_map.103 = (f32[128,16,128]{2,1,0:T(8,128)}, f32[16,16]{1,0:T(8,128)}, f32[8,128]{1,0:T(8,128)}, s32[8,128]{1,0:T(8,128)}) custom-call(s32[1024]{0:T(1024)S(1)} %bitcast.31, f32[32,1,512]{2,1,0:T(1,128)S(1)} %all_to_all.15.sums, f32[16,128]{1,0:T(8,128)S(1)} %get-tuple-element.105.inverse, f32[33,16,128]{2,1,0:T(8,128)S(1)} %get-tuple-element.100.first.rest_0_, ...), custom_call_target="tpu_custom_call" | custom-call | tf_op jit(solution)/shard_map/pallas_call | solution.py:517
  (31 shorter events, 3.4 us)
Async XLA Ops:
  0.8 10.2 %copy-start = (f32[1,1,128,8]{2,3,1,0:T(8,128)S(1)}, f32[1,1,128,8]{2,3,1,0:T(8,128)}, u32[]{:S(2)}) copy-start(f32[1,1,128,8]{2,3,1,0:T(8,128)} %param.8) | copy-start | bytes 12292
  0.8 10.2 %copy-start.1 = (s32[1,1,128,8]{2,3,1,0:T(8,128)S(1)}, s32[1,1,128,8]{2,3,1,0:T(8,128)}, u32[]{:S(2)}) copy-start(s32[1,1,128,8]{2,3,1,0:T(8,128)} %param.9) | copy-start | bytes 12292
  0.8 10.2 %copy-start.2 = (s32[1,1,128]{2,1,0:T(1,128)S(1)}, s32[1,1,128]{2,1,0:T(1,128)}, u32[]{:S(2)}) copy-start(s32[1,1,128]{2,1,0:T(1,128)} %param.11) | copy-start | bytes 1540
  2.7 8.6 %collective-permute-start = (f32[8,16,128]{2,1,0:T(8,128)S(1)}, f32[8,16,128]{2,1,0:T(8,128)S(1)}, u32[]{:S(2)}, u32[]{:S(2)}) collective-permute-start(f32[8,16,128]{2,1,0:T(8,128)S(1)} %get-tuple-element.57), channel_id=1, source_target_pairs={{0,8},{8,0},{16,24},{24,16},{1,9},{9,1},{17,25},{25,17},{2,10},{10... | collective-permute-start | bytes 196616 | tf_op jit(solution)/shard_map/ppermute | solution.py:376
  5.8 6.1 %collective-permute-start.1 = (f32[8,16,128]{2,1,0:T(8,128)S(1)}, f32[8,16,128]{2,1,0:T(8,128)S(1)}, u32[]{:S(2)}, u32[]{:S(2)}) collective-permute-start(f32[8,16,128]{2,1,0:T(8,128)S(1)} %get-tuple-element.58), channel_id=1, source_target_pairs={{8,16},{16,8},{24,0},{0,24},{9,17},{17,9},{25,1},{1,25},{10,18},{1... | collective-permute-start | bytes 196616 | tf_op jit(solution)/shard_map/ppermute | solution.py:376
  8.3 3.6 %collective-permute-start.2 = (f32[8,16,128]{2,1,0:T(8,128)S(1)}, f32[8,16,128]{2,1,0:T(8,128)S(1)}, u32[]{:S(2)}, u32[]{:S(2)}) collective-permute-start(f32[8,16,128]{2,1,0:T(8,128)S(1)} %get-tuple-element.59), channel_id=1, source_target_pairs={{0,1},{1,0},{2,3},{3,2},{4,5},{5,4},{6,7},{7,6},{8,9},{9,8},{10,11... | collective-permute-start | bytes 196616 | tf_op jit(solution)/shard_map/ppermute | solution.py:376
  8.3 4.6 %collective-permute-start.3 = (f32[8,16,128]{2,1,0:T(8,128)S(1)}, f32[8,16,128]{2,1,0:T(8,128)S(1)}, u32[]{:S(2)}, u32[]{:S(2)}) collective-permute-start(f32[8,16,128]{2,1,0:T(8,128)S(1)} %get-tuple-element.60), channel_id=1, source_target_pairs={{1,2},{2,1},{3,4},{4,3},{5,6},{6,5},{7,0},{0,7},{9,10},{10,9},{11,... | collective-permute-start | bytes 196616 | tf_op jit(solution)/shard_map/ppermute | solution.py:376
  16.8 5.5 %collective-permute-start.4 = (f32[8,16,128]{2,1,0:T(8,128)S(1)}, f32[8,16,128]{2,1,0:T(8,128)S(1)}, u32[]{:S(2)}, u32[]{:S(2)}) collective-permute-start(f32[8,16,128]{2,1,0:T(8,128)S(1)} %get-tuple-element.71), channel_id=1, source_target_pairs={{0,8},{8,0},{16,24},{24,16},{1,9},{9,1},{17,25},{25,17},{2,10},{10... | collective-permute-start | bytes 196616 | tf_op jit(solution)/shard_map/ppermute | solution.py:376
  17.5 6.1 %collective-permute-start.5 = (f32[8,16,128]{2,1,0:T(8,128)S(1)}, f32[8,16,128]{2,1,0:T(8,128)S(1)}, u32[]{:S(2)}, u32[]{:S(2)}) collective-permute-start(f32[8,16,128]{2,1,0:T(8,128)S(1)} %get-tuple-element.72), channel_id=1, source_target_pairs={{8,16},{16,8},{24,0},{0,24},{9,17},{17,9},{25,1},{1,25},{10,18},{1... | collective-permute-start | bytes 196616 | tf_op jit(solution)/shard_map/ppermute | solution.py:376
  18.4 5.2 %collective-permute-start.6 = (f32[8,16,128]{2,1,0:T(8,128)S(1)}, f32[8,16,128]{2,1,0:T(8,128)S(1)}, u32[]{:S(2)}, u32[]{:S(2)}) collective-permute-start(f32[8,16,128]{2,1,0:T(8,128)S(1)} %get-tuple-element.73), channel_id=1, source_target_pairs={{0,1},{1,0},{2,3},{3,2},{4,5},{5,4},{6,7},{7,6},{8,9},{9,8},{10,11... | collective-permute-start | bytes 196616 | tf_op jit(solution)/shard_map/ppermute | solution.py:376
  18.4 5.2 %collective-permute-start.7 = (f32[8,16,128]{2,1,0:T(8,128)S(1)}, f32[8,16,128]{2,1,0:T(8,128)S(1)}, u32[]{:S(2)}, u32[]{:S(2)}) collective-permute-start(f32[8,16,128]{2,1,0:T(8,128)S(1)} %get-tuple-element.74), channel_id=1, source_target_pairs={{1,2},{2,1},{3,4},{4,3},{5,6},{6,5},{7,0},{0,7},{9,10},{10,9},{11,... | collective-permute-start | bytes 196616 | tf_op jit(solution)/shard_map/ppermute | solution.py:376
  23.6 15.4 %all-to-all-start = ((f32[32,1,256]{2,1,0:T(1,128)}), f32[32,1,256]{2,1,0:T(1,128)S(1)}, u32[]{:S(2)}, u32[]{:S(2)}) async-start(f32[32,1,256]{2,1,0:T(1,128)} %shard_map.97), calls=%async_computation | async-start | bytes 65536 | tf_op jit(solution)/shard_map/all_to_all | solution.py:394
  32.3 9.3 %collective-permute-start.8 = (f32[8,16,128]{2,1,0:T(8,128)}, f32[8,16,128]{2,1,0:T(8,128)S(1)}, u32[]{:S(2)}, u32[]{:S(2)}) collective-permute-start(f32[8,16,128]{2,1,0:T(8,128)} %get-tuple-element.84), channel_id=1, source_target_pairs={{0,8},{8,0},{16,24},{24,16},{1,9},{9,1},{17,25},{25,17},{2,10},{10... | collective-permute-start | bytes 196616 | tf_op jit(solution)/shard_map/ppermute | solution.py:376
  34.1 7.5 %collective-permute-start.9 = (f32[8,16,128]{2,1,0:T(8,128)S(1)}, f32[8,16,128]{2,1,0:T(8,128)S(1)}, u32[]{:S(2)}, u32[]{:S(2)}) collective-permute-start(f32[8,16,128]{2,1,0:T(8,128)S(1)} %get-tuple-element.85), channel_id=1, source_target_pairs={{8,16},{16,8},{24,0},{0,24},{9,17},{17,9},{25,1},{1,25},{10,18},{1... | collective-permute-start | bytes 196616 | tf_op jit(solution)/shard_map/ppermute | solution.py:376
  36.5 5.1 %collective-permute-start.10 = (f32[8,16,128]{2,1,0:T(8,128)S(1)}, f32[8,16,128]{2,1,0:T(8,128)S(1)}, u32[]{:S(2)}, u32[]{:S(2)}) collective-permute-start(f32[8,16,128]{2,1,0:T(8,128)S(1)} %get-tuple-element.86), channel_id=1, source_target_pairs={{0,1},{1,0},{2,3},{3,2},{4,5},{5,4},{6,7},{7,6},{8,9},{9,8},{10,11... | collective-permute-start | bytes 196616 | tf_op jit(solution)/shard_map/ppermute | solution.py:376
  36.5 5.1 %collective-permute-start.11 = (f32[8,16,128]{2,1,0:T(8,128)S(1)}, f32[8,16,128]{2,1,0:T(8,128)S(1)}, u32[]{:S(2)}, u32[]{:S(2)}) collective-permute-start(f32[8,16,128]{2,1,0:T(8,128)S(1)} %get-tuple-element.87), channel_id=1, source_target_pairs={{1,2},{2,1},{3,4},{4,3},{5,6},{6,5},{7,0},{0,7},{9,10},{10,9},{11,... | collective-permute-start | bytes 196616 | tf_op jit(solution)/shard_map/ppermute | solution.py:376
  41.6 10.5 %all-to-all-start.1 = ((f32[32,1,256]{2,1,0:T(1,128)}), f32[32,1,256]{2,1,0:T(1,128)S(1)}, u32[]{:S(2)}, u32[]{:S(2)}) async-start(f32[32,1,256]{2,1,0:T(1,128)} %get-tuple-element.98), calls=%async_computation.1 | async-start | bytes 65536 | tf_op jit(solution)/shard_map/all_to_all | solution.py:394
  46.8 26.3 %collective-permute-start.12 = (f32[33,16,128]{2,1,0:T(8,128)S(1)}, f32[33,16,128]{2,1,0:T(8,128)S(1)}, u32[]{:S(2)}, u32[]{:S(2)}) collective-permute-start(f32[33,16,128]{2,1,0:T(8,128)S(1)} %get-tuple-element.100.first.rest_0_), channel_id=1, source_target_pairs={{0,4},{1,5},{2,6},{3,7},{4,0},{5,1},{6,2},{7,3},{8,12},{9,13},{10,... | collective-permute-start | bytes 811016 | tf_op jit(solution)/shard_map/ppermute | solution.py:498
  52.1 21.0 %collective-permute-start.13 = (f32[32,16,128]{2,1,0:T(8,128)S(1)}, f32[32,16,128]{2,1,0:T(8,128)S(1)}, u32[]{:S(2)}, u32[]{:S(2)}) collective-permute-start(f32[32,16,128]{2,1,0:T(8,128)S(1)} %get-tuple-element.101.rest_0_.rest_1_), channel_id=1, source_target_pairs={{0,4},{1,5},{2,6},{3,7},{4,0},{5,1},{6,2},{7,3},{8,12},{9,13},{10,... | collective-permute-start | bytes 786440 | tf_op jit(solution)/shard_map/ppermute | solution.py:508
  52.7 20.4 %collective-permute-start.14 = (f32[32,16,128]{2,1,0:T(8,128)S(1)}, f32[32,16,128]{2,1,0:T(8,128)S(1)}, u32[]{:S(2)}, u32[]{:S(2)}) collective-permute-start(f32[32,16,128]{2,1,0:T(8,128)S(1)} %get-tuple-element.102.rest_1_.rest_2_), channel_id=1, source_target_pairs={{0,4},{1,5},{2,6},{3,7},{4,0},{5,1},{6,2},{7,3},{8,12},{9,13},{10,... | collective-permute-start | bytes 786440 | tf_op jit(solution)/shard_map/ppermute | solution.py:508
  54.1 19.0 %collective-permute-start.15 = (f32[32,16,128]{2,1,0:T(8,128)S(1)}, f32[32,16,128]{2,1,0:T(8,128)S(1)}, u32[]{:S(2)}, u32[]{:S(2)}) collective-permute-start(f32[32,16,128]{2,1,0:T(8,128)S(1)} %get-tuple-element.103.rest_2_.rest_3_), channel_id=1, source_target_pairs={{0,4},{1,5},{2,6},{3,7},{4,0},{5,1},{6,2},{7,3},{8,12},{9,13},{10,... | collective-permute-start | bytes 786440 | tf_op jit(solution)/shard_map/ppermute | solution.py:508

commit v6 on v5

--- a/solution.py
+++ b/solution.py
@@ -368,12 +368,19 @@
 
 
 def pairs(x, axis, odd):
-    size = lax.axis_size(axis)
+    sizes = [lax.axis_size(name) for name in AXES]
+    along = AXES.index(axis)
     swap = []
-    for low in range(odd, size, 2):
-        high = (low + 1) % size
-        swap += [(low, high), (high, low)]
-    return lax.ppermute(x, axis, swap)
+    for here in range(sizes[0] * sizes[1]):
+        place = list(divmod(here, sizes[1]))
+        if not odd:
+            place[along] ^= 1
+        elif place[along] in (0, sizes[along] - 1):
+            place[1 - along] ^= 1
+        else:
+            place[along] += 1 if place[along] % 2 else -1
+        swap.append((here, place[0] * sizes[1] + place[1]))
+    return lax.ppermute(x, AXES, swap)
 
 
 def in_hbm(x):
@@ -381,12 +388,9 @@
 
 
 def halo(sent):
-    near = (
-        pairs(sent[0], "gx", 0),
-        pairs(sent[1], "gx", 1),
-        pairs(sent[2], "gy", 0),
-        pairs(sent[3], "gy", 1),
-    )
+    near = [None] * 4
+    for n, axis, odd in ((3, "gy", 1), (0, "gx", 0), (1, "gx", 1), (2, "gy", 0)):
+        near[n] = pairs(sent[n], axis, odd)
     return near
 
 
@@ -475,7 +479,7 @@
     image, sent = operator(block, near)
     near = halo(sent)
     packed = call(gram_kernel, gram_rows, [VMEM], VMEM, cost=small)(image)
-    image, packed, *near = lax.optimization_barrier((image, packed, *near))
+    image, packed = lax.optimization_barrier((image, packed))
     sums = everywhere(packed)
     image, sent = operator(image, near)
     near = halo(sent)

time: 76.8 us -> 71.4 us (0.930)
  starting transfers between devices: 30.8 us -> 26.5 us
  waiting for transfers between devices: 3.33 us -> 2.17 us
    ppermute x12, starting transfers between devices: 19 us -> 14.1 us  [pairs(): return lax.ppermute(x, AXES, swap)]
    ppermute x12, waiting for transfers between devices: 2.94 us -> 1.79 us  [pairs(): return lax.ppermute(x, AXES, swap)]
  transfers between devices with their start and end apart: 18 -> 18, of which waited for: 4 -> 2; matrix products, arithmetic and copies ran while one was open for 0% -> 0% of each run, Pallas kernels for 22% -> 24%
where the time goes in v6:
time: 71.4 us; the launch traced here: 71.2 us
  starting transfers between devices  26.5 us (37%)
  Pallas kernels  26.1 us (37%)
  blocking collectives  15.2 us (21%)
  waiting for transfers between devices  2.17 us (3%)
  between operations  1.01 us (1%)
    all_to_all x1, blocking collectives, everywhere(): return lax.all_to_all(rows, AXES, 0, 0, tiled=True)  15.2 us
    ppermute x12, starting transfers between devices, pairs(): return lax.ppermute(x, AXES, swap)  14.1 us
    pallas_call x2, Pallas kernels, operator(): call(operator_kernel, [whole] + [piece] * 4, [SMEM] * 3 + [HBM] + [VMEM]...  8.43 us
    all_to_all x2, starting transfers between devices, everywhere(): return lax.all_to_all(rows, AXES, 0, 0, tiled=True)  8.16 us
    pallas_call x1, Pallas kernels, per_device(): call(final_kernel, [whole, shape(cols, cols), shape(slots, count), shape(...  3.27 us
    pallas_call x1, Pallas kernels, per_device(): call(last_rest_kernel, [shape(size, cols, cells)] * (CHUNKS - 1), [SMEM]...  3.26 us
    pallas_call x1, Pallas kernels, per_device(): call(sums_kernel, [shape(devices, 1, 2 * cols * cols), square], [SMEM] +...  3.17 us
    pallas_call x1, Pallas kernels, per_device(): call(scale_kernel, [blocks, square, gram_rows], [VMEM] * 2, [VMEM] * 3, c...  2.6 us
  transfers between devices with their start and end apart: 18, of which 2 were waited for; matrix products, arithmetic and copies ran while one was open for 0% of the time, Pallas kernels for 24%

profile of v6, /device:TPU:0, one launch (start us, length us, event | category | flops | bytes accessed | tf_op | source)
XLA Modules:
  0.0 71.2 jit_solution(10325540361450857025)
XLA Ops:
  0.8 1.9 %shard_map.93 = (f32[128,16,128]{2,1,0:T(8,128)S(1)}, f32[8,128,128]{2,1,0:T(8,128)S(1)}, f32[8,16,128]{2,1,0:T(8,128)S(1)}, f32[8,16,128]{2,1,0:T(8,128)S(1)}, ...) custom-call(s32[8]{0:T(128)S(1)} %stack.35.plan, s32[4,8]{1,0:T(4,128)} %bitcast.44, f32[128,16,128]{2,1,0:T(8,128)} %bitcast.43, ...), custom_call_target="tpu_custom_call" | custom-call | tf_op jit(solution)/shard_map/pallas_call | solution.py:431
  2.7 3.1 %collective-permute-start = (f32[8,16,128]{2,1,0:T(8,128)S(1)}, f32[8,16,128]{2,1,0:T(8,128)S(1)}, u32[]{:S(2)}, u32[]{:S(2)}) collective-permute-start(f32[8,16,128]{2,1,0:T(8,128)S(1)} %get-tuple-element.53), channel_id=1, source_target_pairs={{0,8},{1,9},{2,10},{3,11},{4,12},{5,13},{6,14},{7,15},{8,0},{9,1},... | collective-permute-start | bytes 196616 | tf_op jit(solution)/shard_map/ppermute | solution.py:383
  5.8 0.5 collective-permute-start.2
  6.3 2.6 %collective-permute-start.3 = (f32[8,16,128]{2,1,0:T(8,128)S(1)}, f32[8,16,128]{2,1,0:T(8,128)S(1)}, u32[]{:S(2)}, u32[]{:S(2)}) collective-permute-start(f32[8,16,128]{2,1,0:T(8,128)S(1)} %get-tuple-element.56), channel_id=1, source_target_pairs={{0,8},{1,2},{2,1},{3,4},{4,3},{5,6},{6,5},{7,15},{8,0},{9,10},{10,... | collective-permute-start | bytes 196616 | tf_op jit(solution)/shard_map/ppermute | solution.py:383
  9.5 1.7 %collective-permute-done.3.h3 = f32[8,16,128]{2,1,0:T(8,128)S(1)} collective-permute-done((f32[8,16,128]{2,1,0:T(8,128)S(1)}, f32[8,16,128]{2,1,0:T(8,128)S(1)}, u32[]{:S(2)}, u32[]{:S(2)}) %collective-permute-start.3) | collective-permute-done | bytes 65568 | tf_op jit(solution)/shard_map/ppermute | solution.py:383
  11.2 3.9 %shard_map.96 = (f32[128,16,128]{2,1,0:T(8,128)S(1)}, f32[8,16,128]{2,1,0:T(8,128)S(1)}, f32[8,16,128]{2,1,0:T(8,128)S(1)}, f32[8,16,128]{2,1,0:T(8,128)S(1)}, f32[8,16,128]{2,1,0:T(8,128)S(1)}) custom-call(s32[8]{0:T(128)S(1)} %stack.35.plan, s32[1024]{0:T(1024)S(1)} %bitcast.38, f32[1024]{0:T(1024)S(1)} %bitcast.33, ...), custom_call_target="tpu_custom_call", output_to_operand_aliasing={{0}: (4, {})} | custom-call | flops 1610612736 | tf_op jit(solution)/shard_map/pallas_call | solution.py:459
  15.1 2.1 %collective-permute-start.4 = (f32[8,16,128]{2,1,0:T(8,128)S(1)}, f32[8,16,128]{2,1,0:T(8,128)S(1)}, u32[]{:S(2)}, u32[]{:S(2)}) collective-permute-start(f32[8,16,128]{2,1,0:T(8,128)S(1)} %get-tuple-element.69), channel_id=1, source_target_pairs={{0,8},{1,9},{2,10},{3,11},{4,12},{5,13},{6,14},{7,15},{8,0},{9,1},... | collective-permute-start | bytes 196616 | tf_op jit(solution)/shard_map/ppermute | solution.py:383
  18.1 1.3 %shard_map.97 = f32[32,1,256]{2,1,0:T(1,128)} custom-call(f32[128,16,128]{2,1,0:T(8,128)S(1)} %get-tuple-element.68.image.block), custom_call_target="tpu_custom_call" | custom-call | flops 268435456 | tf_op jit(solution)/shard_map/pallas_call | solution.py:481
  19.4 4.2 %all-to-all-start = ((f32[32,1,256]{2,1,0:T(1,128)}), f32[32,1,256]{2,1,0:T(1,128)S(1)}, u32[]{:S(2)}, u32[]{:S(2)}) async-start(f32[32,1,256]{2,1,0:T(1,128)} %shard_map.97), calls=%async_computation | async-start | bytes 65536 | tf_op jit(solution)/shard_map/all_to_all | solution.py:398
  23.7 4.5 %shard_map.98 = (f32[128,16,128]{2,1,0:T(8,128)S(1)}, f32[8,16,128]{2,1,0:T(8,128)}, f32[8,16,128]{2,1,0:T(8,128)S(1)}, f32[8,16,128]{2,1,0:T(8,128)S(1)}, f32[8,16,128]{2,1,0:T(8,128)S(1)}) custom-call(s32[8]{0:T(128)S(1)} %stack.35.plan, s32[1024]{0:T(1024)S(1)} %bitcast.39, f32[1024]{0:T(1024)S(1)} %bitcast.34, ...), custom_call_target="tpu_custom_call", output_to_operand_aliasing={{0}: (4, {})} | custom-call | flops 1610612736 | tf_op jit(solution)/shard_map/pallas_call | solution.py:459
  28.3 1.8 %collective-permute-start.8 = (f32[8,16,128]{2,1,0:T(8,128)}, f32[8,16,128]{2,1,0:T(8,128)S(1)}, u32[]{:S(2)}, u32[]{:S(2)}) collective-permute-start(f32[8,16,128]{2,1,0:T(8,128)} %get-tuple-element.76), channel_id=1, source_target_pairs={{0,8},{1,9},{2,10},{3,11},{4,12},{5,13},{6,14},{7,15},{8,0},{9,1},... | collective-permute-start | bytes 196616 | tf_op jit(solution)/shard_map/ppermute | solution.py:383
  30.1 0.5 collective-permute-start.10
  30.6 2.4 %collective-permute-start.11 = (f32[8,16,128]{2,1,0:T(8,128)S(1)}, f32[8,16,128]{2,1,0:T(8,128)S(1)}, u32[]{:S(2)}, u32[]{:S(2)}) collective-permute-start(f32[8,16,128]{2,1,0:T(8,128)S(1)} %get-tuple-element.79), channel_id=1, source_target_pairs={{0,8},{1,2},{2,1},{3,4},{4,3},{5,6},{6,5},{7,15},{8,0},{9,10},{10,... | collective-permute-start | bytes 196616 | tf_op jit(solution)/shard_map/ppermute | solution.py:383
  33.1 2.6 %shard_map.99 = (f32[160,16,128]{2,1,0:T(8,128)S(1)}, f32[16,128]{1,0:T(8,128)S(1)}, f32[32,1,256]{2,1,0:T(1,128)}) custom-call(f32[32,1,256]{2,1,0:T(1,128)S(1)} %all-to-all-done.sums, f32[128,16,128]{2,1,0:T(8,128)S(1)} %get-tuple-element.73.image), custom_call_target="tpu_custom_call" | custom-call | flops 268435456 | tf_op jit(solution)/shard_map/pallas_call | solution.py:486
  35.7 3.9 %all-to-all-start.1 = ((f32[32,1,256]{2,1,0:T(1,128)}), f32[32,1,256]{2,1,0:T(1,128)S(1)}, u32[]{:S(2)}, u32[]{:S(2)}) async-start(f32[32,1,256]{2,1,0:T(1,128)} %get-tuple-element.90), calls=%async_computation.1 | async-start | bytes 65536 | tf_op jit(solution)/shard_map/all_to_all | solution.py:398
  39.6 1.8 %shard_map.100 = (f32[33,16,128]{2,1,0:T(8,128)S(1)}, f32[160,16,128]{2,1,0:T(8,128)S(1)}) custom-call(s32[8]{0:T(128)S(1)} %stack.35.plan, s32[1024]{0:T(1024)S(1)} %bitcast.40, f32[1024]{0:T(1024)S(1)} %bitcast.35, s32[1024]{0:T(1024)S(1)} %bitcast.28, f32[160,16,128]{2,1,0:T(8,128)S(1)} %get-tuple-element.74.own, ...), custom_call_target="tpu_custom_call", output_to_operand_aliasing={{1}: (4, {})} | custom-call | flops 402653184 | tf_op jit(solution)/shard_map/pallas_call | solution.py:492
  41.4 1.7 %collective-permute-start.12 = (f32[33,16,128]{2,1,0:T(8,128)S(1)}, f32[33,16,128]{2,1,0:T(8,128)S(1)}, u32[]{:S(2)}, u32[]{:S(2)}) collective-permute-start(f32[33,16,128]{2,1,0:T(8,128)S(1)} %get-tuple-element.92.first.rest_0_), channel_id=1, source_target_pairs={{0,4},{1,5},{2,6},{3,7},{4,0},{5,1},{6,2},{7,3},{8,12},{9,13},{10,... | collective-permute-start | bytes 811016 | tf_op jit(solution)/shard_map/ppermute | solution.py:502
  43.1 3.3 %shard_map.101 = (f32[32,16,128]{2,1,0:T(8,128)S(1)}, f32[32,16,128]{2,1,0:T(8,128)S(1)}, f32[32,16,128]{2,1,0:T(8,128)S(1)}) custom-call(s32[1024]{0:T(1024)S(1)} %bitcast.41, f32[1024]{0:T(1024)S(1)} %bitcast.36, s32[1024]{0:T(1024)S(1)} %bitcast.29, f32[160,16,128]{2,1,0:T(8,128)S(1)} %get-tuple-element.86.full, bf16[1024,256]{1,0:T(8,128)(2,1)S(1)} %shard_map.95.tiles), custom_call_target="tpu_custom_call" | custom-call | flops 1207959552 | tf_op jit(solution)/shard_map/pallas_call | solution.py:503
  46.7 0.6 collective-permute-start.13
  47.3 1.5 %collective-permute-start.14 = (f32[32,16,128]{2,1,0:T(8,128)S(1)}, f32[32,16,128]{2,1,0:T(8,128)S(1)}, u32[]{:S(2)}, u32[]{:S(2)}) collective-permute-start(f32[32,16,128]{2,1,0:T(8,128)S(1)} %get-tuple-element.94.rest_1_.rest_2_), channel_id=1, source_target_pairs={{0,4},{1,5},{2,6},{3,7},{4,0},{5,1},{6,2},{7,3},{8,12},{9,13},{10,... | collective-permute-start | bytes 786440 | tf_op jit(solution)/shard_map/ppermute | solution.py:512
  48.7 0.5 collective-permute-start.15
  49.3 3.2 %shard_map.102 = (f32[32,1,512]{2,1,0:T(1,128)S(1)}, f32[16,128]{1,0:T(8,128)S(1)}) custom-call(s32[1024]{0:T(1024)S(1)} %bitcast.30, f32[32,1,256]{2,1,0:T(1,128)S(1)} %all-to-all-done.1.sums, f32[160,16,128]{2,1,0:T(8,128)S(1)} %get-tuple-element.86.full, f32[33,16,128]{2,1,0:T(8,128)S(1)} %get-tuple-element.92.first.rest_0_, ...), custom_call_target="tpu_custom_call" | custom-call | tf_op jit(solution)/shard_map/pallas_call | solution.py:514
  52.5 15.2 %all_to_all.15.sums = f32[32,1,512]{2,1,0:T(1,128)S(1)} all-to-all(f32[32,1,512]{2,1,0:T(1,128)S(1)} %get-tuple-element.96), channel_id=1, replica_groups=mesh['gx'=4,'gy'=8] {'gx','gy'}, dimensions={0} | all-to-all | bytes 131072 | tf_op jit(solution)/shard_map/all_to_all | solution.py:398
  67.7 3.3 %shard_map.103 = (f32[128,16,128]{2,1,0:T(8,128)}, f32[16,16]{1,0:T(8,128)}, f32[8,128]{1,0:T(8,128)}, s32[8,128]{1,0:T(8,128)}) custom-call(s32[1024]{0:T(1024)S(1)} %bitcast.31, f32[32,1,512]{2,1,0:T(1,128)S(1)} %all_to_all.15.sums, f32[16,128]{1,0:T(8,128)S(1)} %get-tuple-element.97.inverse, f32[33,16,128]{2,1,0:T(8,128)S(1)} %get-tuple-element.92.first.rest_0_, ...), custom_call_target="tpu_custom_call" | custom-call | tf_op jit(solution)/shard_map/pallas_call | solution.py:521
  (31 shorter events, 1.9 us)
Async XLA Ops:
  0.8 8.3 %copy-start = (f32[1,1,128,8]{2,3,1,0:T(8,128)S(1)}, f32[1,1,128,8]{2,3,1,0:T(8,128)}, u32[]{:S(2)}) copy-start(f32[1,1,128,8]{2,3,1,0:T(8,128)} %param.8) | copy-start | bytes 12292
  0.8 8.3 %copy-start.1 = (s32[1,1,128,8]{2,3,1,0:T(8,128)S(1)}, s32[1,1,128,8]{2,3,1,0:T(8,128)}, u32[]{:S(2)}) copy-start(s32[1,1,128,8]{2,3,1,0:T(8,128)} %param.9) | copy-start | bytes 12292
  0.8 8.3 %copy-start.2 = (s32[1,1,128]{2,1,0:T(1,128)S(1)}, s32[1,1,128]{2,1,0:T(1,128)}, u32[]{:S(2)}) copy-start(s32[1,1,128]{2,1,0:T(1,128)} %param.11) | copy-start | bytes 1540
  2.7 6.7 %collective-permute-start = (f32[8,16,128]{2,1,0:T(8,128)S(1)}, f32[8,16,128]{2,1,0:T(8,128)S(1)}, u32[]{:S(2)}, u32[]{:S(2)}) collective-permute-start(f32[8,16,128]{2,1,0:T(8,128)S(1)} %get-tuple-element.53), channel_id=1, source_target_pairs={{0,8},{1,9},{2,10},{3,11},{4,12},{5,13},{6,14},{7,15},{8,0},{9,1},... | collective-permute-start | bytes 196616 | tf_op jit(solution)/shard_map/ppermute | solution.py:383
  5.8 3.6 %collective-permute-start.1 = (f32[8,16,128]{2,1,0:T(8,128)S(1)}, f32[8,16,128]{2,1,0:T(8,128)S(1)}, u32[]{:S(2)}, u32[]{:S(2)}) collective-permute-start(f32[8,16,128]{2,1,0:T(8,128)S(1)} %get-tuple-element.54), channel_id=1, source_target_pairs={{0,1},{1,0},{2,3},{3,2},{4,5},{5,4},{6,7},{7,6},{8,16},{9,17},{10,... | collective-permute-start | bytes 196616 | tf_op jit(solution)/shard_map/ppermute | solution.py:383
  5.8 3.7 %collective-permute-start.2 = (f32[8,16,128]{2,1,0:T(8,128)S(1)}, f32[8,16,128]{2,1,0:T(8,128)S(1)}, u32[]{:S(2)}, u32[]{:S(2)}) collective-permute-start(f32[8,16,128]{2,1,0:T(8,128)S(1)} %get-tuple-element.55), channel_id=1, source_target_pairs={{0,1},{1,0},{2,3},{3,2},{4,5},{5,4},{6,7},{7,6},{8,9},{9,8},{10,11... | collective-permute-start | bytes 196616 | tf_op jit(solution)/shard_map/ppermute | solution.py:383
  6.3 4.9 %collective-permute-start.3 = (f32[8,16,128]{2,1,0:T(8,128)S(1)}, f32[8,16,128]{2,1,0:T(8,128)S(1)}, u32[]{:S(2)}, u32[]{:S(2)}) collective-permute-start(f32[8,16,128]{2,1,0:T(8,128)S(1)} %get-tuple-element.56), channel_id=1, source_target_pairs={{0,8},{1,2},{2,1},{3,4},{4,3},{5,6},{6,5},{7,15},{8,0},{9,10},{10,... | collective-permute-start | bytes 196616 | tf_op jit(solution)/shard_map/ppermute | solution.py:383
  15.1 8.6 %collective-permute-start.4 = (f32[8,16,128]{2,1,0:T(8,128)S(1)}, f32[8,16,128]{2,1,0:T(8,128)S(1)}, u32[]{:S(2)}, u32[]{:S(2)}) collective-permute-start(f32[8,16,128]{2,1,0:T(8,128)S(1)} %get-tuple-element.69), channel_id=1, source_target_pairs={{0,8},{1,9},{2,10},{3,11},{4,12},{5,13},{6,14},{7,15},{8,0},{9,1},... | collective-permute-start | bytes 196616 | tf_op jit(solution)/shard_map/ppermute | solution.py:383
  17.2 6.5 %collective-permute-start.5 = (f32[8,16,128]{2,1,0:T(8,128)S(1)}, f32[8,16,128]{2,1,0:T(8,128)S(1)}, u32[]{:S(2)}, u32[]{:S(2)}) collective-permute-start(f32[8,16,128]{2,1,0:T(8,128)S(1)} %get-tuple-element.70), channel_id=1, source_target_pairs={{0,1},{1,0},{2,3},{3,2},{4,5},{5,4},{6,7},{7,6},{8,16},{9,17},{10,... | collective-permute-start | bytes 196616 | tf_op jit(solution)/shard_map/ppermute | solution.py:383
  17.3 6.5 %collective-permute-start.6 = (f32[8,16,128]{2,1,0:T(8,128)S(1)}, f32[8,16,128]{2,1,0:T(8,128)S(1)}, u32[]{:S(2)}, u32[]{:S(2)}) collective-permute-start(f32[8,16,128]{2,1,0:T(8,128)S(1)} %get-tuple-element.71), channel_id=1, source_target_pairs={{0,1},{1,0},{2,3},{3,2},{4,5},{5,4},{6,7},{7,6},{8,9},{9,8},{10,11... | collective-permute-start | bytes 196616 | tf_op jit(solution)/shard_map/ppermute | solution.py:383
  17.7 6.0 %collective-permute-start.7 = (f32[8,16,128]{2,1,0:T(8,128)S(1)}, f32[8,16,128]{2,1,0:T(8,128)S(1)}, u32[]{:S(2)}, u32[]{:S(2)}) collective-permute-start(f32[8,16,128]{2,1,0:T(8,128)S(1)} %get-tuple-element.72), channel_id=1, source_target_pairs={{0,8},{1,2},{2,1},{3,4},{4,3},{5,6},{6,5},{7,15},{8,0},{9,10},{10,... | collective-permute-start | bytes 196616 | tf_op jit(solution)/shard_map/ppermute | solution.py:383
  19.4 13.6 %all-to-all-start = ((f32[32,1,256]{2,1,0:T(1,128)}), f32[32,1,256]{2,1,0:T(1,128)S(1)}, u32[]{:S(2)}, u32[]{:S(2)}) async-start(f32[32,1,256]{2,1,0:T(1,128)} %shard_map.97), calls=%async_computation | async-start | bytes 65536 | tf_op jit(solution)/shard_map/all_to_all | solution.py:398
  28.3 7.4 %collective-permute-start.8 = (f32[8,16,128]{2,1,0:T(8,128)}, f32[8,16,128]{2,1,0:T(8,128)S(1)}, u32[]{:S(2)}, u32[]{:S(2)}) collective-permute-start(f32[8,16,128]{2,1,0:T(8,128)} %get-tuple-element.76), channel_id=1, source_target_pairs={{0,8},{1,9},{2,10},{3,11},{4,12},{5,13},{6,14},{7,15},{8,0},{9,1},... | collective-permute-start | bytes 196616 | tf_op jit(solution)/shard_map/ppermute | solution.py:383
  30.1 5.6 %collective-permute-start.9 = (f32[8,16,128]{2,1,0:T(8,128)S(1)}, f32[8,16,128]{2,1,0:T(8,128)S(1)}, u32[]{:S(2)}, u32[]{:S(2)}) collective-permute-start(f32[8,16,128]{2,1,0:T(8,128)S(1)} %get-tuple-element.77), channel_id=1, source_target_pairs={{0,1},{1,0},{2,3},{3,2},{4,5},{5,4},{6,7},{7,6},{8,16},{9,17},{10,... | collective-permute-start | bytes 196616 | tf_op jit(solution)/shard_map/ppermute | solution.py:383
  30.1 5.6 %collective-permute-start.10 = (f32[8,16,128]{2,1,0:T(8,128)S(1)}, f32[8,16,128]{2,1,0:T(8,128)S(1)}, u32[]{:S(2)}, u32[]{:S(2)}) collective-permute-start(f32[8,16,128]{2,1,0:T(8,128)S(1)} %get-tuple-element.78), channel_id=1, source_target_pairs={{0,1},{1,0},{2,3},{3,2},{4,5},{5,4},{6,7},{7,6},{8,9},{9,8},{10,11... | collective-permute-start | bytes 196616 | tf_op jit(solution)/shard_map/ppermute | solution.py:383
  30.6 5.1 %collective-permute-start.11 = (f32[8,16,128]{2,1,0:T(8,128)S(1)}, f32[8,16,128]{2,1,0:T(8,128)S(1)}, u32[]{:S(2)}, u32[]{:S(2)}) collective-permute-start(f32[8,16,128]{2,1,0:T(8,128)S(1)} %get-tuple-element.79), channel_id=1, source_target_pairs={{0,8},{1,2},{2,1},{3,4},{4,3},{5,6},{6,5},{7,15},{8,0},{9,10},{10,... | collective-permute-start | bytes 196616 | tf_op jit(solution)/shard_map/ppermute | solution.py:383
  35.7 11.0 %all-to-all-start.1 = ((f32[32,1,256]{2,1,0:T(1,128)}), f32[32,1,256]{2,1,0:T(1,128)S(1)}, u32[]{:S(2)}, u32[]{:S(2)}) async-start(f32[32,1,256]{2,1,0:T(1,128)} %get-tuple-element.90), calls=%async_computation.1 | async-start | bytes 65536 | tf_op jit(solution)/shard_map/all_to_all | solution.py:398
  41.4 26.3 %collective-permute-start.12 = (f32[33,16,128]{2,1,0:T(8,128)S(1)}, f32[33,16,128]{2,1,0:T(8,128)S(1)}, u32[]{:S(2)}, u32[]{:S(2)}) collective-permute-start(f32[33,16,128]{2,1,0:T(8,128)S(1)} %get-tuple-element.92.first.rest_0_), channel_id=1, source_target_pairs={{0,4},{1,5},{2,6},{3,7},{4,0},{5,1},{6,2},{7,3},{8,12},{9,13},{10,... | collective-permute-start | bytes 811016 | tf_op jit(solution)/shard_map/ppermute | solution.py:502
  46.7 21.0 %collective-permute-start.13 = (f32[32,16,128]{2,1,0:T(8,128)S(1)}, f32[32,16,128]{2,1,0:T(8,128)S(1)}, u32[]{:S(2)}, u32[]{:S(2)}) collective-permute-start(f32[32,16,128]{2,1,0:T(8,128)S(1)} %get-tuple-element.93.rest_0_.rest_1_), channel_id=1, source_target_pairs={{0,4},{1,5},{2,6},{3,7},{4,0},{5,1},{6,2},{7,3},{8,12},{9,13},{10,... | collective-permute-start | bytes 786440 | tf_op jit(solution)/shard_map/ppermute | solution.py:512
  47.3 20.4 %collective-permute-start.14 = (f32[32,16,128]{2,1,0:T(8,128)S(1)}, f32[32,16,128]{2,1,0:T(8,128)S(1)}, u32[]{:S(2)}, u32[]{:S(2)}) collective-permute-start(f32[32,16,128]{2,1,0:T(8,128)S(1)} %get-tuple-element.94.rest_1_.rest_2_), channel_id=1, source_target_pairs={{0,4},{1,5},{2,6},{3,7},{4,0},{5,1},{6,2},{7,3},{8,12},{9,13},{10,... | collective-permute-start | bytes 786440 | tf_op jit(solution)/shard_map/ppermute | solution.py:512
  48.7 19.0 %collective-permute-start.15 = (f32[32,16,128]{2,1,0:T(8,128)S(1)}, f32[32,16,128]{2,1,0:T(8,128)S(1)}, u32[]{:S(2)}, u32[]{:S(2)}) collective-permute-start(f32[32,16,128]{2,1,0:T(8,128)S(1)} %get-tuple-element.95.rest_2_.rest_3_), channel_id=1, source_target_pairs={{0,4},{1,5},{2,6},{3,7},{4,0},{5,1},{6,2},{7,3},{8,12},{9,13},{10,... | collective-permute-start | bytes 786440 | tf_op jit(solution)/shard_map/ppermute | solution.py:512

commit v7 on v6

--- a/solution.py
+++ b/solution.py
@@ -10,6 +10,7 @@
 F32 = jnp.float32
 BF16 = jnp.bfloat16
 AXES = ("gx", "gy")
+EXCHANGES = (("gy", 1), ("gx", 0), ("gx", 1), ("gy", 0))
 CHUNKS = 4
 VMEM = pl.BlockSpec(memory_space=pltpu.VMEM)
 SMEM = pl.BlockSpec(memory_space=pltpu.SMEM)
@@ -121,20 +122,25 @@
 
 
 def first_sends_kernel(plan, sends_hbm, block_hbm, tiles_hbm, block, tiles, *rest):
-    outs, (sends, sems) = rest[:-2], rest[-2:]
-    copies = [
-        pltpu.make_async_copy(sends_hbm, sends, sems.at[0]),
-        pltpu.make_async_copy(block_hbm, block, sems.at[1]),
-        pltpu.make_async_copy(tiles_hbm, tiles, sems.at[2]),
-    ]
+    outs, (sends, sends_sem, block_sems, tiles_sem) = rest[:-4], rest[-4:]
+    parts = block_sems.shape[0]
+    size = block.shape[0] // parts
+    first = pltpu.make_async_copy(sends_hbm, sends, sends_sem)
+    first.start()
+    copies = []
+    for i in range(parts):
+        part = pl.ds(i * size, size)
+        copies.append(pltpu.make_async_copy(block_hbm.at[part], block.at[part], block_sems.at[i]))
+        copies[i].start()
+    last = pltpu.make_async_copy(tiles_hbm, tiles, tiles_sem)
+    last.start()
+    first.wait()
     for copy in copies:
-        copy.start()
-    copies[0].wait()
-    copies[1].wait()
+        copy.wait()
     for n, out in enumerate(outs):
         for h in range(out.shape[0]):
             out[h] = block[sends[plan[n], h]]
-    copies[2].wait()
+    last.wait()
 
 
 def tiles_kernel(tiles, both_out):
@@ -338,11 +344,12 @@
     total = row_sum(sums)
     left = scaler(eliminate(unpack(total[:, :wide], cols), inverse[...]))
     copies = []
-    for i in range(len(mine)):
-        for g in range(i * size, (i + 1) * size, per):
+    part_size = count // sems.shape[0]
+    for i in range(sems.shape[0]):
+        for g in range(i * part_size, (i + 1) * part_size, per):
             value = rows[pl.ds(order[count] + g, per)].reshape(128, cells)
             ready[g : g + per] = apply_scaler(left, value).reshape(per, cols, cells)
-        part = pl.ds(i * size, size)
+        part = pl.ds(i * part_size, part_size)
         copies.append(pltpu.make_async_copy(ready.at[part], out.at[part], sems.at[i]))
         copies[i].start()
     rayleigh[...] = unpack(total[:, wide:], cols)[:, :cols]
@@ -388,10 +395,7 @@
 
 
 def halo(sent):
-    near = [None] * 4
-    for n, axis, odd in ((3, "gy", 1), (0, "gx", 0), (1, "gx", 1), (2, "gy", 0)):
-        near[n] = pairs(sent[n], axis, odd)
-    return near
+    return [pairs(x, axis, odd) for x, (axis, odd) in zip(sent, EXCHANGES)]
 
 
 def everywhere(rows):
@@ -402,14 +406,14 @@
     return jax.ShapeDtypeStruct(dims, dtype)
 
 
-def exchange_plan(size_x, size_y):
+def exchange_plan():
     numbers, counts = [], []
-    for base, axis, size in ((0, "gx", size_x), (2, "gy", size_y)):
+    for axis, odd in EXCHANGES:
         place = lax.axis_index(axis)
-        odd = place % 2
-        edge = jnp.where(odd == 1, place < size - 1, place > 0).astype(jnp.int32)
-        numbers += [base + 1 - odd, base + odd]
-        counts += [jnp.int32(1), edge]
+        upper = place % 2 if odd else 1 - place % 2
+        inside = jnp.where(upper == 1, place < lax.axis_size(axis) - 1, place > 0)
+        numbers.append(2 * AXES.index(axis) + upper)
+        counts.append(inside.astype(jnp.int32))
     return jnp.stack(numbers + counts).astype(jnp.int32)
 
 
@@ -421,7 +425,7 @@
     slots, width = slot_tiles.shape[0], sends.shape[1]
     size_x, size_y = lax.axis_size("gx"), lax.axis_size("gy")
     devices = size_x * size_y
-    plan = exchange_plan(size_x, size_y)
+    plan = exchange_plan()
     flat_weights = weights.reshape(slots * count)
     flat_columns = columns.reshape(slots * count)
 
@@ -433,7 +437,12 @@
         [whole, shape(*slot_tiles.shape)] + [piece] * 4,
         [SMEM] + [HBM] * 3,
         [VMEM] * 6,
-        [pltpu.SMEM(sends.shape, jnp.int32), pltpu.SemaphoreType.DMA((3,))],
+        [
+            pltpu.SMEM(sends.shape, jnp.int32),
+            pltpu.SemaphoreType.DMA,
+            pltpu.SemaphoreType.DMA((8,)),
+            pltpu.SemaphoreType.DMA,
+        ],
     )(plan, in_hbm(sends), in_hbm(block), in_hbm(slot_tiles))
     near = halo(sent)
 
@@ -531,7 +540,7 @@
         [
             pltpu.VMEM((2 * count, cols, cells), F32),
             pltpu.VMEM((count, cols, cells), F32),
-            pltpu.SemaphoreType.DMA((CHUNKS,)),
+            pltpu.SemaphoreType.DMA((8,)),
         ],
     )(order, sums, inverse, first, *later, their_first, *their_later)
     return (

time: 71.4 us -> 70.9 us (level)
  starting transfers between devices: 26.5 us -> 24.8 us
  waiting for transfers between devices: 2.17 us -> 3.26 us
    ppermute x12, starting transfers between devices: 14.1 us -> 10.7 us  [pairs(): return lax.ppermute(x, AXES, swap)]
    all_to_all x2, starting transfers between devices: 8.16 us -> 9.88 us  [everywhere(): return lax.all_to_all(rows, AXES, 0, 0, tiled=True)]
    ppermute x12, waiting for transfers between devices: 1.79 us -> 2.87 us  [pairs(): return lax.ppermute(x, AXES, swap)]
  transfers between devices with their start and end apart: 18 -> 18, of which waited for: 2 -> 4; matrix products, arithmetic and copies ran while one was open for 0% -> 0% of each run, Pallas kernels for 24% -> 24%
where the time goes in v7:
time: 70.9 us; the launch traced here: 70.7 us
  Pallas kernels  26.3 us (37%)
  starting transfers between devices  24.8 us (35%)
  blocking collectives  15.2 us (21%)
  waiting for transfers between devices  3.26 us (5%)
  between operations  1 us (1%)
    all_to_all x1, blocking collectives, everywhere(): return lax.all_to_all(rows, AXES, 0, 0, tiled=True)  15.2 us
    ppermute x12, starting transfers between devices, pairs(): return lax.ppermute(x, AXES, swap)  10.7 us
    all_to_all x2, starting transfers between devices, everywhere(): return lax.all_to_all(rows, AXES, 0, 0, tiled=True)  9.88 us
    pallas_call x2, Pallas kernels, operator(): call(operator_kernel, [whole] + [piece] * 4, [SMEM] * 3 + [HBM] + [VMEM]...  8.43 us
    pallas_call x1, Pallas kernels, per_device(): call(final_kernel, [whole, shape(cols, cols), shape(slots, count), shape(...  3.26 us
    pallas_call x1, Pallas kernels, per_device(): call(last_rest_kernel, [shape(size, cols, cells)] * (CHUNKS - 1), [SMEM]...  3.26 us
    pallas_call x1, Pallas kernels, per_device(): call(sums_kernel, [shape(devices, 1, 2 * cols * cols), square], [SMEM] +...  3.17 us
    ppermute x12, waiting for transfers between devices, pairs(): return lax.ppermute(x, AXES, swap)  2.87 us
  transfers between devices with their start and end apart: 18, of which 4 were waited for; matrix products, arithmetic and copies ran while one was open for 0% of the time, Pallas kernels for 24%

profile of v7, /device:TPU:0, one launch (start us, length us, event | category | flops | bytes accessed | tf_op | source)
XLA Modules:
  0.0 70.7 jit_solution(11868177147800865684)
XLA Ops:
  0.8 2.1 %shard_map.93 = (f32[128,16,128]{2,1,0:T(8,128)S(1)}, f32[8,128,128]{2,1,0:T(8,128)S(1)}, f32[8,16,128]{2,1,0:T(8,128)S(1)}, f32[8,16,128]{2,1,0:T(8,128)S(1)}, ...) custom-call(s32[8]{0:T(128)S(1)} %stack.51.plan, s32[4,8]{1,0:T(4,128)} %bitcast.46, f32[128,16,128]{2,1,0:T(8,128)} %bitcast.45, ...), custom_call_target="tpu_custom_call" | custom-call | tf_op jit(solution)/shard_map/pallas_call | solution.py:435
  2.9 3.1 %collective-permute-start = (f32[8,16,128]{2,1,0:T(8,128)S(1)}, f32[8,16,128]{2,1,0:T(8,128)S(1)}, u32[]{:S(2)}, u32[]{:S(2)}) collective-permute-start(f32[8,16,128]{2,1,0:T(8,128)S(1)} %get-tuple-element.53), channel_id=1, source_target_pairs={{0,8},{1,2},{2,1},{3,4},{4,3},{5,6},{6,5},{7,15},{8,0},{9,10},{10,... | collective-permute-start | bytes 196616 | tf_op jit(solution)/shard_map/ppermute | solution.py:390
  6.1 1.2 %collective-permute-start.2 = (f32[8,16,128]{2,1,0:T(8,128)S(1)}, f32[8,16,128]{2,1,0:T(8,128)S(1)}, u32[]{:S(2)}, u32[]{:S(2)}) collective-permute-start(f32[8,16,128]{2,1,0:T(8,128)S(1)} %get-tuple-element.55), channel_id=1, source_target_pairs={{0,1},{1,0},{2,3},{3,2},{4,5},{5,4},{6,7},{7,6},{8,16},{9,17},{10,... | collective-permute-start | bytes 196616 | tf_op jit(solution)/shard_map/ppermute | solution.py:390
  7.8 0.5 collective-permute-done.h0
  8.2 2.0 %collective-permute-done.1.h1 = f32[8,16,128]{2,1,0:T(8,128)S(1)} collective-permute-done((f32[8,16,128]{2,1,0:T(8,128)S(1)}, f32[8,16,128]{2,1,0:T(8,128)S(1)}, u32[]{:S(2)}, u32[]{:S(2)}) %collective-permute-start.1) | collective-permute-done | bytes 65568 | tf_op jit(solution)/shard_map/ppermute | solution.py:390
  10.2 3.9 %shard_map.96 = (f32[128,16,128]{2,1,0:T(8,128)S(1)}, f32[8,16,128]{2,1,0:T(8,128)S(1)}, f32[8,16,128]{2,1,0:T(8,128)S(1)}, f32[8,16,128]{2,1,0:T(8,128)S(1)}, f32[8,16,128]{2,1,0:T(8,128)S(1)}) custom-call(s32[8]{0:T(128)S(1)} %stack.51.plan, s32[1024]{0:T(1024)S(1)} %bitcast.40, f32[1024]{0:T(1024)S(1)} %bitcast.35, ...), custom_call_target="tpu_custom_call", output_to_operand_aliasing={{0}: (4, {})} | custom-call | flops 1610612736 | tf_op jit(solution)/shard_map/pallas_call | solution.py:468
  14.2 2.5 %collective-permute-start.4 = (f32[8,16,128]{2,1,0:T(8,128)S(1)}, f32[8,16,128]{2,1,0:T(8,128)S(1)}, u32[]{:S(2)}, u32[]{:S(2)}) collective-permute-start(f32[8,16,128]{2,1,0:T(8,128)S(1)} %get-tuple-element.69), channel_id=1, source_target_pairs={{0,8},{1,2},{2,1},{3,4},{4,3},{5,6},{6,5},{7,15},{8,0},{9,10},{10,... | collective-permute-start | bytes 196616 | tf_op jit(solution)/shard_map/ppermute | solution.py:390
  17.3 1.3 %shard_map.97 = f32[32,1,256]{2,1,0:T(1,128)} custom-call(f32[128,16,128]{2,1,0:T(8,128)S(1)} %get-tuple-element.68.image.block), custom_call_target="tpu_custom_call" | custom-call | flops 268435456 | tf_op jit(solution)/shard_map/pallas_call | solution.py:490
  18.6 4.8 %all-to-all-start = ((f32[32,1,256]{2,1,0:T(1,128)}), f32[32,1,256]{2,1,0:T(1,128)S(1)}, u32[]{:S(2)}, u32[]{:S(2)}) async-start(f32[32,1,256]{2,1,0:T(1,128)} %shard_map.97), calls=%async_computation | async-start | bytes 65536 | tf_op jit(solution)/shard_map/all_to_all | solution.py:402
  23.4 4.5 %shard_map.98 = (f32[128,16,128]{2,1,0:T(8,128)S(1)}, f32[8,16,128]{2,1,0:T(8,128)}, f32[8,16,128]{2,1,0:T(8,128)S(1)}, f32[8,16,128]{2,1,0:T(8,128)S(1)}, f32[8,16,128]{2,1,0:T(8,128)S(1)}) custom-call(s32[8]{0:T(128)S(1)} %stack.51.plan, s32[1024]{0:T(1024)S(1)} %bitcast.41, f32[1024]{0:T(1024)S(1)} %bitcast.36, ...), custom_call_target="tpu_custom_call", output_to_operand_aliasing={{0}: (4, {})} | custom-call | flops 1610612736 | tf_op jit(solution)/shard_map/pallas_call | solution.py:468
  27.9 1.8 %collective-permute-start.8 = (f32[8,16,128]{2,1,0:T(8,128)}, f32[8,16,128]{2,1,0:T(8,128)S(1)}, u32[]{:S(2)}, u32[]{:S(2)}) collective-permute-start(f32[8,16,128]{2,1,0:T(8,128)} %get-tuple-element.76), channel_id=1, source_target_pairs={{0,8},{1,2},{2,1},{3,4},{4,3},{5,6},{6,5},{7,15},{8,0},{9,10},{10,... | collective-permute-start | bytes 196616 | tf_op jit(solution)/shard_map/ppermute | solution.py:390
  30.0 1.0 %collective-permute-start.10 = (f32[8,16,128]{2,1,0:T(8,128)S(1)}, f32[8,16,128]{2,1,0:T(8,128)S(1)}, u32[]{:S(2)}, u32[]{:S(2)}) collective-permute-start(f32[8,16,128]{2,1,0:T(8,128)S(1)} %get-tuple-element.78), channel_id=1, source_target_pairs={{0,1},{1,0},{2,3},{3,2},{4,5},{5,4},{6,7},{7,6},{8,16},{9,17},{10,... | collective-permute-start | bytes 196616 | tf_op jit(solution)/shard_map/ppermute | solution.py:390
  31.1 2.6 %shard_map.99 = (f32[160,16,128]{2,1,0:T(8,128)S(1)}, f32[16,128]{1,0:T(8,128)S(1)}, f32[32,1,256]{2,1,0:T(1,128)}) custom-call(f32[32,1,256]{2,1,0:T(1,128)S(1)} %all-to-all-done.sums, f32[128,16,128]{2,1,0:T(8,128)S(1)} %get-tuple-element.73.image), custom_call_target="tpu_custom_call" | custom-call | flops 268435456 | tf_op jit(solution)/shard_map/pallas_call | solution.py:495
  34.0 5.1 %all-to-all-start.1 = ((f32[32,1,256]{2,1,0:T(1,128)}), f32[32,1,256]{2,1,0:T(1,128)S(1)}, u32[]{:S(2)}, u32[]{:S(2)}) async-start(f32[32,1,256]{2,1,0:T(1,128)} %get-tuple-element.90), calls=%async_computation.1 | async-start | bytes 65536 | tf_op jit(solution)/shard_map/all_to_all | solution.py:402
  39.1 1.8 %shard_map.100 = (f32[33,16,128]{2,1,0:T(8,128)S(1)}, f32[160,16,128]{2,1,0:T(8,128)S(1)}) custom-call(s32[8]{0:T(128)S(1)} %stack.51.plan, s32[1024]{0:T(1024)S(1)} %bitcast.42, f32[1024]{0:T(1024)S(1)} %bitcast.37, s32[1024]{0:T(1024)S(1)} %bitcast.30, f32[160,16,128]{2,1,0:T(8,128)S(1)} %get-tuple-element.74.own, ...), custom_call_target="tpu_custom_call", output_to_operand_aliasing={{1}: (4, {})} | custom-call | flops 402653184 | tf_op jit(solution)/shard_map/pallas_call | solution.py:501
  40.9 1.7 %collective-permute-start.12 = (f32[33,16,128]{2,1,0:T(8,128)S(1)}, f32[33,16,128]{2,1,0:T(8,128)S(1)}, u32[]{:S(2)}, u32[]{:S(2)}) collective-permute-start(f32[33,16,128]{2,1,0:T(8,128)S(1)} %get-tuple-element.92.first.rest_0_), channel_id=1, source_target_pairs={{0,4},{1,5},{2,6},{3,7},{4,0},{5,1},{6,2},{7,3},{8,12},{9,13},{10,... | collective-permute-start | bytes 811016 | tf_op jit(solution)/shard_map/ppermute | solution.py:511
  42.6 3.3 %shard_map.101 = (f32[32,16,128]{2,1,0:T(8,128)S(1)}, f32[32,16,128]{2,1,0:T(8,128)S(1)}, f32[32,16,128]{2,1,0:T(8,128)S(1)}) custom-call(s32[1024]{0:T(1024)S(1)} %bitcast.43, f32[1024]{0:T(1024)S(1)} %bitcast.38, s32[1024]{0:T(1024)S(1)} %bitcast.31, f32[160,16,128]{2,1,0:T(8,128)S(1)} %get-tuple-element.86.full, bf16[1024,256]{1,0:T(8,128)(2,1)S(1)} %shard_map.95.tiles), custom_call_target="tpu_custom_call" | custom-call | flops 1207959552 | tf_op jit(solution)/shard_map/pallas_call | solution.py:512
  45.8 0.4 all-to-all-done.1.sums
  46.2 0.6 collective-permute-start.13
  46.8 1.5 %collective-permute-start.14 = (f32[32,16,128]{2,1,0:T(8,128)S(1)}, f32[32,16,128]{2,1,0:T(8,128)S(1)}, u32[]{:S(2)}, u32[]{:S(2)}) collective-permute-start(f32[32,16,128]{2,1,0:T(8,128)S(1)} %get-tuple-element.94.rest_1_.rest_2_), channel_id=1, source_target_pairs={{0,4},{1,5},{2,6},{3,7},{4,0},{5,1},{6,2},{7,3},{8,12},{9,13},{10,... | collective-permute-start | bytes 786440 | tf_op jit(solution)/shard_map/ppermute | solution.py:521
  48.3 0.5 collective-permute-start.15
  48.8 3.2 %shard_map.102 = (f32[32,1,512]{2,1,0:T(1,128)S(1)}, f32[16,128]{1,0:T(8,128)S(1)}) custom-call(s32[1024]{0:T(1024)S(1)} %bitcast.32, f32[32,1,256]{2,1,0:T(1,128)S(1)} %all-to-all-done.1.sums, f32[160,16,128]{2,1,0:T(8,128)S(1)} %get-tuple-element.86.full, f32[33,16,128]{2,1,0:T(8,128)S(1)} %get-tuple-element.92.first.rest_0_, ...), custom_call_target="tpu_custom_call" | custom-call | tf_op jit(solution)/shard_map/pallas_call | solution.py:523
  52.0 15.2 %all_to_all.15.sums = f32[32,1,512]{2,1,0:T(1,128)S(1)} all-to-all(f32[32,1,512]{2,1,0:T(1,128)S(1)} %get-tuple-element.96), channel_id=1, replica_groups=mesh['gx'=4,'gy'=8] {'gx','gy'}, dimensions={0} | all-to-all | bytes 131072 | tf_op jit(solution)/shard_map/all_to_all | solution.py:402
  67.2 3.3 %shard_map.103 = (f32[128,16,128]{2,1,0:T(8,128)}, f32[16,16]{1,0:T(8,128)}, f32[8,128]{1,0:T(8,128)}, s32[8,128]{1,0:T(8,128)}) custom-call(s32[1024]{0:T(1024)S(1)} %bitcast.33, f32[32,1,512]{2,1,0:T(1,128)S(1)} %all_to_all.15.sums, f32[16,128]{1,0:T(8,128)S(1)} %get-tuple-element.97.inverse, f32[33,16,128]{2,1,0:T(8,128)S(1)} %get-tuple-element.92.first.rest_0_, ...), custom_call_target="tpu_custom_call" | custom-call | tf_op jit(solution)/shard_map/pallas_call | solution.py:530
  (31 shorter events, 1.9 us)
Async XLA Ops:
  0.8 6.6 %copy-start = (f32[1,1,128,8]{2,3,1,0:T(8,128)S(1)}, f32[1,1,128,8]{2,3,1,0:T(8,128)}, u32[]{:S(2)}) copy-start(f32[1,1,128,8]{2,3,1,0:T(8,128)} %param.8) | copy-start | bytes 12292
  0.8 6.6 %copy-start.1 = (s32[1,1,128,8]{2,3,1,0:T(8,128)S(1)}, s32[1,1,128,8]{2,3,1,0:T(8,128)}, u32[]{:S(2)}) copy-start(s32[1,1,128,8]{2,3,1,0:T(8,128)} %param.9) | copy-start | bytes 12292
  0.8 6.6 %copy-start.2 = (s32[1,1,128]{2,1,0:T(1,128)S(1)}, s32[1,1,128]{2,1,0:T(1,128)}, u32[]{:S(2)}) copy-start(s32[1,1,128]{2,1,0:T(1,128)} %param.11) | copy-start | bytes 1540
  2.9 5.3 %collective-permute-start = (f32[8,16,128]{2,1,0:T(8,128)S(1)}, f32[8,16,128]{2,1,0:T(8,128)S(1)}, u32[]{:S(2)}, u32[]{:S(2)}) collective-permute-start(f32[8,16,128]{2,1,0:T(8,128)S(1)} %get-tuple-element.53), channel_id=1, source_target_pairs={{0,8},{1,2},{2,1},{3,4},{4,3},{5,6},{6,5},{7,15},{8,0},{9,10},{10,... | collective-permute-start | bytes 196616 | tf_op jit(solution)/shard_map/ppermute | solution.py:390
  6.0 4.3 %collective-permute-start.1 = (f32[8,16,128]{2,1,0:T(8,128)S(1)}, f32[8,16,128]{2,1,0:T(8,128)S(1)}, u32[]{:S(2)}, u32[]{:S(2)}) collective-permute-start(f32[8,16,128]{2,1,0:T(8,128)S(1)} %get-tuple-element.54), channel_id=1, source_target_pairs={{0,8},{1,9},{2,10},{3,11},{4,12},{5,13},{6,14},{7,15},{8,0},{9,1},... | collective-permute-start | bytes 196616 | tf_op jit(solution)/shard_map/ppermute | solution.py:390
  6.1 4.2 %collective-permute-start.2 = (f32[8,16,128]{2,1,0:T(8,128)S(1)}, f32[8,16,128]{2,1,0:T(8,128)S(1)}, u32[]{:S(2)}, u32[]{:S(2)}) collective-permute-start(f32[8,16,128]{2,1,0:T(8,128)S(1)} %get-tuple-element.55), channel_id=1, source_target_pairs={{0,1},{1,0},{2,3},{3,2},{4,5},{5,4},{6,7},{7,6},{8,16},{9,17},{10,... | collective-permute-start | bytes 196616 | tf_op jit(solution)/shard_map/ppermute | solution.py:390
  7.3 2.9 %collective-permute-start.3 = (f32[8,16,128]{2,1,0:T(8,128)S(1)}, f32[8,16,128]{2,1,0:T(8,128)S(1)}, u32[]{:S(2)}, u32[]{:S(2)}) collective-permute-start(f32[8,16,128]{2,1,0:T(8,128)S(1)} %get-tuple-element.56), channel_id=1, source_target_pairs={{0,1},{1,0},{2,3},{3,2},{4,5},{5,4},{6,7},{7,6},{8,9},{9,8},{10,11... | collective-permute-start | bytes 196616 | tf_op jit(solution)/shard_map/ppermute | solution.py:390
  14.2 9.2 %collective-permute-start.4 = (f32[8,16,128]{2,1,0:T(8,128)S(1)}, f32[8,16,128]{2,1,0:T(8,128)S(1)}, u32[]{:S(2)}, u32[]{:S(2)}) collective-permute-start(f32[8,16,128]{2,1,0:T(8,128)S(1)} %get-tuple-element.69), channel_id=1, source_target_pairs={{0,8},{1,2},{2,1},{3,4},{4,3},{5,6},{6,5},{7,15},{8,0},{9,10},{10,... | collective-permute-start | bytes 196616 | tf_op jit(solution)/shard_map/ppermute | solution.py:390
  16.7 6.7 %collective-permute-start.5 = (f32[8,16,128]{2,1,0:T(8,128)S(1)}, f32[8,16,128]{2,1,0:T(8,128)S(1)}, u32[]{:S(2)}, u32[]{:S(2)}) collective-permute-start(f32[8,16,128]{2,1,0:T(8,128)S(1)} %get-tuple-element.70), channel_id=1, source_target_pairs={{0,8},{1,9},{2,10},{3,11},{4,12},{5,13},{6,14},{7,15},{8,0},{9,1},... | collective-permute-start | bytes 196616 | tf_op jit(solution)/shard_map/ppermute | solution.py:390
  16.8 6.6 %collective-permute-start.6 = (f32[8,16,128]{2,1,0:T(8,128)S(1)}, f32[8,16,128]{2,1,0:T(8,128)S(1)}, u32[]{:S(2)}, u32[]{:S(2)}) collective-permute-start(f32[8,16,128]{2,1,0:T(8,128)S(1)} %get-tuple-element.71), channel_id=1, source_target_pairs={{0,1},{1,0},{2,3},{3,2},{4,5},{5,4},{6,7},{7,6},{8,16},{9,17},{10,... | collective-permute-start | bytes 196616 | tf_op jit(solution)/shard_map/ppermute | solution.py:390
  16.9 6.4 %collective-permute-start.7 = (f32[8,16,128]{2,1,0:T(8,128)S(1)}, f32[8,16,128]{2,1,0:T(8,128)S(1)}, u32[]{:S(2)}, u32[]{:S(2)}) collective-permute-start(f32[8,16,128]{2,1,0:T(8,128)S(1)} %get-tuple-element.72), channel_id=1, source_target_pairs={{0,1},{1,0},{2,3},{3,2},{4,5},{5,4},{6,7},{7,6},{8,9},{9,8},{10,11... | collective-permute-start | bytes 196616 | tf_op jit(solution)/shard_map/ppermute | solution.py:390
  18.6 12.5 %all-to-all-start = ((f32[32,1,256]{2,1,0:T(1,128)}), f32[32,1,256]{2,1,0:T(1,128)S(1)}, u32[]{:S(2)}, u32[]{:S(2)}) async-start(f32[32,1,256]{2,1,0:T(1,128)} %shard_map.97), calls=%async_computation | async-start | bytes 65536 | tf_op jit(solution)/shard_map/all_to_all | solution.py:402
  27.9 5.7 %collective-permute-start.8 = (f32[8,16,128]{2,1,0:T(8,128)}, f32[8,16,128]{2,1,0:T(8,128)S(1)}, u32[]{:S(2)}, u32[]{:S(2)}) collective-permute-start(f32[8,16,128]{2,1,0:T(8,128)} %get-tuple-element.76), channel_id=1, source_target_pairs={{0,8},{1,2},{2,1},{3,4},{4,3},{5,6},{6,5},{7,15},{8,0},{9,10},{10,... | collective-permute-start | bytes 196616 | tf_op jit(solution)/shard_map/ppermute | solution.py:390
  29.8 4.3 %collective-permute-start.9 = (f32[8,16,128]{2,1,0:T(8,128)S(1)}, f32[8,16,128]{2,1,0:T(8,128)S(1)}, u32[]{:S(2)}, u32[]{:S(2)}) collective-permute-start(f32[8,16,128]{2,1,0:T(8,128)S(1)} %get-tuple-element.77), channel_id=1, source_target_pairs={{0,8},{1,9},{2,10},{3,11},{4,12},{5,13},{6,14},{7,15},{8,0},{9,1},... | collective-permute-start | bytes 196616 | tf_op jit(solution)/shard_map/ppermute | solution.py:390
  30.0 4.0 %collective-permute-start.10 = (f32[8,16,128]{2,1,0:T(8,128)S(1)}, f32[8,16,128]{2,1,0:T(8,128)S(1)}, u32[]{:S(2)}, u32[]{:S(2)}) collective-permute-start(f32[8,16,128]{2,1,0:T(8,128)S(1)} %get-tuple-element.78), channel_id=1, source_target_pairs={{0,1},{1,0},{2,3},{3,2},{4,5},{5,4},{6,7},{7,6},{8,16},{9,17},{10,... | collective-permute-start | bytes 196616 | tf_op jit(solution)/shard_map/ppermute | solution.py:390
  31.1 3.0 %collective-permute-start.11 = (f32[8,16,128]{2,1,0:T(8,128)S(1)}, f32[8,16,128]{2,1,0:T(8,128)S(1)}, u32[]{:S(2)}, u32[]{:S(2)}) collective-permute-start(f32[8,16,128]{2,1,0:T(8,128)S(1)} %get-tuple-element.79), channel_id=1, source_target_pairs={{0,1},{1,0},{2,3},{3,2},{4,5},{5,4},{6,7},{7,6},{8,9},{9,8},{10,11... | collective-permute-start | bytes 196616 | tf_op jit(solution)/shard_map/ppermute | solution.py:390
  34.0 12.2 %all-to-all-start.1 = ((f32[32,1,256]{2,1,0:T(1,128)}), f32[32,1,256]{2,1,0:T(1,128)S(1)}, u32[]{:S(2)}, u32[]{:S(2)}) async-start(f32[32,1,256]{2,1,0:T(1,128)} %get-tuple-element.90), calls=%async_computation.1 | async-start | bytes 65536 | tf_op jit(solution)/shard_map/all_to_all | solution.py:402
  40.9 26.3 %collective-permute-start.12 = (f32[33,16,128]{2,1,0:T(8,128)S(1)}, f32[33,16,128]{2,1,0:T(8,128)S(1)}, u32[]{:S(2)}, u32[]{:S(2)}) collective-permute-start(f32[33,16,128]{2,1,0:T(8,128)S(1)} %get-tuple-element.92.first.rest_0_), channel_id=1, source_target_pairs={{0,4},{1,5},{2,6},{3,7},{4,0},{5,1},{6,2},{7,3},{8,12},{9,13},{10,... | collective-permute-start | bytes 811016 | tf_op jit(solution)/shard_map/ppermute | solution.py:511
  46.2 21.0 %collective-permute-start.13 = (f32[32,16,128]{2,1,0:T(8,128)S(1)}, f32[32,16,128]{2,1,0:T(8,128)S(1)}, u32[]{:S(2)}, u32[]{:S(2)}) collective-permute-start(f32[32,16,128]{2,1,0:T(8,128)S(1)} %get-tuple-element.93.rest_0_.rest_1_), channel_id=1, source_target_pairs={{0,4},{1,5},{2,6},{3,7},{4,0},{5,1},{6,2},{7,3},{8,12},{9,13},{10,... | collective-permute-start | bytes 786440 | tf_op jit(solution)/shard_map/ppermute | solution.py:521
  46.8 20.4 %collective-permute-start.14 = (f32[32,16,128]{2,1,0:T(8,128)S(1)}, f32[32,16,128]{2,1,0:T(8,128)S(1)}, u32[]{:S(2)}, u32[]{:S(2)}) collective-permute-start(f32[32,16,128]{2,1,0:T(8,128)S(1)} %get-tuple-element.94.rest_1_.rest_2_), channel_id=1, source_target_pairs={{0,4},{1,5},{2,6},{3,7},{4,0},{5,1},{6,2},{7,3},{8,12},{9,13},{10,... | collective-permute-start | bytes 786440 | tf_op jit(solution)/shard_map/ppermute | solution.py:521
  48.3 19.0 %collective-permute-start.15 = (f32[32,16,128]{2,1,0:T(8,128)S(1)}, f32[32,16,128]{2,1,0:T(8,128)S(1)}, u32[]{:S(2)}, u32[]{:S(2)}) collective-permute-start(f32[32,16,128]{2,1,0:T(8,128)S(1)} %get-tuple-element.95.rest_2_.rest_3_), channel_id=1, source_target_pairs={{0,4},{1,5},{2,6},{3,7},{4,0},{5,1},{6,2},{7,3},{8,12},{9,13},{10,... | collective-permute-start | bytes 786440 | tf_op jit(solution)/shard_map/ppermute | solution.py:521

commit v8 on v7

--- a/solution.py
+++ b/solution.py
@@ -12,6 +12,7 @@
 AXES = ("gx", "gy")
 EXCHANGES = (("gy", 1), ("gx", 0), ("gx", 1), ("gy", 0))
 CHUNKS = 4
+PIECES = 4
 VMEM = pl.BlockSpec(memory_space=pltpu.VMEM)
 SMEM = pl.BlockSpec(memory_space=pltpu.SMEM)
 ANY = pl.BlockSpec(memory_space=pl.ANY)
@@ -257,8 +258,9 @@
     chunks, slots = rest[:-4], (rest[-4:-2], rest[-2:])
     _, cols, cells = full.shape
     step = slots[0][0].shape[0] // cols
-    parts = len(chunks)
-    count = (parts + 1) * step
+    count = step + sum(chunk.shape[0] for chunk in chunks)
+    parts = count // step - 1
+    chunks = iter(chunks)
 
     def load(part):
         rows = [order[part * step + r] for r in range(step)]
@@ -268,8 +270,12 @@
     for part in range(1, parts + 1):
         if part < parts:
             load(part + 1)
-        value = multiply(*slots[part % 2], tiles)
-        chunks[part - 1][...] = value.reshape(step, cols, cells)
+        value = multiply(*slots[part % 2], tiles).reshape(step, cols, cells)
+        done = 0
+        while done < step:
+            chunk = next(chunks)
+            chunk[...] = value[done : done + chunk.shape[0]]
+            done += chunk.shape[0]
 
 
 def row_sum(sums):
@@ -316,7 +322,7 @@
     inv = eliminate(unpack(row_sum(sums), cols), identity(cols))
     inverse[...] = inv
     left = scaler(inv)
-    count = (first.shape[0] - 1) * (len(later) + 1)
+    count = first.shape[0] - 1 + sum(chunk.shape[0] for chunk in later)
     own = groups_of(first.at[: first.shape[0] - 1])
     for chunk in later:
         own = own + groups_of(chunk)
@@ -331,18 +337,31 @@
     put_rows(packed, jnp.concatenate([gram, cross], 1))
 
 
-def final_kernel(order, sums, inverse, *rest):
-    chunks, (out, rayleigh, weights, columns, rows, ready, sems) = rest[:-7], rest[-7:]
+def factor_kernel(order, sums, inverse, mine, theirs, total_inverse, rayleigh, weights, columns):
+    cols = inverse.shape[0]
+    slots, count = weights.shape
+    wide = cols * cols
+    total = row_sum(sums)
+    total_inverse[...] = eliminate(unpack(total[:, :wide], cols), inverse[...])
+    rayleigh[...] = unpack(total[:, wide:], cols)[:, :cols]
+    last = mine.shape[0] - 1
+    both = jnp.concatenate([mine[last], theirs[last]], 1)
+    moved = pltpu.roll(both, 2 * count - order[count], 1)[:, :count]
+    weights[...] = moved[:slots]
+    columns[...] = moved[slots:].astype(jnp.int32)
+
+
+def final_kernel(order, inverse, *rest):
+    chunks, (out, rows, ready, sems) = rest[:-4], rest[-4:]
     mine, theirs = chunks[: len(chunks) // 2], chunks[len(chunks) // 2 :]
-    slots, count = weights.shape
-    cols, cells = out.shape[1:]
-    size, per = count // len(mine), 128 // cols
-    wide = cols * cols
-    for i in range(len(mine)):
-        rows[i * size : (i + 1) * size] = mine[i][:size]
-        rows[count + i * size : count + (i + 1) * size] = theirs[i][:size]
-    total = row_sum(sums)
-    left = scaler(eliminate(unpack(total[:, :wide], cols), inverse[...]))
+    count, cols, cells = out.shape
+    size, per = mine[0].shape[0] - 1, 128 // cols
+    for start, chunks in ((0, mine), (count, theirs)):
+        for i, chunk in enumerate(chunks):
+            stop = start + (chunk.shape[0] if i else size)
+            rows[start:stop] = chunk[: stop - start]
+            start = stop
+    left = scaler(inverse[...])
     copies = []
     part_size = count // sems.shape[0]
     for i in range(sems.shape[0]):
@@ -352,11 +371,6 @@
         part = pl.ds(i * part_size, part_size)
         copies.append(pltpu.make_async_copy(ready.at[part], out.at[part], sems.at[i]))
         copies[i].start()
-    rayleigh[...] = unpack(total[:, wide:], cols)[:, :cols]
-    both = jnp.concatenate([mine[0][size], theirs[0][size]], 1)
-    moved = pltpu.roll(both, 2 * count - order[count], 1)[:, :count]
-    weights[...] = moved[:slots]
-    columns[...] = moved[slots:].astype(jnp.int32)
     for copy in copies:
         copy.wait()
 
@@ -440,7 +454,7 @@
         [
             pltpu.SMEM(sends.shape, jnp.int32),
             pltpu.SemaphoreType.DMA,
-            pltpu.SemaphoreType.DMA((8,)),
+            pltpu.SemaphoreType.DMA((1,)),
             pltpu.SemaphoreType.DMA,
         ],
     )(plan, in_hbm(sends), in_hbm(block), in_hbm(slot_tiles))
@@ -509,40 +523,50 @@
     )(plan, flat_columns, flat_weights, order, full, *near, tiles, inverse, meta)
     swap = [(j, j ^ (size_y // 2)) for j in range(size_y)]
     their_first = lax.ppermute(first, "gy", swap)
+    later_sizes = [size] + [size // PIECES] * (PIECES * (CHUNKS - 2))
     later = call(
         last_rest_kernel,
-        [shape(size, cols, cells)] * (CHUNKS - 1),
+        [shape(n, cols, cells) for n in later_sizes],
         [SMEM] * 3 + [VMEM] * 2,
-        [VMEM] * (CHUNKS - 1),
+        [VMEM] * len(later_sizes),
         [half] * 4,
         cost=(work[0] // CHUNKS * (CHUNKS - 1), 0),
     )(flat_columns, flat_weights, order, full, tiles)
-    later, sums = lax.optimization_barrier((later, sums))
-    their_later = [lax.ppermute(x, "gy", swap) for x in later]
+    second, sums = lax.optimization_barrier((later[0], sums))
+    their_second = lax.ppermute(second, "gy", swap)
 
     packed, inverse = call(
         sums_kernel,
         [shape(devices, 1, 2 * cols * cols), square],
-        [SMEM] + [VMEM] * (2 + CHUNKS),
+        [SMEM] + [VMEM] * (3 + len(later)),
         [VMEM] * 2,
     )(order, sums, full, first, *later)
+    packed, *last = lax.optimization_barrier((packed, *later[1:]))
     sums = everywhere(packed)
-    moved_basis, rayleigh, moved_weights, moved_columns = call(
-        final_kernel,
+    their_later = [their_second] + [lax.ppermute(x, "gy", swap) for x in last]
+    inverse, rayleigh, moved_weights, moved_columns = call(
+        factor_kernel,
         [
-            whole,
+            square,
             shape(cols, cols),
             shape(slots, count),
             shape(slots, count, dtype=jnp.int32),
         ],
-        [SMEM] + [VMEM] * (2 + 2 * CHUNKS),
-        [ANY] + [VMEM] * 3,
+        [SMEM] + [VMEM] * 4,
+        [VMEM] * 4,
+        cost=small,
+    )(order, sums, inverse, first, their_first)
+    moved_basis = call(
+        final_kernel,
+        whole,
+        [SMEM] + [VMEM] * (3 + 2 * len(later)),
+        ANY,
         [
             pltpu.VMEM((2 * count, cols, cells), F32),
             pltpu.VMEM((count, cols, cells), F32),
             pltpu.SemaphoreType.DMA((8,)),
         ],
-    )(order, sums, inverse, first, *later, their_first, *their_later)
+    )(order, inverse, first, *later, their_first, *their_later)
     return (
         moved_basis[None, None],
         moved_weights.T[None, None],

time: 70.9 us -> 73.1 us (1.031)
  blocking collectives: 15.2 us -> 0 us
  starting transfers between devices: 24.8 us -> 38.2 us
  waiting for transfers between devices: 3.26 us -> 5.97 us
  Pallas kernels: 26.3 us -> 27.5 us
    all_to_all x1 -> x0, blocking collectives: 15.2 us -> none  [everywhere(): return lax.all_to_all(rows, AXES, 0, 0, tiled=True)]
    ppermute x3 -> x9, starting transfers between devices: 2.59 us -> 11.7 us  [the longest x8 11.1 us: per_device(): their_later = [their_second] + [lax.ppermute(x, 'gy', swap) for x in last]]
    all_to_all x2 -> x3, starting transfers between devices: 9.88 us -> 14.2 us  [everywhere(): return lax.all_to_all(rows, AXES, 0, 0, tiled=True)]
    ppermute x3 -> x9, waiting for transfers between devices: 0.01 us -> 2.74 us  [the longest x8 2.73 us: per_device(): their_later = [their_second] + [lax.ppermute(x, 'gy', swap) for x in last]]
    pallas_call x2 -> x3, Pallas kernels: 6.52 us -> 7.26 us  [the longest x1 3.26 us: per_device(): call(last_rest_kernel, [shape(n, cols, cells) for n in later_sizes], [SME...]
  transfers between devices with their start and end apart: 18 -> 25, of which waited for: 4 -> 7; matrix products, arithmetic and copies ran while one was open for 0% -> 0% of each run, Pallas kernels for 24% -> 27%
where the time goes in v8:
time: 73.1 us; the launch traced here: 72.8 us
  starting transfers between devices  38.2 us (52%)
  Pallas kernels  27.5 us (38%)
  waiting for transfers between devices  5.97 us (8%)
  between operations  1 us (1%)
    all_to_all x3, starting transfers between devices, everywhere(): return lax.all_to_all(rows, AXES, 0, 0, tiled=True)  14.2 us
    ppermute x8, starting transfers between devices, per_device(): their_later = [their_second] + [lax.ppermute(x, 'gy', swap) for x in last]  11.1 us
    ppermute x12, starting transfers between devices, pairs(): return lax.ppermute(x, AXES, swap)  10.7 us
    pallas_call x2, Pallas kernels, operator(): call(operator_kernel, [whole] + [piece] * 4, [SMEM] * 3 + [HBM] + [VMEM]...  8.42 us
    pallas_call x1, Pallas kernels, per_device(): call(sums_kernel, [shape(devices, 1, 2 * cols * cols), square], [SMEM] +...  3.8 us
    pallas_call x1, Pallas kernels, per_device(): call(last_rest_kernel, [shape(n, cols, cells) for n in later_sizes], [SME...  3.26 us
    ppermute x12, waiting for transfers between devices, pairs(): return lax.ppermute(x, AXES, swap)  2.87 us
    ppermute x8, waiting for transfers between devices, per_device(): their_later = [their_second] + [lax.ppermute(x, 'gy', swap) for x in last]  2.73 us
  transfers between devices with their start and end apart: 25, of which 7 were waited for; matrix products, arithmetic and copies ran while one was open for 0% of the time, Pallas kernels for 27%

profile of v8, /device:TPU:0, one launch (start us, length us, event | category | flops | bytes accessed | tf_op | source)
XLA Modules:
  0.0 72.8 jit_solution(12644384231649762635)
XLA Ops:
  0.8 1.9 %shard_map.93 = (f32[128,16,128]{2,1,0:T(8,128)S(1)}, f32[8,128,128]{2,1,0:T(8,128)S(1)}, f32[8,16,128]{2,1,0:T(8,128)S(1)}, f32[8,16,128]{2,1,0:T(8,128)S(1)}, ...) custom-call(s32[8]{0:T(128)S(1)} %stack.51.plan, s32[4,8]{1,0:T(4,128)} %bitcast.48, f32[128,16,128]{2,1,0:T(8,128)} %bitcast.46, ...), custom_call_target="tpu_custom_call" | custom-call | tf_op jit(solution)/shard_map/pallas_call | solution.py:449
  2.7 3.1 %collective-permute-start = (f32[8,16,128]{2,1,0:T(8,128)S(1)}, f32[8,16,128]{2,1,0:T(8,128)S(1)}, u32[]{:S(2)}, u32[]{:S(2)}) collective-permute-start(f32[8,16,128]{2,1,0:T(8,128)S(1)} %get-tuple-element.66), channel_id=1, source_target_pairs={{0,8},{1,2},{2,1},{3,4},{4,3},{5,6},{6,5},{7,15},{8,0},{9,10},{10,... | collective-permute-start | bytes 196616 | tf_op jit(solution)/shard_map/ppermute | solution.py:404
  8.1 2.0 %collective-permute-done.1.h1 = f32[8,16,128]{2,1,0:T(8,128)S(1)} collective-permute-done((f32[8,16,128]{2,1,0:T(8,128)S(1)}, f32[8,16,128]{2,1,0:T(8,128)S(1)}, u32[]{:S(2)}, u32[]{:S(2)}) %collective-permute-start.1) | collective-permute-done | bytes 65568 | tf_op jit(solution)/shard_map/ppermute | solution.py:404
  10.1 3.9 %shard_map.96 = (f32[128,16,128]{2,1,0:T(8,128)S(1)}, f32[8,16,128]{2,1,0:T(8,128)S(1)}, f32[8,16,128]{2,1,0:T(8,128)S(1)}, f32[8,16,128]{2,1,0:T(8,128)S(1)}, f32[8,16,128]{2,1,0:T(8,128)S(1)}) custom-call(s32[8]{0:T(128)S(1)} %stack.51.plan, s32[1024]{0:T(1024)S(1)} %bitcast.41, f32[1024]{0:T(1024)S(1)} %bitcast.36, ...), custom_call_target="tpu_custom_call", output_to_operand_aliasing={{0}: (4, {})} | custom-call | flops 1610612736 | tf_op jit(solution)/shard_map/pallas_call | solution.py:482
  14.0 2.5 %collective-permute-start.4 = (f32[8,16,128]{2,1,0:T(8,128)S(1)}, f32[8,16,128]{2,1,0:T(8,128)S(1)}, u32[]{:S(2)}, u32[]{:S(2)}) collective-permute-start(f32[8,16,128]{2,1,0:T(8,128)S(1)} %get-tuple-element.82), channel_id=1, source_target_pairs={{0,8},{1,2},{2,1},{3,4},{4,3},{5,6},{6,5},{7,15},{8,0},{9,10},{10,... | collective-permute-start | bytes 196616 | tf_op jit(solution)/shard_map/ppermute | solution.py:404
  18.4 4.8 %all-to-all-start = ((f32[32,1,256]{2,1,0:T(1,128)}), f32[32,1,256]{2,1,0:T(1,128)S(1)}, u32[]{:S(2)}, u32[]{:S(2)}) async-start(f32[32,1,256]{2,1,0:T(1,128)} %shard_map.97), calls=%async_computation | async-start | bytes 65536 | tf_op jit(solution)/shard_map/all_to_all | solution.py:416
  23.2 4.5 %shard_map.98 = (f32[128,16,128]{2,1,0:T(8,128)S(1)}, f32[8,16,128]{2,1,0:T(8,128)}, f32[8,16,128]{2,1,0:T(8,128)S(1)}, f32[8,16,128]{2,1,0:T(8,128)S(1)}, f32[8,16,128]{2,1,0:T(8,128)S(1)}) custom-call(s32[8]{0:T(128)S(1)} %stack.51.plan, s32[1024]{0:T(1024)S(1)} %bitcast.42, f32[1024]{0:T(1024)S(1)} %bitcast.37, ...), custom_call_target="tpu_custom_call", output_to_operand_aliasing={{0}: (4, {})} | custom-call | flops 1610612736 | tf_op jit(solution)/shard_map/pallas_call | solution.py:482
  27.8 1.8 %collective-permute-start.8 = (f32[8,16,128]{2,1,0:T(8,128)}, f32[8,16,128]{2,1,0:T(8,128)S(1)}, u32[]{:S(2)}, u32[]{:S(2)}) collective-permute-start(f32[8,16,128]{2,1,0:T(8,128)} %get-tuple-element.89), channel_id=1, source_target_pairs={{0,8},{1,2},{2,1},{3,4},{4,3},{5,6},{6,5},{7,15},{8,0},{9,10},{10,... | collective-permute-start | bytes 196616 | tf_op jit(solution)/shard_map/ppermute | solution.py:404
  30.9 2.6 %shard_map.99 = (f32[160,16,128]{2,1,0:T(8,128)S(1)}, f32[16,128]{1,0:T(8,128)S(1)}, f32[32,1,256]{2,1,0:T(1,128)}) custom-call(f32[32,1,256]{2,1,0:T(1,128)S(1)} %all-to-all-done.sums, f32[128,16,128]{2,1,0:T(8,128)S(1)} %get-tuple-element.86.image), custom_call_target="tpu_custom_call" | custom-call | flops 268435456 | tf_op jit(solution)/shard_map/pallas_call | solution.py:509
  33.9 5.1 %all-to-all-start.1 = ((f32[32,1,256]{2,1,0:T(1,128)}), f32[32,1,256]{2,1,0:T(1,128)S(1)}, u32[]{:S(2)}, u32[]{:S(2)}) async-start(f32[32,1,256]{2,1,0:T(1,128)} %get-tuple-element.101), calls=%async_computation.1 | async-start | bytes 65536 | tf_op jit(solution)/shard_map/all_to_all | solution.py:416
  39.0 1.8 %shard_map.100 = (f32[33,16,128]{2,1,0:T(8,128)S(1)}, f32[160,16,128]{2,1,0:T(8,128)S(1)}) custom-call(s32[8]{0:T(128)S(1)} %stack.51.plan, s32[1024]{0:T(1024)S(1)} %bitcast.43, f32[1024]{0:T(1024)S(1)} %bitcast.38, s32[1024]{0:T(1024)S(1)} %bitcast.30, f32[160,16,128]{2,1,0:T(8,128)S(1)} %get-tuple-element.87.own, ...), custom_call_target="tpu_custom_call", output_to_operand_aliasing={{1}: (4, {})} | custom-call | flops 402653184 | tf_op jit(solution)/shard_map/pallas_call | solution.py:515
  40.8 1.7 %collective-permute-start.12 = (f32[33,16,128]{2,1,0:T(8,128)S(1)}, f32[33,16,128]{2,1,0:T(8,128)S(1)}, u32[]{:S(2)}, u32[]{:S(2)}) collective-permute-start(f32[33,16,128]{2,1,0:T(8,128)S(1)} %get-tuple-element.103.first.mine.rest_0_), channel_id=1, source_target_pairs={{0,4},{1,5},{2,6},{3,7},{4,0},{5,1},{6,2},{7,3},{8,12},{9,13},{10,... | collective-permute-start | bytes 811016 | tf_op jit(solution)/shard_map/ppermute | solution.py:525
  42.4 3.3 %shard_map.101 = (f32[32,16,128]{2,1,0:T(8,128)S(1)}, f32[8,16,128]{2,1,0:T(8,128)S(1)}, f32[8,16,128]{2,1,0:T(8,128)S(1)}, f32[8,16,128]{2,1,0:T(8,128)S(1)}, f...) custom-call(s32[1024]{0:T(1024)S(1)} %bitcast.44, ...), custom_call_target="tpu_custom_call" | custom-call | flops 1207959552 | tf_op jit(solution)/shard_map/pallas_call | solution.py:527
  46.6 3.8 %shard_map.102 = (f32[32,1,512]{2,1,0:T(1,128)}, f32[16,128]{1,0:T(8,128)S(1)}) custom-call(s32[1024]{0:T(1024)S(1)} %bitcast.32, f32[32,1,256]{2,1,0:T(1,128)S(1)} %all-to-all-done.1.sums, f32[160,16,128]{2,1,0:T(8,128)S(1)} %get-tuple-element.99.full, f32[33,16,128]{2,1,0:T(8,128)S(1)} %get-tuple-element.103.first.mine.rest_0_, ...), custom_call_target="tpu_custom_call" | custom-call | tf_op jit(solution)/shard_map/pallas_call | solution.py:538
  50.4 1.5 %collective-permute-start.14 = (f32[8,16,128]{2,1,0:T(8,128)S(1)}, f32[8,16,128]{2,1,0:T(8,128)S(1)}, u32[]{:S(2)}, u32[]{:S(2)}) collective-permute-start(f32[8,16,128]{2,1,0:T(8,128)S(1)} %get-tuple-element.117.rest_1_.rest_2_), channel_id=1, source_target_pairs={{0,4},{1,5},{2,6},{3,7},{4,0},{5,1},{6,2},{7,3},{8,12},{9,13},{10,... | collective-permute-start | bytes 196616 | tf_op jit(solution)/shard_map/ppermute | solution.py:546
  51.9 4.4 %all-to-all-start.2 = ((f32[32,1,512]{2,1,0:T(1,128)}), f32[32,1,512]{2,1,0:T(1,128)S(1)}, u32[]{:S(2)}, u32[]{:S(2)}) async-start(f32[32,1,512]{2,1,0:T(1,128)} %get-tuple-element.113), calls=%async_computation.2 | async-start | bytes 131072 | tf_op jit(solution)/shard_map/all_to_all | solution.py:416
  56.2 1.8 %collective-permute-start.15 = (f32[8,16,128]{2,1,0:T(8,128)S(1)}, f32[8,16,128]{2,1,0:T(8,128)S(1)}, u32[]{:S(2)}, u32[]{:S(2)}) collective-permute-start(f32[8,16,128]{2,1,0:T(8,128)S(1)} %get-tuple-element.118.rest_2_.rest_3_), channel_id=1, source_target_pairs={{0,4},{1,5},{2,6},{3,7},{4,0},{5,1},{6,2},{7,3},{8,12},{9,13},{10,... | collective-permute-start | bytes 196616 | tf_op jit(solution)/shard_map/ppermute | solution.py:546
  58.3 1.8 %collective-permute-start.17 = (f32[8,16,128]{2,1,0:T(8,128)S(1)}, f32[8,16,128]{2,1,0:T(8,128)S(1)}, u32[]{:S(2)}, u32[]{:S(2)}) collective-permute-start(f32[8,16,128]{2,1,0:T(8,128)S(1)} %get-tuple-element.120.rest_4_.rest_5_), channel_id=1, source_target_pairs={{0,4},{1,5},{2,6},{3,7},{4,0},{5,1},{6,2},{7,3},{8,12},{9,13},{10,... | collective-permute-start | bytes 196616 | tf_op jit(solution)/shard_map/ppermute | solution.py:546
  61.0 2.3 %collective-permute-start.18 = (f32[8,16,128]{2,1,0:T(8,128)S(1)}, f32[8,16,128]{2,1,0:T(8,128)S(1)}, u32[]{:S(2)}, u32[]{:S(2)}) collective-permute-start(f32[8,16,128]{2,1,0:T(8,128)S(1)} %get-tuple-element.121.rest_5_.rest_6_), channel_id=1, source_target_pairs={{0,4},{1,5},{2,6},{3,7},{4,0},{5,1},{6,2},{7,3},{8,12},{9,13},{10,... | collective-permute-start | bytes 196616 | tf_op jit(solution)/shard_map/ppermute | solution.py:546
  63.3 1.5 %collective-permute-start.19 = (f32[8,16,128]{2,1,0:T(8,128)S(1)}, f32[8,16,128]{2,1,0:T(8,128)S(1)}, u32[]{:S(2)}, u32[]{:S(2)}) collective-permute-start(f32[8,16,128]{2,1,0:T(8,128)S(1)} %get-tuple-element.122.rest_6_.rest_7_), channel_id=1, source_target_pairs={{0,4},{1,5},{2,6},{3,7},{4,0},{5,1},{6,2},{7,3},{8,12},{9,13},{10,... | collective-permute-start | bytes 196616 | tf_op jit(solution)/shard_map/ppermute | solution.py:546
  64.8 1.4 %collective-permute-start.20 = (f32[8,16,128]{2,1,0:T(8,128)S(1)}, f32[8,16,128]{2,1,0:T(8,128)S(1)}, u32[]{:S(2)}, u32[]{:S(2)}) collective-permute-start(f32[8,16,128]{2,1,0:T(8,128)S(1)} %get-tuple-element.123.rest_7_.rest_8_), channel_id=1, source_target_pairs={{0,4},{1,5},{2,6},{3,7},{4,0},{5,1},{6,2},{7,3},{8,12},{9,13},{10,... | collective-permute-start | bytes 196616 | tf_op jit(solution)/shard_map/ppermute | solution.py:546
  66.8 1.8 %shard_map.103 = (f32[16,128]{1,0:T(8,128)S(1)}, f32[16,16]{1,0:T(8,128)}, f32[8,128]{1,0:T(8,128)}, s32[8,128]{1,0:T(8,128)}) custom-call(s32[1024]{0:T(1024)S(1)} %bitcast.33, f32[32,1,512]{2,1,0:T(1,128)S(1)} %all-to-all-done.2.sums, f32[16,128]{1,0:T(8,128)S(1)} %get-tuple-element.114.inverse, f32[33,16,128]{2,1,0:T(8,128)S(1)} %get-tuple-element.103.first.mine.rest_0_, ...), custom_call_target="tpu_custom_call" | custom-call | flops 268435456 | tf_op jit(solution)/shard_map/pallas_call | solution.py:547
  69.1 1.4 %collective-permute-done.21.rest_19_ = f32[8,16,128]{2,1,0:T(8,128)S(1)} collective-permute-done((f32[8,16,128]{2,1,0:T(8,128)S(1)}, f32[8,16,128]{2,1,0:T(8,128)S(1)}, u32[]{:S(2)}, u32[]{:S(2)}) %collective-permute-start.21) | collective-permute-done | bytes 65568 | tf_op jit(solution)/shard_map/ppermute | solution.py:546
  70.5 2.2 %shard_map.104 = f32[128,16,128]{2,1,0:T(8,128)} custom-call(s32[1024]{0:T(1024)S(1)} %bitcast.34, f32[16,128]{1,0:T(8,128)S(1)} %get-tuple-element.115.inverse, f32[33,16,128]{2,1,0:T(8,128)S(1)} %get-tuple-element.103.first.mine.rest_0_, f32[32,16,128]{2,1,0:T(8,128)S(1)} %get-tuple-element.116.rest_0_.rest_1_, ...), custom_call_target="tpu_custom_call" | custom-call | tf_op jit(solution)/shard_map/pallas_call | solution.py:559
  (45 shorter events, 9.1 us)
Async XLA Ops:
  2.7 5.3 %collective-permute-start = (f32[8,16,128]{2,1,0:T(8,128)S(1)}, f32[8,16,128]{2,1,0:T(8,128)S(1)}, u32[]{:S(2)}, u32[]{:S(2)}) collective-permute-start(f32[8,16,128]{2,1,0:T(8,128)S(1)} %get-tuple-element.66), channel_id=1, source_target_pairs={{0,8},{1,2},{2,1},{3,4},{4,3},{5,6},{6,5},{7,15},{8,0},{9,10},{10,... | collective-permute-start | bytes 196616 | tf_op jit(solution)/shard_map/ppermute | solution.py:404
  5.8 4.3 %collective-permute-start.1 = (f32[8,16,128]{2,1,0:T(8,128)S(1)}, f32[8,16,128]{2,1,0:T(8,128)S(1)}, u32[]{:S(2)}, u32[]{:S(2)}) collective-permute-start(f32[8,16,128]{2,1,0:T(8,128)S(1)} %get-tuple-element.67), channel_id=1, source_target_pairs={{0,8},{1,9},{2,10},{3,11},{4,12},{5,13},{6,14},{7,15},{8,0},{9,1},... | collective-permute-start | bytes 196616 | tf_op jit(solution)/shard_map/ppermute | solution.py:404
  5.9 4.2 %collective-permute-start.2 = (f32[8,16,128]{2,1,0:T(8,128)S(1)}, f32[8,16,128]{2,1,0:T(8,128)S(1)}, u32[]{:S(2)}, u32[]{:S(2)}) collective-permute-start(f32[8,16,128]{2,1,0:T(8,128)S(1)} %get-tuple-element.68), channel_id=1, source_target_pairs={{0,1},{1,0},{2,3},{3,2},{4,5},{5,4},{6,7},{7,6},{8,16},{9,17},{10,... | collective-permute-start | bytes 196616 | tf_op jit(solution)/shard_map/ppermute | solution.py:404
  14.0 9.2 %collective-permute-start.4 = (f32[8,16,128]{2,1,0:T(8,128)S(1)}, f32[8,16,128]{2,1,0:T(8,128)S(1)}, u32[]{:S(2)}, u32[]{:S(2)}) collective-permute-start(f32[8,16,128]{2,1,0:T(8,128)S(1)} %get-tuple-element.82), channel_id=1, source_target_pairs={{0,8},{1,2},{2,1},{3,4},{4,3},{5,6},{6,5},{7,15},{8,0},{9,10},{10,... | collective-permute-start | bytes 196616 | tf_op jit(solution)/shard_map/ppermute | solution.py:404
  16.5 6.7 %collective-permute-start.5 = (f32[8,16,128]{2,1,0:T(8,128)S(1)}, f32[8,16,128]{2,1,0:T(8,128)S(1)}, u32[]{:S(2)}, u32[]{:S(2)}) collective-permute-start(f32[8,16,128]{2,1,0:T(8,128)S(1)} %get-tuple-element.83), channel_id=1, source_target_pairs={{0,8},{1,9},{2,10},{3,11},{4,12},{5,13},{6,14},{7,15},{8,0},{9,1},... | collective-permute-start | bytes 196616 | tf_op jit(solution)/shard_map/ppermute | solution.py:404
  16.6 6.6 %collective-permute-start.6 = (f32[8,16,128]{2,1,0:T(8,128)S(1)}, f32[8,16,128]{2,1,0:T(8,128)S(1)}, u32[]{:S(2)}, u32[]{:S(2)}) collective-permute-start(f32[8,16,128]{2,1,0:T(8,128)S(1)} %get-tuple-element.84), channel_id=1, source_target_pairs={{0,1},{1,0},{2,3},{3,2},{4,5},{5,4},{6,7},{7,6},{8,16},{9,17},{10,... | collective-permute-start | bytes 196616 | tf_op jit(solution)/shard_map/ppermute | solution.py:404
  16.8 6.4 %collective-permute-start.7 = (f32[8,16,128]{2,1,0:T(8,128)S(1)}, f32[8,16,128]{2,1,0:T(8,128)S(1)}, u32[]{:S(2)}, u32[]{:S(2)}) collective-permute-start(f32[8,16,128]{2,1,0:T(8,128)S(1)} %get-tuple-element.85), channel_id=1, source_target_pairs={{0,1},{1,0},{2,3},{3,2},{4,5},{5,4},{6,7},{7,6},{8,9},{9,8},{10,11... | collective-permute-start | bytes 196616 | tf_op jit(solution)/shard_map/ppermute | solution.py:404
  18.4 12.5 %all-to-all-start = ((f32[32,1,256]{2,1,0:T(1,128)}), f32[32,1,256]{2,1,0:T(1,128)S(1)}, u32[]{:S(2)}, u32[]{:S(2)}) async-start(f32[32,1,256]{2,1,0:T(1,128)} %shard_map.97), calls=%async_computation | async-start | bytes 65536 | tf_op jit(solution)/shard_map/all_to_all | solution.py:416
  27.8 5.7 %collective-permute-start.8 = (f32[8,16,128]{2,1,0:T(8,128)}, f32[8,16,128]{2,1,0:T(8,128)S(1)}, u32[]{:S(2)}, u32[]{:S(2)}) collective-permute-start(f32[8,16,128]{2,1,0:T(8,128)} %get-tuple-element.89), channel_id=1, source_target_pairs={{0,8},{1,2},{2,1},{3,4},{4,3},{5,6},{6,5},{7,15},{8,0},{9,10},{10,... | collective-permute-start | bytes 196616 | tf_op jit(solution)/shard_map/ppermute | solution.py:404
  29.6 4.3 %collective-permute-start.9 = (f32[8,16,128]{2,1,0:T(8,128)S(1)}, f32[8,16,128]{2,1,0:T(8,128)S(1)}, u32[]{:S(2)}, u32[]{:S(2)}) collective-permute-start(f32[8,16,128]{2,1,0:T(8,128)S(1)} %get-tuple-element.90), channel_id=1, source_target_pairs={{0,8},{1,9},{2,10},{3,11},{4,12},{5,13},{6,14},{7,15},{8,0},{9,1},... | collective-permute-start | bytes 196616 | tf_op jit(solution)/shard_map/ppermute | solution.py:404
  29.8 4.0 %collective-permute-start.10 = (f32[8,16,128]{2,1,0:T(8,128)S(1)}, f32[8,16,128]{2,1,0:T(8,128)S(1)}, u32[]{:S(2)}, u32[]{:S(2)}) collective-permute-start(f32[8,16,128]{2,1,0:T(8,128)S(1)} %get-tuple-element.91), channel_id=1, source_target_pairs={{0,1},{1,0},{2,3},{3,2},{4,5},{5,4},{6,7},{7,6},{8,16},{9,17},{10,... | collective-permute-start | bytes 196616 | tf_op jit(solution)/shard_map/ppermute | solution.py:404
  30.9 3.0 %collective-permute-start.11 = (f32[8,16,128]{2,1,0:T(8,128)S(1)}, f32[8,16,128]{2,1,0:T(8,128)S(1)}, u32[]{:S(2)}, u32[]{:S(2)}) collective-permute-start(f32[8,16,128]{2,1,0:T(8,128)S(1)} %get-tuple-element.92), channel_id=1, source_target_pairs={{0,1},{1,0},{2,3},{3,2},{4,5},{5,4},{6,7},{7,6},{8,9},{9,8},{10,11... | collective-permute-start | bytes 196616 | tf_op jit(solution)/shard_map/ppermute | solution.py:404
  33.9 12.2 %all-to-all-start.1 = ((f32[32,1,256]{2,1,0:T(1,128)}), f32[32,1,256]{2,1,0:T(1,128)S(1)}, u32[]{:S(2)}, u32[]{:S(2)}) async-start(f32[32,1,256]{2,1,0:T(1,128)} %get-tuple-element.101), calls=%async_computation.1 | async-start | bytes 65536 | tf_op jit(solution)/shard_map/all_to_all | solution.py:416
  40.8 25.4 %collective-permute-start.12 = (f32[33,16,128]{2,1,0:T(8,128)S(1)}, f32[33,16,128]{2,1,0:T(8,128)S(1)}, u32[]{:S(2)}, u32[]{:S(2)}) collective-permute-start(f32[33,16,128]{2,1,0:T(8,128)S(1)} %get-tuple-element.103.first.mine.rest_0_), channel_id=1, source_target_pairs={{0,4},{1,5},{2,6},{3,7},{4,0},{5,1},{6,2},{7,3},{8,12},{9,13},{10,... | collective-permute-start | bytes 811016 | tf_op jit(solution)/shard_map/ppermute | solution.py:525
  46.0 24.4 %collective-permute-start.13 = (f32[32,16,128]{2,1,0:T(8,128)S(1)}, f32[32,16,128]{2,1,0:T(8,128)S(1)}, u32[]{:S(2)}, u32[]{:S(2)}) collective-permute-start(f32[32,16,128]{2,1,0:T(8,128)S(1)} %get-tuple-element.116.rest_0_.rest_1_), channel_id=1, source_target_pairs={{0,4},{1,5},{2,6},{3,7},{4,0},{5,1},{6,2},{7,3},{8,12},{9,13},{10,... | collective-permute-start | bytes 786440 | tf_op jit(solution)/shard_map/ppermute | solution.py:536
  50.4 7.9 %collective-permute-start.14 = (f32[8,16,128]{2,1,0:T(8,128)S(1)}, f32[8,16,128]{2,1,0:T(8,128)S(1)}, u32[]{:S(2)}, u32[]{:S(2)}) collective-permute-start(f32[8,16,128]{2,1,0:T(8,128)S(1)} %get-tuple-element.117.rest_1_.rest_2_), channel_id=1, source_target_pairs={{0,4},{1,5},{2,6},{3,7},{4,0},{5,1},{6,2},{7,3},{8,12},{9,13},{10,... | collective-permute-start | bytes 196616 | tf_op jit(solution)/shard_map/ppermute | solution.py:546
  51.9 14.9 %all-to-all-start.2 = ((f32[32,1,512]{2,1,0:T(1,128)}), f32[32,1,512]{2,1,0:T(1,128)S(1)}, u32[]{:S(2)}, u32[]{:S(2)}) async-start(f32[32,1,512]{2,1,0:T(1,128)} %get-tuple-element.113), calls=%async_computation.2 | async-start | bytes 131072 | tf_op jit(solution)/shard_map/all_to_all | solution.py:416
  56.2 4.8 %collective-permute-start.15 = (f32[8,16,128]{2,1,0:T(8,128)S(1)}, f32[8,16,128]{2,1,0:T(8,128)S(1)}, u32[]{:S(2)}, u32[]{:S(2)}) collective-permute-start(f32[8,16,128]{2,1,0:T(8,128)S(1)} %get-tuple-element.118.rest_2_.rest_3_), channel_id=1, source_target_pairs={{0,4},{1,5},{2,6},{3,7},{4,0},{5,1},{6,2},{7,3},{8,12},{9,13},{10,... | collective-permute-start | bytes 196616 | tf_op jit(solution)/shard_map/ppermute | solution.py:546
  58.1 5.2 %collective-permute-start.16 = (f32[8,16,128]{2,1,0:T(8,128)S(1)}, f32[8,16,128]{2,1,0:T(8,128)S(1)}, u32[]{:S(2)}, u32[]{:S(2)}) collective-permute-start(f32[8,16,128]{2,1,0:T(8,128)S(1)} %get-tuple-element.119.rest_3_.rest_4_), channel_id=1, source_target_pairs={{0,4},{1,5},{2,6},{3,7},{4,0},{5,1},{6,2},{7,3},{8,12},{9,13},{10,... | collective-permute-start | bytes 196616 | tf_op jit(solution)/shard_map/ppermute | solution.py:546
  58.3 6.5 %collective-permute-start.17 = (f32[8,16,128]{2,1,0:T(8,128)S(1)}, f32[8,16,128]{2,1,0:T(8,128)S(1)}, u32[]{:S(2)}, u32[]{:S(2)}) collective-permute-start(f32[8,16,128]{2,1,0:T(8,128)S(1)} %get-tuple-element.120.rest_4_.rest_5_), channel_id=1, source_target_pairs={{0,4},{1,5},{2,6},{3,7},{4,0},{5,1},{6,2},{7,3},{8,12},{9,13},{10,... | collective-permute-start | bytes 196616 | tf_op jit(solution)/shard_map/ppermute | solution.py:546
  61.0 7.6 %collective-permute-start.18 = (f32[8,16,128]{2,1,0:T(8,128)S(1)}, f32[8,16,128]{2,1,0:T(8,128)S(1)}, u32[]{:S(2)}, u32[]{:S(2)}) collective-permute-start(f32[8,16,128]{2,1,0:T(8,128)S(1)} %get-tuple-element.121.rest_5_.rest_6_), channel_id=1, source_target_pairs={{0,4},{1,5},{2,6},{3,7},{4,0},{5,1},{6,2},{7,3},{8,12},{9,13},{10,... | collective-permute-start | bytes 196616 | tf_op jit(solution)/shard_map/ppermute | solution.py:546
  63.3 5.4 %collective-permute-start.19 = (f32[8,16,128]{2,1,0:T(8,128)S(1)}, f32[8,16,128]{2,1,0:T(8,128)S(1)}, u32[]{:S(2)}, u32[]{:S(2)}) collective-permute-start(f32[8,16,128]{2,1,0:T(8,128)S(1)} %get-tuple-element.122.rest_6_.rest_7_), channel_id=1, source_target_pairs={{0,4},{1,5},{2,6},{3,7},{4,0},{5,1},{6,2},{7,3},{8,12},{9,13},{10,... | collective-permute-start | bytes 196616 | tf_op jit(solution)/shard_map/ppermute | solution.py:546
  64.8 4.3 %collective-permute-start.20 = (f32[8,16,128]{2,1,0:T(8,128)S(1)}, f32[8,16,128]{2,1,0:T(8,128)S(1)}, u32[]{:S(2)}, u32[]{:S(2)}) collective-permute-start(f32[8,16,128]{2,1,0:T(8,128)S(1)} %get-tuple-element.123.rest_7_.rest_8_), channel_id=1, source_target_pairs={{0,4},{1,5},{2,6},{3,7},{4,0},{5,1},{6,2},{7,3},{8,12},{9,13},{10,... | collective-permute-start | bytes 196616 | tf_op jit(solution)/shard_map/ppermute | solution.py:546
  66.2 4.3 %collective-permute-start.21 = (f32[8,16,128]{2,1,0:T(8,128)S(1)}, f32[8,16,128]{2,1,0:T(8,128)S(1)}, u32[]{:S(2)}, u32[]{:S(2)}) collective-permute-start(f32[8,16,128]{2,1,0:T(8,128)S(1)} %get-tuple-element.124.rest_8_.rest_9_), channel_id=1, source_target_pairs={{0,4},{1,5},{2,6},{3,7},{4,0},{5,1},{6,2},{7,3},{8,12},{9,13},{10,... | collective-permute-start | bytes 196616 | tf_op jit(solution)/shard_map/ppermute | solution.py:546
  (4 other events, 22.4 us)

commit v9 on v8

--- a/solution.py
+++ b/solution.py
@@ -12,7 +12,8 @@
 AXES = ("gx", "gy")
 EXCHANGES = (("gy", 1), ("gx", 0), ("gx", 1), ("gy", 0))
 CHUNKS = 4
-PIECES = 4
+SHARES = (2, 2, 1, 1)
+AHEAD = 2
 VMEM = pl.BlockSpec(memory_space=pltpu.VMEM)
 SMEM = pl.BlockSpec(memory_space=pltpu.SMEM)
 ANY = pl.BlockSpec(memory_space=pl.ANY)
@@ -260,7 +261,6 @@
     step = slots[0][0].shape[0] // cols
     count = step + sum(chunk.shape[0] for chunk in chunks)
     parts = count // step - 1
-    chunks = iter(chunks)
 
     def load(part):
         rows = [order[part * step + r] for r in range(step)]
@@ -271,11 +271,13 @@
         if part < parts:
             load(part + 1)
         value = multiply(*slots[part % 2], tiles).reshape(step, cols, cells)
-        done = 0
-        while done < step:
-            chunk = next(chunks)
-            chunk[...] = value[done : done + chunk.shape[0]]
-            done += chunk.shape[0]
+        low, start = (part - 1) * step, 0
+        for chunk in chunks:
+            stop = start + chunk.shape[0]
+            a, b = max(start, low), min(stop, low + step)
+            if a < b:
+                chunk[a - start : b - start] = value[a - low : b - low]
+            start = stop
 
 
 def row_sum(sums):
@@ -523,7 +525,7 @@
     )(plan, flat_columns, flat_weights, order, full, *near, tiles, inverse, meta)
     swap = [(j, j ^ (size_y // 2)) for j in range(size_y)]
     their_first = lax.ppermute(first, "gy", swap)
-    later_sizes = [size] + [size // PIECES] * (PIECES * (CHUNKS - 2))
+    later_sizes = [(count - size) * n // sum(SHARES) for n in SHARES]
     later = call(
         last_rest_kernel,
         [shape(n, cols, cells) for n in later_sizes],
@@ -532,8 +534,8 @@
         [half] * 4,
         cost=(work[0] // CHUNKS * (CHUNKS - 1), 0),
     )(flat_columns, flat_weights, order, full, tiles)
-    second, sums = lax.optimization_barrier((later[0], sums))
-    their_second = lax.ppermute(second, "gy", swap)
+    *ahead, sums = lax.optimization_barrier((*later[:AHEAD], sums))
+    their_later = [lax.ppermute(x, "gy", swap) for x in ahead]
 
     packed, inverse = call(
         sums_kernel,
@@ -541,9 +543,9 @@
         [SMEM] + [VMEM] * (3 + len(later)),
         [VMEM] * 2,
     )(order, sums, full, first, *later)
-    packed, *last = lax.optimization_barrier((packed, *later[1:]))
+    packed, *last = lax.optimization_barrier((packed, *later[AHEAD:]))
     sums = everywhere(packed)
-    their_later = [their_second] + [lax.ppermute(x, "gy", swap) for x in last]
+    their_later += [lax.ppermute(x, "gy", swap) for x in last]
     inverse, rayleigh, moved_weights, moved_columns = call(
         factor_kernel,
         [

time: 73.1 us -> 69.1 us (0.945)
  starting transfers between devices: 38.2 us -> 30.7 us
  waiting for transfers between devices: 5.97 us -> 10.1 us
    ppermute x9 -> x4, starting transfers between devices: 11.7 us -> 4.13 us  [the longest x2 2.09 us: per_device(): their_later += [lax.ppermute(x, 'gy', swap) for x in last]]
    all_to_all x3, waiting for transfers between devices: 0.36 us -> 5.96 us  [everywhere(): return lax.all_to_all(rows, AXES, 0, 0, tiled=True)]
    ppermute x9 -> x4, waiting for transfers between devices: 2.74 us -> 1.49 us  [the longest x2 1.48 us: per_device(): their_later += [lax.ppermute(x, 'gy', swap) for x in last]]
  transfers between devices with their start and end apart: 25 -> 20, of which waited for: 7 -> 7; matrix products, arithmetic and copies ran while one was open for 0% -> 0% of each run, Pallas kernels for 27% -> 27%
where the time goes in v9:
time: 69.1 us; the launch traced here: 68.8 us
  starting transfers between devices  30.7 us (44%)
  Pallas kernels  26.9 us (39%)
  waiting for transfers between devices  10.1 us (15%)
  between operations  0.99 us (1%)
    all_to_all x3, starting transfers between devices, everywhere(): return lax.all_to_all(rows, AXES, 0, 0, tiled=True)  14.2 us
    ppermute x12, starting transfers between devices, pairs(): return lax.ppermute(x, AXES, swap)  10.7 us
    pallas_call x2, Pallas kernels, operator(): call(operator_kernel, [whole] + [piece] * 4, [SMEM] * 3 + [HBM] + [VMEM]...  7.79 us
    all_to_all x3, waiting for transfers between devices, everywhere(): return lax.all_to_all(rows, AXES, 0, 0, tiled=True)  5.96 us
    pallas_call x1, Pallas kernels, per_device(): call(sums_kernel, [shape(devices, 1, 2 * cols * cols), square], [SMEM] +...  3.81 us
    pallas_call x1, Pallas kernels, per_device(): call(last_rest_kernel, [shape(n, cols, cells) for n in later_sizes], [SME...  3.26 us
    ppermute x12, waiting for transfers between devices, pairs(): return lax.ppermute(x, AXES, swap)  2.69 us
    pallas_call x1, Pallas kernels, per_device(): call(scale_kernel, [blocks, square, gram_rows], [VMEM] * 2, [VMEM] * 3, c...  2.6 us
  transfers between devices with their start and end apart: 20, of which 7 were waited for; matrix products, arithmetic and copies ran while one was open for 0% of the time, Pallas kernels for 27%

profile of v9, /device:TPU:0, one launch (start us, length us, event | category | flops | bytes accessed | tf_op | source)
XLA Modules:
  0.0 68.8 jit_solution(6031794784097036341)
XLA Ops:
  0.8 1.9 %shard_map.93 = (f32[128,16,128]{2,1,0:T(8,128)S(1)}, f32[8,128,128]{2,1,0:T(8,128)S(1)}, f32[8,16,128]{2,1,0:T(8,128)S(1)}, f32[8,16,128]{2,1,0:T(8,128)S(1)}, ...) custom-call(s32[8]{0:T(128)S(1)} %stack.51.plan, s32[4,8]{1,0:T(4,128)} %bitcast.48, f32[128,16,128]{2,1,0:T(8,128)} %bitcast.46, ...), custom_call_target="tpu_custom_call" | custom-call | tf_op jit(solution)/shard_map/pallas_call | solution.py:451
  2.7 3.1 %collective-permute-start = (f32[8,16,128]{2,1,0:T(8,128)S(1)}, f32[8,16,128]{2,1,0:T(8,128)S(1)}, u32[]{:S(2)}, u32[]{:S(2)}) collective-permute-start(f32[8,16,128]{2,1,0:T(8,128)S(1)} %get-tuple-element.56), channel_id=1, source_target_pairs={{0,8},{1,2},{2,1},{3,4},{4,3},{5,6},{6,5},{7,15},{8,0},{9,10},{10,... | collective-permute-start | bytes 196616 | tf_op jit(solution)/shard_map/ppermute | solution.py:406
  5.9 1.2 %collective-permute-start.2 = (f32[8,16,128]{2,1,0:T(8,128)S(1)}, f32[8,16,128]{2,1,0:T(8,128)S(1)}, u32[]{:S(2)}, u32[]{:S(2)}) collective-permute-start(f32[8,16,128]{2,1,0:T(8,128)S(1)} %get-tuple-element.58), channel_id=1, source_target_pairs={{0,1},{1,0},{2,3},{3,2},{4,5},{5,4},{6,7},{7,6},{8,16},{9,17},{10,... | collective-permute-start | bytes 196616 | tf_op jit(solution)/shard_map/ppermute | solution.py:406
  8.1 2.0 %collective-permute-done.1.h1 = f32[8,16,128]{2,1,0:T(8,128)S(1)} collective-permute-done((f32[8,16,128]{2,1,0:T(8,128)S(1)}, f32[8,16,128]{2,1,0:T(8,128)S(1)}, u32[]{:S(2)}, u32[]{:S(2)}) %collective-permute-start.1) | collective-permute-done | bytes 65568 | tf_op jit(solution)/shard_map/ppermute | solution.py:406
  10.1 3.9 %shard_map.96 = (f32[128,16,128]{2,1,0:T(8,128)S(1)}, f32[8,16,128]{2,1,0:T(8,128)S(1)}, f32[8,16,128]{2,1,0:T(8,128)S(1)}, f32[8,16,128]{2,1,0:T(8,128)S(1)}, f32[8,16,128]{2,1,0:T(8,128)S(1)}) custom-call(s32[8]{0:T(128)S(1)} %stack.51.plan, s32[1024]{0:T(1024)S(1)} %bitcast.41, f32[1024]{0:T(1024)S(1)} %bitcast.36, ...), custom_call_target="tpu_custom_call", output_to_operand_aliasing={{0}: (4, {})} | custom-call | flops 1610612736 | tf_op jit(solution)/shard_map/pallas_call | solution.py:484
  14.0 2.5 %collective-permute-start.4 = (f32[8,16,128]{2,1,0:T(8,128)S(1)}, f32[8,16,128]{2,1,0:T(8,128)S(1)}, u32[]{:S(2)}, u32[]{:S(2)}) collective-permute-start(f32[8,16,128]{2,1,0:T(8,128)S(1)} %get-tuple-element.72), channel_id=1, source_target_pairs={{0,8},{1,2},{2,1},{3,4},{4,3},{5,6},{6,5},{7,15},{8,0},{9,10},{10,... | collective-permute-start | bytes 196616 | tf_op jit(solution)/shard_map/ppermute | solution.py:406
  17.1 1.3 %shard_map.97 = f32[32,1,256]{2,1,0:T(1,128)} custom-call(f32[128,16,128]{2,1,0:T(8,128)S(1)} %get-tuple-element.71.image.block), custom_call_target="tpu_custom_call" | custom-call | flops 268435456 | tf_op jit(solution)/shard_map/pallas_call | solution.py:506
  18.4 4.8 %all-to-all-start = ((f32[32,1,256]{2,1,0:T(1,128)}), f32[32,1,256]{2,1,0:T(1,128)S(1)}, u32[]{:S(2)}, u32[]{:S(2)}) async-start(f32[32,1,256]{2,1,0:T(1,128)} %shard_map.97), calls=%async_computation | async-start | bytes 65536 | tf_op jit(solution)/shard_map/all_to_all | solution.py:418
  23.3 3.9 %shard_map.98 = (f32[128,16,128]{2,1,0:T(8,128)S(1)}, f32[8,16,128]{2,1,0:T(8,128)S(1)}, f32[8,16,128]{2,1,0:T(8,128)S(1)}, f32[8,16,128]{2,1,0:T(8,128)S(1)}, f32[8,16,128]{2,1,0:T(8,128)S(1)}) custom-call(s32[8]{0:T(128)S(1)} %stack.51.plan, s32[1024]{0:T(1024)S(1)} %bitcast.42, f32[1024]{0:T(1024)S(1)} %bitcast.37, ...), custom_call_target="tpu_custom_call", output_to_operand_aliasing={{0}: (4, {})} | custom-call | flops 1610612736 | tf_op jit(solution)/shard_map/pallas_call | solution.py:484
  27.2 1.8 %collective-permute-start.8 = (f32[8,16,128]{2,1,0:T(8,128)S(1)}, f32[8,16,128]{2,1,0:T(8,128)S(1)}, u32[]{:S(2)}, u32[]{:S(2)}) collective-permute-start(f32[8,16,128]{2,1,0:T(8,128)S(1)} %get-tuple-element.79), channel_id=1, source_target_pairs={{0,8},{1,2},{2,1},{3,4},{4,3},{5,6},{6,5},{7,15},{8,0},{9,10},{10,... | collective-permute-start | bytes 196616 | tf_op jit(solution)/shard_map/ppermute | solution.py:406
  29.3 1.0 %collective-permute-start.10 = (f32[8,16,128]{2,1,0:T(8,128)S(1)}, f32[8,16,128]{2,1,0:T(8,128)S(1)}, u32[]{:S(2)}, u32[]{:S(2)}) collective-permute-start(f32[8,16,128]{2,1,0:T(8,128)S(1)} %get-tuple-element.81), channel_id=1, source_target_pairs={{0,1},{1,0},{2,3},{3,2},{4,5},{5,4},{6,7},{7,6},{8,16},{9,17},{10,... | collective-permute-start | bytes 196616 | tf_op jit(solution)/shard_map/ppermute | solution.py:406
  30.5 2.6 %shard_map.99 = (f32[160,16,128]{2,1,0:T(8,128)S(1)}, f32[16,128]{1,0:T(8,128)S(1)}, f32[32,1,256]{2,1,0:T(1,128)}) custom-call(f32[32,1,256]{2,1,0:T(1,128)S(1)} %all-to-all-done.sums, f32[128,16,128]{2,1,0:T(8,128)S(1)} %get-tuple-element.76.image), custom_call_target="tpu_custom_call" | custom-call | flops 268435456 | tf_op jit(solution)/shard_map/pallas_call | solution.py:511
  33.3 5.1 %all-to-all-start.1 = ((f32[32,1,256]{2,1,0:T(1,128)}), f32[32,1,256]{2,1,0:T(1,128)S(1)}, u32[]{:S(2)}, u32[]{:S(2)}) async-start(f32[32,1,256]{2,1,0:T(1,128)} %get-tuple-element.92), calls=%async_computation.1 | async-start | bytes 65536 | tf_op jit(solution)/shard_map/all_to_all | solution.py:418
  38.4 1.8 %shard_map.100 = (f32[33,16,128]{2,1,0:T(8,128)S(1)}, f32[160,16,128]{2,1,0:T(8,128)S(1)}) custom-call(s32[8]{0:T(128)S(1)} %stack.51.plan, s32[1024]{0:T(1024)S(1)} %bitcast.43, f32[1024]{0:T(1024)S(1)} %bitcast.38, s32[1024]{0:T(1024)S(1)} %bitcast.30, f32[160,16,128]{2,1,0:T(8,128)S(1)} %get-tuple-element.77.own, ...), custom_call_target="tpu_custom_call", output_to_operand_aliasing={{1}: (4, {})} | custom-call | flops 402653184 | tf_op jit(solution)/shard_map/pallas_call | solution.py:517
  40.2 1.7 %collective-permute-start.12 = (f32[33,16,128]{2,1,0:T(8,128)S(1)}, f32[33,16,128]{2,1,0:T(8,128)S(1)}, u32[]{:S(2)}, u32[]{:S(2)}) collective-permute-start(f32[33,16,128]{2,1,0:T(8,128)S(1)} %get-tuple-element.94.first.mine.rest_0_), channel_id=1, source_target_pairs={{0,4},{1,5},{2,6},{3,7},{4,0},{5,1},{6,2},{7,3},{8,12},{9,13},{10,... | collective-permute-start | bytes 811016 | tf_op jit(solution)/shard_map/ppermute | solution.py:527
  41.8 3.3 %shard_map.101 = (f32[32,16,128]{2,1,0:T(8,128)S(1)}, f32[32,16,128]{2,1,0:T(8,128)S(1)}, f32[16,16,128]{2,1,0:T(8,128)S(1)}, f32[16,16,128]{2,1,0:T(8,128)S(1)}) custom-call(s32[1024]{0:T(1024)S(1)} %bitcast.44, f32[1024]{0:T(1024)S(1)} %bitcast.39, s32[1024]{0:T(1024)S(1)} %bitcast.31, f32[160,16,128]{2,1,0:T(8,128)S(1)} %get-tuple-element.89.full, ...), custom_call_target="tpu_custom_call" | custom-call | flops 1207959552 | tf_op jit(solution)/shard_map/pallas_call | solution.py:529
  46.0 1.5 %collective-permute-start.14 = (f32[32,16,128]{2,1,0:T(8,128)S(1)}, f32[32,16,128]{2,1,0:T(8,128)S(1)}, u32[]{:S(2)}, u32[]{:S(2)}) collective-permute-start(f32[32,16,128]{2,1,0:T(8,128)S(1)} %get-tuple-element.102.rest_1_.rest_2_), channel_id=1, source_target_pairs={{0,4},{1,5},{2,6},{3,7},{4,0},{5,1},{6,2},{7,3},{8,12},{9,13},{10,... | collective-permute-start | bytes 786440 | tf_op jit(solution)/shard_map/ppermute | solution.py:538
  47.5 3.8 %shard_map.102 = (f32[32,1,512]{2,1,0:T(1,128)}, f32[16,128]{1,0:T(8,128)S(1)}) custom-call(s32[1024]{0:T(1024)S(1)} %bitcast.32, f32[32,1,256]{2,1,0:T(1,128)S(1)} %all-to-all-done.1.sums, f32[160,16,128]{2,1,0:T(8,128)S(1)} %get-tuple-element.89.full, f32[33,16,128]{2,1,0:T(8,128)S(1)} %get-tuple-element.94.first.mine.rest_0_, ...), custom_call_target="tpu_custom_call" | custom-call | tf_op jit(solution)/shard_map/pallas_call | solution.py:540
  51.3 4.3 %all-to-all-start.2 = ((f32[32,1,512]{2,1,0:T(1,128)}), f32[32,1,512]{2,1,0:T(1,128)S(1)}, u32[]{:S(2)}, u32[]{:S(2)}) async-start(f32[32,1,512]{2,1,0:T(1,128)} %get-tuple-element.98), calls=%async_computation.2 | async-start | bytes 131072 | tf_op jit(solution)/shard_map/all_to_all | solution.py:418
  55.6 1.8 %collective-permute-start.15 = (f32[16,16,128]{2,1,0:T(8,128)S(1)}, f32[16,16,128]{2,1,0:T(8,128)S(1)}, u32[]{:S(2)}, u32[]{:S(2)}) collective-permute-start(f32[16,16,128]{2,1,0:T(8,128)S(1)} %get-tuple-element.103.rest_2_.rest_3_), channel_id=1, source_target_pairs={{0,4},{1,5},{2,6},{3,7},{4,0},{5,1},{6,2},{7,3},{8,12},{9,13},{10,... | collective-permute-start | bytes 393224 | tf_op jit(solution)/shard_map/ppermute | solution.py:548
  57.7 5.4 %all-to-all-done.2.sums = f32[32,1,512]{2,1,0:T(1,128)S(1)} async-done(((f32[32,1,512]{2,1,0:T(1,128)}), f32[32,1,512]{2,1,0:T(1,128)S(1)}, u32[]{:S(2)}, u32[]{:S(2)}) %all-to-all-start.2) | async-done | bytes 65568 | tf_op jit(solution)/shard_map/all_to_all | solution.py:418
  63.2 1.8 %shard_map.103 = (f32[16,128]{1,0:T(8,128)S(1)}, f32[16,16]{1,0:T(8,128)}, f32[8,128]{1,0:T(8,128)}, s32[8,128]{1,0:T(8,128)}) custom-call(s32[1024]{0:T(1024)S(1)} %bitcast.33, f32[32,1,512]{2,1,0:T(1,128)S(1)} %all-to-all-done.2.sums, f32[16,128]{1,0:T(8,128)S(1)} %get-tuple-element.99.inverse, f32[33,16,128]{2,1,0:T(8,128)S(1)} %get-tuple-element.94.first.mine.rest_0_, ...), custom_call_target="tpu_custom_call" | custom-call | flops 268435456 | tf_op jit(solution)/shard_map/pallas_call | solution.py:549
  65.0 1.5 %collective-permute-done.16.rest_9_ = f32[16,16,128]{2,1,0:T(8,128)S(1)} collective-permute-done((f32[16,16,128]{2,1,0:T(8,128)S(1)}, f32[16,16,128]{2,1,0:T(8,128)S(1)}, u32[]{:S(2)}, u32[]{:S(2)}) %collective-permute-start.16) | collective-permute-done | bytes 131104 | tf_op jit(solution)/shard_map/ppermute | solution.py:548
  66.5 2.2 %shard_map.104 = f32[128,16,128]{2,1,0:T(8,128)} custom-call(s32[1024]{0:T(1024)S(1)} %bitcast.34, f32[16,128]{1,0:T(8,128)S(1)} %get-tuple-element.100.inverse, f32[33,16,128]{2,1,0:T(8,128)S(1)} %get-tuple-element.94.first.mine.rest_0_, f32[32,16,128]{2,1,0:T(8,128)S(1)} %get-tuple-element.101.rest_0_.rest_1_, ...), custom_call_target="tpu_custom_call" | custom-call | tf_op jit(solution)/shard_map/pallas_call | solution.py:561
  (35 shorter events, 3.5 us)
Async XLA Ops:
  0.8 6.5 %copy-start = (f32[1,1,128,8]{2,3,1,0:T(8,128)S(1)}, f32[1,1,128,8]{2,3,1,0:T(8,128)}, u32[]{:S(2)}) copy-start(f32[1,1,128,8]{2,3,1,0:T(8,128)} %param.8) | copy-start | bytes 12292
  0.8 6.5 %copy-start.1 = (s32[1,1,128,8]{2,3,1,0:T(8,128)S(1)}, s32[1,1,128,8]{2,3,1,0:T(8,128)}, u32[]{:S(2)}) copy-start(s32[1,1,128,8]{2,3,1,0:T(8,128)} %param.9) | copy-start | bytes 12292
  0.8 6.5 %copy-start.2 = (s32[1,1,128]{2,1,0:T(1,128)S(1)}, s32[1,1,128]{2,1,0:T(1,128)}, u32[]{:S(2)}) copy-start(s32[1,1,128]{2,1,0:T(1,128)} %param.11) | copy-start | bytes 1540
  2.7 5.3 %collective-permute-start = (f32[8,16,128]{2,1,0:T(8,128)S(1)}, f32[8,16,128]{2,1,0:T(8,128)S(1)}, u32[]{:S(2)}, u32[]{:S(2)}) collective-permute-start(f32[8,16,128]{2,1,0:T(8,128)S(1)} %get-tuple-element.56), channel_id=1, source_target_pairs={{0,8},{1,2},{2,1},{3,4},{4,3},{5,6},{6,5},{7,15},{8,0},{9,10},{10,... | collective-permute-start | bytes 196616 | tf_op jit(solution)/shard_map/ppermute | solution.py:406
  5.8 4.3 %collective-permute-start.1 = (f32[8,16,128]{2,1,0:T(8,128)S(1)}, f32[8,16,128]{2,1,0:T(8,128)S(1)}, u32[]{:S(2)}, u32[]{:S(2)}) collective-permute-start(f32[8,16,128]{2,1,0:T(8,128)S(1)} %get-tuple-element.57), channel_id=1, source_target_pairs={{0,8},{1,9},{2,10},{3,11},{4,12},{5,13},{6,14},{7,15},{8,0},{9,1},... | collective-permute-start | bytes 196616 | tf_op jit(solution)/shard_map/ppermute | solution.py:406
  5.9 4.2 %collective-permute-start.2 = (f32[8,16,128]{2,1,0:T(8,128)S(1)}, f32[8,16,128]{2,1,0:T(8,128)S(1)}, u32[]{:S(2)}, u32[]{:S(2)}) collective-permute-start(f32[8,16,128]{2,1,0:T(8,128)S(1)} %get-tuple-element.58), channel_id=1, source_target_pairs={{0,1},{1,0},{2,3},{3,2},{4,5},{5,4},{6,7},{7,6},{8,16},{9,17},{10,... | collective-permute-start | bytes 196616 | tf_op jit(solution)/shard_map/ppermute | solution.py:406
  7.1 2.9 %collective-permute-start.3 = (f32[8,16,128]{2,1,0:T(8,128)S(1)}, f32[8,16,128]{2,1,0:T(8,128)S(1)}, u32[]{:S(2)}, u32[]{:S(2)}) collective-permute-start(f32[8,16,128]{2,1,0:T(8,128)S(1)} %get-tuple-element.59), channel_id=1, source_target_pairs={{0,1},{1,0},{2,3},{3,2},{4,5},{5,4},{6,7},{7,6},{8,9},{9,8},{10,11... | collective-permute-start | bytes 196616 | tf_op jit(solution)/shard_map/ppermute | solution.py:406
  14.0 9.2 %collective-permute-start.4 = (f32[8,16,128]{2,1,0:T(8,128)S(1)}, f32[8,16,128]{2,1,0:T(8,128)S(1)}, u32[]{:S(2)}, u32[]{:S(2)}) collective-permute-start(f32[8,16,128]{2,1,0:T(8,128)S(1)} %get-tuple-element.72), channel_id=1, source_target_pairs={{0,8},{1,2},{2,1},{3,4},{4,3},{5,6},{6,5},{7,15},{8,0},{9,10},{10,... | collective-permute-start | bytes 196616 | tf_op jit(solution)/shard_map/ppermute | solution.py:406
  16.5 6.7 %collective-permute-start.5 = (f32[8,16,128]{2,1,0:T(8,128)S(1)}, f32[8,16,128]{2,1,0:T(8,128)S(1)}, u32[]{:S(2)}, u32[]{:S(2)}) collective-permute-start(f32[8,16,128]{2,1,0:T(8,128)S(1)} %get-tuple-element.73), channel_id=1, source_target_pairs={{0,8},{1,9},{2,10},{3,11},{4,12},{5,13},{6,14},{7,15},{8,0},{9,1},... | collective-permute-start | bytes 196616 | tf_op jit(solution)/shard_map/ppermute | solution.py:406
  16.6 6.7 %collective-permute-start.6 = (f32[8,16,128]{2,1,0:T(8,128)S(1)}, f32[8,16,128]{2,1,0:T(8,128)S(1)}, u32[]{:S(2)}, u32[]{:S(2)}) collective-permute-start(f32[8,16,128]{2,1,0:T(8,128)S(1)} %get-tuple-element.74), channel_id=1, source_target_pairs={{0,1},{1,0},{2,3},{3,2},{4,5},{5,4},{6,7},{7,6},{8,16},{9,17},{10,... | collective-permute-start | bytes 196616 | tf_op jit(solution)/shard_map/ppermute | solution.py:406
  16.8 6.5 %collective-permute-start.7 = (f32[8,16,128]{2,1,0:T(8,128)S(1)}, f32[8,16,128]{2,1,0:T(8,128)S(1)}, u32[]{:S(2)}, u32[]{:S(2)}) collective-permute-start(f32[8,16,128]{2,1,0:T(8,128)S(1)} %get-tuple-element.75), channel_id=1, source_target_pairs={{0,1},{1,0},{2,3},{3,2},{4,5},{5,4},{6,7},{7,6},{8,9},{9,8},{10,11... | collective-permute-start | bytes 196616 | tf_op jit(solution)/shard_map/ppermute | solution.py:406
  18.4 12.1 %all-to-all-start = ((f32[32,1,256]{2,1,0:T(1,128)}), f32[32,1,256]{2,1,0:T(1,128)S(1)}, u32[]{:S(2)}, u32[]{:S(2)}) async-start(f32[32,1,256]{2,1,0:T(1,128)} %shard_map.97), calls=%async_computation | async-start | bytes 65536 | tf_op jit(solution)/shard_map/all_to_all | solution.py:418
  27.2 5.9 %collective-permute-start.8 = (f32[8,16,128]{2,1,0:T(8,128)S(1)}, f32[8,16,128]{2,1,0:T(8,128)S(1)}, u32[]{:S(2)}, u32[]{:S(2)}) collective-permute-start(f32[8,16,128]{2,1,0:T(8,128)S(1)} %get-tuple-element.79), channel_id=1, source_target_pairs={{0,8},{1,2},{2,1},{3,4},{4,3},{5,6},{6,5},{7,15},{8,0},{9,10},{10,... | collective-permute-start | bytes 196616 | tf_op jit(solution)/shard_map/ppermute | solution.py:406
  29.0 4.3 %collective-permute-start.9 = (f32[8,16,128]{2,1,0:T(8,128)S(1)}, f32[8,16,128]{2,1,0:T(8,128)S(1)}, u32[]{:S(2)}, u32[]{:S(2)}) collective-permute-start(f32[8,16,128]{2,1,0:T(8,128)S(1)} %get-tuple-element.80), channel_id=1, source_target_pairs={{0,8},{1,9},{2,10},{3,11},{4,12},{5,13},{6,14},{7,15},{8,0},{9,1},... | collective-permute-start | bytes 196616 | tf_op jit(solution)/shard_map/ppermute | solution.py:406
  29.3 4.0 %collective-permute-start.10 = (f32[8,16,128]{2,1,0:T(8,128)S(1)}, f32[8,16,128]{2,1,0:T(8,128)S(1)}, u32[]{:S(2)}, u32[]{:S(2)}) collective-permute-start(f32[8,16,128]{2,1,0:T(8,128)S(1)} %get-tuple-element.81), channel_id=1, source_target_pairs={{0,1},{1,0},{2,3},{3,2},{4,5},{5,4},{6,7},{7,6},{8,16},{9,17},{10,... | collective-permute-start | bytes 196616 | tf_op jit(solution)/shard_map/ppermute | solution.py:406
  30.3 3.0 %collective-permute-start.11 = (f32[8,16,128]{2,1,0:T(8,128)S(1)}, f32[8,16,128]{2,1,0:T(8,128)S(1)}, u32[]{:S(2)}, u32[]{:S(2)}) collective-permute-start(f32[8,16,128]{2,1,0:T(8,128)S(1)} %get-tuple-element.82), channel_id=1, source_target_pairs={{0,1},{1,0},{2,3},{3,2},{4,5},{5,4},{6,7},{7,6},{8,9},{9,8},{10,11... | collective-permute-start | bytes 196616 | tf_op jit(solution)/shard_map/ppermute | solution.py:406
  33.3 12.2 %all-to-all-start.1 = ((f32[32,1,256]{2,1,0:T(1,128)}), f32[32,1,256]{2,1,0:T(1,128)S(1)}, u32[]{:S(2)}, u32[]{:S(2)}) async-start(f32[32,1,256]{2,1,0:T(1,128)} %get-tuple-element.92), calls=%async_computation.1 | async-start | bytes 65536 | tf_op jit(solution)/shard_map/all_to_all | solution.py:418
  40.2 23.0 %collective-permute-start.12 = (f32[33,16,128]{2,1,0:T(8,128)S(1)}, f32[33,16,128]{2,1,0:T(8,128)S(1)}, u32[]{:S(2)}, u32[]{:S(2)}) collective-permute-start(f32[33,16,128]{2,1,0:T(8,128)S(1)} %get-tuple-element.94.first.mine.rest_0_), channel_id=1, source_target_pairs={{0,4},{1,5},{2,6},{3,7},{4,0},{5,1},{6,2},{7,3},{8,12},{9,13},{10,... | collective-permute-start | bytes 811016 | tf_op jit(solution)/shard_map/ppermute | solution.py:527
  45.5 21.0 %collective-permute-start.13 = (f32[32,16,128]{2,1,0:T(8,128)S(1)}, f32[32,16,128]{2,1,0:T(8,128)S(1)}, u32[]{:S(2)}, u32[]{:S(2)}) collective-permute-start(f32[32,16,128]{2,1,0:T(8,128)S(1)} %get-tuple-element.101.rest_0_.rest_1_), channel_id=1, source_target_pairs={{0,4},{1,5},{2,6},{3,7},{4,0},{5,1},{6,2},{7,3},{8,12},{9,13},{10,... | collective-permute-start | bytes 786440 | tf_op jit(solution)/shard_map/ppermute | solution.py:538
  46.0 20.4 %collective-permute-start.14 = (f32[32,16,128]{2,1,0:T(8,128)S(1)}, f32[32,16,128]{2,1,0:T(8,128)S(1)}, u32[]{:S(2)}, u32[]{:S(2)}) collective-permute-start(f32[32,16,128]{2,1,0:T(8,128)S(1)} %get-tuple-element.102.rest_1_.rest_2_), channel_id=1, source_target_pairs={{0,4},{1,5},{2,6},{3,7},{4,0},{5,1},{6,2},{7,3},{8,12},{9,13},{10,... | collective-permute-start | bytes 786440 | tf_op jit(solution)/shard_map/ppermute | solution.py:538
  51.3 11.8 %all-to-all-start.2 = ((f32[32,1,512]{2,1,0:T(1,128)}), f32[32,1,512]{2,1,0:T(1,128)S(1)}, u32[]{:S(2)}, u32[]{:S(2)}) async-start(f32[32,1,512]{2,1,0:T(1,128)} %get-tuple-element.98), calls=%async_computation.2 | async-start | bytes 131072 | tf_op jit(solution)/shard_map/all_to_all | solution.py:418
  55.6 9.3 %collective-permute-start.15 = (f32[16,16,128]{2,1,0:T(8,128)S(1)}, f32[16,16,128]{2,1,0:T(8,128)S(1)}, u32[]{:S(2)}, u32[]{:S(2)}) collective-permute-start(f32[16,16,128]{2,1,0:T(8,128)S(1)} %get-tuple-element.103.rest_2_.rest_3_), channel_id=1, source_target_pairs={{0,4},{1,5},{2,6},{3,7},{4,0},{5,1},{6,2},{7,3},{8,12},{9,13},{10,... | collective-permute-start | bytes 393224 | tf_op jit(solution)/shard_map/ppermute | solution.py:548
  57.5 9.0 %collective-permute-start.16 = (f32[16,16,128]{2,1,0:T(8,128)S(1)}, f32[16,16,128]{2,1,0:T(8,128)S(1)}, u32[]{:S(2)}, u32[]{:S(2)}) collective-permute-start(f32[16,16,128]{2,1,0:T(8,128)S(1)} %get-tuple-element.104.rest_3_.rest_4_), channel_id=1, source_target_pairs={{0,4},{1,5},{2,6},{3,7},{4,0},{5,1},{6,2},{7,3},{8,12},{9,13},{10,... | collective-permute-start | bytes 393224 | tf_op jit(solution)/shard_map/ppermute | solution.py:548

commit v10 on v9

--- a/solution.py
+++ b/solution.py
@@ -12,7 +12,8 @@
 AXES = ("gx", "gy")
 EXCHANGES = (("gy", 1), ("gx", 0), ("gx", 1), ("gy", 0))
 CHUNKS = 4
-SHARES = (2, 2, 1, 1)
+FIRST = 2
+SHARES = (3, 3, 2)
 AHEAD = 2
 VMEM = pl.BlockSpec(memory_space=pltpu.VMEM)
 SMEM = pl.BlockSpec(memory_space=pltpu.SMEM)
@@ -245,33 +246,44 @@
 
 
 def last_first_kernel(plan, columns, weights, order, own, h0, h1, h2, h3, tiles, inv, meta, *rest):
-    chunk, full, high, low = rest
+    chunk, full, slots = rest[0], rest[1], (rest[2:4], rest[4:6])
     _, cols, cells = full.shape
     count = full.shape[0] - 4 * h0.shape[0]
-    step = high.shape[0] // cols
+    step = slots[0][0].shape[0] // cols
+    parts = chunk.shape[0] // step
+
+    def load(part):
+        rows = [order[part * step + r] for r in range(step)]
+        gather(*slots[part % 2], full, columns, weights, rows, count)
+
     fill(full, count, (h0, h1, h2, h3), plan, scaler(inv[...]))
-    gather(high, low, full, columns, weights, [order[r] for r in range(step)], count)
-    chunk[:step] = multiply(high, low, tiles).reshape(step, cols, cells)
-    chunk[step] = meta[...]
+    load(0)
+    for part in range(parts):
+        if part + 1 < parts:
+            load(part + 1)
+        value = multiply(*slots[part % 2], tiles).reshape(step, cols, cells)
+        chunk[part * step : (part + 1) * step] = value
+    chunk[parts * step] = meta[...]
 
 
 def last_rest_kernel(columns, weights, order, full, tiles, *rest):
     chunks, slots = rest[:-4], (rest[-4:-2], rest[-2:])
     _, cols, cells = full.shape
     step = slots[0][0].shape[0] // cols
-    count = step + sum(chunk.shape[0] for chunk in chunks)
-    parts = count // step - 1
+    count = columns.shape[0] * cells // tiles.shape[0]
+    begin = (count - sum(chunk.shape[0] for chunk in chunks)) // step
+    parts = count // step
 
     def load(part):
         rows = [order[part * step + r] for r in range(step)]
         gather(*slots[part % 2], full, columns, weights, rows, count)
 
-    load(1)
-    for part in range(1, parts + 1):
-        if part < parts:
+    load(begin)
+    for part in range(begin, parts):
+        if part + 1 < parts:
             load(part + 1)
         value = multiply(*slots[part % 2], tiles).reshape(step, cols, cells)
-        low, start = (part - 1) * step, 0
+        low, start = (part - begin) * step, 0
         for chunk in chunks:
             stop = start + chunk.shape[0]
             a, b = max(start, low), min(stop, low + step)
@@ -516,26 +528,25 @@
 
     first, full = call(
         last_first_kernel,
-        [shape(size + 1, cols, cells), blocks],
+        [shape(FIRST * size + 1, cols, cells), blocks],
         [SMEM] * 4 + [VMEM] * 8,
         [VMEM] * 2,
-        [half] * 2,
-        cost=(work[0] // CHUNKS, 0),
+        [half] * 4,
+        cost=(work[0] // CHUNKS * FIRST, 0),
         input_output_aliases={4: 1},
     )(plan, flat_columns, flat_weights, order, full, *near, tiles, inverse, meta)
     swap = [(j, j ^ (size_y // 2)) for j in range(size_y)]
     their_first = lax.ppermute(first, "gy", swap)
-    later_sizes = [(count - size) * n // sum(SHARES) for n in SHARES]
+    later_sizes = [(count - FIRST * size) * n // sum(SHARES) for n in SHARES]
     later = call(
         last_rest_kernel,
         [shape(n, cols, cells) for n in later_sizes],
         [SMEM] * 3 + [VMEM] * 2,
         [VMEM] * len(later_sizes),
         [half] * 4,
-        cost=(work[0] // CHUNKS * (CHUNKS - 1), 0),
+        cost=(work[0] // CHUNKS * (CHUNKS - FIRST), 0),
     )(flat_columns, flat_weights, order, full, tiles)
-    *ahead, sums = lax.optimization_barrier((*later[:AHEAD], sums))
-    their_later = [lax.ppermute(x, "gy", swap) for x in ahead]
+    their_later = [lax.ppermute(x, "gy", swap) for x in later[:AHEAD]]
 
     packed, inverse = call(
         sums_kernel,

time: 69.1 us -> 71.5 us (1.035)
  waiting for transfers between devices: 10.1 us -> 13.5 us
    all_to_all x3, waiting for transfers between devices: 5.96 us -> 10.8 us  [everywhere(): return lax.all_to_all(rows, AXES, 0, 0, tiled=True)]
    ppermute x2 -> x1, waiting for transfers between devices: 1.48 us -> 0.01 us  [per_device(): their_later += [lax.ppermute(x, 'gy', swap) for x in last]]
    pallas_call x1, Pallas kernels: 3.26 us -> 2.07 us  [per_device(): call(last_rest_kernel, [shape(n, cols, cells) for n in later_sizes], [SME...]
    ppermute x2 -> x1, starting transfers between devices: 2.09 us -> 1.83 us  [per_device(): their_later += [lax.ppermute(x, 'gy', swap) for x in last]]
  transfers between devices with their start and end apart: 20 -> 19, of which waited for: 7 -> 6; matrix products, arithmetic and copies ran while one was open for 0% -> 0% of each run, Pallas kernels for 27% -> 22%
where the time goes in v10:
time: 71.5 us; the launch traced here: 71.3 us
  starting transfers between devices  30.5 us (43%)
  Pallas kernels  26.3 us (37%)
  waiting for transfers between devices  13.5 us (19%)
  between operations  0.84 us (1%)
    all_to_all x3, starting transfers between devices, everywhere(): return lax.all_to_all(rows, AXES, 0, 0, tiled=True)  14.3 us
    all_to_all x3, waiting for transfers between devices, everywhere(): return lax.all_to_all(rows, AXES, 0, 0, tiled=True)  10.8 us
    ppermute x12, starting transfers between devices, pairs(): return lax.ppermute(x, AXES, swap)  10.6 us
    pallas_call x2, Pallas kernels, operator(): call(operator_kernel, [whole] + [piece] * 4, [SMEM] * 3 + [HBM] + [VMEM]...  7.81 us
    pallas_call x1, Pallas kernels, per_device(): call(sums_kernel, [shape(devices, 1, 2 * cols * cols), square], [SMEM] +...  3.8 us
    ppermute x12, waiting for transfers between devices, pairs(): return lax.ppermute(x, AXES, swap)  2.68 us
    pallas_call x1, Pallas kernels, per_device(): call(scale_kernel, [blocks, square, gram_rows], [VMEM] * 2, [VMEM] * 3, c...  2.6 us
    pallas_call x1, Pallas kernels, per_device(): call(last_first_kernel, [shape(FIRST * size + 1, cols, cells), blocks], [...  2.36 us
  transfers between devices with their start and end apart: 19, of which 6 were waited for; matrix products, arithmetic and copies ran while one was open for 0% of the time, Pallas kernels for 22%

profile of v10, /device:TPU:0, one launch (start us, length us, event | category | flops | bytes accessed | tf_op | source)
XLA Modules:
  0.0 71.3 jit_solution(18363785169035543842)
XLA Ops:
  0.8 1.9 %shard_map.93 = (f32[128,16,128]{2,1,0:T(8,128)S(1)}, f32[8,128,128]{2,1,0:T(8,128)S(1)}, f32[8,16,128]{2,1,0:T(8,128)S(1)}, f32[8,16,128]{2,1,0:T(8,128)S(1)}, ...) custom-call(s32[8]{0:T(128)S(1)} %stack.51.plan, s32[4,8]{1,0:T(4,128)} %bitcast.48, f32[128,16,128]{2,1,0:T(8,128)} %bitcast.46, ...), custom_call_target="tpu_custom_call" | custom-call | tf_op jit(solution)/shard_map/pallas_call | solution.py:463
  2.7 3.1 %collective-permute-start = (f32[8,16,128]{2,1,0:T(8,128)S(1)}, f32[8,16,128]{2,1,0:T(8,128)S(1)}, u32[]{:S(2)}, u32[]{:S(2)}) collective-permute-start(f32[8,16,128]{2,1,0:T(8,128)S(1)} %get-tuple-element.51), channel_id=1, source_target_pairs={{0,8},{1,2},{2,1},{3,4},{4,3},{5,6},{6,5},{7,15},{8,0},{9,10},{10,... | collective-permute-start | bytes 196616 | tf_op jit(solution)/shard_map/ppermute | solution.py:418
  5.9 1.2 %collective-permute-start.2 = (f32[8,16,128]{2,1,0:T(8,128)S(1)}, f32[8,16,128]{2,1,0:T(8,128)S(1)}, u32[]{:S(2)}, u32[]{:S(2)}) collective-permute-start(f32[8,16,128]{2,1,0:T(8,128)S(1)} %get-tuple-element.53), channel_id=1, source_target_pairs={{0,1},{1,0},{2,3},{3,2},{4,5},{5,4},{6,7},{7,6},{8,16},{9,17},{10,... | collective-permute-start | bytes 196616 | tf_op jit(solution)/shard_map/ppermute | solution.py:418
  8.1 2.0 %collective-permute-done.1.h1 = f32[8,16,128]{2,1,0:T(8,128)S(1)} collective-permute-done((f32[8,16,128]{2,1,0:T(8,128)S(1)}, f32[8,16,128]{2,1,0:T(8,128)S(1)}, u32[]{:S(2)}, u32[]{:S(2)}) %collective-permute-start.1) | collective-permute-done | bytes 65568 | tf_op jit(solution)/shard_map/ppermute | solution.py:418
  10.1 3.9 %shard_map.96 = (f32[128,16,128]{2,1,0:T(8,128)S(1)}, f32[8,16,128]{2,1,0:T(8,128)S(1)}, f32[8,16,128]{2,1,0:T(8,128)S(1)}, f32[8,16,128]{2,1,0:T(8,128)S(1)}, f32[8,16,128]{2,1,0:T(8,128)S(1)}) custom-call(s32[8]{0:T(128)S(1)} %stack.51.plan, s32[1024]{0:T(1024)S(1)} %bitcast.41, f32[1024]{0:T(1024)S(1)} %bitcast.36, ...), custom_call_target="tpu_custom_call", output_to_operand_aliasing={{0}: (4, {})} | custom-call | flops 1610612736 | tf_op jit(solution)/shard_map/pallas_call | solution.py:496
  14.0 2.5 %collective-permute-start.4 = (f32[8,16,128]{2,1,0:T(8,128)S(1)}, f32[8,16,128]{2,1,0:T(8,128)S(1)}, u32[]{:S(2)}, u32[]{:S(2)}) collective-permute-start(f32[8,16,128]{2,1,0:T(8,128)S(1)} %get-tuple-element.67), channel_id=1, source_target_pairs={{0,8},{1,2},{2,1},{3,4},{4,3},{5,6},{6,5},{7,15},{8,0},{9,10},{10,... | collective-permute-start | bytes 196616 | tf_op jit(solution)/shard_map/ppermute | solution.py:418
  17.1 1.3 %shard_map.97 = f32[32,1,256]{2,1,0:T(1,128)} custom-call(f32[128,16,128]{2,1,0:T(8,128)S(1)} %get-tuple-element.66.image.block), custom_call_target="tpu_custom_call" | custom-call | flops 268435456 | tf_op jit(solution)/shard_map/pallas_call | solution.py:518
  18.4 4.8 %all-to-all-start = ((f32[32,1,256]{2,1,0:T(1,128)}), f32[32,1,256]{2,1,0:T(1,128)S(1)}, u32[]{:S(2)}, u32[]{:S(2)}) async-start(f32[32,1,256]{2,1,0:T(1,128)} %shard_map.97), calls=%async_computation | async-start | bytes 65536 | tf_op jit(solution)/shard_map/all_to_all | solution.py:430
  23.2 3.9 %shard_map.98 = (f32[128,16,128]{2,1,0:T(8,128)S(1)}, f32[8,16,128]{2,1,0:T(8,128)S(1)}, f32[8,16,128]{2,1,0:T(8,128)S(1)}, f32[8,16,128]{2,1,0:T(8,128)S(1)}, f32[8,16,128]{2,1,0:T(8,128)S(1)}) custom-call(s32[8]{0:T(128)S(1)} %stack.51.plan, s32[1024]{0:T(1024)S(1)} %bitcast.42, f32[1024]{0:T(1024)S(1)} %bitcast.37, ...), custom_call_target="tpu_custom_call", output_to_operand_aliasing={{0}: (4, {})} | custom-call | flops 1610612736 | tf_op jit(solution)/shard_map/pallas_call | solution.py:496
  27.2 1.8 %collective-permute-start.8 = (f32[8,16,128]{2,1,0:T(8,128)S(1)}, f32[8,16,128]{2,1,0:T(8,128)S(1)}, u32[]{:S(2)}, u32[]{:S(2)}) collective-permute-start(f32[8,16,128]{2,1,0:T(8,128)S(1)} %get-tuple-element.73), channel_id=1, source_target_pairs={{0,8},{1,2},{2,1},{3,4},{4,3},{5,6},{6,5},{7,15},{8,0},{9,10},{10,... | collective-permute-start | bytes 196616 | tf_op jit(solution)/shard_map/ppermute | solution.py:418
  29.3 1.0 %collective-permute-start.10 = (f32[8,16,128]{2,1,0:T(8,128)S(1)}, f32[8,16,128]{2,1,0:T(8,128)S(1)}, u32[]{:S(2)}, u32[]{:S(2)}) collective-permute-start(f32[8,16,128]{2,1,0:T(8,128)S(1)} %get-tuple-element.75), channel_id=1, source_target_pairs={{0,1},{1,0},{2,3},{3,2},{4,5},{5,4},{6,7},{7,6},{8,16},{9,17},{10,... | collective-permute-start | bytes 196616 | tf_op jit(solution)/shard_map/ppermute | solution.py:418
  30.5 2.6 %shard_map.99 = (f32[160,16,128]{2,1,0:T(8,128)S(1)}, f32[16,128]{1,0:T(8,128)S(1)}, f32[32,1,256]{2,1,0:T(1,128)}) custom-call(f32[32,1,256]{2,1,0:T(1,128)S(1)} %all-to-all-done.sums, f32[128,16,128]{2,1,0:T(8,128)S(1)} %get-tuple-element.71.image), custom_call_target="tpu_custom_call" | custom-call | flops 268435456 | tf_op jit(solution)/shard_map/pallas_call | solution.py:523
  33.3 2.4 %shard_map.100 = (f32[65,16,128]{2,1,0:T(8,128)S(1)}, f32[160,16,128]{2,1,0:T(8,128)S(1)}) custom-call(s32[8]{0:T(128)S(1)} %stack.51.plan, s32[1024]{0:T(1024)S(1)} %bitcast.43, f32[1024]{0:T(1024)S(1)} %bitcast.38, s32[1024]{0:T(1024)S(1)} %bitcast.30, f32[160,16,128]{2,1,0:T(8,128)S(1)} %get-tuple-element.78.own, ...), custom_call_target="tpu_custom_call", output_to_operand_aliasing={{1}: (4, {})} | custom-call | flops 805306368 | tf_op jit(solution)/shard_map/pallas_call | solution.py:529
  35.6 1.6 %collective-permute-start.12 = (f32[65,16,128]{2,1,0:T(8,128)S(1)}, f32[65,16,128]{2,1,0:T(8,128)S(1)}, u32[]{:S(2)}, u32[]{:S(2)}) collective-permute-start(f32[65,16,128]{2,1,0:T(8,128)S(1)} %get-tuple-element.86.first.mine.rest_0_), channel_id=1, source_target_pairs={{0,4},{1,5},{2,6},{3,7},{4,0},{5,1},{6,2},{7,3},{8,12},{9,13},{10,... | collective-permute-start | bytes 1597448 | tf_op jit(solution)/shard_map/ppermute | solution.py:539
  37.2 4.6 %all-to-all-start.1 = ((f32[32,1,256]{2,1,0:T(1,128)}), f32[32,1,256]{2,1,0:T(1,128)S(1)}, u32[]{:S(2)}, u32[]{:S(2)}) async-start(f32[32,1,256]{2,1,0:T(1,128)} %get-tuple-element.77), calls=%async_computation.1 | async-start | bytes 65536 | tf_op jit(solution)/shard_map/all_to_all | solution.py:430
  41.8 2.1 %shard_map.101 = (f32[24,16,128]{2,1,0:T(8,128)S(1)}, f32[24,16,128]{2,1,0:T(8,128)S(1)}, f32[16,16,128]{2,1,0:T(8,128)S(1)}) custom-call(s32[1024]{0:T(1024)S(1)} %bitcast.44, f32[1024]{0:T(1024)S(1)} %bitcast.39, s32[1024]{0:T(1024)S(1)} %bitcast.31, f32[160,16,128]{2,1,0:T(8,128)S(1)} %get-tuple-element.85.full, bf16[1024,256]{1,0:T(8,128)(2,1)S(1)} %shard_map.95.tiles), custom_call_target="tpu_custom_call" | custom-call | flops 805306368 | tf_op jit(solution)/shard_map/pallas_call | solution.py:541
  43.9 1.8 %collective-permute-start.13 = (f32[24,16,128]{2,1,0:T(8,128)S(1)}, f32[24,16,128]{2,1,0:T(8,128)S(1)}, u32[]{:S(2)}, u32[]{:S(2)}) collective-permute-start(f32[24,16,128]{2,1,0:T(8,128)S(1)} %get-tuple-element.87.rest_0_.rest_1_), channel_id=1, source_target_pairs={{0,4},{1,5},{2,6},{3,7},{4,0},{5,1},{6,2},{7,3},{8,12},{9,13},{10,... | collective-permute-start | bytes 589832 | tf_op jit(solution)/shard_map/ppermute | solution.py:549
  46.0 5.0 %all-to-all-done.1.sums = f32[32,1,256]{2,1,0:T(1,128)S(1)} async-done(((f32[32,1,256]{2,1,0:T(1,128)}), f32[32,1,256]{2,1,0:T(1,128)S(1)}, u32[]{:S(2)}, u32[]{:S(2)}) %all-to-all-start.1) | async-done | bytes 32800 | tf_op jit(solution)/shard_map/all_to_all | solution.py:430
  51.0 3.8 %shard_map.102 = (f32[32,1,512]{2,1,0:T(1,128)}, f32[16,128]{1,0:T(8,128)S(1)}) custom-call(s32[1024]{0:T(1024)S(1)} %bitcast.32, f32[32,1,256]{2,1,0:T(1,128)S(1)} %all-to-all-done.1.sums, f32[160,16,128]{2,1,0:T(8,128)S(1)} %get-tuple-element.85.full, f32[65,16,128]{2,1,0:T(8,128)S(1)} %get-tuple-element.86.first.mine.rest_0_, ...), custom_call_target="tpu_custom_call" | custom-call | tf_op jit(solution)/shard_map/pallas_call | solution.py:551
  54.8 5.0 %all-to-all-start.2 = ((f32[32,1,512]{2,1,0:T(1,128)}), f32[32,1,512]{2,1,0:T(1,128)S(1)}, u32[]{:S(2)}, u32[]{:S(2)}) async-start(f32[32,1,512]{2,1,0:T(1,128)} %get-tuple-element.91), calls=%async_computation.2 | async-start | bytes 131072 | tf_op jit(solution)/shard_map/all_to_all | solution.py:430
  59.8 1.8 %collective-permute-start.15 = (f32[16,16,128]{2,1,0:T(8,128)S(1)}, f32[16,16,128]{2,1,0:T(8,128)S(1)}, u32[]{:S(2)}, u32[]{:S(2)}) collective-permute-start(f32[16,16,128]{2,1,0:T(8,128)S(1)} %get-tuple-element.94.rest_2_.rest_3_), channel_id=1, source_target_pairs={{0,4},{1,5},{2,6},{3,7},{4,0},{5,1},{6,2},{7,3},{8,12},{9,13},{10,... | collective-permute-start | bytes 393224 | tf_op jit(solution)/shard_map/ppermute | solution.py:559
  61.7 5.6 %all-to-all-done.2.sums = f32[32,1,512]{2,1,0:T(1,128)S(1)} async-done(((f32[32,1,512]{2,1,0:T(1,128)}), f32[32,1,512]{2,1,0:T(1,128)S(1)}, u32[]{:S(2)}, u32[]{:S(2)}) %all-to-all-start.2) | async-done | bytes 65568 | tf_op jit(solution)/shard_map/all_to_all | solution.py:430
  67.2 1.8 %shard_map.103 = (f32[16,128]{1,0:T(8,128)S(1)}, f32[16,16]{1,0:T(8,128)}, f32[8,128]{1,0:T(8,128)}, s32[8,128]{1,0:T(8,128)}) custom-call(s32[1024]{0:T(1024)S(1)} %bitcast.33, f32[32,1,512]{2,1,0:T(1,128)S(1)} %all-to-all-done.2.sums, f32[16,128]{1,0:T(8,128)S(1)} %get-tuple-element.92.inverse, f32[65,16,128]{2,1,0:T(8,128)S(1)} %get-tuple-element.86.first.mine.rest_0_, ...), custom_call_target="tpu_custom_call" | custom-call | flops 268435456 | tf_op jit(solution)/shard_map/pallas_call | solution.py:560
  69.1 2.2 %shard_map.104 = f32[128,16,128]{2,1,0:T(8,128)} custom-call(s32[1024]{0:T(1024)S(1)} %bitcast.34, f32[16,128]{1,0:T(8,128)S(1)} %get-tuple-element.93.inverse, f32[65,16,128]{2,1,0:T(8,128)S(1)} %get-tuple-element.86.first.mine.rest_0_, f32[24,16,128]{2,1,0:T(8,128)S(1)} %get-tuple-element.87.rest_0_.rest_1_, ...), custom_call_target="tpu_custom_call" | custom-call | tf_op jit(solution)/shard_map/pallas_call | solution.py:572
  (33 shorter events, 2.6 us)
Async XLA Ops:
  0.8 6.5 %copy-start = (f32[1,1,128,8]{2,3,1,0:T(8,128)S(1)}, f32[1,1,128,8]{2,3,1,0:T(8,128)}, u32[]{:S(2)}) copy-start(f32[1,1,128,8]{2,3,1,0:T(8,128)} %param.8) | copy-start | bytes 12292
  0.8 6.5 %copy-start.1 = (s32[1,1,128,8]{2,3,1,0:T(8,128)S(1)}, s32[1,1,128,8]{2,3,1,0:T(8,128)}, u32[]{:S(2)}) copy-start(s32[1,1,128,8]{2,3,1,0:T(8,128)} %param.9) | copy-start | bytes 12292
  0.8 6.5 %copy-start.2 = (s32[1,1,128]{2,1,0:T(1,128)S(1)}, s32[1,1,128]{2,1,0:T(1,128)}, u32[]{:S(2)}) copy-start(s32[1,1,128]{2,1,0:T(1,128)} %param.11) | copy-start | bytes 1540
  2.7 5.3 %collective-permute-start = (f32[8,16,128]{2,1,0:T(8,128)S(1)}, f32[8,16,128]{2,1,0:T(8,128)S(1)}, u32[]{:S(2)}, u32[]{:S(2)}) collective-permute-start(f32[8,16,128]{2,1,0:T(8,128)S(1)} %get-tuple-element.51), channel_id=1, source_target_pairs={{0,8},{1,2},{2,1},{3,4},{4,3},{5,6},{6,5},{7,15},{8,0},{9,10},{10,... | collective-permute-start | bytes 196616 | tf_op jit(solution)/shard_map/ppermute | solution.py:418
  5.8 4.3 %collective-permute-start.1 = (f32[8,16,128]{2,1,0:T(8,128)S(1)}, f32[8,16,128]{2,1,0:T(8,128)S(1)}, u32[]{:S(2)}, u32[]{:S(2)}) collective-permute-start(f32[8,16,128]{2,1,0:T(8,128)S(1)} %get-tuple-element.52), channel_id=1, source_target_pairs={{0,8},{1,9},{2,10},{3,11},{4,12},{5,13},{6,14},{7,15},{8,0},{9,1},... | collective-permute-start | bytes 196616 | tf_op jit(solution)/shard_map/ppermute | solution.py:418
  5.9 4.2 %collective-permute-start.2 = (f32[8,16,128]{2,1,0:T(8,128)S(1)}, f32[8,16,128]{2,1,0:T(8,128)S(1)}, u32[]{:S(2)}, u32[]{:S(2)}) collective-permute-start(f32[8,16,128]{2,1,0:T(8,128)S(1)} %get-tuple-element.53), channel_id=1, source_target_pairs={{0,1},{1,0},{2,3},{3,2},{4,5},{5,4},{6,7},{7,6},{8,16},{9,17},{10,... | collective-permute-start | bytes 196616 | tf_op jit(solution)/shard_map/ppermute | solution.py:418
  7.1 2.9 %collective-permute-start.3 = (f32[8,16,128]{2,1,0:T(8,128)S(1)}, f32[8,16,128]{2,1,0:T(8,128)S(1)}, u32[]{:S(2)}, u32[]{:S(2)}) collective-permute-start(f32[8,16,128]{2,1,0:T(8,128)S(1)} %get-tuple-element.54), channel_id=1, source_target_pairs={{0,1},{1,0},{2,3},{3,2},{4,5},{5,4},{6,7},{7,6},{8,9},{9,8},{10,11... | collective-permute-start | bytes 196616 | tf_op jit(solution)/shard_map/ppermute | solution.py:418
  14.0 9.2 %collective-permute-start.4 = (f32[8,16,128]{2,1,0:T(8,128)S(1)}, f32[8,16,128]{2,1,0:T(8,128)S(1)}, u32[]{:S(2)}, u32[]{:S(2)}) collective-permute-start(f32[8,16,128]{2,1,0:T(8,128)S(1)} %get-tuple-element.67), channel_id=1, source_target_pairs={{0,8},{1,2},{2,1},{3,4},{4,3},{5,6},{6,5},{7,15},{8,0},{9,10},{10,... | collective-permute-start | bytes 196616 | tf_op jit(solution)/shard_map/ppermute | solution.py:418
  16.5 6.7 %collective-permute-start.5 = (f32[8,16,128]{2,1,0:T(8,128)S(1)}, f32[8,16,128]{2,1,0:T(8,128)S(1)}, u32[]{:S(2)}, u32[]{:S(2)}) collective-permute-start(f32[8,16,128]{2,1,0:T(8,128)S(1)} %get-tuple-element.68), channel_id=1, source_target_pairs={{0,8},{1,9},{2,10},{3,11},{4,12},{5,13},{6,14},{7,15},{8,0},{9,1},... | collective-permute-start | bytes 196616 | tf_op jit(solution)/shard_map/ppermute | solution.py:418
  16.6 6.6 %collective-permute-start.6 = (f32[8,16,128]{2,1,0:T(8,128)S(1)}, f32[8,16,128]{2,1,0:T(8,128)S(1)}, u32[]{:S(2)}, u32[]{:S(2)}) collective-permute-start(f32[8,16,128]{2,1,0:T(8,128)S(1)} %get-tuple-element.69), channel_id=1, source_target_pairs={{0,1},{1,0},{2,3},{3,2},{4,5},{5,4},{6,7},{7,6},{8,16},{9,17},{10,... | collective-permute-start | bytes 196616 | tf_op jit(solution)/shard_map/ppermute | solution.py:418
  16.8 6.4 %collective-permute-start.7 = (f32[8,16,128]{2,1,0:T(8,128)S(1)}, f32[8,16,128]{2,1,0:T(8,128)S(1)}, u32[]{:S(2)}, u32[]{:S(2)}) collective-permute-start(f32[8,16,128]{2,1,0:T(8,128)S(1)} %get-tuple-element.70), channel_id=1, source_target_pairs={{0,1},{1,0},{2,3},{3,2},{4,5},{5,4},{6,7},{7,6},{8,9},{9,8},{10,11... | collective-permute-start | bytes 196616 | tf_op jit(solution)/shard_map/ppermute | solution.py:418
  18.4 12.0 %all-to-all-start = ((f32[32,1,256]{2,1,0:T(1,128)}), f32[32,1,256]{2,1,0:T(1,128)S(1)}, u32[]{:S(2)}, u32[]{:S(2)}) async-start(f32[32,1,256]{2,1,0:T(1,128)} %shard_map.97), calls=%async_computation | async-start | bytes 65536 | tf_op jit(solution)/shard_map/all_to_all | solution.py:430
  27.2 5.9 %collective-permute-start.8 = (f32[8,16,128]{2,1,0:T(8,128)S(1)}, f32[8,16,128]{2,1,0:T(8,128)S(1)}, u32[]{:S(2)}, u32[]{:S(2)}) collective-permute-start(f32[8,16,128]{2,1,0:T(8,128)S(1)} %get-tuple-element.73), channel_id=1, source_target_pairs={{0,8},{1,2},{2,1},{3,4},{4,3},{5,6},{6,5},{7,15},{8,0},{9,10},{10,... | collective-permute-start | bytes 196616 | tf_op jit(solution)/shard_map/ppermute | solution.py:418
  29.0 4.3 %collective-permute-start.9 = (f32[8,16,128]{2,1,0:T(8,128)S(1)}, f32[8,16,128]{2,1,0:T(8,128)S(1)}, u32[]{:S(2)}, u32[]{:S(2)}) collective-permute-start(f32[8,16,128]{2,1,0:T(8,128)S(1)} %get-tuple-element.74), channel_id=1, source_target_pairs={{0,8},{1,9},{2,10},{3,11},{4,12},{5,13},{6,14},{7,15},{8,0},{9,1},... | collective-permute-start | bytes 196616 | tf_op jit(solution)/shard_map/ppermute | solution.py:418
  29.3 4.0 %collective-permute-start.10 = (f32[8,16,128]{2,1,0:T(8,128)S(1)}, f32[8,16,128]{2,1,0:T(8,128)S(1)}, u32[]{:S(2)}, u32[]{:S(2)}) collective-permute-start(f32[8,16,128]{2,1,0:T(8,128)S(1)} %get-tuple-element.75), channel_id=1, source_target_pairs={{0,1},{1,0},{2,3},{3,2},{4,5},{5,4},{6,7},{7,6},{8,16},{9,17},{10,... | collective-permute-start | bytes 196616 | tf_op jit(solution)/shard_map/ppermute | solution.py:418
  30.3 3.0 %collective-permute-start.11 = (f32[8,16,128]{2,1,0:T(8,128)S(1)}, f32[8,16,128]{2,1,0:T(8,128)S(1)}, u32[]{:S(2)}, u32[]{:S(2)}) collective-permute-start(f32[8,16,128]{2,1,0:T(8,128)S(1)} %get-tuple-element.76), channel_id=1, source_target_pairs={{0,1},{1,0},{2,3},{3,2},{4,5},{5,4},{6,7},{7,6},{8,9},{9,8},{10,11... | collective-permute-start | bytes 196616 | tf_op jit(solution)/shard_map/ppermute | solution.py:418
  35.6 31.6 %collective-permute-start.12 = (f32[65,16,128]{2,1,0:T(8,128)S(1)}, f32[65,16,128]{2,1,0:T(8,128)S(1)}, u32[]{:S(2)}, u32[]{:S(2)}) collective-permute-start(f32[65,16,128]{2,1,0:T(8,128)S(1)} %get-tuple-element.86.first.mine.rest_0_), channel_id=1, source_target_pairs={{0,4},{1,5},{2,6},{3,7},{4,0},{5,1},{6,2},{7,3},{8,12},{9,13},{10,... | collective-permute-start | bytes 1597448 | tf_op jit(solution)/shard_map/ppermute | solution.py:539
  37.2 13.8 %all-to-all-start.1 = ((f32[32,1,256]{2,1,0:T(1,128)}), f32[32,1,256]{2,1,0:T(1,128)S(1)}, u32[]{:S(2)}, u32[]{:S(2)}) async-start(f32[32,1,256]{2,1,0:T(1,128)} %get-tuple-element.77), calls=%async_computation.1 | async-start | bytes 65536 | tf_op jit(solution)/shard_map/all_to_all | solution.py:430
  43.9 25.2 %collective-permute-start.13 = (f32[24,16,128]{2,1,0:T(8,128)S(1)}, f32[24,16,128]{2,1,0:T(8,128)S(1)}, u32[]{:S(2)}, u32[]{:S(2)}) collective-permute-start(f32[24,16,128]{2,1,0:T(8,128)S(1)} %get-tuple-element.87.rest_0_.rest_1_), channel_id=1, source_target_pairs={{0,4},{1,5},{2,6},{3,7},{4,0},{5,1},{6,2},{7,3},{8,12},{9,13},{10,... | collective-permute-start | bytes 589832 | tf_op jit(solution)/shard_map/ppermute | solution.py:549
  45.7 23.4 %collective-permute-start.14 = (f32[24,16,128]{2,1,0:T(8,128)S(1)}, f32[24,16,128]{2,1,0:T(8,128)S(1)}, u32[]{:S(2)}, u32[]{:S(2)}) collective-permute-start(f32[24,16,128]{2,1,0:T(8,128)S(1)} %get-tuple-element.88.rest_1_.rest_2_), channel_id=1, source_target_pairs={{0,4},{1,5},{2,6},{3,7},{4,0},{5,1},{6,2},{7,3},{8,12},{9,13},{10,... | collective-permute-start | bytes 589832 | tf_op jit(solution)/shard_map/ppermute | solution.py:549
  54.8 12.4 %all-to-all-start.2 = ((f32[32,1,512]{2,1,0:T(1,128)}), f32[32,1,512]{2,1,0:T(1,128)S(1)}, u32[]{:S(2)}, u32[]{:S(2)}) async-start(f32[32,1,512]{2,1,0:T(1,128)} %get-tuple-element.91), calls=%async_computation.2 | async-start | bytes 131072 | tf_op jit(solution)/shard_map/all_to_all | solution.py:430
  59.8 9.2 %collective-permute-start.15 = (f32[16,16,128]{2,1,0:T(8,128)S(1)}, f32[16,16,128]{2,1,0:T(8,128)S(1)}, u32[]{:S(2)}, u32[]{:S(2)}) collective-permute-start(f32[16,16,128]{2,1,0:T(8,128)S(1)} %get-tuple-element.94.rest_2_.rest_3_), channel_id=1, source_target_pairs={{0,4},{1,5},{2,6},{3,7},{4,0},{5,1},{6,2},{7,3},{8,12},{9,13},{10,... | collective-permute-start | bytes 393224 | tf_op jit(solution)/shard_map/ppermute | solution.py:559

commit v11 on v9

--- a/solution.py
+++ b/solution.py
@@ -348,7 +348,7 @@
     rayleigh[...] = unpack(total[:, wide:], cols)[:, :cols]
     last = mine.shape[0] - 1
     both = jnp.concatenate([mine[last], theirs[last]], 1)
-    moved = pltpu.roll(both, 2 * count - order[count], 1)[:, :count]
+    moved = pltpu.roll(both, lax.rem(2 * count - order[count], 2 * count), 1)[:, :count]
     weights[...] = moved[:slots]
     columns[...] = moved[slots:].astype(jnp.int32)
 

time: 69.1 us -> 69 us (level)
  no operation moved by 1% of the time
where the time goes in v11:
time: 69 us; the launch traced here: 68.8 us
  starting transfers between devices  30.7 us (44%)
  Pallas kernels  26.9 us (39%)
  waiting for transfers between devices  10.1 us (15%)
  between operations  0.99 us (1%)
    all_to_all x3, starting transfers between devices, everywhere(): return lax.all_to_all(rows, AXES, 0, 0, tiled=True)  14.2 us
    ppermute x12, starting transfers between devices, pairs(): return lax.ppermute(x, AXES, swap)  10.7 us
    pallas_call x2, Pallas kernels, operator(): call(operator_kernel, [whole] + [piece] * 4, [SMEM] * 3 + [HBM] + [VMEM]...  7.78 us
    all_to_all x3, waiting for transfers between devices, everywhere(): return lax.all_to_all(rows, AXES, 0, 0, tiled=True)  5.95 us
    pallas_call x1, Pallas kernels, per_device(): call(sums_kernel, [shape(devices, 1, 2 * cols * cols), square], [SMEM] +...  3.81 us
    pallas_call x1, Pallas kernels, per_device(): call(last_rest_kernel, [shape(n, cols, cells) for n in later_sizes], [SME...  3.26 us
    ppermute x12, waiting for transfers between devices, pairs(): return lax.ppermute(x, AXES, swap)  2.69 us
    pallas_call x1, Pallas kernels, per_device(): call(scale_kernel, [blocks, square, gram_rows], [VMEM] * 2, [VMEM] * 3, c...  2.6 us
  transfers between devices with their start and end apart: 20, of which 7 were waited for; matrix products, arithmetic and copies ran while one was open for 0% of the time, Pallas kernels for 27%

profile of v11, /device:TPU:0, one launch (start us, length us, event | category | flops | bytes accessed | tf_op | source)
XLA Modules:
  0.0 68.8 jit_solution(4279897498267675847)
XLA Ops:
  0.8 1.9 %shard_map.93 = (f32[128,16,128]{2,1,0:T(8,128)S(1)}, f32[8,128,128]{2,1,0:T(8,128)S(1)}, f32[8,16,128]{2,1,0:T(8,128)S(1)}, f32[8,16,128]{2,1,0:T(8,128)S(1)}, ...) custom-call(s32[8]{0:T(128)S(1)} %stack.51.plan, s32[4,8]{1,0:T(4,128)} %bitcast.48, f32[128,16,128]{2,1,0:T(8,128)} %bitcast.46, ...), custom_call_target="tpu_custom_call" | custom-call | tf_op jit(solution)/shard_map/pallas_call | solution.py:451
  2.7 3.1 %collective-permute-start = (f32[8,16,128]{2,1,0:T(8,128)S(1)}, f32[8,16,128]{2,1,0:T(8,128)S(1)}, u32[]{:S(2)}, u32[]{:S(2)}) collective-permute-start(f32[8,16,128]{2,1,0:T(8,128)S(1)} %get-tuple-element.56), channel_id=1, source_target_pairs={{0,8},{1,2},{2,1},{3,4},{4,3},{5,6},{6,5},{7,15},{8,0},{9,10},{10,... | collective-permute-start | bytes 196616 | tf_op jit(solution)/shard_map/ppermute | solution.py:406
  5.9 1.2 %collective-permute-start.2 = (f32[8,16,128]{2,1,0:T(8,128)S(1)}, f32[8,16,128]{2,1,0:T(8,128)S(1)}, u32[]{:S(2)}, u32[]{:S(2)}) collective-permute-start(f32[8,16,128]{2,1,0:T(8,128)S(1)} %get-tuple-element.58), channel_id=1, source_target_pairs={{0,1},{1,0},{2,3},{3,2},{4,5},{5,4},{6,7},{7,6},{8,16},{9,17},{10,... | collective-permute-start | bytes 196616 | tf_op jit(solution)/shard_map/ppermute | solution.py:406
  8.1 2.0 %collective-permute-done.1.h1 = f32[8,16,128]{2,1,0:T(8,128)S(1)} collective-permute-done((f32[8,16,128]{2,1,0:T(8,128)S(1)}, f32[8,16,128]{2,1,0:T(8,128)S(1)}, u32[]{:S(2)}, u32[]{:S(2)}) %collective-permute-start.1) | collective-permute-done | bytes 65568 | tf_op jit(solution)/shard_map/ppermute | solution.py:406
  10.1 3.9 %shard_map.96 = (f32[128,16,128]{2,1,0:T(8,128)S(1)}, f32[8,16,128]{2,1,0:T(8,128)S(1)}, f32[8,16,128]{2,1,0:T(8,128)S(1)}, f32[8,16,128]{2,1,0:T(8,128)S(1)}, f32[8,16,128]{2,1,0:T(8,128)S(1)}) custom-call(s32[8]{0:T(128)S(1)} %stack.51.plan, s32[1024]{0:T(1024)S(1)} %bitcast.41, f32[1024]{0:T(1024)S(1)} %bitcast.36, ...), custom_call_target="tpu_custom_call", output_to_operand_aliasing={{0}: (4, {})} | custom-call | flops 1610612736 | tf_op jit(solution)/shard_map/pallas_call | solution.py:484
  14.0 2.5 %collective-permute-start.4 = (f32[8,16,128]{2,1,0:T(8,128)S(1)}, f32[8,16,128]{2,1,0:T(8,128)S(1)}, u32[]{:S(2)}, u32[]{:S(2)}) collective-permute-start(f32[8,16,128]{2,1,0:T(8,128)S(1)} %get-tuple-element.72), channel_id=1, source_target_pairs={{0,8},{1,2},{2,1},{3,4},{4,3},{5,6},{6,5},{7,15},{8,0},{9,10},{10,... | collective-permute-start | bytes 196616 | tf_op jit(solution)/shard_map/ppermute | solution.py:406
  17.1 1.3 %shard_map.97 = f32[32,1,256]{2,1,0:T(1,128)} custom-call(f32[128,16,128]{2,1,0:T(8,128)S(1)} %get-tuple-element.71.image.block), custom_call_target="tpu_custom_call" | custom-call | flops 268435456 | tf_op jit(solution)/shard_map/pallas_call | solution.py:506
  18.4 4.8 %all-to-all-start = ((f32[32,1,256]{2,1,0:T(1,128)}), f32[32,1,256]{2,1,0:T(1,128)S(1)}, u32[]{:S(2)}, u32[]{:S(2)}) async-start(f32[32,1,256]{2,1,0:T(1,128)} %shard_map.97), calls=%async_computation | async-start | bytes 65536 | tf_op jit(solution)/shard_map/all_to_all | solution.py:418
  23.2 3.9 %shard_map.98 = (f32[128,16,128]{2,1,0:T(8,128)S(1)}, f32[8,16,128]{2,1,0:T(8,128)S(1)}, f32[8,16,128]{2,1,0:T(8,128)S(1)}, f32[8,16,128]{2,1,0:T(8,128)S(1)}, f32[8,16,128]{2,1,0:T(8,128)S(1)}) custom-call(s32[8]{0:T(128)S(1)} %stack.51.plan, s32[1024]{0:T(1024)S(1)} %bitcast.42, f32[1024]{0:T(1024)S(1)} %bitcast.37, ...), custom_call_target="tpu_custom_call", output_to_operand_aliasing={{0}: (4, {})} | custom-call | flops 1610612736 | tf_op jit(solution)/shard_map/pallas_call | solution.py:484
  27.1 1.8 %collective-permute-start.8 = (f32[8,16,128]{2,1,0:T(8,128)S(1)}, f32[8,16,128]{2,1,0:T(8,128)S(1)}, u32[]{:S(2)}, u32[]{:S(2)}) collective-permute-start(f32[8,16,128]{2,1,0:T(8,128)S(1)} %get-tuple-element.79), channel_id=1, source_target_pairs={{0,8},{1,2},{2,1},{3,4},{4,3},{5,6},{6,5},{7,15},{8,0},{9,10},{10,... | collective-permute-start | bytes 196616 | tf_op jit(solution)/shard_map/ppermute | solution.py:406
  29.2 1.1 %collective-permute-start.10 = (f32[8,16,128]{2,1,0:T(8,128)S(1)}, f32[8,16,128]{2,1,0:T(8,128)S(1)}, u32[]{:S(2)}, u32[]{:S(2)}) collective-permute-start(f32[8,16,128]{2,1,0:T(8,128)S(1)} %get-tuple-element.81), channel_id=1, source_target_pairs={{0,1},{1,0},{2,3},{3,2},{4,5},{5,4},{6,7},{7,6},{8,16},{9,17},{10,... | collective-permute-start | bytes 196616 | tf_op jit(solution)/shard_map/ppermute | solution.py:406
  30.5 2.6 %shard_map.99 = (f32[160,16,128]{2,1,0:T(8,128)S(1)}, f32[16,128]{1,0:T(8,128)S(1)}, f32[32,1,256]{2,1,0:T(1,128)}) custom-call(f32[32,1,256]{2,1,0:T(1,128)S(1)} %all-to-all-done.sums, f32[128,16,128]{2,1,0:T(8,128)S(1)} %get-tuple-element.76.image), custom_call_target="tpu_custom_call" | custom-call | flops 268435456 | tf_op jit(solution)/shard_map/pallas_call | solution.py:511
  33.3 5.1 %all-to-all-start.1 = ((f32[32,1,256]{2,1,0:T(1,128)}), f32[32,1,256]{2,1,0:T(1,128)S(1)}, u32[]{:S(2)}, u32[]{:S(2)}) async-start(f32[32,1,256]{2,1,0:T(1,128)} %get-tuple-element.92), calls=%async_computation.1 | async-start | bytes 65536 | tf_op jit(solution)/shard_map/all_to_all | solution.py:418
  38.4 1.8 %shard_map.100 = (f32[33,16,128]{2,1,0:T(8,128)S(1)}, f32[160,16,128]{2,1,0:T(8,128)S(1)}) custom-call(s32[8]{0:T(128)S(1)} %stack.51.plan, s32[1024]{0:T(1024)S(1)} %bitcast.43, f32[1024]{0:T(1024)S(1)} %bitcast.38, s32[1024]{0:T(1024)S(1)} %bitcast.30, f32[160,16,128]{2,1,0:T(8,128)S(1)} %get-tuple-element.77.own, ...), custom_call_target="tpu_custom_call", output_to_operand_aliasing={{1}: (4, {})} | custom-call | flops 402653184 | tf_op jit(solution)/shard_map/pallas_call | solution.py:517
  40.1 1.7 %collective-permute-start.12 = (f32[33,16,128]{2,1,0:T(8,128)S(1)}, f32[33,16,128]{2,1,0:T(8,128)S(1)}, u32[]{:S(2)}, u32[]{:S(2)}) collective-permute-start(f32[33,16,128]{2,1,0:T(8,128)S(1)} %get-tuple-element.94.first.mine.rest_0_), channel_id=1, source_target_pairs={{0,4},{1,5},{2,6},{3,7},{4,0},{5,1},{6,2},{7,3},{8,12},{9,13},{10,... | collective-permute-start | bytes 811016 | tf_op jit(solution)/shard_map/ppermute | solution.py:527
  41.8 3.3 %shard_map.101 = (f32[32,16,128]{2,1,0:T(8,128)S(1)}, f32[32,16,128]{2,1,0:T(8,128)S(1)}, f32[16,16,128]{2,1,0:T(8,128)S(1)}, f32[16,16,128]{2,1,0:T(8,128)S(1)}) custom-call(s32[1024]{0:T(1024)S(1)} %bitcast.44, f32[1024]{0:T(1024)S(1)} %bitcast.39, s32[1024]{0:T(1024)S(1)} %bitcast.31, f32[160,16,128]{2,1,0:T(8,128)S(1)} %get-tuple-element.89.full, ...), custom_call_target="tpu_custom_call" | custom-call | flops 1207959552 | tf_op jit(solution)/shard_map/pallas_call | solution.py:529
  46.0 1.5 %collective-permute-start.14 = (f32[32,16,128]{2,1,0:T(8,128)S(1)}, f32[32,16,128]{2,1,0:T(8,128)S(1)}, u32[]{:S(2)}, u32[]{:S(2)}) collective-permute-start(f32[32,16,128]{2,1,0:T(8,128)S(1)} %get-tuple-element.102.rest_1_.rest_2_), channel_id=1, source_target_pairs={{0,4},{1,5},{2,6},{3,7},{4,0},{5,1},{6,2},{7,3},{8,12},{9,13},{10,... | collective-permute-start | bytes 786440 | tf_op jit(solution)/shard_map/ppermute | solution.py:538
  47.5 3.8 %shard_map.102 = (f32[32,1,512]{2,1,0:T(1,128)}, f32[16,128]{1,0:T(8,128)S(1)}) custom-call(s32[1024]{0:T(1024)S(1)} %bitcast.32, f32[32,1,256]{2,1,0:T(1,128)S(1)} %all-to-all-done.1.sums, f32[160,16,128]{2,1,0:T(8,128)S(1)} %get-tuple-element.89.full, f32[33,16,128]{2,1,0:T(8,128)S(1)} %get-tuple-element.94.first.mine.rest_0_, ...), custom_call_target="tpu_custom_call" | custom-call | tf_op jit(solution)/shard_map/pallas_call | solution.py:540
  51.3 4.3 %all-to-all-start.2 = ((f32[32,1,512]{2,1,0:T(1,128)}), f32[32,1,512]{2,1,0:T(1,128)S(1)}, u32[]{:S(2)}, u32[]{:S(2)}) async-start(f32[32,1,512]{2,1,0:T(1,128)} %get-tuple-element.98), calls=%async_computation.2 | async-start | bytes 131072 | tf_op jit(solution)/shard_map/all_to_all | solution.py:418
  55.6 1.8 %collective-permute-start.15 = (f32[16,16,128]{2,1,0:T(8,128)S(1)}, f32[16,16,128]{2,1,0:T(8,128)S(1)}, u32[]{:S(2)}, u32[]{:S(2)}) collective-permute-start(f32[16,16,128]{2,1,0:T(8,128)S(1)} %get-tuple-element.103.rest_2_.rest_3_), channel_id=1, source_target_pairs={{0,4},{1,5},{2,6},{3,7},{4,0},{5,1},{6,2},{7,3},{8,12},{9,13},{10,... | collective-permute-start | bytes 393224 | tf_op jit(solution)/shard_map/ppermute | solution.py:548
  57.7 5.4 %all-to-all-done.2.sums = f32[32,1,512]{2,1,0:T(1,128)S(1)} async-done(((f32[32,1,512]{2,1,0:T(1,128)}), f32[32,1,512]{2,1,0:T(1,128)S(1)}, u32[]{:S(2)}, u32[]{:S(2)}) %all-to-all-start.2) | async-done | bytes 65568 | tf_op jit(solution)/shard_map/all_to_all | solution.py:418
  63.1 1.8 %shard_map.103 = (f32[16,128]{1,0:T(8,128)S(1)}, f32[16,16]{1,0:T(8,128)}, f32[8,128]{1,0:T(8,128)}, s32[8,128]{1,0:T(8,128)}) custom-call(s32[1024]{0:T(1024)S(1)} %bitcast.33, f32[32,1,512]{2,1,0:T(1,128)S(1)} %all-to-all-done.2.sums, f32[16,128]{1,0:T(8,128)S(1)} %get-tuple-element.99.inverse, f32[33,16,128]{2,1,0:T(8,128)S(1)} %get-tuple-element.94.first.mine.rest_0_, ...), custom_call_target="tpu_custom_call" | custom-call | flops 268435456 | tf_op jit(solution)/shard_map/pallas_call | solution.py:549
  65.0 1.5 %collective-permute-done.16.rest_9_ = f32[16,16,128]{2,1,0:T(8,128)S(1)} collective-permute-done((f32[16,16,128]{2,1,0:T(8,128)S(1)}, f32[16,16,128]{2,1,0:T(8,128)S(1)}, u32[]{:S(2)}, u32[]{:S(2)}) %collective-permute-start.16) | collective-permute-done | bytes 131104 | tf_op jit(solution)/shard_map/ppermute | solution.py:548
  66.4 2.2 %shard_map.104 = f32[128,16,128]{2,1,0:T(8,128)} custom-call(s32[1024]{0:T(1024)S(1)} %bitcast.34, f32[16,128]{1,0:T(8,128)S(1)} %get-tuple-element.100.inverse, f32[33,16,128]{2,1,0:T(8,128)S(1)} %get-tuple-element.94.first.mine.rest_0_, f32[32,16,128]{2,1,0:T(8,128)S(1)} %get-tuple-element.101.rest_0_.rest_1_, ...), custom_call_target="tpu_custom_call" | custom-call | tf_op jit(solution)/shard_map/pallas_call | solution.py:561
  (35 shorter events, 3.5 us)
Async XLA Ops:
  0.8 6.5 %copy-start = (f32[1,1,128,8]{2,3,1,0:T(8,128)S(1)}, f32[1,1,128,8]{2,3,1,0:T(8,128)}, u32[]{:S(2)}) copy-start(f32[1,1,128,8]{2,3,1,0:T(8,128)} %param.8) | copy-start | bytes 12292
  0.8 6.5 %copy-start.1 = (s32[1,1,128,8]{2,3,1,0:T(8,128)S(1)}, s32[1,1,128,8]{2,3,1,0:T(8,128)}, u32[]{:S(2)}) copy-start(s32[1,1,128,8]{2,3,1,0:T(8,128)} %param.9) | copy-start | bytes 12292
  0.8 6.5 %copy-start.2 = (s32[1,1,128]{2,1,0:T(1,128)S(1)}, s32[1,1,128]{2,1,0:T(1,128)}, u32[]{:S(2)}) copy-start(s32[1,1,128]{2,1,0:T(1,128)} %param.11) | copy-start | bytes 1540
  2.7 5.3 %collective-permute-start = (f32[8,16,128]{2,1,0:T(8,128)S(1)}, f32[8,16,128]{2,1,0:T(8,128)S(1)}, u32[]{:S(2)}, u32[]{:S(2)}) collective-permute-start(f32[8,16,128]{2,1,0:T(8,128)S(1)} %get-tuple-element.56), channel_id=1, source_target_pairs={{0,8},{1,2},{2,1},{3,4},{4,3},{5,6},{6,5},{7,15},{8,0},{9,10},{10,... | collective-permute-start | bytes 196616 | tf_op jit(solution)/shard_map/ppermute | solution.py:406
  5.8 4.3 %collective-permute-start.1 = (f32[8,16,128]{2,1,0:T(8,128)S(1)}, f32[8,16,128]{2,1,0:T(8,128)S(1)}, u32[]{:S(2)}, u32[]{:S(2)}) collective-permute-start(f32[8,16,128]{2,1,0:T(8,128)S(1)} %get-tuple-element.57), channel_id=1, source_target_pairs={{0,8},{1,9},{2,10},{3,11},{4,12},{5,13},{6,14},{7,15},{8,0},{9,1},... | collective-permute-start | bytes 196616 | tf_op jit(solution)/shard_map/ppermute | solution.py:406
  5.9 4.2 %collective-permute-start.2 = (f32[8,16,128]{2,1,0:T(8,128)S(1)}, f32[8,16,128]{2,1,0:T(8,128)S(1)}, u32[]{:S(2)}, u32[]{:S(2)}) collective-permute-start(f32[8,16,128]{2,1,0:T(8,128)S(1)} %get-tuple-element.58), channel_id=1, source_target_pairs={{0,1},{1,0},{2,3},{3,2},{4,5},{5,4},{6,7},{7,6},{8,16},{9,17},{10,... | collective-permute-start | bytes 196616 | tf_op jit(solution)/shard_map/ppermute | solution.py:406
  7.1 2.9 %collective-permute-start.3 = (f32[8,16,128]{2,1,0:T(8,128)S(1)}, f32[8,16,128]{2,1,0:T(8,128)S(1)}, u32[]{:S(2)}, u32[]{:S(2)}) collective-permute-start(f32[8,16,128]{2,1,0:T(8,128)S(1)} %get-tuple-element.59), channel_id=1, source_target_pairs={{0,1},{1,0},{2,3},{3,2},{4,5},{5,4},{6,7},{7,6},{8,9},{9,8},{10,11... | collective-permute-start | bytes 196616 | tf_op jit(solution)/shard_map/ppermute | solution.py:406
  14.0 9.2 %collective-permute-start.4 = (f32[8,16,128]{2,1,0:T(8,128)S(1)}, f32[8,16,128]{2,1,0:T(8,128)S(1)}, u32[]{:S(2)}, u32[]{:S(2)}) collective-permute-start(f32[8,16,128]{2,1,0:T(8,128)S(1)} %get-tuple-element.72), channel_id=1, source_target_pairs={{0,8},{1,2},{2,1},{3,4},{4,3},{5,6},{6,5},{7,15},{8,0},{9,10},{10,... | collective-permute-start | bytes 196616 | tf_op jit(solution)/shard_map/ppermute | solution.py:406
  16.5 6.7 %collective-permute-start.5 = (f32[8,16,128]{2,1,0:T(8,128)S(1)}, f32[8,16,128]{2,1,0:T(8,128)S(1)}, u32[]{:S(2)}, u32[]{:S(2)}) collective-permute-start(f32[8,16,128]{2,1,0:T(8,128)S(1)} %get-tuple-element.73), channel_id=1, source_target_pairs={{0,8},{1,9},{2,10},{3,11},{4,12},{5,13},{6,14},{7,15},{8,0},{9,1},... | collective-permute-start | bytes 196616 | tf_op jit(solution)/shard_map/ppermute | solution.py:406
  16.6 6.6 %collective-permute-start.6 = (f32[8,16,128]{2,1,0:T(8,128)S(1)}, f32[8,16,128]{2,1,0:T(8,128)S(1)}, u32[]{:S(2)}, u32[]{:S(2)}) collective-permute-start(f32[8,16,128]{2,1,0:T(8,128)S(1)} %get-tuple-element.74), channel_id=1, source_target_pairs={{0,1},{1,0},{2,3},{3,2},{4,5},{5,4},{6,7},{7,6},{8,16},{9,17},{10,... | collective-permute-start | bytes 196616 | tf_op jit(solution)/shard_map/ppermute | solution.py:406
  16.8 6.4 %collective-permute-start.7 = (f32[8,16,128]{2,1,0:T(8,128)S(1)}, f32[8,16,128]{2,1,0:T(8,128)S(1)}, u32[]{:S(2)}, u32[]{:S(2)}) collective-permute-start(f32[8,16,128]{2,1,0:T(8,128)S(1)} %get-tuple-element.75), channel_id=1, source_target_pairs={{0,1},{1,0},{2,3},{3,2},{4,5},{5,4},{6,7},{7,6},{8,9},{9,8},{10,11... | collective-permute-start | bytes 196616 | tf_op jit(solution)/shard_map/ppermute | solution.py:406
  18.4 12.0 %all-to-all-start = ((f32[32,1,256]{2,1,0:T(1,128)}), f32[32,1,256]{2,1,0:T(1,128)S(1)}, u32[]{:S(2)}, u32[]{:S(2)}) async-start(f32[32,1,256]{2,1,0:T(1,128)} %shard_map.97), calls=%async_computation | async-start | bytes 65536 | tf_op jit(solution)/shard_map/all_to_all | solution.py:418
  27.1 5.9 %collective-permute-start.8 = (f32[8,16,128]{2,1,0:T(8,128)S(1)}, f32[8,16,128]{2,1,0:T(8,128)S(1)}, u32[]{:S(2)}, u32[]{:S(2)}) collective-permute-start(f32[8,16,128]{2,1,0:T(8,128)S(1)} %get-tuple-element.79), channel_id=1, source_target_pairs={{0,8},{1,2},{2,1},{3,4},{4,3},{5,6},{6,5},{7,15},{8,0},{9,10},{10,... | collective-permute-start | bytes 196616 | tf_op jit(solution)/shard_map/ppermute | solution.py:406
  29.0 4.3 %collective-permute-start.9 = (f32[8,16,128]{2,1,0:T(8,128)S(1)}, f32[8,16,128]{2,1,0:T(8,128)S(1)}, u32[]{:S(2)}, u32[]{:S(2)}) collective-permute-start(f32[8,16,128]{2,1,0:T(8,128)S(1)} %get-tuple-element.80), channel_id=1, source_target_pairs={{0,8},{1,9},{2,10},{3,11},{4,12},{5,13},{6,14},{7,15},{8,0},{9,1},... | collective-permute-start | bytes 196616 | tf_op jit(solution)/shard_map/ppermute | solution.py:406
  29.2 4.0 %collective-permute-start.10 = (f32[8,16,128]{2,1,0:T(8,128)S(1)}, f32[8,16,128]{2,1,0:T(8,128)S(1)}, u32[]{:S(2)}, u32[]{:S(2)}) collective-permute-start(f32[8,16,128]{2,1,0:T(8,128)S(1)} %get-tuple-element.81), channel_id=1, source_target_pairs={{0,1},{1,0},{2,3},{3,2},{4,5},{5,4},{6,7},{7,6},{8,16},{9,17},{10,... | collective-permute-start | bytes 196616 | tf_op jit(solution)/shard_map/ppermute | solution.py:406
  30.3 3.0 %collective-permute-start.11 = (f32[8,16,128]{2,1,0:T(8,128)S(1)}, f32[8,16,128]{2,1,0:T(8,128)S(1)}, u32[]{:S(2)}, u32[]{:S(2)}) collective-permute-start(f32[8,16,128]{2,1,0:T(8,128)S(1)} %get-tuple-element.82), channel_id=1, source_target_pairs={{0,1},{1,0},{2,3},{3,2},{4,5},{5,4},{6,7},{7,6},{8,9},{9,8},{10,11... | collective-permute-start | bytes 196616 | tf_op jit(solution)/shard_map/ppermute | solution.py:406
  33.3 12.2 %all-to-all-start.1 = ((f32[32,1,256]{2,1,0:T(1,128)}), f32[32,1,256]{2,1,0:T(1,128)S(1)}, u32[]{:S(2)}, u32[]{:S(2)}) async-start(f32[32,1,256]{2,1,0:T(1,128)} %get-tuple-element.92), calls=%async_computation.1 | async-start | bytes 65536 | tf_op jit(solution)/shard_map/all_to_all | solution.py:418
  40.1 23.0 %collective-permute-start.12 = (f32[33,16,128]{2,1,0:T(8,128)S(1)}, f32[33,16,128]{2,1,0:T(8,128)S(1)}, u32[]{:S(2)}, u32[]{:S(2)}) collective-permute-start(f32[33,16,128]{2,1,0:T(8,128)S(1)} %get-tuple-element.94.first.mine.rest_0_), channel_id=1, source_target_pairs={{0,4},{1,5},{2,6},{3,7},{4,0},{5,1},{6,2},{7,3},{8,12},{9,13},{10,... | collective-permute-start | bytes 811016 | tf_op jit(solution)/shard_map/ppermute | solution.py:527
  45.4 21.0 %collective-permute-start.13 = (f32[32,16,128]{2,1,0:T(8,128)S(1)}, f32[32,16,128]{2,1,0:T(8,128)S(1)}, u32[]{:S(2)}, u32[]{:S(2)}) collective-permute-start(f32[32,16,128]{2,1,0:T(8,128)S(1)} %get-tuple-element.101.rest_0_.rest_1_), channel_id=1, source_target_pairs={{0,4},{1,5},{2,6},{3,7},{4,0},{5,1},{6,2},{7,3},{8,12},{9,13},{10,... | collective-permute-start | bytes 786440 | tf_op jit(solution)/shard_map/ppermute | solution.py:538
  46.0 20.4 %collective-permute-start.14 = (f32[32,16,128]{2,1,0:T(8,128)S(1)}, f32[32,16,128]{2,1,0:T(8,128)S(1)}, u32[]{:S(2)}, u32[]{:S(2)}) collective-permute-start(f32[32,16,128]{2,1,0:T(8,128)S(1)} %get-tuple-element.102.rest_1_.rest_2_), channel_id=1, source_target_pairs={{0,4},{1,5},{2,6},{3,7},{4,0},{5,1},{6,2},{7,3},{8,12},{9,13},{10,... | collective-permute-start | bytes 786440 | tf_op jit(solution)/shard_map/ppermute | solution.py:538
  51.3 11.8 %all-to-all-start.2 = ((f32[32,1,512]{2,1,0:T(1,128)}), f32[32,1,512]{2,1,0:T(1,128)S(1)}, u32[]{:S(2)}, u32[]{:S(2)}) async-start(f32[32,1,512]{2,1,0:T(1,128)} %get-tuple-element.98), calls=%async_computation.2 | async-start | bytes 131072 | tf_op jit(solution)/shard_map/all_to_all | solution.py:418
  55.6 9.3 %collective-permute-start.15 = (f32[16,16,128]{2,1,0:T(8,128)S(1)}, f32[16,16,128]{2,1,0:T(8,128)S(1)}, u32[]{:S(2)}, u32[]{:S(2)}) collective-permute-start(f32[16,16,128]{2,1,0:T(8,128)S(1)} %get-tuple-element.103.rest_2_.rest_3_), channel_id=1, source_target_pairs={{0,4},{1,5},{2,6},{3,7},{4,0},{5,1},{6,2},{7,3},{8,12},{9,13},{10,... | collective-permute-start | bytes 393224 | tf_op jit(solution)/shard_map/ppermute | solution.py:548
  57.5 9.0 %collective-permute-start.16 = (f32[16,16,128]{2,1,0:T(8,128)S(1)}, f32[16,16,128]{2,1,0:T(8,128)S(1)}, u32[]{:S(2)}, u32[]{:S(2)}) collective-permute-start(f32[16,16,128]{2,1,0:T(8,128)S(1)} %get-tuple-element.104.rest_3_.rest_4_), channel_id=1, source_target_pairs={{0,4},{1,5},{2,6},{3,7},{4,0},{5,1},{6,2},{7,3},{8,12},{9,13},{10,... | collective-permute-start | bytes 393224 | tf_op jit(solution)/shard_map/ppermute | solution.py:548
